TPU v7x, 32 devices: a whole 2x2x4 slice. The times are simulated.
32 devices in a mesh: ctx: 8 (over z, x), fsdp: 4 (over y, core).
Axes of the slice: x: 2, y: 2, z: 4, core: 2. Of those that a mesh axis runs over, the one named last changes fastest.
Arguments:
- hidden: bfloat16 [4, 1024, 768], P('fsdp', 'ctx'), may hold values from -6 to 6
- neighbours: bfloat16 [4, 16, 256, 768], P('fsdp', 'ctx'), may hold values from -6 to 6
- cotangent: bfloat16 [4, 1024, 768], P('fsdp', 'ctx'), may hold values from -6 to 6
- stretch_deal: int32 [4, 16], P('fsdp'), may hold values from 0 to 15, as said below
- seq_lengths: int32 [4, 3], P('fsdp'), may hold values from 1 to 8, 16 in all within a row
- norm_gains: bfloat16 [3, 768], P(None, 'fsdp'), may hold values from 0.5 to 1.5
- attn_qkv: bfloat16 [768, 2304], P('fsdp'), may hold values from -0.21875 to 0.21875
- attn_out: bfloat16 [768, 768], P('fsdp'), may hold values from -1.5 to 1.5
- cross_q: bfloat16 [768, 768], P('fsdp'), may hold values from -0.21875 to 0.21875
- cross_kv: bfloat16 [768, 1536], P('fsdp'), may hold values from -0.21875 to 0.21875
- cross_out: bfloat16 [768, 768], P('fsdp'), may hold values from -0.875 to 0.875
- mlp_in: bfloat16 [768, 3072], P('fsdp'), may hold values from -0.21875 to 0.21875
- mlp_out: bfloat16 [3072, 768], P('fsdp'), may hold values from -0.109375 to 0.109375
Outputs:
- layer_out: float32 [4, 1024, 768], P('fsdp', 'ctx')
- grad_hidden: float32 [4, 1024, 768], P('fsdp', 'ctx')
- grad_neighbours: float32 [4, 16, 256, 768], P('fsdp', 'ctx')
- grad_norm_gains: float32 [3, 768], P(None, 'fsdp')
- grad_attn_qkv: float32 [768, 2304], P('fsdp')
- grad_attn_out: float32 [768, 768], P('fsdp')
- grad_cross_q: float32 [768, 768], P('fsdp')
- grad_cross_kv: float32 [768, 1536], P('fsdp')
- grad_cross_out: float32 [768, 768], P('fsdp')
- grad_mlp_in: float32 [768, 3072], P('fsdp')
- grad_mlp_out: float32 [3072, 768], P('fsdp')
Inputs may be any that keep to these rules, and one draw needn't show every extreme that they name: `stretch_deal`: each row is a permutation of the 16 stretches of a group; the 2 slots of one device hold a block of 1 given stretches in a row, then the mirror block counted from the group's end. `seq_lengths`: A row holds the lengths of a group's sequences, which fill its 16 stretches in given order.
All inputs are finite; a program needn't handle non-finite values.
Results may differ from a plain program's by a relative error of at most 0.025.
Values may be sent and summed in bfloat16 or wider, within the bound.
No kernel may reach another device: no remote copies, remote signals or barrier semaphores. Data moves between devices by JAX's collectives and lax.ppermute only.
A program may use at most 256 MiB of HBM per device.

v0:
```python
import jax
import jax.numpy as jnp
from jax import lax
from jax.sharding import PartitionSpec as P

H = 12
STRETCH = 64


NORM_EPS = 1e-06
MASKED_SCORE = -1e30


def rms_norm(values, norm_gain):
    return (
        values * lax.rsqrt(jnp.mean(values * values, axis=-1, keepdims=True) + NORM_EPS) * norm_gain
    )


def gelu_exact(values):
    return jax.nn.gelu(values, approximate=False)


def to_low(values):
    return values.astype(jnp.bfloat16)


def matmul(left, right):
    return jnp.dot(left, right, preferred_element_type=jnp.float32)


def left_product(left, right):
    return jnp.einsum("td,te->de", left, right, preferred_element_type=jnp.float32)


def right_product(left, right):
    return jnp.einsum("te,de->td", left, right, preferred_element_type=jnp.float32)


def visible_mask(query_pos, query_seq, key_pos, key_seq):
    return (query_seq[:, None] == key_seq[None, :]) & (key_pos[None, :] <= query_pos[:, None])


def local(
    hidden,
    neighbours,
    cotangent,
    stretch_deal,
    seq_lengths,
    norm_gains,
    attn_qkv,
    attn_out,
    cross_q,
    cross_kv,
    cross_out,
    mlp_in,
    mlp_out,
):
    gathered = (
        lax.all_gather(norm_gains, "fsdp", axis=1, tiled=True),
        lax.all_gather(attn_qkv, "fsdp", axis=0, tiled=True),
        lax.all_gather(attn_out, "fsdp", axis=0, tiled=True),
        lax.all_gather(cross_q, "fsdp", axis=0, tiled=True),
        lax.all_gather(cross_kv, "fsdp", axis=0, tiled=True),
        lax.all_gather(cross_out, "fsdp", axis=0, tiled=True),
        lax.all_gather(mlp_in, "fsdp", axis=0, tiled=True),
        lax.all_gather(mlp_out, "fsdp", axis=0, tiled=True),
    )
    gain_rows = gathered[0].astype(jnp.float32)
    w_qkv = gathered[1]
    w_out = gathered[2]
    w_cq = gathered[3]
    w_ckv = gathered[4]
    w_cout = gathered[5]
    w_in = gathered[6]
    w_down = gathered[7]
    input_rows = hidden[0].astype(jnp.float32)
    tok_count = input_rows.shape[0]
    feature_width = input_rows.shape[1]
    head_size = feature_width // H
    score_scale = head_size ** (-0.5)
    stretch_count = tok_count // STRETCH
    ctx_index = lax.axis_index("ctx")
    deal_row = stretch_deal[0]
    lengths_row = seq_lengths[0]
    group_tok = deal_row.shape[0] * STRETCH
    block_rows = min(512, group_tok)
    block_count = group_tok // block_rows
    seq_ends = jnp.cumsum(lengths_row)
    seq_starts = seq_ends - lengths_row
    slot_seq = jnp.sum((seq_ends[None, :] <= deal_row[:, None]).astype(jnp.int32), axis=1)
    slot_first = jnp.any(seq_starts[None, :] == deal_row[:, None], axis=1)
    offsets = jnp.arange(STRETCH, dtype=jnp.int32)
    token_pos = (deal_row[:, None] * STRETCH + offsets[None, :]).reshape(group_tok)
    token_seq = (slot_seq[:, None] + 0 * offsets[None, :]).reshape(group_tok)
    query_pos = lax.dynamic_slice_in_dim(token_pos, ctx_index * tok_count, tok_count)
    query_seq = lax.dynamic_slice_in_dim(token_seq, ctx_index * tok_count, tok_count)
    keep_stretch = 1.0 - lax.dynamic_slice_in_dim(
        slot_first.astype(jnp.float32), ctx_index * stretch_count, stretch_count
    )
    keep_rows = jnp.repeat(keep_stretch, STRETCH)[:, None]
    norm_one, norm_one_back = jax.vjp(rms_norm, input_rows, gain_rows[0])
    norm_one_low = to_low(norm_one)
    projected = matmul(norm_one_low, w_qkv)
    query_low = to_low(projected[:, :feature_width])
    key_low = to_low(projected[:, feature_width : 2 * feature_width])
    value_low = to_low(projected[:, 2 * feature_width :])
    keys_all, values_all = (
        lax.all_gather(key_low, "ctx", axis=0, tiled=True),
        lax.all_gather(value_low, "ctx", axis=0, tiled=True),
    )
    query_heads = query_low.reshape(tok_count, H, head_size)

    def key_block(block_index):
        row_start = block_index * block_rows
        key_heads = lax.dynamic_slice_in_dim(keys_all, row_start, block_rows).reshape(
            block_rows, H, head_size
        )
        value_heads = lax.dynamic_slice_in_dim(values_all, row_start, block_rows).reshape(
            block_rows, H, head_size
        )
        key_pos = lax.dynamic_slice_in_dim(token_pos, row_start, block_rows)
        key_seq = lax.dynamic_slice_in_dim(token_seq, row_start, block_rows)
        visible = visible_mask(query_pos, query_seq, key_pos, key_seq)[None]
        scores = (
            jnp.einsum("qhd,khd->hqk", query_heads, key_heads, preferred_element_type=jnp.float32)
            * score_scale
        )
        return (scores, visible, key_heads, value_heads)

    def online_step(block_index, state):
        row_peak, row_total, running = state
        scores, visible, key_heads, value_heads = key_block(block_index)
        masked = jnp.where(visible, scores, MASKED_SCORE)
        new_peak = jnp.maximum(row_peak, jnp.max(masked, axis=-1))
        rescale = jnp.exp(row_peak - new_peak)
        weights = jnp.where(visible, jnp.exp(masked - new_peak[..., None]), 0.0)
        new_total = row_total * rescale + jnp.sum(weights, axis=-1)
        new_running = running * jnp.transpose(rescale)[:, :, None] + jnp.einsum(
            "hqk,khd->qhd", to_low(weights), value_heads, preferred_element_type=jnp.float32
        )
        return (new_peak, new_total, new_running)

    start_state = (
        jnp.full((H, tok_count), MASKED_SCORE, jnp.float32),
        jnp.zeros((H, tok_count), jnp.float32),
        jnp.zeros((tok_count, H, head_size), jnp.float32),
    )
    row_peak, row_total, running = lax.fori_loop(0, block_count, online_step, start_state)
    log_total = row_peak + jnp.log(row_total)
    attended = running / jnp.transpose(row_total)[:, :, None]

    def block_probs(scores, visible):
        return jnp.where(visible, jnp.exp(scores - log_total[..., None]), 0.0)

    attended_low = to_low(attended.reshape(tok_count, feature_width))
    after_attn = input_rows + matmul(attended_low, w_out)
    norm_two, norm_two_back = jax.vjp(rms_norm, after_attn, gain_rows[1])
    norm_two_low = to_low(norm_two)
    cross_query = to_low(matmul(norm_two_low, w_cq)).reshape(stretch_count, STRETCH, H, head_size)
    enc_rows = neighbours[0].reshape(-1, feature_width)
    cross_proj = matmul(enc_rows, w_ckv)
    cross_key = to_low(cross_proj[:, :feature_width]).reshape(stretch_count, -1, H, head_size)
    cross_value = to_low(cross_proj[:, feature_width:]).reshape(stretch_count, -1, H, head_size)
    cross_scores = (
        jnp.einsum("cqhd,ckhd->chqk", cross_query, cross_key, preferred_element_type=jnp.float32)
        * score_scale
    )
    cross_probs = jax.nn.softmax(cross_scores, axis=-1)
    cross_low = to_low(cross_probs)
    cross_rows = jnp.einsum(
        "chqk,ckhd->cqhd", cross_low, cross_value, preferred_element_type=jnp.float32
    )
    cross_rows_low = to_low(cross_rows.reshape(tok_count, feature_width))
    after_cross = after_attn + keep_rows * matmul(cross_rows_low, w_cout)
    norm_three, norm_three_back = jax.vjp(rms_norm, after_cross, gain_rows[2])
    norm_three_low = to_low(norm_three)
    inner_rows = matmul(norm_three_low, w_in)
    activation, activation_back = jax.vjp(gelu_exact, inner_rows)
    activation_low = to_low(activation)
    layer_out = after_cross + matmul(activation_low, w_down)
    regathered = (
        lax.all_gather(attn_qkv, "fsdp", axis=0, tiled=True),
        lax.all_gather(attn_out, "fsdp", axis=0, tiled=True),
        lax.all_gather(cross_q, "fsdp", axis=0, tiled=True),
        lax.all_gather(cross_kv, "fsdp", axis=0, tiled=True),
        lax.all_gather(cross_out, "fsdp", axis=0, tiled=True),
        lax.all_gather(mlp_in, "fsdp", axis=0, tiled=True),
        lax.all_gather(mlp_out, "fsdp", axis=0, tiled=True),
    )
    w_qkv = regathered[0]
    w_out = regathered[1]
    w_cq = regathered[2]
    w_ckv = regathered[3]
    w_cout = regathered[4]
    w_in = regathered[5]
    w_down = regathered[6]
    grad_out = cotangent[0].astype(jnp.float32)
    grad_branch = cotangent[0]
    grad_down = left_product(activation_low, grad_branch)
    grad_activation = right_product(grad_branch, w_down)
    grad_inner = to_low(activation_back(grad_activation)[0])
    grad_in = left_product(norm_three_low, grad_inner)
    grad_norm3 = right_product(grad_inner, w_in)
    grad_after_norm3, grad_gain3 = norm_three_back(grad_norm3)
    grad_after_cross = grad_out + grad_after_norm3
    grad_cross_branch = to_low(keep_rows * grad_after_cross)
    grad_cout = left_product(cross_rows_low, grad_cross_branch)
    grad_cross_rows = to_low(right_product(grad_cross_branch, w_cout)).reshape(
        stretch_count, STRETCH, H, head_size
    )
    cross_dprobs = jnp.einsum(
        "cqhd,ckhd->chqk", grad_cross_rows, cross_value, preferred_element_type=jnp.float32
    )
    cross_dscores = to_low(
        cross_probs * (cross_dprobs - jnp.sum(cross_probs * cross_dprobs, axis=-1, keepdims=True))
    )
    grad_cross_query = to_low(
        score_scale
        * jnp.einsum(
            "chqk,ckhd->cqhd", cross_dscores, cross_key, preferred_element_type=jnp.float32
        )
    ).reshape(tok_count, feature_width)
    grad_cross_key = to_low(
        score_scale
        * jnp.einsum(
            "chqk,cqhd->ckhd", cross_dscores, cross_query, preferred_element_type=jnp.float32
        )
    ).reshape(-1, feature_width)
    grad_cross_value = to_low(
        jnp.einsum(
            "chqk,cqhd->ckhd", cross_low, grad_cross_rows, preferred_element_type=jnp.float32
        )
    ).reshape(-1, feature_width)
    grad_cq = left_product(norm_two_low, grad_cross_query)
    grad_norm2 = right_product(grad_cross_query, w_cq)
    grad_cross_pair = jnp.concatenate([grad_cross_key, grad_cross_value], axis=1)
    grad_ckv = left_product(enc_rows, grad_cross_pair)
    grad_enc = right_product(grad_cross_pair, w_ckv).reshape(neighbours.shape)
    grad_after_norm2, grad_gain2 = norm_two_back(grad_norm2)
    grad_after_attn = grad_after_cross + grad_after_norm2
    grad_attn_branch = to_low(grad_after_attn)
    grad_attn_out = left_product(attended_low, grad_attn_branch)
    grad_attended = to_low(right_product(grad_attn_branch, w_out))
    grad_heads = grad_attended.reshape(tok_count, H, head_size)
    row_delta = jnp.transpose(jnp.sum(grad_heads.astype(jnp.float32) * attended, axis=-1))

    def score_grads(block_index):
        scores, visible, key_heads, value_heads = key_block(block_index)
        attn_probs = block_probs(scores, visible)
        grad_probs = jnp.einsum(
            "qhd,khd->hqk", grad_heads, value_heads, preferred_element_type=jnp.float32
        )
        grad_scores = to_low(attn_probs * (grad_probs - row_delta[..., None]))
        return (attn_probs, grad_scores, key_heads)

    def summed_step(carried, block_index):
        attn_probs, grad_scores, key_heads = score_grads(block_index)
        carried = carried + score_scale * jnp.einsum(
            "hqk,khd->qhd", grad_scores, key_heads, preferred_element_type=jnp.float32
        )
        key_terms = score_scale * jnp.einsum(
            "hqk,qhd->khd", grad_scores, query_heads, preferred_element_type=jnp.float32
        )
        value_terms = jnp.einsum(
            "hqk,qhd->khd", to_low(attn_probs), grad_heads, preferred_element_type=jnp.float32
        )
        return (
            carried,
            (
                key_terms.reshape(block_rows, feature_width),
                value_terms.reshape(block_rows, feature_width),
            ),
        )

    grad_query, key_value_terms = lax.scan(
        summed_step,
        jnp.zeros((tok_count, H, head_size), jnp.float32),
        jnp.arange(block_count, dtype=jnp.int32),
    )
    grad_key, grad_value = (
        lax.psum_scatter(
            key_value_terms[0].reshape(group_tok, feature_width),
            "ctx",
            scatter_dimension=0,
            tiled=True,
        ),
        lax.psum_scatter(
            key_value_terms[1].reshape(group_tok, feature_width),
            "ctx",
            scatter_dimension=0,
            tiled=True,
        ),
    )
    grad_qkv_low = jnp.concatenate(
        [
            to_low(grad_query.reshape(tok_count, feature_width)),
            to_low(grad_key),
            to_low(grad_value),
        ],
        axis=1,
    )
    grad_qkv = left_product(norm_one_low, grad_qkv_low)
    grad_norm1 = right_product(grad_qkv_low, w_qkv)
    grad_input_norm, grad_gain1 = norm_one_back(grad_norm1)
    grad_input = grad_after_attn + grad_input_norm
    grad_gains = jnp.stack([grad_gain1, grad_gain2, grad_gain3])
    shares = (
        lax.psum_scatter(
            grad_gains.astype(jnp.bfloat16), "fsdp", scatter_dimension=1, tiled=True
        ).astype(jnp.float32),
        lax.psum_scatter(
            grad_qkv.astype(jnp.bfloat16), "fsdp", scatter_dimension=0, tiled=True
        ).astype(jnp.float32),
        lax.psum_scatter(
            grad_attn_out.astype(jnp.bfloat16), "fsdp", scatter_dimension=0, tiled=True
        ).astype(jnp.float32),
        lax.psum_scatter(
            grad_cq.astype(jnp.bfloat16), "fsdp", scatter_dimension=0, tiled=True
        ).astype(jnp.float32),
        lax.psum_scatter(
            grad_ckv.astype(jnp.bfloat16), "fsdp", scatter_dimension=0, tiled=True
        ).astype(jnp.float32),
        lax.psum_scatter(
            grad_cout.astype(jnp.bfloat16), "fsdp", scatter_dimension=0, tiled=True
        ).astype(jnp.float32),
        lax.psum_scatter(
            grad_in.astype(jnp.bfloat16), "fsdp", scatter_dimension=0, tiled=True
        ).astype(jnp.float32),
        lax.psum_scatter(
            grad_down.astype(jnp.bfloat16), "fsdp", scatter_dimension=0, tiled=True
        ).astype(jnp.float32),
    )
    share_gains, share_qkv, share_out, share_cq, share_ckv, share_cout, share_in, share_down = (
        shares
    )
    totals = lax.psum(
        (share_gains, share_qkv, share_out, share_cq, share_ckv, share_cout, share_in, share_down),
        "ctx",
    )
    return (
        layer_out[None],
        grad_input[None],
        grad_enc,
        totals[0],
        totals[1],
        totals[2],
        totals[3],
        totals[4],
        totals[5],
        totals[6],
        totals[7],
    )


def solution(mesh):
    return jax.shard_map(
        local,
        mesh=mesh,
        in_specs=(
            P("fsdp", "ctx", None),
            P("fsdp", "ctx", None, None),
            P("fsdp", "ctx", None),
            P("fsdp", None),
            P("fsdp", None),
            P(None, "fsdp"),
            P("fsdp", None),
            P("fsdp", None),
            P("fsdp", None),
            P("fsdp", None),
            P("fsdp", None),
            P("fsdp", None),
            P("fsdp", None),
        ),
        out_specs=(
            P("fsdp", "ctx", None),
            P("fsdp", "ctx", None),
            P("fsdp", "ctx", None, None),
            P(None, "fsdp"),
            P("fsdp", None),
            P("fsdp", None),
            P("fsdp", None),
            P("fsdp", None),
            P("fsdp", None),
            P("fsdp", None),
            P("fsdp", None),
        ),
        check_vma=False,
    )
```

profile of v0, /device:TPU:0, one launch (start us, length us, event | category | flops | bytes accessed | tf_op | source)
XLA Modules:
  0.0 1194.1 jit_solution(62980351649556590)
XLA Ops:
  8.7 6.3 all-gather
  16.4 26.7 %all-gather.11.cloned.1.call-done = bf16[768,2304]{1,0:T(8,128)(2,1)} async-done(((bf16[192,2304]{1,0:T(8,128)(2,1)}), bf16[768,2304]{1,0:T(8,128)(2,1)}) %all-gather.11.cloned.1.call-update) | async-done | bytes 3538960 | tf_op jit(solution)/shard_map/all_gather | solution.py:61
  43.1 2.7 convolution_convert_fusion.3
  53.4 15.4 %all-gather.19.cloned.1.call-done = bf16[768,1536]{1,0:T(8,128)(2,1)} async-done(((bf16[192,1536]{1,0:T(8,128)(2,1)}), bf16[768,1536]{1,0:T(8,128)(2,1)}) %all-gather.19.cloned.1.call-update) | async-done | bytes 2359312 | tf_op jit(solution)/shard_map/all_gather | solution.py:64
  68.8 3.0 convolution_convert_fusion.5
  74.9 40.9 %all-gather.13.cloned.1.call-done = bf16[1024,768]{1,0:T(8,128)(2,1)} async-done(((bf16[128,768]{1,0:T(8,128)(2,1)}), bf16[1024,768]{1,0:T(8,128)(2,1)}) %all-gather.13.cloned.1.call-update) | async-done | bytes 1572880 | tf_op jit(solution)/shard_map/all_gather | solution.py:109
  117.5 43.9 %all-gather.15.cloned.1.call-done = bf16[1024,768]{1,0:T(8,128)(2,1)} async-done(((bf16[128,768]{1,0:T(8,128)(2,1)}), bf16[1024,768]{1,0:T(8,128)(2,1)}) %all-gather.15.cloned.1.call-update) | async-done | bytes 1572880 | tf_op jit(solution)/shard_map/all_gather | solution.py:110
  161.4 2.6 copy.179
  164.0 18.8 %while.33 = (s32[]{:T(128)}, f32[12,128]{1,0:T(8,128)S(1)}, f32[12,128]{1,0:T(8,128)S(1)}, f32[128,12,64]{0,2,1:T(8,128)}, s32[128]{0:T(128)S(1)}, /*index=5*/s3...) while((s32[]{:T(128)}, f32[12,128]{1,0:T(8,128)S(1)}, ...), condition=%wide.region_6.7_spmd.clone, body=%wide.region_3.0_spmd.clone.sunk | while | flops 212050944 | bytes 28095732 | solution.py:149
  165.6 2.5 fusion.168
  168.1 3.0 fusion.170
  174.6 2.5 fusion.168
  177.1 2.8 fusion.170
  180.0 2.8 fusion.172
  185.7 12.3 %all-gather.21.cloned.1.call-done = bf16[768,768]{1,0:T(8,128)(2,1)} async-done(((bf16[192,768]{1,0:T(8,128)(2,1)}), bf16[768,768]{1,0:T(8,128)(2,1)}) %all-gather.21.cloned.1.call-update) | async-done | bytes 1179664 | tf_op jit(solution)/shard_map/all_gather | solution.py:63
  202.2 3.1 fusion.90
  209.9 7.2 all-gather.23.cloned.1.call-done
  219.9 36.2 %all-gather.25.cloned.1.call-done = bf16[768,3072]{1,0:T(8,128)(2,1)} async-done(((bf16[192,3072]{1,0:T(8,128)(2,1)}), bf16[768,3072]{1,0:T(8,128)(2,1)}) %all-gather.25.cloned.1.call-update) | async-done | bytes 4718608 | tf_op jit(solution)/shard_map/all_gather | solution.py:66
  256.1 8.5 multiply_convert_fusion.2
  264.7 30.5 %all-gather.27.cloned.1.call-done = bf16[3072,768]{1,0:T(8,128)(2,1)} async-done(((bf16[768,768]{1,0:T(8,128)(2,1)}), bf16[3072,768]{1,0:T(8,128)(2,1)}) %all-gather.27.cloned.1.call-update) | async-done | bytes 4718608 | tf_op jit(solution)/shard_map/all_gather | solution.py:67
  295.2 5.3 add_convert_fusion
  314.2 2.6 multiply_reduce_fusion.2
  320.6 36.1 %while.34 = (s32[]{:T(128)}, f32[128,12,64]{0,2,1:T(8,128)}, f32[2,512,768]{2,1,0:T(8,128)}, f32[2,512,768]{2,1,0:T(8,128)}, s32[2]{0:T(128)S(1)}, /*index=5*/bf...) while((s32[]{:T(128)}, f32[128,12,64]{0,2,1:T(8,128)}, ...), condition=%wide.region_17.18_spmd.clone, body=%wide.region_16.17_spmd.clone.sunk | while | flops 512065536 | bytes 87846616 | solution.py:276
  334.8 3.9 constant_dynamic-update-slice_fusion.5
  343.3 2.6 fusion.185
  352.9 3.8 constant_dynamic-update-slice_fusion.5
  356.8 3.6 copy.198
  360.4 3.7 copy.196
  374.8 2.8 fusion.30
  377.6 4.3 copy.210
  383.0 52.6 %reduce-scatter.17.cloned.1.call-done = f32[128,768]{0,1:T(8,128)} async-done(((f32[1024,768]{0,1:T(8,128)}), f32[128,768]{0,1:T(8,128)}) %reduce-scatter.17.cloned.1.call-update) | async-done | bytes 393232 | tf_op jit(solution)/shard_map/reduce_scatter | solution.py:288
  436.6 77.0 %reduce-scatter.15.cloned.1.call-done = f32[128,768]{0,1:T(8,128)} async-done(((f32[1024,768]{0,1:T(8,128)}), f32[128,768]{0,1:T(8,128)}) %reduce-scatter.15.cloned.1.call-update) | async-done | bytes 393232 | tf_op jit(solution)/shard_map/reduce_scatter | solution.py:282
  514.7 4.1 fusion.54
  519.9 3.7 convolution_convert_fusion.1
  524.7 3.7 convolution_convert_fusion
  528.7 3.0 convolution_convert_fusion.2
  531.7 4.1 fusion.45
  535.8 2.6 fusion.94
  538.4 3.4 reduce-scatter.21.cloned.1.call-done
  541.8 28.5 %reduce-scatter.23.cloned.1.call-done = bf16[192,768]{1,0:T(8,128)(2,1)} async-done(((bf16[768,768]{1,0:T(8,128)(2,1)}), bf16[192,768]{1,0:T(8,128)(2,1)}) %reduce-scatter.23.cloned.1.call-update) | async-done | bytes 294928 | tf_op jit(solution)/shard_map/reduce_scatter | solution.py:318
  570.3 28.2 %reduce-scatter.25.cloned.1.call-done = bf16[192,768]{1,0:T(8,128)(2,1)} async-done(((bf16[768,768]{1,0:T(8,128)(2,1)}), bf16[192,768]{1,0:T(8,128)(2,1)}) %reduce-scatter.25.cloned.1.call-update) | async-done | bytes 294928 | tf_op jit(solution)/shard_map/reduce_scatter | solution.py:324
  598.5 36.2 %reduce-scatter.33.cloned.1.call-done = bf16[192,1536]{1,0:T(8,128)(2,1)} async-done(((bf16[768,1536]{1,0:T(8,128)(2,1)}), bf16[192,1536]{1,0:T(8,128)(2,1)}) %reduce-scatter.33.cloned.1.call-update) | async-done | bytes 589840
  636.9 20.4 %reduce-scatter.31.cloned.1.call-done = bf16[192,3]{1,0:T(8,128)(2,1)} async-done(((bf16[768,3]{1,0:T(8,128)(2,1)}), bf16[192,3]{1,0:T(8,128)(2,1)}) %reduce-scatter.31.cloned.1.call-update) | async-done | bytes 1168
  658.2 49.4 %reduce-scatter.27.cloned.1.call-done = bf16[192,3072]{1,0:T(8,128)(2,1)} async-done(((bf16[768,3072]{1,0:T(8,128)(2,1)}), bf16[192,3072]{1,0:T(8,128)(2,1)}) %reduce-scatter.27.cloned.1.call-update) | async-done | bytes 1179664 | tf_op jit(solution)/shard_map/reduce_scatter | solution.py:327
  707.6 50.4 %reduce-scatter.29.cloned.1.call-done = bf16[768,768]{1,0:T(8,128)(2,1)} async-done(((bf16[3072,768]{1,0:T(8,128)(2,1)}), bf16[768,768]{1,0:T(8,128)(2,1)}) %reduce-scatter.29.cloned.1.call-update) | async-done | bytes 1179664 | tf_op jit(solution)/shard_map/reduce_scatter | solution.py:330
  758.0 43.1 %reduce-scatter.19.cloned.1.call-done = bf16[192,2304]{1,0:T(8,128)(2,1)} async-done(((bf16[768,2304]{1,0:T(8,128)(2,1)}), bf16[192,2304]{1,0:T(8,128)(2,1)}) %reduce-scatter.19.cloned.1.call-update) | async-done | bytes 884752 | tf_op jit(solution)/shard_map/reduce_scatter | solution.py:312
  801.1 383.1 %all-reduce.2 = (f32[3,192]{1,0:T(4,128)}, f32[192,2304]{1,0:T(8,128)}, f32[192,768]{1,0:T(8,128)}, f32[192,768]{1,0:T(8,128)}, f32[192,1536]{0,1:T(8,128)}, /*i...) all-reduce(bf16[3,192]{1,0:T(4,128)(2,1)S(1)} %copy.209, ...), channel_id=1, replica_groups=mesh['ctx'=8,'fsdp'=4] {'ctx'}, use_global_device_ids=true, to_apply=%region_25.26 | all-reduce | flops 2359872 | bytes 14159232 | tf_op jit(solution)/shard_map/psum | solution.py:337
  1184.2 2.9 copy.203
  (385 shorter events, 95.1 us)
Async XLA Ops:
  7.2 61.6 %copy-start = (bf16[1,2,256,768]{3,2,1,0:T(8,128)(2,1)S(1)}, bf16[1,2,256,768]{3,2,1,0:T(8,128)(2,1)}, u32[]{:S(2)}) copy-start(bf16[1,2,256,768]{3,2,1,0:T(8,128)(2,1)} %param.18) | copy-start | bytes 2359300
  7.2 8.6 copy-start.14
  7.2 35.9 %all-gather.11.cloned.1.call-start = ((), (), s32[]{:S(2)}) async-start(), calls=%async_computation.10 | async-start | bytes 4423680 | tf_op jit(solution)/shard_map/all_gather | solution.py:61
  7.9 60.9 %all-gather.19.cloned.1.call-start = ((), (), s32[]{:S(2)}) async-start(), calls=%async_computation.14 | async-start | bytes 2949120 | tf_op jit(solution)/shard_map/all_gather | solution.py:64
  8.7 107.1 %all-gather.13.cloned.1.call-start = ((), (), s32[]{:S(2)}) async-start(), calls=%async_computation.11 | async-start | bytes 1769472 | tf_op jit(solution)/shard_map/all_gather | solution.py:109
  15.8 30.0 %copy-start.52 = (f32[768]{0:T(1024)}, f32[768]{0:T(1024)S(1)}, u32[]{:S(2)}) copy-start(f32[768]{0:T(1024)S(1)} %get-tuple-element.596) | copy-start | bytes 9220
  16.4 29.4 %copy-start.77 = (f32[128]{0:T(128)}, f32[128]{0:T(128)S(1)}, u32[]{:S(2)}) copy-start(f32[128]{0:T(128)S(1)} %fusion.77) | copy-start | bytes 1540
  46.6 114.8 %all-gather.15.cloned.1.call-start = ((), (), s32[]{:S(2)}) async-start(), calls=%async_computation.12 | async-start | bytes 1769472 | tf_op jit(solution)/shard_map/all_gather | solution.py:110
  47.2 136.6 %all-gather.17.cloned.1.call-start = ((), (), s32[]{:S(2)}) async-start(), calls=%async_computation.13 | async-start | bytes 1474560 | tf_op jit(solution)/shard_map/all_gather | solution.py:62
  47.8 150.2 %all-gather.21.cloned.1.call-start = ((), (), s32[]{:S(2)}) async-start(), calls=%async_computation.15 | async-start | bytes 1474560 | tf_op jit(solution)/shard_map/all_gather | solution.py:63
  48.4 168.7 %all-gather.23.cloned.1.call-start = ((), (), s32[]{:S(2)}) async-start(), calls=%async_computation.16 | async-start | bytes 1474560 | tf_op jit(solution)/shard_map/all_gather | solution.py:65
  49.1 207.0 %all-gather.25.cloned.1.call-start = ((), (), s32[]{:S(2)}) async-start(), calls=%async_computation.17 | async-start | bytes 5898240 | tf_op jit(solution)/shard_map/all_gather | solution.py:66
  49.9 245.3 %all-gather.27.cloned.1.call-start = ((), (), s32[]{:S(2)}) async-start(), calls=%async_computation.18 | async-start | bytes 5898240 | tf_op jit(solution)/shard_map/all_gather | solution.py:67
  50.6 385.0 %reduce-scatter.17.cloned.1.call-start = ((), (), s32[]{:S(2)}) async-start(), calls=%async_computation.20 | async-start | bytes 3538944 | tf_op jit(solution)/shard_map/reduce_scatter | solution.py:288
  51.2 20.7 %copy-start.56 = (s32[1024]{0:T(1024)}, s32[1024]{0:T(1024)S(1)}, u32[]{:S(2)}) copy-start(s32[1024]{0:T(1024)S(1)} %reshape.301) | copy-start | bytes 12292
  51.3 20.6 %copy-start.59 = (s32[1024]{0:T(1024)}, s32[1024]{0:T(1024)S(1)}, u32[]{:S(2)}) copy-start(s32[1024]{0:T(1024)S(1)} %add.173) | copy-start | bytes 12292
  117.5 46.5 %copy-start.57 = (s32[1024]{0:T(1024)S(1)}, s32[1024]{0:T(1024)}, u32[]{:S(2)}) copy-start(s32[1024]{0:T(1024)} %copy-done.56) | copy-start | bytes 12292
  117.5 46.5 %copy-start.60 = (s32[1024]{0:T(1024)S(1)}, s32[1024]{0:T(1024)}, u32[]{:S(2)}) copy-start(s32[1024]{0:T(1024)} %copy-done.59) | copy-start | bytes 12292
  117.5 46.5 %copy-start.68 = (s32[128]{0:T(128)S(1)}, s32[128]{0:T(128)}, u32[]{:S(2)}) copy-start(s32[128]{0:T(128)} %dynamic_slice.53) | copy-start | bytes 1540
  117.5 46.5 %copy-start.70 = (s32[128]{0:T(128)S(1)}, s32[128]{0:T(128)}, u32[]{:S(2)}) copy-start(s32[128]{0:T(128)} %dynamic_slice.54) | copy-start | bytes 1540
  182.8 15.2 %copy-start.62 = (f32[768]{0:T(1024)S(1)}, f32[768]{0:T(1024)}, u32[]{:S(2)}) copy-start(f32[768]{0:T(1024)} %get-tuple-element.595) | copy-start | bytes 9220
  183.8 15.8 %copy-start.34 = (bf16[128,12,64]{0,2,1:T(8,128)(2,1)}, bf16[128,12,64]{0,2,1:T(8,128)(2,1)S(1)}, u32[]{:S(2)}) copy-start(bf16[128,12,64]{0,2,1:T(8,128)(2,1)S(1)} %fusion.69) | copy-start | bytes 589828
  185.7 15.1 %copy-start.86 = (f32[128]{0:T(128)}, f32[128]{0:T(128)S(1)}, u32[]{:S(2)}) copy-start(f32[128]{0:T(128)S(1)} %get-tuple-element.672) | copy-start | bytes 1540
  185.7 131.8 %copy-start.8 = (f32[128,768]{1,0:T(8,128)}, f32[128,768]{1,0:T(8,128)S(1)}, u32[]{:S(2)}) copy-start(f32[128,768]{1,0:T(8,128)S(1)} %get-tuple-element.673) | copy-start | bytes 1179652
  185.7 15.1 %copy-start.79 = (f32[128]{0:T(128)}, f32[128]{0:T(128)S(1)}, u32[]{:S(2)}) copy-start(f32[128]{0:T(128)S(1)} %fusion.78) | copy-start | bytes 1540
  202.2 5.3 copy-start.27
  209.9 54.8 %copy-start.38 = (bf16[128,768]{0,1:T(8,128)(2,1)}, bf16[128,768]{0,1:T(8,128)(2,1)S(1)}, u32[]{:S(2)}) copy-start(bf16[128,768]{0,1:T(8,128)(2,1)S(1)} %convert_element_type.182) | copy-start | bytes 589828
  218.8 84.0 %copy-start.11 = (f32[128,768]{1,0:T(8,128)}, f32[128,768]{1,0:T(8,128)S(1)}, u32[]{:S(2)}) copy-start(f32[128,768]{1,0:T(8,128)S(1)} %get-tuple-element.677) | copy-start | bytes 1179652
  295.2 5.3 copy-start.24
  295.2 5.3 copy-start.54
  295.2 5.3 copy-start.73
  360.4 153.2 %reduce-scatter.15.cloned.1.call-start = ((), (), s32[]{:S(2)}) async-start(), calls=%async_computation.19 | async-start | bytes 3538944 | tf_op jit(solution)/shard_map/reduce_scatter | solution.py:282
  364.3 177.5 %reduce-scatter.21.cloned.1.call-start = ((), (), s32[]{:S(2)}) async-start(), calls=%async_computation.22 | async-start | bytes 1474560 | tf_op jit(solution)/shard_map/reduce_scatter | solution.py:315
  366.8 203.5 %reduce-scatter.23.cloned.1.call-start = ((), (), s32[]{:S(2)}) async-start(), calls=%async_computation.23 | async-start | bytes 1474560 | tf_op jit(solution)/shard_map/reduce_scatter | solution.py:318
  368.5 229.9 %reduce-scatter.25.cloned.1.call-start = ((), (), s32[]{:S(2)}) async-start(), calls=%async_computation.24 | async-start | bytes 1474560 | tf_op jit(solution)/shard_map/reduce_scatter | solution.py:324
  370.2 264.5 %reduce-scatter.33.cloned.1.call-start = ((), (), s32[]{:S(2)}) async-start(), calls=%async_computation.28 | async-start | bytes 2949120
  381.9 132.8 %copy-start.15 = (bf16[1,128,768]{2,1,0:T(8,128)(2,1)S(1)}, bf16[1,128,768]{2,1,0:T(8,128)(2,1)}, u32[]{:S(2)}) copy-start(bf16[1,128,768]{2,1,0:T(8,128)(2,1)} %param.17) | copy-start | bytes 589828
  381.9 132.8 %copy-start.53 = (f32[768]{0:T(1024)S(1)}, f32[768]{0:T(1024)}, u32[]{:S(2)}) copy-start(f32[768]{0:T(1024)} %copy-done.52) | copy-start | bytes 9220
  381.9 132.8 %copy-start.78 = (f32[128]{0:T(128)S(1)}, f32[128]{0:T(128)}, u32[]{:S(2)}) copy-start(f32[128]{0:T(128)} %copy-done.77) | copy-start | bytes 1540
  382.0 275.4 %reduce-scatter.31.cloned.1.call-start = ((), (), s32[]{:S(2)}) async-start(), calls=%async_computation.27 | async-start | bytes 245760
  519.8 187.8 %reduce-scatter.27.cloned.1.call-start = ((), (), s32[]{:S(2)}) async-start(), calls=%async_computation.25 | async-start | bytes 5898240 | tf_op jit(solution)/shard_map/reduce_scatter | solution.py:327
  523.5 234.5 %reduce-scatter.29.cloned.1.call-start = ((), (), s32[]{:S(2)}) async-start(), calls=%async_computation.26 | async-start | bytes 5898240 | tf_op jit(solution)/shard_map/reduce_scatter | solution.py:330
  528.4 272.7 %reduce-scatter.19.cloned.1.call-start = ((), (), s32[]{:S(2)}) async-start(), calls=%async_computation.21 | async-start | bytes 4423680 | tf_op jit(solution)/shard_map/reduce_scatter | solution.py:312
  535.8 100.2 %copy-start.85 = (f32[128]{0:T(128)S(1)}, f32[128]{0:T(128)}, u32[]{:S(2)}) copy-start(f32[128]{0:T(128)} %copy-done.84) | copy-start | bytes 1540
  538.4 97.7 %copy-start.47 = (f32[128,768]{1,0:T(8,128)S(1)}, f32[128,768]{1,0:T(8,128)}, u32[]{:S(2)}) copy-start(f32[128,768]{1,0:T(8,128)} %get-tuple-element.683) | copy-start | bytes 1179652
  541.8 259.3 %copy-start.49 = (bf16[192,768]{1,0:T(8,128)(2,1)S(1)}, bf16[192,768]{1,0:T(8,128)(2,1)}, u32[]{:S(2)}) copy-start(bf16[192,768]{1,0:T(8,128)(2,1)} %reduce-scatter.21.cloned.1.call-done) | copy-start | bytes 884740
  570.3 230.8 %copy-start.50 = (bf16[192,768]{1,0:T(8,128)(2,1)S(1)}, bf16[192,768]{1,0:T(8,128)(2,1)}, u32[]{:S(2)}) copy-start(bf16[192,768]{1,0:T(8,128)(2,1)} %reduce-scatter.23.cloned.1.call-done) | copy-start | bytes 884740
  598.5 202.6 %copy-start.51 = (bf16[192,768]{1,0:T(8,128)(2,1)S(1)}, bf16[192,768]{1,0:T(8,128)(2,1)}, u32[]{:S(2)}) copy-start(bf16[192,768]{1,0:T(8,128)(2,1)} %reduce-scatter.25.cloned.1.call-done) | copy-start | bytes 884740
  (81 other events, 179.3 us)
Sparse Core Ops, SparseCore 0:
  9.6 33.4 all-gather.10
  44.7 24.1 all-gather.18
  71.6 44.1 all-gather.12
  118.4 42.9 all-gather.14
  162.8 16.2 all-gather.16
  180.5 17.4 all-gather.20
  199.6 17.4 all-gather.22
  218.6 37.4 all-gather.24
  257.7 37.4 all-gather.26
  360.5 75.0 reduce-scatter.16
  439.2 74.3 reduce-scatter.14
  516.6 25.0 reduce-scatter.20
  544.5 25.7 reduce-scatter.22
  572.7 25.7 reduce-scatter.24
  601.6 33.0 reduce-scatter.32
  637.5 19.7 reduce-scatter.30
  659.7 47.8 reduce-scatter.26
  710.1 47.8 reduce-scatter.28
  760.6 40.4 reduce-scatter.18
where the time goes:
time: 1200 us; the launch traced here: 1190 us
  waiting for transfers between devices  607 us (51%)
  blocking collectives  389 us (32%)
  matrix products  93.2 us (8%)
  local copies, waits for them, and re-layouts  71.6 us (6%)
  between operations  15.6 us (1%)
  other arithmetic  14 us (1%)
    psum x1, blocking collectives, local(): lax.psum((share_gains, share_qkv, share_out, share_cq, share_ckv, share_c...  383 us
    reduce_scatter x1, waiting for transfers between devices, local(): lax.psum_scatter(key_value_terms[0].reshape(group_tok, feature_width), 'c...  77 us
    unnamed x21, waiting for transfers between devices  61.8 us
    reduce_scatter x1, waiting for transfers between devices, local(): lax.psum_scatter(key_value_terms[1].reshape(group_tok, feature_width), 'c...  52.6 us
    reduce_scatter x1, waiting for transfers between devices, local(): lax.psum_scatter(grad_down.astype(jnp.bfloat16), 'fsdp', scatter_dimensio...  50.4 us
    reduce_scatter x1, waiting for transfers between devices, local(): lax.psum_scatter(grad_in.astype(jnp.bfloat16), 'fsdp', scatter_dimension=...  49.4 us
    all_gather x1, waiting for transfers between devices, local(): lax.all_gather(value_low, 'ctx', axis=0, tiled=True)  43.9 us
    reduce_scatter x1, waiting for transfers between devices, local(): lax.psum_scatter(grad_qkv.astype(jnp.bfloat16), 'fsdp', scatter_dimension...  43.1 us
  transfers between devices with their start and end apart: 19, of which 18 were waited for; matrix products, arithmetic and copies ran while one was open for 9% of the time, Pallas kernels for 0%

commit v1 on v0

v1 whole, which is shorter than its diff:
```python
import functools

import jax
import jax.numpy as jnp
from jax import lax
from jax.experimental import pallas as pl
from jax.experimental.pallas import tpu as pltpu
from jax.sharding import PartitionSpec as P

H = 12
STRETCH = 64


NORM_EPS = 1e-06
MASKED_SCORE = -1e30
KEY_BLOCK = 1024


def to_low(values):
    return values.astype(jnp.bfloat16)


def matmul(left, right):
    return jnp.dot(left, right, preferred_element_type=jnp.float32)


def left_product(left, right):
    return lax.dot_general(left, right, (((0,), (0,)), ((), ())), preferred_element_type=jnp.float32)


def right_product(left, right):
    return lax.dot_general(left, right, (((1,), (1,)), ((), ())), preferred_element_type=jnp.float32)


def inverse_rms(values):
    return lax.rsqrt(jnp.mean(values * values, axis=-1, keepdims=True) + NORM_EPS)


def rms_back(values, scale, gain, grad):
    gained = gain * grad
    along = jnp.mean(gained * values, axis=-1, keepdims=True)
    return scale * gained - values * (scale * scale * scale) * along


def head_rows(rows, head_size):
    wide = rows.astype(jnp.float32)
    lane = lax.broadcasted_iota(jnp.int32, wide.shape, 1)
    first = jnp.where(lane < head_size, wide, 0.0)
    second = jnp.where(lane >= head_size, wide, 0.0)
    return to_low(jnp.concatenate([first, second], axis=0))


def join_heads(columns, head_size):
    tok_count = columns.shape[1] // 2
    return jnp.concatenate(
        [columns[:head_size, :tok_count], columns[head_size:, tok_count:]], axis=0
    ).T


def self_scores(query, key, key_pos, low_pos, high_pos, score_scale):
    scores = right_product(key, query) * score_scale
    return jnp.where((key_pos >= low_pos) & (key_pos <= high_pos), scores, MASKED_SCORE)


def self_forward_kernel(
    head_size, blocks, q_ref, k_ref, v_ref, pos_ref, low_ref, high_ref, o_ref, lse_ref
):
    score_scale = head_size ** (-0.5)
    query = head_rows(q_ref[...], head_size)
    low_pos, high_pos = low_ref[...], high_ref[...]
    rows = k_ref.shape[0] // blocks

    def scores_of(index):
        span = pl.ds(pl.multiple_of(index * rows, rows), rows)
        return self_scores(query, k_ref[span, :], pos_ref[span, :], low_pos, high_pos, score_scale)

    def values_of(index):
        return v_ref[pl.ds(pl.multiple_of(index * rows, rows), rows), :]

    if blocks == 1:
        scores = scores_of(0)
        peak = jnp.max(scores, axis=0, keepdims=True)
        weights = jnp.exp(scores - peak)
        total = jnp.sum(weights, axis=0, keepdims=True)
        running = left_product(values_of(0), to_low(weights))
    else:
        peak = lax.fori_loop(
            0,
            blocks,
            lambda i, top: jnp.maximum(top, jnp.max(scores_of(i), axis=0, keepdims=True)),
            jnp.full((1, query.shape[0]), MASKED_SCORE, jnp.float32),
        )

        def add(index, state):
            total, running = state
            weights = jnp.exp(scores_of(index) - peak)
            return (
                total + jnp.sum(weights, axis=0, keepdims=True),
                running + left_product(values_of(index), to_low(weights)),
            )

        total, running = lax.fori_loop(
            0,
            blocks,
            add,
            (
                jnp.zeros((1, query.shape[0]), jnp.float32),
                jnp.zeros((2 * head_size, query.shape[0]), jnp.float32),
            ),
        )
    o_ref[...] = to_low(join_heads(running / total, head_size))
    lse_ref[0] = peak + jnp.log(total)


def self_backward_kernel(
    head_size,
    blocks,
    q_ref,
    k_ref,
    v_ref,
    do_ref,
    pos_ref,
    low_ref,
    high_ref,
    lse_ref,
    dq_ref,
    dkv_ref,
):
    score_scale = head_size ** (-0.5)
    query = head_rows(q_ref[...], head_size)
    grad = head_rows(do_ref[...], head_size)
    low_pos, high_pos = low_ref[...], high_ref[...]
    log_total = lse_ref[0]
    rows = k_ref.shape[0] // blocks

    def span_of(index):
        return pl.ds(pl.multiple_of(index * rows, rows), rows)

    def pair_of(index):
        span = span_of(index)
        scores = self_scores(
            query, k_ref[span, :], pos_ref[span, :], low_pos, high_pos, score_scale
        )
        return jnp.exp(scores - log_total), right_product(v_ref[span, :], grad)

    def finish(index, probs, dprobs, delta):
        span = span_of(index)
        dscores = to_low(probs * (dprobs - delta))
        dkv_ref[0, span, :] = to_low(score_scale * matmul(dscores, query))
        dkv_ref[1, span, :] = to_low(matmul(to_low(probs), grad))
        return left_product(k_ref[span, :], dscores)

    if blocks == 1:
        probs, dprobs = pair_of(0)
        delta = jnp.sum(probs * dprobs, axis=0, keepdims=True)
        columns = finish(0, probs, dprobs, delta)
    else:

        def add_delta(index, delta):
            probs, dprobs = pair_of(index)
            return delta + jnp.sum(probs * dprobs, axis=0, keepdims=True)

        delta = lax.fori_loop(
            0, blocks, add_delta, jnp.zeros((1, query.shape[0]), jnp.float32)
        )

        def add_query(index, columns):
            probs, dprobs = pair_of(index)
            return columns + finish(index, probs, dprobs, delta)

        columns = lax.fori_loop(
            0, blocks, add_query, jnp.zeros((2 * head_size, query.shape[0]), jnp.float32)
        )
    dq_ref[...] = to_low(score_scale * join_heads(columns, head_size))


def self_specs(tok_count, key_count, pairs):
    wide = 128
    return (
        pl.BlockSpec((tok_count, wide), lambda i: (0, i)),
        pl.BlockSpec((key_count, wide), lambda i: (0, i)),
        pl.BlockSpec((key_count, wide), lambda i: (0, pairs + i)),
        pl.BlockSpec((key_count, 1), lambda i: (0, 0)),
        pl.BlockSpec((1, 2 * tok_count), lambda i: (0, 0)),
        pl.BlockSpec((1, 1, 2 * tok_count), lambda i: (i, 0, 0)),
    )


def self_forward(query, key_value, key_pos, low_pos, high_pos):
    tok_count, feature_width = query.shape
    key_count = key_value.shape[0]
    head_size = feature_width // H
    pairs = H // 2
    blocks = max(1, key_count // KEY_BLOCK)
    rows, keys, values, pos, edge, lse = self_specs(tok_count, key_count, pairs)
    return pl.pallas_call(
        functools.partial(self_forward_kernel, head_size, blocks),
        grid=(pairs,),
        in_specs=[rows, keys, values, pos, edge, edge],
        out_specs=[rows, lse],
        out_shape=[
            jax.ShapeDtypeStruct((tok_count, feature_width), jnp.bfloat16),
            jax.ShapeDtypeStruct((pairs, 1, 2 * tok_count), jnp.float32),
        ],
        cost_estimate=pl.CostEstimate(
            flops=8 * tok_count * key_count * feature_width,
            bytes_accessed=4 * key_count * feature_width,
            transcendentals=H * tok_count * key_count,
        ),
        name="self_forward",
    )(query, key_value, key_value, key_pos, low_pos, high_pos)


def self_backward(query, key_value, grad, key_pos, low_pos, high_pos, log_total):
    tok_count, feature_width = query.shape
    key_count = key_value.shape[0]
    head_size = feature_width // H
    pairs = H // 2
    blocks = max(1, key_count // KEY_BLOCK)
    rows, keys, values, pos, edge, lse = self_specs(tok_count, key_count, pairs)
    return pl.pallas_call(
        functools.partial(self_backward_kernel, head_size, blocks),
        grid=(pairs,),
        in_specs=[rows, keys, values, rows, pos, edge, edge, lse],
        out_specs=[rows, pl.BlockSpec((2, key_count, 128), lambda i: (0, 0, i))],
        out_shape=[
            jax.ShapeDtypeStruct((tok_count, feature_width), jnp.bfloat16),
            jax.ShapeDtypeStruct((2, key_count, feature_width), jnp.bfloat16),
        ],
        cost_estimate=pl.CostEstimate(
            flops=20 * tok_count * key_count * feature_width,
            bytes_accessed=8 * key_count * feature_width,
            transcendentals=H * tok_count * key_count,
        ),
        name="self_backward",
    )(query, key_value, key_value, grad, key_pos, low_pos, high_pos, log_total)


def cross_forward_kernel(head_size, stretches, q_ref, k_ref, v_ref, o_ref):
    score_scale = head_size ** (-0.5)
    keys = k_ref.shape[0] // stretches
    for s in range(stretches):
        rows = pl.ds(s * STRETCH, STRETCH)
        span = pl.ds(s * keys, keys)
        query = head_rows(q_ref[rows, :], head_size)
        scores = right_product(k_ref[span, :], query) * score_scale
        weights = jnp.exp(scores - jnp.max(scores, axis=0, keepdims=True))
        probs = to_low(weights / jnp.sum(weights, axis=0, keepdims=True))
        o_ref[rows, :] = to_low(join_heads(left_product(v_ref[span, :], probs), head_size))


def cross_backward_kernel(head_size, stretches, q_ref, k_ref, v_ref, do_ref, dq_ref, dkv_ref):
    score_scale = head_size ** (-0.5)
    keys = k_ref.shape[0] // stretches
    for s in range(stretches):
        rows = pl.ds(s * STRETCH, STRETCH)
        span = pl.ds(s * keys, keys)
        query = head_rows(q_ref[rows, :], head_size)
        grad = head_rows(do_ref[rows, :], head_size)
        scores = right_product(k_ref[span, :], query) * score_scale
        weights = jnp.exp(scores - jnp.max(scores, axis=0, keepdims=True))
        probs = weights / jnp.sum(weights, axis=0, keepdims=True)
        dprobs = right_product(v_ref[span, :], grad)
        delta = jnp.sum(probs * dprobs, axis=0, keepdims=True)
        dscores = to_low(probs * (dprobs - delta))
        dkv_ref[0, span, :] = to_low(score_scale * matmul(dscores, query))
        dkv_ref[1, span, :] = to_low(matmul(to_low(probs), grad))
        columns = left_product(k_ref[span, :], dscores)
        dq_ref[rows, :] = to_low(score_scale * join_heads(columns, head_size))


def cross_forward(query, key_value, stretches):
    tok_count, feature_width = query.shape
    key_count = key_value.shape[0]
    pairs = H // 2
    rows, keys, values, _, _, _ = self_specs(tok_count, key_count, pairs)
    return pl.pallas_call(
        functools.partial(cross_forward_kernel, feature_width // H, stretches),
        grid=(pairs,),
        in_specs=[rows, keys, values],
        out_specs=rows,
        out_shape=jax.ShapeDtypeStruct((tok_count, feature_width), jnp.bfloat16),
        cost_estimate=pl.CostEstimate(
            flops=8 * tok_count * key_count * feature_width,
            bytes_accessed=4 * key_count * feature_width,
            transcendentals=H * tok_count * key_count,
        ),
        name="cross_forward",
    )(query, key_value, key_value)


def cross_backward(query, key_value, grad, stretches):
    tok_count, feature_width = query.shape
    key_count = key_value.shape[0]
    pairs = H // 2
    rows, keys, values, _, _, _ = self_specs(tok_count, key_count, pairs)
    return pl.pallas_call(
        functools.partial(cross_backward_kernel, feature_width // H, stretches),
        grid=(pairs,),
        in_specs=[rows, keys, values, rows],
        out_specs=[rows, pl.BlockSpec((2, key_count, 128), lambda i: (0, 0, i))],
        out_shape=[
            jax.ShapeDtypeStruct((tok_count, feature_width), jnp.bfloat16),
            jax.ShapeDtypeStruct((2, key_count, feature_width), jnp.bfloat16),
        ],
        cost_estimate=pl.CostEstimate(
            flops=20 * tok_count * key_count * feature_width,
            bytes_accessed=8 * key_count * feature_width,
            transcendentals=H * tok_count * key_count,
        ),
        name="cross_backward",
    )(query, key_value, key_value, grad)


def swap(values, axis, bit):
    count = lax.axis_size(axis)
    return lax.ppermute(values, axis, [(i, i ^ bit) for i in range(count)])


def assemble_kernel(index_ref, *refs):
    pieces, out_ref = refs[:-1], refs[-1]
    rows = pieces[0].shape[0]
    for j, piece in enumerate(pieces):
        place = (index_ref[0] ^ j) * rows
        out_ref[pl.ds(pl.multiple_of(place, rows), rows), :] = piece[...]


def assemble(index, pieces):
    rows, width = pieces[0].shape
    count = len(pieces)
    tile = width
    for size in (768, 512, 256):
        if width % size == 0:
            tile = size
            break
    return pl.pallas_call(
        assemble_kernel,
        grid_spec=pltpu.PrefetchScalarGridSpec(
            num_scalar_prefetch=1,
            grid=(width // tile,),
            in_specs=[pl.BlockSpec((rows, tile), lambda i, _: (0, i))] * count,
            out_specs=pl.BlockSpec((rows * count, tile), lambda i, _: (0, i)),
        ),
        out_shape=jax.ShapeDtypeStruct((rows * count, width), pieces[0].dtype),
        cost_estimate=pl.CostEstimate(
            flops=0, bytes_accessed=4 * rows * count * width, transcendentals=0
        ),
        name="assemble",
    )(index, *pieces)


def gather_weight(index, share):
    sibling = swap(share, "fsdp", 1)
    across = swap(share, "fsdp", 2)
    across_sibling = swap(across, "fsdp", 1)
    return assemble(index, [share, sibling, across, across_sibling])


def column_blocks(values, index, count):
    width = values.shape[1] // count
    cut = [
        lax.dynamic_slice_in_dim(values, (index ^ j) * width, width, axis=1) for j in (0, 2, 1, 3)
    ]
    return cut[0], cut[1], jnp.concatenate(cut[2:], axis=1)


def share_of_product(index, terms, count):
    cut = [(column_blocks(left, index, count), right) for left, right in terms]

    def total(which):
        return sum(left_product(blocks[which], right) for blocks, right in cut)

    received = swap(to_low(total(2)), "fsdp", 1)
    rows = received.shape[0] // 2
    across = swap(to_low(total(1) + received[rows:].astype(jnp.float32)), "fsdp", 2)
    return to_low(
        total(0) + received[:rows].astype(jnp.float32) + across.astype(jnp.float32)
    )


def reduce_over_ctx(share):
    part = lax.psum_scatter(share, "ctx", scatter_dimension=0, tiled=True)
    return lax.all_gather(part, "ctx", axis=0, tiled=True)


def local(
    hidden,
    neighbours,
    cotangent,
    stretch_deal,
    seq_lengths,
    norm_gains,
    attn_qkv,
    attn_out,
    cross_q,
    cross_kv,
    cross_out,
    mlp_in,
    mlp_out,
):
    shares = lax.axis_size("fsdp")
    fsdp_index = lax.axis_index("fsdp")
    ctx_index = lax.axis_index("ctx")
    place = fsdp_index.astype(jnp.int32).reshape(1)
    hidden_all = lax.all_gather(hidden[0], "ctx", axis=0, tiled=True)
    w_qkv = gather_weight(place, attn_qkv)
    w_ckv = gather_weight(place, cross_kv)
    w_out = gather_weight(place, attn_out)
    w_cq = gather_weight(place, cross_q)
    w_cout = gather_weight(place, cross_out)
    w_in = gather_weight(place, mlp_in)
    w_down = gather_weight(place, mlp_out)
    gain_rows = lax.all_gather(norm_gains, "fsdp", axis=1, tiled=True).astype(jnp.float32)

    tok_count, feature_width = hidden.shape[1:]
    stretch_count = tok_count // STRETCH
    deal_row = stretch_deal[0]
    lengths_row = seq_lengths[0]
    group_tok = deal_row.shape[0] * STRETCH
    seq_ends = jnp.cumsum(lengths_row)
    seq_starts = seq_ends - lengths_row
    slot_start = jnp.max(
        jnp.where(seq_starts[None, :] <= deal_row[:, None], seq_starts[None, :], 0), axis=1
    )
    offsets = jnp.arange(STRETCH, dtype=jnp.int32)
    token_pos = (deal_row[:, None] * STRETCH + offsets[None, :]).reshape(group_tok)
    own_deal = lax.dynamic_slice_in_dim(deal_row, ctx_index * stretch_count, stretch_count)
    own_start = lax.dynamic_slice_in_dim(slot_start, ctx_index * stretch_count, stretch_count)
    keep_rows = jnp.repeat((own_deal != own_start).astype(jnp.float32), STRETCH)[:, None]
    high_pos = jnp.tile((own_deal[:, None] * STRETCH + offsets[None, :]).reshape(1, tok_count), (1, 2))
    low_pos = jnp.tile(jnp.repeat(own_start * STRETCH, STRETCH).reshape(1, tok_count), (1, 2))
    key_pos = token_pos.reshape(group_tok, 1)

    rows_all = hidden_all.astype(jnp.float32)
    scale_all = inverse_rms(rows_all)
    norm_all = to_low(rows_all * scale_all * gain_rows[0])
    key_value = to_low(matmul(norm_all, w_qkv[:, feature_width:]))
    input_rows = hidden[0].astype(jnp.float32)
    scale_one = inverse_rms(input_rows)
    norm_one = to_low(input_rows * scale_one * gain_rows[0])
    query = to_low(matmul(norm_one, w_qkv[:, :feature_width]))
    attended, log_total = self_forward(query, key_value, key_pos, low_pos, high_pos)
    after_attn = input_rows + matmul(attended, w_out)
    scale_two = inverse_rms(after_attn)
    norm_two = to_low(after_attn * scale_two * gain_rows[1])
    cross_query = to_low(matmul(norm_two, w_cq))
    enc_rows = neighbours[0].reshape(-1, feature_width)
    cross_key_value = to_low(matmul(enc_rows, w_ckv))
    cross_rows = cross_forward(cross_query, cross_key_value, stretch_count)
    after_cross = after_attn + keep_rows * matmul(cross_rows, w_cout)
    scale_three = inverse_rms(after_cross)
    norm_three = to_low(after_cross * scale_three * gain_rows[2])
    inner_rows = matmul(norm_three, w_in)
    share_below = 0.5 * (1.0 + lax.erf(inner_rows * (2.0 ** -0.5)))
    activation = to_low(inner_rows * share_below)
    slope = share_below + inner_rows * jnp.exp(-0.5 * inner_rows * inner_rows) * (
        (2.0 * jnp.pi) ** -0.5
    )
    layer_out = after_cross + matmul(activation, w_down)

    grad_out = cotangent[0].astype(jnp.float32)
    grad_inner = to_low(right_product(cotangent[0], w_down) * slope)
    grad_norm3 = right_product(grad_inner, w_in)
    grad_gain3 = jnp.sum(grad_norm3 * after_cross * scale_three, axis=0)
    grad_after_cross = grad_out + rms_back(after_cross, scale_three, gain_rows[2], grad_norm3)
    grad_cross_branch = to_low(keep_rows * grad_after_cross)
    grad_cross_rows = to_low(right_product(grad_cross_branch, w_cout))
    grad_cross_query, grad_cross_pair = cross_backward(
        cross_query, cross_key_value, grad_cross_rows, stretch_count
    )
    grad_norm2 = right_product(grad_cross_query, w_cq)
    grad_gain2 = jnp.sum(grad_norm2 * after_attn * scale_two, axis=0)
    grad_after_attn = grad_after_cross + rms_back(
        after_attn, scale_two, gain_rows[1], grad_norm2
    )
    grad_attn_branch = to_low(grad_after_attn)
    grad_attended = to_low(right_product(grad_attn_branch, w_out))
    grad_query, grad_pair = self_backward(
        query, key_value, grad_attended, key_pos, low_pos, high_pos, log_total
    )
    grad_norm1_all = right_product(
        grad_pair[0], w_qkv[:, feature_width : 2 * feature_width]
    ) + right_product(grad_pair[1], w_qkv[:, 2 * feature_width :])
    grad_norm1_query = right_product(grad_query, w_qkv[:, :feature_width])
    grad_norm1 = (
        lax.psum_scatter(to_low(grad_norm1_all), "ctx", scatter_dimension=0, tiled=True).astype(
            jnp.float32
        )
        + grad_norm1_query
    )
    grad_input = grad_after_attn + rms_back(input_rows, scale_one, gain_rows[0], grad_norm1)
    grad_gain1 = jnp.sum(grad_norm1_all * rows_all * scale_all, axis=0) + jnp.sum(
        grad_norm1_query * input_rows * scale_one, axis=0
    )
    grad_enc = right_product(grad_cross_pair[0], w_ckv[:, :feature_width]) + right_product(
        grad_cross_pair[1], w_ckv[:, feature_width:]
    )

    product = functools.partial(share_of_product, fsdp_index, count=shares)
    part_down = product([(activation, cotangent[0])])
    part_in = product([(norm_three, grad_inner)])
    part_cout = product([(cross_rows, grad_cross_branch)])
    part_cq = product([(norm_two, grad_cross_query)])
    part_ck = product([(enc_rows, grad_cross_pair[0])])
    part_cv = product([(enc_rows, grad_cross_pair[1])])
    part_out = product([(attended, grad_attn_branch)])
    part_q = product([(norm_one, grad_query)])
    part_k = product([(norm_all, grad_pair[0])])
    part_v = product([(norm_all, grad_pair[1])])
    share_rows = feature_width // shares
    total_mlp = reduce_over_ctx(
        jnp.concatenate([part_in, part_down.reshape(share_rows, -1)], axis=1)
    ).astype(jnp.float32)
    total_cross = reduce_over_ctx(
        jnp.concatenate([part_cout, part_cq, part_ck, part_cv], axis=1)
    ).astype(jnp.float32)
    total_attn = reduce_over_ctx(
        jnp.concatenate([part_out, part_q, part_k, part_v], axis=1)
    ).astype(jnp.float32)
    grad_gains = lax.psum(jnp.stack([grad_gain1, grad_gain2, grad_gain3]), ("ctx", "fsdp"))
    grad_gains = lax.dynamic_slice_in_dim(grad_gains, fsdp_index * share_rows, share_rows, axis=1)
    inner_width = mlp_in.shape[1]
    return (
        layer_out[None],
        grad_input[None],
        grad_enc.reshape(neighbours.shape),
        grad_gains,
        total_attn[:, feature_width:],
        total_attn[:, :feature_width],
        total_cross[:, feature_width : 2 * feature_width],
        total_cross[:, 2 * feature_width :],
        total_cross[:, :feature_width],
        total_mlp[:, :inner_width],
        total_mlp[:, inner_width:].reshape(mlp_out.shape),
    )


def solution(mesh):
    return jax.shard_map(
        local,
        mesh=mesh,
        in_specs=(
            P("fsdp", "ctx", None),
            P("fsdp", "ctx", None, None),
            P("fsdp", "ctx", None),
            P("fsdp", None),
            P("fsdp", None),
            P(None, "fsdp"),
            P("fsdp", None),
            P("fsdp", None),
            P("fsdp", None),
            P("fsdp", None),
            P("fsdp", None),
            P("fsdp", None),
            P("fsdp", None),
        ),
        out_specs=(
            P("fsdp", "ctx", None),
            P("fsdp", "ctx", None),
            P("fsdp", "ctx", None, None),
            P(None, "fsdp"),
            P("fsdp", None),
            P("fsdp", None),
            P("fsdp", None),
            P("fsdp", None),
            P("fsdp", None),
            P("fsdp", None),
            P("fsdp", None),
        ),
        check_vma=False,
    )
```

time: 1200 us -> 708 us (0.59)
  blocking collectives: 389 us -> 54.4 us
  waiting for transfers between devices: 607 us -> 412 us
  Pallas kernels: 0 us -> 56.9 us
  local copies, waits for them, and re-layouts: 71.6 us -> 30 us
  starting transfers between devices: 1.01 us -> 28.3 us
  matrix products: 93.2 us -> 79.9 us
  other arithmetic: 14 us -> 26.2 us
    psum x1, blocking collectives: 383 us -> 40 us  [local(): lax.psum(jnp.stack([grad_gain1, grad_gain2, grad_gain3]), ('ctx', 'fsdp'))]
    reduce_scatter x8 -> x4, waiting for transfers between devices: 333 us -> 170 us  [the longest x3 111 us: reduce_over_ctx(): part = lax.psum_scatter(share, 'ctx', scatter_dimension=0, tiled=True)]
    ppermute x0 -> x41, waiting for transfers between devices: none -> 154 us  [swap(): return lax.ppermute(values, axis, [(i, i ^ bit) for i in range(count)])]
    all_gather x9 -> x4, waiting for transfers between devices: 213 us -> 87.6 us  [the longest x3 87.6 us: reduce_over_ctx(): return lax.all_gather(part, 'ctx', axis=0, tiled=True)]
    unnamed x21 -> x8, waiting for transfers between devices: 61.8 us -> 0.61 us
    pallas_call x0 -> x11, Pallas kernels: none -> 56.9 us  [the longest x7 24.5 us: assemble(): pl.pallas_call(assemble_kernel, grid_spec=pltpu.PrefetchScalarGridSpec(nu...]
    ppermute x0 -> x41, starting transfers between devices: none -> 27.8 us  [swap(): return lax.ppermute(values, axis, [(i, i ^ bit) for i in range(count)])]
    unnamed x170 -> x154, local copies, waits for them, and re-layouts: 23.1 us -> 3.11 us
  transfers between devices with their start and end apart: 19 -> 49, of which waited for: 18 -> 19; matrix products, arithmetic and copies ran while one was open for 9% -> 12% of each run, Pallas kernels for 0% -> 3%
where the time goes in v1:
time: 708 us; the launch traced here: 703 us
  waiting for transfers between devices  412 us (58%)
  matrix products  79.9 us (11%)
  Pallas kernels  56.9 us (8%)
  blocking collectives  54.4 us (8%)
  local copies, waits for them, and re-layouts  30 us (4%)
  starting transfers between devices  28.3 us (4%)
  other arithmetic  26.2 us (4%)
  between operations  15.3 us (2%)
    ppermute x41, waiting for transfers between devices, swap(): return lax.ppermute(values, axis, [(i, i ^ bit) for i in range(count)])  154 us
    reduce_scatter x3, waiting for transfers between devices, reduce_over_ctx(): part = lax.psum_scatter(share, 'ctx', scatter_dimension=0, tiled=True)  111 us
    all_gather x3, waiting for transfers between devices, reduce_over_ctx(): return lax.all_gather(part, 'ctx', axis=0, tiled=True)  87.6 us
    reduce_scatter x1, waiting for transfers between devices, local(): lax.psum_scatter(to_low(grad_norm1_all), 'ctx', scatter_dimension=0, tile...  59.1 us
    psum x1, blocking collectives, local(): lax.psum(jnp.stack([grad_gain1, grad_gain2, grad_gain3]), ('ctx', 'fsdp'))  40 us
    dot_general x30, matrix products, left_product(): lax.dot_general(left, right, (((0,), (0,)), ((), ())), preferred_element_...  34.5 us
    ppermute x41, starting transfers between devices, swap(): return lax.ppermute(values, axis, [(i, i ^ bit) for i in range(count)])  27.8 us
    pallas_call x7, Pallas kernels, assemble(): pl.pallas_call(assemble_kernel, grid_spec=pltpu.PrefetchScalarGridSpec(nu...  24.5 us
  transfers between devices with their start and end apart: 49, of which 19 were waited for; matrix products, arithmetic and copies ran while one was open for 12% of the time, Pallas kernels for 3%

profile of v1, /device:TPU:0, one launch (start us, length us, event | category | flops | bytes accessed | tf_op | source)
XLA Modules:
  0.0 702.7 jit_solution(10333189555075894498)
XLA Ops:
  7.8 2.6 collective-permute-start.4
  11.0 14.4 %all-gather.1 = bf16[4,192,3]{1,2,0:T(4,128)(2,1)S(1)} all-gather(bf16[1,192,3]{1,2,0:T(4,128)(2,1)} %bitcast.160), channel_id=1, replica_groups=mesh['ctx'=8,'fsdp'=4] {'fsdp'}, dimensions={0}, use_global_device_ids=true | all-gather | bytes 5760 | tf_op jit(solution)/shard_map/all_gather | solution.py:413
  30.4 6.0 collective-permute-done.13.refs_2_
  43.1 6.0 collective-permute-done.10.refs_2_
  51.3 66.7 %collective-permute-done.1.refs_2_ = bf16[192,2304]{1,0:T(8,128)(2,1)} collective-permute-done((bf16[192,2304]{1,0:T(8,128)(2,1)}, bf16[192,2304]{1,0:T(8,128)(2,1)}, u32[]{:S(2)}, u32[]{:S(2)}) %collective-permute-start.1) | collective-permute-done | bytes 884768 | tf_op jit(solution)/shard_map/ppermute | solution.py:317
  124.9 2.3 assemble.8
  127.3 2.4 assemble.9
  129.6 2.3 assemble.11
  132.0 2.9 assemble.10
  134.8 4.2 fusion.7.k_ref.v_ref
  139.0 4.7 assemble.7
  143.8 2.3 convolution_convert_fusion.13.q_ref
  146.0 5.1 assemble.12
  151.1 4.8 assemble.13
  160.8 4.0 convolution_convert_fusion.1.k_ref.v_ref
  166.0 7.6 %self_forward.1 = (bf16[128,768]{1,0:T(8,128)(2,1)}, f32[6,1,256]{2,1,0:T(1,128)}) custom-call(bf16[128,768]{1,0:T(8,128)(2,1)} %convolution_convert_fusion.13.q_ref, bf16[1024,1536]{1,0:T(8,128)(2,1)} %convolution_convert_fusion.1.k_ref.v_ref, bf16[1024,1536]{1,0:T(8,128)(2,1)} %convolution_convert_fusion.1.k_ref.v_ref, s32[1024,1]{1,0:T(8,128)} %add.363.pos_ref, ...), custom_call_target="tpu_custom_call" | custom-call | flops 805306368 | bytes 3145728 | tf_op jit(solution)/shard_map/self_forward/pallas_call | solution.py:196
  178.5 7.0 cross_forward.1
  189.9 4.8 multiply_convert_fusion
  196.5 2.3 multiply_reduce_fusion
  201.4 7.2 %cross_backward.1 = (bf16[128,768]{1,0:T(8,128)(2,1)}, bf16[2,512,768]{2,1,0:T(8,128)(2,1)}) custom-call(bf16[128,768]{1,0:T(8,128)(2,1)} %convolution_convert_fusion.12.q_ref, bf16[512,1536]{1,0:T(8,128)(2,1)} %fusion.7.k_ref.v_ref, bf16[512,1536]{1,0:T(8,128)(2,1)} %fusion.7.k_ref.v_ref, bf16[128,768]{1,0:T(8,128)(2,1)} %convolution_convert_fusion.11.do_ref), custom_call_target="tpu_custom_call" | custom-call | flops 1006632960 | bytes 3145728 | tf_op jit(solution)/shard_map/cross_backward/pallas_call | solution.py:297
  212.8 10.6 %self_backward.1 = (bf16[128,768]{1,0:T(8,128)(2,1)}, bf16[2,1024,768]{2,1,0:T(8,128)(2,1)}) custom-call(bf16[128,768]{1,0:T(8,128)(2,1)} %convolution_convert_fusion.13.q_ref, bf16[1024,1536]{1,0:T(8,128)(2,1)} %convolution_convert_fusion.1.k_ref.v_ref, bf16[1024,1536]{1,0:T(8,128)(2,1)} %convolution_convert_fusion.1.k_ref.v_ref, ...), custom_call_target="tpu_custom_call" | custom-call | flops 2013265920 | bytes 6291456 | tf_op jit(solution)/shard_map/self_backward/pallas_call | solution.py:221
  223.5 2.5 fusion.28
  241.7 2.3 convolution_convert_fusion
  253.5 7.1 %collective-permute-done.28 = bf16[192,768]{1,0:T(8,128)(2,1)S(1)} collective-permute-done((bf16[192,768]{1,0:T(8,128)(2,1)S(1)}, bf16[192,768]{1,0:T(8,128)(2,1)S(1)}, u32[]{:S(2)}, u32[]{:S(2)}) %collective-permute-start.28) | collective-permute-done | bytes 294944 | tf_op jit(solution)/shard_map/ppermute | solution.py:317
  262.4 4.5 collective-permute-done.26
  268.7 4.5 collective-permute-done.22
  273.3 5.5 collective-permute-done.24
  292.2 3.1 collective-permute-done.34
  295.4 6.2 collective-permute-done.30
  302.7 3.7 collective-permute-done.32
  307.4 2.9 add_convert_fusion.1
  312.1 2.9 add_convert_fusion.3
  319.0 20.6 %collective-permute-done.40 = bf16[768,768]{1,0:T(8,128)(2,1)} collective-permute-done((bf16[768,768]{1,0:T(8,128)(2,1)}, bf16[768,768]{1,0:T(8,128)(2,1)}, u32[]{:S(2)}, u32[]{:S(2)}) %collective-permute-start.40) | collective-permute-done | bytes 1179680 | tf_op jit(solution)/shard_map/ppermute | solution.py:317
  339.6 3.2 add_convert_fusion
  342.8 3.3 reshape.181
  346.1 16.4 %collective-permute-done.38 = bf16[192,3072]{1,0:T(8,128)(2,1)} collective-permute-done((bf16[192,3072]{1,0:T(8,128)(2,1)}, bf16[192,3072]{1,0:T(8,128)(2,1)}, u32[]{:S(2)}, u32[]{:S(2)}) %collective-permute-start.38) | collective-permute-done | bytes 1179680 | tf_op jit(solution)/shard_map/ppermute | solution.py:317
  366.3 3.3 fusion.19
  369.6 4.0 fusion.6
  374.3 38.9 %reduce-scatter.9.cloned.1.call-done = bf16[24,3072]{1,0:T(8,128)(2,1)} async-done(((bf16[192,3072]{1,0:T(8,128)(2,1)}), bf16[24,3072]{1,0:T(8,128)(2,1)}) %reduce-scatter.9.cloned.1.call-update) | async-done | bytes 147472 | tf_op jit(solution)/shard_map/reduce_scatter | solution.py:382
  413.3 71.8 %reduce-scatter.11.cloned.1.call-done = bf16[24,6144]{1,0:T(8,128)(2,1)} async-done(((bf16[192,6144]{1,0:T(8,128)(2,1)}), bf16[24,6144]{1,0:T(8,128)(2,1)}) %reduce-scatter.11.cloned.1.call-update) | async-done | bytes 294928 | tf_op jit(solution)/shard_map/reduce_scatter | solution.py:382
  485.2 2.2 fusion.36
  489.4 3.9 fusion.35
  493.4 59.1 %reduce-scatter.5.cloned.1.call-done = bf16[128,768]{1,0:T(8,128)(2,1)} async-done(((bf16[1024,768]{1,0:T(8,128)(2,1)}), bf16[128,768]{1,0:T(8,128)(2,1)}) %reduce-scatter.5.cloned.1.call-update) | async-done | bytes 196624 | tf_op jit(solution)/shard_map/reduce_scatter | solution.py:486
  554.5 40.0 %psum.7 = f32[3,768]{1,0:T(4,128)S(1)} all-reduce(f32[3,768]{1,0:T(4,128)S(1)} %pad_maximum_fusion.9), channel_id=1, replica_groups=mesh['ctx'=8,'fsdp'=4] {'ctx','fsdp'}, use_global_device_ids=true, to_apply=%region_14.15 | all-reduce | flops 2304 | bytes 18432 | tf_op jit(solution)/shard_map/psum | solution.py:520
  599.3 37.7 %all-gather.9.cloned.1.call-done = bf16[192,3072]{1,0:T(8,128)(2,1)} async-done(((bf16[24,3072]{1,0:T(8,128)(2,1)}), bf16[192,3072]{1,0:T(8,128)(2,1)}) %all-gather.9.cloned.1.call-update) | async-done | bytes 1179664 | tf_op jit(solution)/shard_map/all_gather | solution.py:383
  637.0 2.3 slice.197
  640.4 49.9 %all-gather.11.cloned.1.call-done = bf16[192,6144]{1,0:T(8,128)(2,1)} async-done(((bf16[24,6144]{1,0:T(8,128)(2,1)}), bf16[192,6144]{1,0:T(8,128)(2,1)}) %all-gather.11.cloned.1.call-update) | async-done | bytes 2359312 | tf_op jit(solution)/shard_map/all_gather | solution.py:383
  690.3 3.6 fusion.196
  (344 shorter events, 111.7 us)
Async XLA Ops:
  7.2 148.8 %all-gather.13.cloned.1.call-start = ((), (), s32[]{:S(2)}) async-start(), calls=%async_computation.11 | async-start | bytes 1769472 | tf_op jit(solution)/shard_map/all_gather | solution.py:405
  7.2 19.0 %collective-permute-start.3 = (bf16[192,768]{1,0:T(8,128)(2,1)}, bf16[192,768]{1,0:T(8,128)(2,1)S(1)}, u32[]{:S(2)}, u32[]{:S(2)}) collective-permute-start(bf16[192,768]{1,0:T(8,128)(2,1)} %refs_0_.8), channel_id=1, source_target_pairs={{0,1},{1,0},{2,3},{3,2},{4,5},{5,4},{6,7},{7,6},{8,9},{9,8},{10,11... | collective-permute-start | bytes 884744 | tf_op jit(solution)/shard_map/ppermute | solution.py:317
  7.8 20.3 %collective-permute-start.4 = (bf16[192,768]{1,0:T(8,128)(2,1)}, bf16[192,768]{1,0:T(8,128)(2,1)S(1)}, u32[]{:S(2)}, u32[]{:S(2)}) collective-permute-start(bf16[192,768]{1,0:T(8,128)(2,1)} %refs_0_.8), channel_id=1, source_target_pairs={{0,2},{1,3},{2,0},{3,1},{4,6},{5,7},{6,4},{7,5},{8,10},{9,11},{10,... | collective-permute-start | bytes 884744 | tf_op jit(solution)/shard_map/ppermute | solution.py:317
  10.3 17.7 %collective-permute-start.6 = (bf16[192,768]{1,0:T(8,128)(2,1)}, bf16[192,768]{1,0:T(8,128)(2,1)S(1)}, u32[]{:S(2)}, u32[]{:S(2)}) collective-permute-start(bf16[192,768]{1,0:T(8,128)(2,1)} %refs_0_.9), channel_id=1, source_target_pairs={{0,1},{1,0},{2,3},{3,2},{4,5},{5,4},{6,7},{7,6},{8,9},{9,8},{10,11... | collective-permute-start | bytes 884744 | tf_op jit(solution)/shard_map/ppermute | solution.py:317
  10.5 18.1 %collective-permute-start.7 = (bf16[192,768]{1,0:T(8,128)(2,1)}, bf16[192,768]{1,0:T(8,128)(2,1)S(1)}, u32[]{:S(2)}, u32[]{:S(2)}) collective-permute-start(bf16[192,768]{1,0:T(8,128)(2,1)} %refs_0_.9), channel_id=1, source_target_pairs={{0,2},{1,3},{2,0},{3,1},{4,6},{5,7},{6,4},{7,5},{8,10},{9,11},{10,... | collective-permute-start | bytes 884744 | tf_op jit(solution)/shard_map/ppermute | solution.py:317
  10.8 362.9 %reduce-scatter.7.cloned.1.call-start = ((), (), s32[]{:S(2)}) async-start(), calls=%async_computation.5 | async-start | bytes 1327104 | tf_op jit(solution)/shard_map/reduce_scatter | solution.py:382
  10.9 18.5 %collective-permute-start.12 = (bf16[192,768]{1,0:T(8,128)(2,1)}, bf16[192,768]{1,0:T(8,128)(2,1)S(1)}, u32[]{:S(2)}, u32[]{:S(2)}) collective-permute-start(bf16[192,768]{1,0:T(8,128)(2,1)} %refs_0_.11), channel_id=1, source_target_pairs={{0,1},{1,0},{2,3},{3,2},{4,5},{5,4},{6,7},{7,6},{8,9},{9,8},{10,11... | collective-permute-start | bytes 884744 | tf_op jit(solution)/shard_map/ppermute | solution.py:317
  26.3 10.2 %collective-permute-start.13 = (bf16[192,768]{1,0:T(8,128)(2,1)}, bf16[192,768]{1,0:T(8,128)(2,1)}, u32[]{:S(2)}, u32[]{:S(2)}) collective-permute-start(bf16[192,768]{1,0:T(8,128)(2,1)} %refs_0_.11), channel_id=1, source_target_pairs={{0,2},{1,3},{2,0},{3,1},{4,6},{5,7},{6,4},{7,5},{8,10},{9,11},{10,... | collective-permute-start | bytes 884744 | tf_op jit(solution)/shard_map/ppermute | solution.py:317
  28.1 12.6 %collective-permute-start.9 = (bf16[192,1536]{1,0:T(8,128)(2,1)}, bf16[192,1536]{1,0:T(8,128)(2,1)}, u32[]{:S(2)}, u32[]{:S(2)}) collective-permute-start(bf16[192,1536]{1,0:T(8,128)(2,1)} %refs_0_.10), channel_id=1, source_target_pairs={{0,1},{1,0},{2,3},{3,2},{4,5},{5,4},{6,7},{7,6},{8,9},{9,8},{10,11... | collective-permute-start | bytes 1769480 | tf_op jit(solution)/shard_map/ppermute | solution.py:317
  28.1 10.1 %collective-permute-start.5 = (bf16[192,768]{1,0:T(8,128)(2,1)S(1)}, bf16[192,768]{1,0:T(8,128)(2,1)}, u32[]{:S(2)}, u32[]{:S(2)}) collective-permute-start(bf16[192,768]{1,0:T(8,128)(2,1)S(1)} %collective-permute-done.4.refs_2_), channel_id=1, source_target_pairs={{0,1},{1,0},{2,3},{3,2},{4,5},{5,4},{6,7},{7,6},{8,9},{9,8},{10,11... | collective-permute-start | bytes 884744 | tf_op jit(solution)/shard_map/ppermute | solution.py:317
  28.6 10.0 %collective-permute-start.8 = (bf16[192,768]{1,0:T(8,128)(2,1)S(1)}, bf16[192,768]{1,0:T(8,128)(2,1)}, u32[]{:S(2)}, u32[]{:S(2)}) collective-permute-start(bf16[192,768]{1,0:T(8,128)(2,1)S(1)} %collective-permute-done.7.refs_2_), channel_id=1, source_target_pairs={{0,1},{1,0},{2,3},{3,2},{4,5},{5,4},{6,7},{7,6},{8,9},{9,8},{10,11... | collective-permute-start | bytes 884744 | tf_op jit(solution)/shard_map/ppermute | solution.py:317
  29.4 19.7 %collective-permute-start.10 = (bf16[192,1536]{1,0:T(8,128)(2,1)}, bf16[192,1536]{1,0:T(8,128)(2,1)}, u32[]{:S(2)}, u32[]{:S(2)}) collective-permute-start(bf16[192,1536]{1,0:T(8,128)(2,1)} %refs_0_.10), channel_id=1, source_target_pairs={{0,2},{1,3},{2,0},{3,1},{4,6},{5,7},{6,4},{7,5},{8,10},{9,11},{10,... | collective-permute-start | bytes 1769480 | tf_op jit(solution)/shard_map/ppermute | solution.py:317
  36.4 82.1 %collective-permute-start.16 = (bf16[192,3072]{1,0:T(8,128)(2,1)}, bf16[192,3072]{1,0:T(8,128)(2,1)S(1)}, u32[]{:S(2)}, u32[]{:S(2)}) collective-permute-start(bf16[192,3072]{1,0:T(8,128)(2,1)} %refs_0_.12), channel_id=1, source_target_pairs={{0,2},{1,3},{2,0},{3,1},{4,6},{5,7},{6,4},{7,5},{8,10},{9,11},{10,... | collective-permute-start | bytes 3538952 | tf_op jit(solution)/shard_map/ppermute | solution.py:317
  38.2 80.4 %collective-permute-start.19 = (bf16[768,768]{1,0:T(8,128)(2,1)}, bf16[768,768]{1,0:T(8,128)(2,1)S(1)}, u32[]{:S(2)}, u32[]{:S(2)}) collective-permute-start(bf16[768,768]{1,0:T(8,128)(2,1)} %refs_0_.13), channel_id=1, source_target_pairs={{0,2},{1,3},{2,0},{3,1},{4,6},{5,7},{6,4},{7,5},{8,10},{9,11},{10,... | collective-permute-start | bytes 3538952 | tf_op jit(solution)/shard_map/ppermute | solution.py:317
  40.5 10.3 %collective-permute-start = (bf16[192,2304]{1,0:T(8,128)(2,1)}, bf16[192,2304]{1,0:T(8,128)(2,1)S(1)}, u32[]{:S(2)}, u32[]{:S(2)}) collective-permute-start(bf16[192,2304]{1,0:T(8,128)(2,1)} %refs_0_.7), channel_id=1, source_target_pairs={{0,1},{1,0},{2,3},{3,2},{4,5},{5,4},{6,7},{7,6},{8,9},{9,8},{10,11... | collective-permute-start | bytes 2654216 | tf_op jit(solution)/shard_map/ppermute | solution.py:317
  40.6 77.4 %collective-permute-start.1 = (bf16[192,2304]{1,0:T(8,128)(2,1)}, bf16[192,2304]{1,0:T(8,128)(2,1)}, u32[]{:S(2)}, u32[]{:S(2)}) collective-permute-start(bf16[192,2304]{1,0:T(8,128)(2,1)} %refs_0_.7), channel_id=1, source_target_pairs={{0,2},{1,3},{2,0},{3,1},{4,6},{5,7},{6,4},{7,5},{8,10},{9,11},{10,... | collective-permute-start | bytes 2654216 | tf_op jit(solution)/shard_map/ppermute | solution.py:317
  49.1 68.9 %collective-permute-start.11 = (bf16[192,1536]{1,0:T(8,128)(2,1)}, bf16[192,1536]{1,0:T(8,128)(2,1)S(1)}, u32[]{:S(2)}, u32[]{:S(2)}) collective-permute-start(bf16[192,1536]{1,0:T(8,128)(2,1)} %collective-permute-done.10.refs_2_), channel_id=1, source_target_pairs={{0,1},{1,0},{2,3},{3,2},{4,5},{5,4},{6,7},{7,6},{8,9},{9,8},{10,11... | collective-permute-start | bytes 1769480 | tf_op jit(solution)/shard_map/ppermute | solution.py:317
  50.8 95.3 %collective-permute-start.15 = (bf16[192,3072]{1,0:T(8,128)(2,1)}, bf16[192,3072]{1,0:T(8,128)(2,1)}, u32[]{:S(2)}, u32[]{:S(2)}) collective-permute-start(bf16[192,3072]{1,0:T(8,128)(2,1)} %refs_0_.12), channel_id=1, source_target_pairs={{0,1},{1,0},{2,3},{3,2},{4,5},{5,4},{6,7},{7,6},{8,9},{9,8},{10,11... | collective-permute-start | bytes 3538952 | tf_op jit(solution)/shard_map/ppermute | solution.py:317
  118.0 33.1 %collective-permute-start.18 = (bf16[768,768]{1,0:T(8,128)(2,1)}, bf16[768,768]{1,0:T(8,128)(2,1)}, u32[]{:S(2)}, u32[]{:S(2)}) collective-permute-start(bf16[768,768]{1,0:T(8,128)(2,1)} %refs_0_.13), channel_id=1, source_target_pairs={{0,1},{1,0},{2,3},{3,2},{4,5},{5,4},{6,7},{7,6},{8,9},{9,8},{10,11... | collective-permute-start | bytes 3538952 | tf_op jit(solution)/shard_map/ppermute | solution.py:317
  118.0 21.0 %collective-permute-start.2 = (bf16[192,2304]{1,0:T(8,128)(2,1)}, bf16[192,2304]{1,0:T(8,128)(2,1)}, u32[]{:S(2)}, u32[]{:S(2)}) collective-permute-start(bf16[192,2304]{1,0:T(8,128)(2,1)} %collective-permute-done.1.refs_2_), channel_id=1, source_target_pairs={{0,1},{1,0},{2,3},{3,2},{4,5},{5,4},{6,7},{7,6},{8,9},{9,8},{10,11... | collective-permute-start | bytes 2654216 | tf_op jit(solution)/shard_map/ppermute | solution.py:317
  118.5 27.5 %collective-permute-start.17 = (bf16[192,3072]{1,0:T(8,128)(2,1)S(1)}, bf16[192,3072]{1,0:T(8,128)(2,1)}, u32[]{:S(2)}, u32[]{:S(2)}) collective-permute-start(bf16[192,3072]{1,0:T(8,128)(2,1)S(1)} %collective-permute-done.16.refs_2_), channel_id=1, source_target_pairs={{0,1},{1,0},{2,3},{3,2},{4,5},{5,4},{6,7},{7,6},{8,9},{9,8},{10,11... | collective-permute-start | bytes 3538952 | tf_op jit(solution)/shard_map/ppermute | solution.py:317
  118.6 32.5 %collective-permute-start.20 = (bf16[768,768]{1,0:T(8,128)(2,1)S(1)}, bf16[768,768]{1,0:T(8,128)(2,1)}, u32[]{:S(2)}, u32[]{:S(2)}) collective-permute-start(bf16[768,768]{1,0:T(8,128)(2,1)S(1)} %collective-permute-done.19.refs_2_), channel_id=1, source_target_pairs={{0,1},{1,0},{2,3},{3,2},{4,5},{5,4},{6,7},{7,6},{8,9},{9,8},{10,11... | collective-permute-start | bytes 3538952 | tf_op jit(solution)/shard_map/ppermute | solution.py:317
  236.4 10.3 %collective-permute-start.35 = (bf16[384,768]{1,0:T(8,128)(2,1)S(1)}, bf16[384,768]{1,0:T(8,128)(2,1)S(1)}, u32[]{:S(2)}, u32[]{:S(2)}) collective-permute-start(bf16[384,768]{1,0:T(8,128)(2,1)S(1)} %convolution_convert_fusion.8), channel_id=1, source_target_pairs={{0,1},{1,0},{2,3},{3,2},{4,5},{5,4},{6,7},{7,6},{8,9},{9,8},{10,11... | collective-permute-start | bytes 1769480 | tf_op jit(solution)/shard_map/ppermute | solution.py:317
  236.7 11.5 %collective-permute-start.33 = (bf16[384,768]{1,0:T(8,128)(2,1)S(1)}, bf16[384,768]{1,0:T(8,128)(2,1)S(1)}, u32[]{:S(2)}, u32[]{:S(2)}) collective-permute-start(bf16[384,768]{1,0:T(8,128)(2,1)S(1)} %convolution_convert_fusion.9), channel_id=1, source_target_pairs={{0,1},{1,0},{2,3},{3,2},{4,5},{5,4},{6,7},{7,6},{8,9},{9,8},{10,11... | collective-permute-start | bytes 1769480 | tf_op jit(solution)/shard_map/ppermute | solution.py:317
  236.9 8.9 %collective-permute-start.27 = (bf16[384,768]{1,0:T(8,128)(2,1)S(1)}, bf16[384,768]{1,0:T(8,128)(2,1)S(1)}, u32[]{:S(2)}, u32[]{:S(2)}) collective-permute-start(bf16[384,768]{1,0:T(8,128)(2,1)S(1)} %fusion.31), channel_id=1, source_target_pairs={{0,1},{1,0},{2,3},{3,2},{4,5},{5,4},{6,7},{7,6},{8,9},{9,8},{10,11... | collective-permute-start | bytes 1769480 | tf_op jit(solution)/shard_map/ppermute | solution.py:317
  237.2 12.4 %collective-permute-start.25 = (bf16[384,768]{1,0:T(8,128)(2,1)S(1)}, bf16[384,768]{1,0:T(8,128)(2,1)S(1)}, u32[]{:S(2)}, u32[]{:S(2)}) collective-permute-start(bf16[384,768]{1,0:T(8,128)(2,1)S(1)} %fusion.28), channel_id=1, source_target_pairs={{0,1},{1,0},{2,3},{3,2},{4,5},{5,4},{6,7},{7,6},{8,9},{9,8},{10,11... | collective-permute-start | bytes 1769480 | tf_op jit(solution)/shard_map/ppermute | solution.py:317
  238.7 43.4 %collective-permute-start.29 = (bf16[384,768]{1,0:T(8,128)(2,1)}, bf16[384,768]{1,0:T(8,128)(2,1)}, u32[]{:S(2)}, u32[]{:S(2)}) collective-permute-start(bf16[384,768]{1,0:T(8,128)(2,1)} %convolution_convert_fusion.5), channel_id=1, source_target_pairs={{0,1},{1,0},{2,3},{3,2},{4,5},{5,4},{6,7},{7,6},{8,9},{9,8},{10,11... | collective-permute-start | bytes 1769480 | tf_op jit(solution)/shard_map/ppermute | solution.py:317
  245.8 38.0 %collective-permute-start.31 = (bf16[384,768]{1,0:T(8,128)(2,1)}, bf16[384,768]{1,0:T(8,128)(2,1)}, u32[]{:S(2)}, u32[]{:S(2)}) collective-permute-start(bf16[384,768]{1,0:T(8,128)(2,1)} %convolution_convert_fusion.4), channel_id=1, source_target_pairs={{0,1},{1,0},{2,3},{3,2},{4,5},{5,4},{6,7},{7,6},{8,9},{9,8},{10,11... | collective-permute-start | bytes 1769480 | tf_op jit(solution)/shard_map/ppermute | solution.py:317
  246.7 4.0 collective-permute-start.21
  248.3 4.5 collective-permute-start.23
  249.7 62.5 %collective-permute-start.37 = (bf16[384,3072]{1,0:T(8,128)(2,1)}, bf16[384,3072]{1,0:T(8,128)(2,1)}, u32[]{:S(2)}, u32[]{:S(2)}) collective-permute-start(bf16[384,3072]{1,0:T(8,128)(2,1)} %convolution_convert_fusion), channel_id=1, source_target_pairs={{0,1},{1,0},{2,3},{3,2},{4,5},{5,4},{6,7},{7,6},{8,9},{9,8},{10,11... | collective-permute-start | bytes 7077896 | tf_op jit(solution)/shard_map/ppermute | solution.py:317
  250.6 9.9 %collective-permute-start.28 = (bf16[192,768]{1,0:T(8,128)(2,1)S(1)}, bf16[192,768]{1,0:T(8,128)(2,1)S(1)}, u32[]{:S(2)}, u32[]{:S(2)}) collective-permute-start(bf16[192,768]{1,0:T(8,128)(2,1)S(1)} %add_convert_fusion.13), channel_id=1, source_target_pairs={{0,2},{1,3},{2,0},{3,1},{4,6},{5,7},{6,4},{7,5},{8,10},{9,11},{10,... | collective-permute-start | bytes 884744 | tf_op jit(solution)/shard_map/ppermute | solution.py:317
  252.8 14.1 %collective-permute-start.26 = (bf16[192,768]{1,0:T(8,128)(2,1)S(1)}, bf16[192,768]{1,0:T(8,128)(2,1)S(1)}, u32[]{:S(2)}, u32[]{:S(2)}) collective-permute-start(bf16[192,768]{1,0:T(8,128)(2,1)S(1)} %add_convert_fusion.15), channel_id=1, source_target_pairs={{0,2},{1,3},{2,0},{3,1},{4,6},{5,7},{6,4},{7,5},{8,10},{9,11},{10,... | collective-permute-start | bytes 884744 | tf_op jit(solution)/shard_map/ppermute | solution.py:317
  260.5 12.6 %collective-permute-start.22 = (bf16[192,768]{1,0:T(8,128)(2,1)S(1)}, bf16[192,768]{1,0:T(8,128)(2,1)S(1)}, u32[]{:S(2)}, u32[]{:S(2)}) collective-permute-start(bf16[192,768]{1,0:T(8,128)(2,1)S(1)} %add_convert_fusion.19), channel_id=1, source_target_pairs={{0,2},{1,3},{2,0},{3,1},{4,6},{5,7},{6,4},{7,5},{8,10},{9,11},{10,... | collective-permute-start | bytes 884744 | tf_op jit(solution)/shard_map/ppermute | solution.py:317
  266.9 12.0 %collective-permute-start.24 = (bf16[192,768]{1,0:T(8,128)(2,1)S(1)}, bf16[192,768]{1,0:T(8,128)(2,1)S(1)}, u32[]{:S(2)}, u32[]{:S(2)}) collective-permute-start(bf16[192,768]{1,0:T(8,128)(2,1)S(1)} %add_convert_fusion.17), channel_id=1, source_target_pairs={{0,2},{1,3},{2,0},{3,1},{4,6},{5,7},{6,4},{7,5},{8,10},{9,11},{10,... | collective-permute-start | bytes 884744 | tf_op jit(solution)/shard_map/ppermute | solution.py:317
  273.2 34.2 %collective-permute-start.39 = (bf16[1536,768]{1,0:T(8,128)(2,1)}, bf16[1536,768]{1,0:T(8,128)(2,1)}, u32[]{:S(2)}, u32[]{:S(2)}) collective-permute-start(bf16[1536,768]{1,0:T(8,128)(2,1)} %convolution_convert_fusion.2), channel_id=1, source_target_pairs={{0,1},{1,0},{2,3},{3,2},{4,5},{5,4},{6,7},{7,6},{8,9},{9,8},{10,11... | collective-permute-start | bytes 7077896 | tf_op jit(solution)/shard_map/ppermute | solution.py:317
  278.8 10.3 %collective-permute-start.36 = (bf16[192,768]{1,0:T(8,128)(2,1)}, bf16[192,768]{1,0:T(8,128)(2,1)}, u32[]{:S(2)}, u32[]{:S(2)}) collective-permute-start(bf16[192,768]{1,0:T(8,128)(2,1)} %add_convert_fusion.5), channel_id=1, source_target_pairs={{0,2},{1,3},{2,0},{3,1},{4,6},{5,7},{6,4},{7,5},{8,10},{9,11},{10,... | collective-permute-start | bytes 884744 | tf_op jit(solution)/shard_map/ppermute | solution.py:317
  281.9 131.4 %reduce-scatter.9.cloned.1.call-start = ((), (), s32[]{:S(2)}) async-start(), calls=%async_computation.7 | async-start | bytes 1327104 | tf_op jit(solution)/shard_map/reduce_scatter | solution.py:382
  282.1 13.2 %collective-permute-start.34 = (bf16[192,768]{1,0:T(8,128)(2,1)}, bf16[192,768]{1,0:T(8,128)(2,1)S(1)}, u32[]{:S(2)}, u32[]{:S(2)}) collective-permute-start(bf16[192,768]{1,0:T(8,128)(2,1)} %add_convert_fusion.7), channel_id=1, source_target_pairs={{0,2},{1,3},{2,0},{3,1},{4,6},{5,7},{6,4},{7,5},{8,10},{9,11},{10,... | collective-permute-start | bytes 884744 | tf_op jit(solution)/shard_map/ppermute | solution.py:317
  283.8 17.9 %collective-permute-start.30 = (bf16[192,768]{1,0:T(8,128)(2,1)S(1)}, bf16[192,768]{1,0:T(8,128)(2,1)S(1)}, u32[]{:S(2)}, u32[]{:S(2)}) collective-permute-start(bf16[192,768]{1,0:T(8,128)(2,1)S(1)} %add_convert_fusion.11), channel_id=1, source_target_pairs={{0,2},{1,3},{2,0},{3,1},{4,6},{5,7},{6,4},{7,5},{8,10},{9,11},{10,... | collective-permute-start | bytes 884744 | tf_op jit(solution)/shard_map/ppermute | solution.py:317
  289.1 17.3 %collective-permute-start.32 = (bf16[192,768]{1,0:T(8,128)(2,1)S(1)}, bf16[192,768]{1,0:T(8,128)(2,1)S(1)}, u32[]{:S(2)}, u32[]{:S(2)}) collective-permute-start(bf16[192,768]{1,0:T(8,128)(2,1)S(1)} %add_convert_fusion.9), channel_id=1, source_target_pairs={{0,2},{1,3},{2,0},{3,1},{4,6},{5,7},{6,4},{7,5},{8,10},{9,11},{10,... | collective-permute-start | bytes 884744 | tf_op jit(solution)/shard_map/ppermute | solution.py:317
  310.4 29.2 %collective-permute-start.40 = (bf16[768,768]{1,0:T(8,128)(2,1)}, bf16[768,768]{1,0:T(8,128)(2,1)}, u32[]{:S(2)}, u32[]{:S(2)}) collective-permute-start(bf16[768,768]{1,0:T(8,128)(2,1)} %add_convert_fusion.1), channel_id=1, source_target_pairs={{0,2},{1,3},{2,0},{3,1},{4,6},{5,7},{6,4},{7,5},{8,10},{9,11},{10,... | collective-permute-start | bytes 3538952 | tf_op jit(solution)/shard_map/ppermute | solution.py:317
  315.0 47.5 %collective-permute-start.38 = (bf16[192,3072]{1,0:T(8,128)(2,1)}, bf16[192,3072]{1,0:T(8,128)(2,1)}, u32[]{:S(2)}, u32[]{:S(2)}) collective-permute-start(bf16[192,3072]{1,0:T(8,128)(2,1)} %add_convert_fusion.3), channel_id=1, source_target_pairs={{0,2},{1,3},{2,0},{3,1},{4,6},{5,7},{6,4},{7,5},{8,10},{9,11},{10,... | collective-permute-start | bytes 3538952 | tf_op jit(solution)/shard_map/ppermute | solution.py:317
  316.5 168.6 %reduce-scatter.11.cloned.1.call-start = ((), (), s32[]{:S(2)}) async-start(), calls=%async_computation.9 | async-start | bytes 2654208 | tf_op jit(solution)/shard_map/reduce_scatter | solution.py:382
  366.2 186.2 %reduce-scatter.5.cloned.1.call-start = ((), (), s32[]{:S(2)}) async-start(), calls=%async_computation.4 | async-start | bytes 1769472 | tf_op jit(solution)/shard_map/reduce_scatter | solution.py:486
  373.7 222.4 %all-gather.7.cloned.1.call-start = ((), (), s32[]{:S(2)}) async-start(), calls=%async_computation.6 | async-start | bytes 1327104 | tf_op jit(solution)/shard_map/all_gather | solution.py:383
  374.3 262.8 %all-gather.9.cloned.1.call-start = ((), (), s32[]{:S(2)}) async-start(), calls=%async_computation.8 | async-start | bytes 1327104 | tf_op jit(solution)/shard_map/all_gather | solution.py:383
  413.2 277.1 %all-gather.11.cloned.1.call-start = ((), (), s32[]{:S(2)}) async-start(), calls=%async_computation.10 | async-start | bytes 2654208 | tf_op jit(solution)/shard_map/all_gather | solution.py:383
  (78 other events, 1342.3 us)
Sparse Core Ops, SparseCore 0:
  10.9 46.1 all-gather.12
  282.0 64.3 reduce-scatter.6
  350.3 62.8 reduce-scatter.8
  417.1 67.9 reduce-scatter.10
  488.4 64.0 reduce-scatter.4
  554.7 40.0 all-gather.6
  597.2 39.8 all-gather.8
  639.5 50.8 all-gather.10

commit v2 on v1

--- a/solution.py
+++ b/solution.py
@@ -356,31 +356,196 @@
     return assemble(index, [share, sibling, across, across_sibling])
 
 
-def column_blocks(values, index, count):
-    width = values.shape[1] // count
-    cut = [
-        lax.dynamic_slice_in_dim(values, (index ^ j) * width, width, axis=1) for j in (0, 2, 1, 3)
-    ]
-    return cut[0], cut[1], jnp.concatenate(cut[2:], axis=1)
-
-
-def share_of_product(index, terms, count):
-    cut = [(column_blocks(left, index, count), right) for left, right in terms]
-
-    def total(which):
-        return sum(left_product(blocks[which], right) for blocks, right in cut)
-
-    received = swap(to_low(total(2)), "fsdp", 1)
-    rows = received.shape[0] // 2
-    across = swap(to_low(total(1) + received[rows:].astype(jnp.float32)), "fsdp", 2)
-    return to_low(
-        total(0) + received[:rows].astype(jnp.float32) + across.astype(jnp.float32)
-    )
-
-
-def reduce_over_ctx(share):
-    part = lax.psum_scatter(share, "ctx", scatter_dimension=0, tiled=True)
-    return lax.all_gather(part, "ctx", axis=0, tiled=True)
+def mirrored(position, count):
+    out = 0
+    for _ in range(count.bit_length() - 1):
+        out, position = 2 * out + position % 2, position // 2
+    return out
+
+
+def chunk_count(rows):
+    count = lax.axis_size("ctx")
+    return count if count & (count - 1) == 0 and rows % (8 * count) == 0 else 1
+
+
+def store_chunks(out_ref, start, held_ref, base, rows, ctx_index, chunks):
+    size = rows // chunks
+    for p in range(chunks):
+        place = base + (ctx_index ^ mirrored(p, chunks)) * size
+        part = held_ref[pl.ds(pl.multiple_of(place, 8), size), :]
+        out_ref[pl.ds(start + p * size, size), :] = part.astype(out_ref.dtype)
+
+
+def products_kernel(tiles, rows, chunks, index_ref, *refs):
+    count = len(tiles)
+    inputs, (keep_ref, send_ref, held_ref) = refs[:-3], refs[-3:]
+    fsdp_index, ctx_index = index_ref[0], index_ref[1]
+    width = held_ref.shape[1]
+    for t, (left, right, column) in enumerate(tiles):
+
+        @pl.when(pl.program_id(0) == t)
+        def _(left=left, right=right, column=column):
+            grads = inputs[right][:, pl.ds(column * width, width)]
+            held_ref[...] = left_product(inputs[left][...], grads)
+
+    for out_ref, order in ((keep_ref, (0, 2)), (send_ref, (1, 3))):
+        for k, j in enumerate(order):
+            store_chunks(
+                out_ref, k * rows, held_ref, (fsdp_index ^ j) * rows, rows, ctx_index, chunks
+            )
+
+
+def wide_products(index, terms):
+    shares = lax.axis_size("fsdp")
+    inputs, tiles = [], []
+    width = terms[0][0].shape[1]
+    for left, right, plane in terms:
+        if not inputs or all(left is not value for value, _ in inputs):
+            inputs.append((left, None))
+        first = next(i for i, (value, _) in enumerate(inputs) if value is left)
+        inputs.append((right, plane))
+        for column in range(right.shape[-1] // width):
+            tiles.append((first, len(inputs) - 1, column))
+    rows = width // shares
+    chunks = chunk_count(rows)
+    specs = []
+    for value, plane in inputs:
+        if value.ndim == 2:
+            specs.append(pl.BlockSpec(value.shape, lambda i, _: (0, 0)))
+        else:
+            specs.append(
+                pl.BlockSpec((None,) + value.shape[1:], lambda i, _, plane=plane: (plane, 0, 0))
+            )
+    total = len(tiles) * width
+    out = jax.ShapeDtypeStruct((2 * rows, total), jnp.bfloat16)
+    out_spec = pl.BlockSpec((2 * rows, width), lambda i, _: (0, i))
+    tokens = sum(left.shape[0] * right.shape[-1] for left, right, _ in terms)
+    return pl.pallas_call(
+        functools.partial(products_kernel, tiles, rows, chunks),
+        grid_spec=pltpu.PrefetchScalarGridSpec(
+            num_scalar_prefetch=1,
+            grid=(len(tiles),),
+            in_specs=specs,
+            out_specs=[out_spec, out_spec],
+            scratch_shapes=[pltpu.VMEM((width, width), jnp.float32)],
+        ),
+        out_shape=[out, out],
+        cost_estimate=pl.CostEstimate(
+            flops=2 * width * tokens, bytes_accessed=8 * rows * total, transcendentals=0
+        ),
+        name="wide_products",
+    )(index, *[value for value, _ in inputs])
+
+
+def tall_kernel(rows, chunks, index_ref, left_ref, right_ref, keep_ref, send_ref, held_ref):
+    held_ref[...] = left_product(left_ref[...], right_ref[...])
+    for out_ref, steps in ((keep_ref, (0, 1)), (send_ref, (2, 3))):
+
+        @pl.when((pl.program_id(0) == steps[0]) | (pl.program_id(0) == steps[1]))
+        def _(out_ref=out_ref):
+            store_chunks(out_ref, 0, held_ref, 0, rows, index_ref[1], chunks)
+
+
+def tall_products(index, left, right):
+    shares = lax.axis_size("fsdp")
+    tokens, depth = left.shape
+    width = right.shape[1]
+    rows = depth // shares
+    chunks = chunk_count(rows)
+    out = jax.ShapeDtypeStruct((2 * rows, width), jnp.bfloat16)
+
+    def share_of(i, index_ref):
+        return (0, index_ref[0] ^ (2 * (i % 2) + i // 2))
+
+    return pl.pallas_call(
+        functools.partial(tall_kernel, rows, chunks),
+        grid_spec=pltpu.PrefetchScalarGridSpec(
+            num_scalar_prefetch=1,
+            grid=(shares,),
+            in_specs=[
+                pl.BlockSpec((tokens, rows), share_of),
+                pl.BlockSpec((tokens, width), lambda i, _: (0, 0)),
+            ],
+            out_specs=[
+                pl.BlockSpec((rows, width), lambda i, _: (jnp.minimum(i, 1), 0)),
+                pl.BlockSpec((rows, width), lambda i, _: (jnp.maximum(i - 2, 0), 0)),
+            ],
+            scratch_shapes=[pltpu.VMEM((rows, width), jnp.float32)],
+        ),
+        out_shape=[out, out],
+        cost_estimate=pl.CostEstimate(
+            flops=2 * tokens * depth * width, bytes_accessed=4 * depth * width, transcendentals=0
+        ),
+        name="tall_products",
+    )(index, left, right)
+
+
+def add_low(*parts):
+    return to_low(sum(part.astype(jnp.float32) for part in parts))
+
+
+def reduce_products(keep, send):
+    rows = keep.shape[0] // 2
+    received = swap(send, "fsdp", 1)
+    across = swap(add_low(keep[rows:], received[rows:]), "fsdp", 2)
+    chunks = chunk_count(rows)
+    if chunks == 1:
+        share = lax.psum(add_low(keep[:rows], received[:rows], across), "ctx")
+        return share[: rows // 2], share[rows // 2 :]
+    parts = (keep[:rows], received[:rows], across)
+    half = rows // 2
+    bit = 1
+    while bit < chunks:
+        sent = add_low(*[part[half:] for part in parts])
+        held = add_low(*[part[:half] for part in parts])
+        parts = (held, swap(sent, "ctx", bit))
+        half, bit = half // 2, 2 * bit
+    gathered = add_low(*parts)
+    while bit > 2:
+        bit = bit // 2
+        gathered = jnp.concatenate([gathered, swap(gathered, "ctx", bit)], axis=0)
+    return gathered, swap(gathered, "ctx", 1)
+
+
+def place_kernel(chunks, index_ref, low_ref, high_ref, out_ref):
+    size = out_ref.shape[0] // chunks
+    per_half = max(1, chunks // 2)
+    if chunks == 1:
+        half = out_ref.shape[0] // 2
+        out_ref[pl.ds(0, half), :] = low_ref[...].astype(jnp.float32)
+        out_ref[pl.ds(half, half), :] = high_ref[...].astype(jnp.float32)
+        return
+    for p in range(chunks):
+        source = low_ref if p < per_half else high_ref
+        part = source[pl.ds((p % per_half) * size, size), :].astype(jnp.float32)
+        place = (index_ref[1] ^ mirrored(p, chunks)) * size
+        out_ref[pl.ds(pl.multiple_of(place, 8), size), :] = part
+
+
+def place_share(index, halves, offset, width):
+    low, high = halves
+    rows = 2 * low.shape[0]
+    tile = 768 if width % 768 == 0 and offset % 768 == 0 else width
+    start = offset // tile
+    spec = pl.BlockSpec((rows // 2, tile), lambda i, _: (0, start + i))
+    return pl.pallas_call(
+        functools.partial(place_kernel, chunk_count(rows)),
+        grid_spec=pltpu.PrefetchScalarGridSpec(
+            num_scalar_prefetch=1,
+            grid=(width // tile,),
+            in_specs=[spec, spec],
+            out_specs=pl.BlockSpec((rows, tile), lambda i, _: (0, i)),
+        ),
+        out_shape=jax.ShapeDtypeStruct((rows, width), jnp.float32),
+        cost_estimate=pl.CostEstimate(
+            flops=0, bytes_accessed=6 * rows * width, transcendentals=0
+        ),
+        name="place_share",
+    )(index, low, high)
+
+
+def gain_gradient(weight, grad, gain):
+    return jnp.sum(weight.astype(jnp.float32) * grad, axis=1) / gain.astype(jnp.float32)
 
 
 def local(
@@ -401,8 +566,13 @@
     shares = lax.axis_size("fsdp")
     fsdp_index = lax.axis_index("fsdp")
     ctx_index = lax.axis_index("ctx")
-    place = fsdp_index.astype(jnp.int32).reshape(1)
-    hidden_all = lax.all_gather(hidden[0], "ctx", axis=0, tiled=True)
+    place = jnp.stack([fsdp_index, ctx_index]).astype(jnp.int32)
+    ctx_count = lax.axis_size("ctx")
+    hidden_all = hidden[0]
+    bit = ctx_count
+    while bit > 1:
+        bit = bit // 2
+        hidden_all = jnp.concatenate([hidden_all, swap(hidden_all, "ctx", bit)], axis=0)
     w_qkv = gather_weight(place, attn_qkv)
     w_ckv = gather_weight(place, cross_kv)
     w_out = gather_weight(place, attn_out)
@@ -410,7 +580,12 @@
     w_cout = gather_weight(place, cross_out)
     w_in = gather_weight(place, mlp_in)
     w_down = gather_weight(place, mlp_out)
-    gain_rows = lax.all_gather(norm_gains, "fsdp", axis=1, tiled=True).astype(jnp.float32)
+    gain_pair = jnp.stack([norm_gains, swap(norm_gains, "fsdp", 1)])
+    gain_pieces = jnp.concatenate([gain_pair, swap(gain_pair, "fsdp", 2)])
+    gain_rows = jnp.concatenate(
+        [lax.dynamic_index_in_dim(gain_pieces, fsdp_index ^ j, 0, False) for j in range(shares)],
+        axis=1,
+    ).astype(jnp.float32)
 
     tok_count, feature_width = hidden.shape[1:]
     stretch_count = tok_count // STRETCH
@@ -423,7 +598,9 @@
         jnp.where(seq_starts[None, :] <= deal_row[:, None], seq_starts[None, :], 0), axis=1
     )
     offsets = jnp.arange(STRETCH, dtype=jnp.int32)
-    token_pos = (deal_row[:, None] * STRETCH + offsets[None, :]).reshape(group_tok)
+    order = jnp.array([mirrored(p, ctx_count) for p in range(ctx_count)], jnp.int32) ^ ctx_index
+    held_deal = deal_row.reshape(ctx_count, stretch_count)[order].reshape(-1)
+    token_pos = (held_deal[:, None] * STRETCH + offsets[None, :]).reshape(group_tok)
     own_deal = lax.dynamic_slice_in_dim(deal_row, ctx_index * stretch_count, stretch_count)
     own_start = lax.dynamic_slice_in_dim(slot_start, ctx_index * stretch_count, stretch_count)
     keep_rows = jnp.repeat((own_deal != own_start).astype(jnp.float32), STRETCH)[:, None]
@@ -461,7 +638,6 @@
     grad_out = cotangent[0].astype(jnp.float32)
     grad_inner = to_low(right_product(cotangent[0], w_down) * slope)
     grad_norm3 = right_product(grad_inner, w_in)
-    grad_gain3 = jnp.sum(grad_norm3 * after_cross * scale_three, axis=0)
     grad_after_cross = grad_out + rms_back(after_cross, scale_three, gain_rows[2], grad_norm3)
     grad_cross_branch = to_low(keep_rows * grad_after_cross)
     grad_cross_rows = to_low(right_product(grad_cross_branch, w_cout))
@@ -469,7 +645,6 @@
         cross_query, cross_key_value, grad_cross_rows, stretch_count
     )
     grad_norm2 = right_product(grad_cross_query, w_cq)
-    grad_gain2 = jnp.sum(grad_norm2 * after_attn * scale_two, axis=0)
     grad_after_attn = grad_after_cross + rms_back(
         after_attn, scale_two, gain_rows[1], grad_norm2
     )
@@ -482,56 +657,69 @@
         grad_pair[0], w_qkv[:, feature_width : 2 * feature_width]
     ) + right_product(grad_pair[1], w_qkv[:, 2 * feature_width :])
     grad_norm1_query = right_product(grad_query, w_qkv[:, :feature_width])
-    grad_norm1 = (
-        lax.psum_scatter(to_low(grad_norm1_all), "ctx", scatter_dimension=0, tiled=True).astype(
-            jnp.float32
-        )
-        + grad_norm1_query
-    )
+    grad_norm1 = to_low(grad_norm1_all)
+    bit = 1
+    while bit < ctx_count:
+        half = grad_norm1.shape[0] // 2
+        grad_norm1 = add_low(grad_norm1[:half], swap(grad_norm1[half:], "ctx", bit))
+        bit = 2 * bit
+    grad_norm1 = grad_norm1.astype(jnp.float32) + grad_norm1_query
     grad_input = grad_after_attn + rms_back(input_rows, scale_one, gain_rows[0], grad_norm1)
-    grad_gain1 = jnp.sum(grad_norm1_all * rows_all * scale_all, axis=0) + jnp.sum(
-        grad_norm1_query * input_rows * scale_one, axis=0
-    )
     grad_enc = right_product(grad_cross_pair[0], w_ckv[:, :feature_width]) + right_product(
         grad_cross_pair[1], w_ckv[:, feature_width:]
     )
 
-    product = functools.partial(share_of_product, fsdp_index, count=shares)
-    part_down = product([(activation, cotangent[0])])
-    part_in = product([(norm_three, grad_inner)])
-    part_cout = product([(cross_rows, grad_cross_branch)])
-    part_cq = product([(norm_two, grad_cross_query)])
-    part_ck = product([(enc_rows, grad_cross_pair[0])])
-    part_cv = product([(enc_rows, grad_cross_pair[1])])
-    part_out = product([(attended, grad_attn_branch)])
-    part_q = product([(norm_one, grad_query)])
-    part_k = product([(norm_all, grad_pair[0])])
-    part_v = product([(norm_all, grad_pair[1])])
-    share_rows = feature_width // shares
-    total_mlp = reduce_over_ctx(
-        jnp.concatenate([part_in, part_down.reshape(share_rows, -1)], axis=1)
-    ).astype(jnp.float32)
-    total_cross = reduce_over_ctx(
-        jnp.concatenate([part_cout, part_cq, part_ck, part_cv], axis=1)
-    ).astype(jnp.float32)
-    total_attn = reduce_over_ctx(
-        jnp.concatenate([part_out, part_q, part_k, part_v], axis=1)
-    ).astype(jnp.float32)
-    grad_gains = lax.psum(jnp.stack([grad_gain1, grad_gain2, grad_gain3]), ("ctx", "fsdp"))
-    grad_gains = lax.dynamic_slice_in_dim(grad_gains, fsdp_index * share_rows, share_rows, axis=1)
-    inner_width = mlp_in.shape[1]
+    halves_down = reduce_products(*tall_products(place, activation, cotangent[0]))
+    halves_in = reduce_products(*wide_products(place, [(norm_three, grad_inner, None)]))
+    halves_cross = reduce_products(
+        *wide_products(
+            place,
+            [
+                (cross_rows, grad_cross_branch, None),
+                (norm_two, grad_cross_query, None),
+                (enc_rows, grad_cross_pair, 0),
+                (enc_rows, grad_cross_pair, 1),
+                (attended, grad_attn_branch, None),
+            ],
+        )
+    )
+    halves_attn = reduce_products(
+        *wide_products(
+            place,
+            [
+                (norm_one, grad_query, None),
+                (norm_all, grad_pair, 0),
+                (norm_all, grad_pair, 1),
+            ],
+        )
+    )
+    d = feature_width
+    total_down = place_share(place, halves_down, 0, d)
+    total_in = place_share(place, halves_in, 0, mlp_in.shape[1])
+    total_cout = place_share(place, halves_cross, 0, d)
+    total_cq = place_share(place, halves_cross, d, d)
+    total_ckv = place_share(place, halves_cross, 2 * d, 2 * d)
+    total_out = place_share(place, halves_cross, 4 * d, d)
+    total_qkv = place_share(place, halves_attn, 0, 3 * d)
+    grad_gains = jnp.stack(
+        [
+            gain_gradient(attn_qkv, total_qkv, norm_gains[0]),
+            gain_gradient(cross_q, total_cq, norm_gains[1]),
+            gain_gradient(mlp_in, total_in, norm_gains[2]),
+        ]
+    )
     return (
         layer_out[None],
         grad_input[None],
         grad_enc.reshape(neighbours.shape),
         grad_gains,
-        total_attn[:, feature_width:],
-        total_attn[:, :feature_width],
-        total_cross[:, feature_width : 2 * feature_width],
-        total_cross[:, 2 * feature_width :],
-        total_cross[:, :feature_width],
-        total_mlp[:, :inner_width],
-        total_mlp[:, inner_width:].reshape(mlp_out.shape),
+        total_qkv,
+        total_out,
+        total_cq,
+        total_ckv,
+        total_cout,
+        total_in,
+        total_down,
     )
 
 

time: 708 us -> 469 us (0.66)
  waiting for transfers between devices: 412 us -> 199 us
  Pallas kernels: 56.9 us -> 113 us
  blocking collectives: 54.4 us -> 0 us
  matrix products: 79.9 us -> 45.7 us
  starting transfers between devices: 28.3 us -> 57.2 us
  local copies, waits for them, and re-layouts: 30 us -> 8.89 us
  between operations: 15.3 us -> 1.92 us
  other arithmetic: 26.2 us -> 38.7 us
    reduce_scatter x4 -> x0, waiting for transfers between devices: 170 us -> none  [the longest x3 111 us: reduce_over_ctx(): part = lax.psum_scatter(share, 'ctx', scatter_dimension=0, tiled=True)]
    all_gather x4 -> x0, waiting for transfers between devices: 87.6 us -> none  [the longest x3 87.6 us: reduce_over_ctx(): return lax.all_gather(part, 'ctx', axis=0, tiled=True)]
    pallas_call x0 -> x11, Pallas kernels: none -> 51.1 us  [the longest x3 22.4 us: wide_products(): pl.pallas_call(functools.partial(products_kernel, tiles, rows, chunks), g...]
    ppermute x41 -> x61, waiting for transfers between devices: 154 us -> 199 us  [swap(): return lax.ppermute(values, axis, [(i, i ^ bit) for i in range(count)])]
    psum x1 -> x0, blocking collectives: 40 us -> none  [local(): lax.psum(jnp.stack([grad_gain1, grad_gain2, grad_gain3]), ('ctx', 'fsdp'))]
    dot_general x30 -> x0, matrix products: 34.5 us -> none  [left_product(): lax.dot_general(left, right, (((0,), (0,)), ((), ())), preferred_element_...]
    ppermute x41 -> x61, starting transfers between devices: 27.8 us -> 57.2 us  [swap(): return lax.ppermute(values, axis, [(i, i ^ bit) for i in range(count)])]
    all_gather x1 -> x0, blocking collectives: 14.4 us -> none  [local(): lax.all_gather(norm_gains, 'fsdp', axis=1, tiled=True).astype(jnp.float32)]
  transfers between devices with their start and end apart: 49 -> 61, of which waited for: 19 -> 27; matrix products, arithmetic and copies ran while one was open for 12% -> 16% of each run, Pallas kernels for 3% -> 15%
where the time goes in v2:
time: 469 us; the launch traced here: 464 us
  waiting for transfers between devices  199 us (42%)
  Pallas kernels  113 us (24%)
  starting transfers between devices  57.2 us (12%)
  matrix products  45.7 us (10%)
  other arithmetic  38.7 us (8%)
  local copies, waits for them, and re-layouts  8.89 us (2%)
    ppermute x61, waiting for transfers between devices, swap(): return lax.ppermute(values, axis, [(i, i ^ bit) for i in range(count)])  199 us
    ppermute x61, starting transfers between devices, swap(): return lax.ppermute(values, axis, [(i, i ^ bit) for i in range(count)])  57.2 us
    pallas_call x7, Pallas kernels, assemble(): pl.pallas_call(assemble_kernel, grid_spec=pltpu.PrefetchScalarGridSpec(nu...  29.5 us
    dot_general x8, matrix products, matmul(): return jnp.dot(left, right, preferred_element_type=jnp.float32)  23.1 us
    dot_general x10, matrix products, right_product(): lax.dot_general(left, right, (((1,), (1,)), ((), ())), preferred_element_...  22.6 us
    pallas_call x3, Pallas kernels, wide_products(): pl.pallas_call(functools.partial(products_kernel, tiles, rows, chunks), g...  22.4 us
    pallas_call x7, Pallas kernels, place_share(): pl.pallas_call(functools.partial(place_kernel, chunk_count(rows)), grid_s...  22.1 us
    convert_element_type x28, other arithmetic, to_low(): return values.astype(jnp.bfloat16)  20.3 us
  transfers between devices with their start and end apart: 61, of which 27 were waited for; matrix products, arithmetic and copies ran while one was open for 16% of the time, Pallas kernels for 15%

profile of v2, /device:TPU:0, one launch (start us, length us, event | category | flops | bytes accessed | tf_op | source)
XLA Modules:
  0.0 463.9 jit_solution(1428073581218780735)
XLA Ops:
  21.4 5.2 %collective-permute-done.18.refs_2_ = bf16[192,768]{1,0:T(8,128)(2,1)S(1)} collective-permute-done((bf16[192,768]{1,0:T(8,128)(2,1)}, bf16[192,768]{1,0:T(8,128)(2,1)S(1)}, u32[]{:S(2)}, u32[]{:S(2)}) %collective-permute-start.18) | collective-permute-done | bytes 294944 | tf_op jit(solution)/shard_map/ppermute | solution.py:317
  26.6 6.3 %collective-permute-done.12.refs_2_ = bf16[192,768]{1,0:T(8,128)(2,1)S(1)} collective-permute-done((bf16[192,768]{1,0:T(8,128)(2,1)}, bf16[192,768]{1,0:T(8,128)(2,1)S(1)}, u32[]{:S(2)}, u32[]{:S(2)}) %collective-permute-start.12) | collective-permute-done | bytes 294944 | tf_op jit(solution)/shard_map/ppermute | solution.py:317
  41.5 4.2 collective-permute-done.15.refs_2_
  51.2 3.0 assemble.8
  54.2 3.0 assemble.11
  57.2 3.1 assemble.9
  60.4 4.1 collective-permute-done.3.refs_2_
  65.0 3.6 assemble.10
  68.6 4.4 fusion.5.k_ref.v_ref
  75.5 14.4 %collective-permute-done.24.refs_2_ = bf16[768,768]{1,0:T(8,128)(2,1)} collective-permute-done((bf16[768,768]{1,0:T(8,128)(2,1)}, bf16[768,768]{1,0:T(8,128)(2,1)}, u32[]{:S(2)}, u32[]{:S(2)}) %collective-permute-start.24) | collective-permute-done | bytes 1179680 | tf_op jit(solution)/shard_map/ppermute | solution.py:317
  89.9 23.8 %collective-permute-done.21.refs_2_ = bf16[192,3072]{1,0:T(8,128)(2,1)} collective-permute-done((bf16[192,3072]{1,0:T(8,128)(2,1)}, bf16[192,3072]{1,0:T(8,128)(2,1)}, u32[]{:S(2)}, u32[]{:S(2)}) %collective-permute-start.21) | collective-permute-done | bytes 1179680 | tf_op jit(solution)/shard_map/ppermute | solution.py:317
  113.7 5.4 %assemble.7 = bf16[768,2304]{1,0:T(8,128)(2,1)} custom-call(s32[2]{0:T(128)} %pad_add_fusion.index_ref, bf16[192,2304]{1,0:T(8,128)(2,1)} %refs_0_.7, bf16[192,2304]{1,0:T(8,128)(2,1)} %collective-permute-done.2.refs_1_, bf16[192,2304]{1,0:T(8,128)(2,1)} %copy-done.30, bf16[192,2304]{1,0:T(8,128)(2,1)} %collective-permute-done.4.refs_3_), custom_call_target="tpu_custom_call" | custom-call | bytes 7077888 | tf_op jit(solution)/shard_map/assemble/pallas_call | solution.py:336
  121.6 5.6 %convolution_convert_fusion.k_ref.v_ref = bf16[1024,1536]{1,0:T(8,128)(2,1)} fusion(bf16[1024,768]{1,0:T(8,128)(2,1)S(1)} %copy-done.23, bf16[768,2304]{1,0:T(8,128)(2,1)} %assemble.7), kind=kOutput, calls=%fused_computation.3 | convolution fusion | flops 2417491968 | bytes 7077888 | tf_op jit(solution)/shard_map/dot_general | solution.py:24
  128.3 7.6 %self_forward.1 = (bf16[128,768]{1,0:T(8,128)(2,1)}, f32[6,1,256]{2,1,0:T(1,128)}) custom-call(bf16[128,768]{1,0:T(8,128)(2,1)} %convolution_convert_fusion.5.q_ref, bf16[1024,1536]{1,0:T(8,128)(2,1)} %convolution_convert_fusion.k_ref.v_ref, bf16[1024,1536]{1,0:T(8,128)(2,1)} %convolution_convert_fusion.k_ref.v_ref, s32[1024,1]{1,0:T(8,128)} %add.346.pos_ref, ...), custom_call_target="tpu_custom_call" | custom-call | flops 805306368 | bytes 3145728 | tf_op jit(solution)/shard_map/self_forward/pallas_call | solution.py:196
  138.5 7.0 %cross_forward.1.refs_0_ = bf16[128,768]{1,0:T(8,128)(2,1)} custom-call(bf16[128,768]{1,0:T(8,128)(2,1)} %convolution_convert_fusion.4.q_ref, bf16[512,1536]{1,0:T(8,128)(2,1)} %fusion.5.k_ref.v_ref, bf16[512,1536]{1,0:T(8,128)(2,1)} %fusion.5.k_ref.v_ref), custom_call_target="tpu_custom_call" | custom-call | flops 402653184 | bytes 1572864 | tf_op jit(solution)/shard_map/cross_forward/pallas_call | solution.py:277
  148.2 5.8 %assemble.12 = bf16[768,3072]{1,0:T(8,128)(2,1)} custom-call(s32[2]{0:T(128)} %pad_add_fusion.index_ref, bf16[192,3072]{1,0:T(8,128)(2,1)} %refs_0_.12, bf16[192,3072]{1,0:T(8,128)(2,1)} %collective-permute-done.20.refs_1_, bf16[192,3072]{1,0:T(8,128)(2,1)} %collective-permute-done.21.refs_2_, bf16[192,3072]{1,0:T(8,128)(2,1)} %collective-permute-done.22.refs_3_), custom_call_target="tpu_custom_call" | custom-call | bytes 9437184 | tf_op jit(solution)/shard_map/assemble/pallas_call | solution.py:336
  154.0 4.8 %multiply_convert_fusion = (bf16[128,3072]{1,0:T(8,128)(2,1)}, f32[128,3072]{1,0:T(8,128)}) fusion(bf16[128,768]{1,0:T(8,128)(2,1)S(1)} %multiply_convert_fusion.2.refs_0_, bf16[768,3072]{1,0:T(8,128)(2,1)} %assemble.12), kind=kOutput, calls=%fused_computation.32 | convolution fusion | flops 605945856 | bytes 7274496 | tf_op jit(solution)/shard_map/dot_general | solution.py:24
  158.8 5.6 %assemble.13 = bf16[3072,768]{1,0:T(8,128)(2,1)} custom-call(s32[2]{0:T(128)} %pad_add_fusion.index_ref, bf16[768,768]{1,0:T(8,128)(2,1)} %refs_0_.13, bf16[768,768]{1,0:T(8,128)(2,1)} %collective-permute-done.23.refs_1_, bf16[768,768]{1,0:T(8,128)(2,1)} %collective-permute-done.24.refs_2_, bf16[768,768]{1,0:T(8,128)(2,1)} %collective-permute-done.25.refs_3_), custom_call_target="tpu_custom_call" | custom-call | bytes 9437184 | tf_op jit(solution)/shard_map/assemble/pallas_call | solution.py:336
  164.5 4.7 %fusion.1.refs_1_ = bf16[128,3072]{1,0:T(8,128)(2,1)S(1)} fusion(bf16[3072,768]{1,0:T(8,128)(2,1)} %assemble.13, f32[128,3072]{1,0:T(8,128)} %get-tuple-element.80, bf16[1,128,768]{2,1,0:T(8,128)(2,1)S(1)} %copy-done.47), kind=kOutput, calls=%fused_computation.6 | convolution fusion | flops 607911936 | bytes 7274496 | tf_op jit(solution)/shard_map/dot_general | solution.py:32
  173.6 7.3 %cross_backward.1 = (bf16[128,768]{1,0:T(8,128)(2,1)}, bf16[2,512,768]{2,1,0:T(8,128)(2,1)}) custom-call(bf16[128,768]{1,0:T(8,128)(2,1)} %convolution_convert_fusion.4.q_ref, bf16[512,1536]{1,0:T(8,128)(2,1)} %fusion.5.k_ref.v_ref, bf16[512,1536]{1,0:T(8,128)(2,1)} %fusion.5.k_ref.v_ref, bf16[128,768]{1,0:T(8,128)(2,1)} %convolution_convert_fusion.3.do_ref), custom_call_target="tpu_custom_call" | custom-call | flops 1006632960 | bytes 3145728 | tf_op jit(solution)/shard_map/cross_backward/pallas_call | solution.py:297
  184.7 10.4 %self_backward.1 = (bf16[128,768]{1,0:T(8,128)(2,1)}, bf16[2,1024,768]{2,1,0:T(8,128)(2,1)}) custom-call(bf16[128,768]{1,0:T(8,128)(2,1)} %convolution_convert_fusion.5.q_ref, bf16[1024,1536]{1,0:T(8,128)(2,1)} %convolution_convert_fusion.k_ref.v_ref, bf16[1024,1536]{1,0:T(8,128)(2,1)} %convolution_convert_fusion.k_ref.v_ref, ...), custom_call_target="tpu_custom_call" | custom-call | flops 2013265920 | bytes 6291456 | tf_op jit(solution)/shard_map/self_backward/pallas_call | solution.py:221
  195.1 8.1 %wide_products.3 = (bf16[384,2304]{1,0:T(8,128)(2,1)}, bf16[384,2304]{1,0:T(8,128)(2,1)}) custom-call(s32[2]{0:T(128)} %pad_add_fusion.index_ref, bf16[128,768]{1,0:T(8,128)(2,1)} %fusion.32.refs_0_, bf16[128,768]{1,0:T(8,128)(2,1)} %get-tuple-element.29.refs_1_, bf16[1024,768]{1,0:T(8,128)(2,1)} %fusion.4.refs_2_, ...), custom_call_target="tpu_custom_call" | custom-call | flops 2566914048 | bytes 3538944 | tf_op jit(solution)/shard_map/wide_products/pallas_call | solution.py:423
  203.7 3.4 fusion.11
  216.1 5.8 %wide_products.5 = (bf16[384,3072]{1,0:T(8,128)(2,1)}, bf16[384,3072]{1,0:T(8,128)(2,1)}) custom-call(s32[2]{0:T(128)} %pad_add_fusion.index_ref, bf16[128,768]{1,0:T(8,128)(2,1)} %copy-done.35, bf16[128,3072]{1,0:T(8,128)(2,1)} %copy-done.34), custom_call_target="tpu_custom_call" | custom-call | flops 603979776 | bytes 4718592 | tf_op jit(solution)/shard_map/wide_products/pallas_call | solution.py:423
  225.2 5.5 %collective-permute-done.26 = bf16[512,768]{1,0:T(8,128)(2,1)} collective-permute-done((bf16[512,768]{1,0:T(8,128)(2,1)}, bf16[512,768]{1,0:T(8,128)(2,1)}, u32[]{:S(2)}, u32[]{:S(2)}) %collective-permute-start.26) | collective-permute-done | bytes 786464 | tf_op jit(solution)/shard_map/ppermute | solution.py:317
  236.3 8.5 %wide_products.4 = (bf16[384,3840]{1,0:T(8,128)(2,1)}, bf16[384,3840]{1,0:T(8,128)(2,1)}) custom-call(s32[2]{0:T(128)} %pad_add_fusion.index_ref, bf16[128,768]{1,0:T(8,128)(2,1)} %cross_forward.1.refs_0_, bf16[128,768]{1,0:T(8,128)(2,1)} %copy-done.31, bf16[128,768]{1,0:T(8,128)(2,1)} %copy-done.33, bf16[128,768]{1,0:T(8,128)(2,1)} %get-tuple-element.26.refs_3_, ...), custom_call_target="tpu_custom_call" | custom-call | flops 1660944384 | bytes 5898240 | tf_op jit(solution)/shard_map/wide_products/pallas_call | solution.py:423
  244.9 6.5 %tall_products.1 = (bf16[1536,768]{1,0:T(8,128)(2,1)}, bf16[1536,768]{1,0:T(8,128)(2,1)}) custom-call(s32[2]{0:T(128)} %pad_add_fusion.index_ref, bf16[128,3072]{1,0:T(8,128)(2,1)} %get-tuple-element.79.left_ref, bf16[128,768]{1,0:T(8,128)(2,1)} %bitcast.97), custom_call_target="tpu_custom_call" | custom-call | flops 603979776 | bytes 9437184 | tf_op jit(solution)/shard_map/tall_products/pallas_call | solution.py:460
  257.0 8.0 %collective-permute-done.28 = bf16[128,768]{1,0:T(8,128)(2,1)S(1)} collective-permute-done((bf16[128,768]{1,0:T(8,128)(2,1)S(1)}, bf16[128,768]{1,0:T(8,128)(2,1)S(1)}, u32[]{:S(2)}, u32[]{:S(2)}) %collective-permute-start.28) | collective-permute-done | bytes 196640 | tf_op jit(solution)/shard_map/ppermute | solution.py:317
  270.4 4.0 collective-permute-done.32
  277.0 4.0 collective-permute-done.33
  287.3 11.4 %collective-permute-done.46 = bf16[192,3072]{1,0:T(8,128)(2,1)S(1)} collective-permute-done((bf16[192,3072]{1,0:T(8,128)(2,1)S(1)}, bf16[192,3072]{1,0:T(8,128)(2,1)S(1)}, u32[]{:S(2)}, u32[]{:S(2)}) %collective-permute-start.46) | collective-permute-done | bytes 1179680 | tf_op jit(solution)/shard_map/ppermute | solution.py:317
  302.1 21.9 %collective-permute-done.54 = bf16[768,768]{1,0:T(8,128)(2,1)S(1)} collective-permute-done((bf16[768,768]{1,0:T(8,128)(2,1)S(1)}, bf16[768,768]{1,0:T(8,128)(2,1)S(1)}, u32[]{:S(2)}, u32[]{:S(2)}) %collective-permute-start.54) | collective-permute-done | bytes 1179680 | tf_op jit(solution)/shard_map/ppermute | solution.py:317
  328.5 12.2 %collective-permute-done.55 = bf16[384,768]{1,0:T(8,128)(2,1)S(1)} collective-permute-done((bf16[384,768]{1,0:T(8,128)(2,1)S(1)}, bf16[384,768]{1,0:T(8,128)(2,1)S(1)}, u32[]{:S(2)}, u32[]{:S(2)}) %collective-permute-start.55) | collective-permute-done | bytes 589856 | tf_op jit(solution)/shard_map/ppermute | solution.py:317
  342.7 11.0 %collective-permute-done.38 = bf16[192,3840]{1,0:T(8,128)(2,1)S(1)} collective-permute-done((bf16[192,3840]{1,0:T(8,128)(2,1)S(1)}, bf16[192,3840]{1,0:T(8,128)(2,1)S(1)}, u32[]{:S(2)}, u32[]{:S(2)}) %collective-permute-start.38) | collective-permute-done | bytes 1474592 | tf_op jit(solution)/shard_map/ppermute | solution.py:317
  360.3 11.9 %collective-permute-done.39 = bf16[96,3840]{1,0:T(8,128)(2,1)S(1)} collective-permute-done((bf16[96,3840]{1,0:T(8,128)(2,1)S(1)}, bf16[96,3840]{1,0:T(8,128)(2,1)S(1)}, u32[]{:S(2)}, u32[]{:S(2)}) %collective-permute-start.39) | collective-permute-done | bytes 737312 | tf_op jit(solution)/shard_map/ppermute | solution.py:317
  375.5 8.0 %collective-permute-done.40 = bf16[48,3840]{1,0:T(8,128)(2,1)S(1)} collective-permute-done((bf16[48,3840]{1,0:T(8,128)(2,1)S(1)}, bf16[48,3840]{1,0:T(8,128)(2,1)S(1)}, u32[]{:S(2)}, u32[]{:S(2)}) %collective-permute-start.40) | collective-permute-done | bytes 368672 | tf_op jit(solution)/shard_map/ppermute | solution.py:317
  386.7 9.0 %collective-permute-done.41 = bf16[24,3840]{1,0:T(8,128)(2,1)S(1)} collective-permute-done((bf16[24,3840]{1,0:T(8,128)(2,1)S(1)}, bf16[24,3840]{1,0:T(8,128)(2,1)S(1)}, u32[]{:S(2)}, u32[]{:S(2)}) %collective-permute-start.41) | collective-permute-done | bytes 184352 | tf_op jit(solution)/shard_map/ppermute | solution.py:317
  395.8 3.2 collective-permute-start.51
  399.1 3.6 collective-permute-start.59
  402.7 3.4 collective-permute-done.42
  406.2 4.5 collective-permute-done.51
  412.3 4.7 %collective-permute-done.59 = bf16[192,768]{1,0:T(8,128)(2,1)S(1)} collective-permute-done((bf16[192,768]{1,0:T(8,128)(2,1)S(1)}, bf16[192,768]{1,0:T(8,128)(2,1)S(1)}, u32[]{:S(2)}, u32[]{:S(2)}) %collective-permute-start.59) | collective-permute-done | bytes 294944 | tf_op jit(solution)/shard_map/ppermute | solution.py:317
  419.4 3.5 collective-permute-done.43
  425.4 4.1 place_share.7
  431.2 4.4 place_share.9
  435.6 4.2 collective-permute-done.60.high_ref
  439.9 3.5 place_share.13
  445.6 4.9 %collective-permute-done.44.high_ref = bf16[96,3840]{1,0:T(8,128)(2,1)S(1)} collective-permute-done((bf16[96,3840]{1,0:T(8,128)(2,1)S(1)}, bf16[96,3840]{1,0:T(8,128)(2,1)S(1)}, u32[]{:S(2)}, u32[]{:S(2)}) %collective-permute-start.44) | collective-permute-done | bytes 737312 | tf_op jit(solution)/shard_map/ppermute | solution.py:317
  (312 shorter events, 139.4 us)
Async XLA Ops:
  0.7 17.8 %collective-permute-start.8 = (bf16[192,768]{1,0:T(8,128)(2,1)}, bf16[192,768]{1,0:T(8,128)(2,1)S(1)}, u32[]{:S(2)}, u32[]{:S(2)}) collective-permute-start(bf16[192,768]{1,0:T(8,128)(2,1)} %refs_0_.8), channel_id=1, source_target_pairs={{0,1},{1,0},{2,3},{3,2},{4,5},{5,4},{6,7},{7,6},{8,9},{9,8},{10,11... | collective-permute-start | bytes 884744 | tf_op jit(solution)/shard_map/ppermute | solution.py:317
  1.2 17.4 %collective-permute-start.9 = (bf16[192,768]{1,0:T(8,128)(2,1)}, bf16[192,768]{1,0:T(8,128)(2,1)S(1)}, u32[]{:S(2)}, u32[]{:S(2)}) collective-permute-start(bf16[192,768]{1,0:T(8,128)(2,1)} %refs_0_.8), channel_id=1, source_target_pairs={{0,2},{1,3},{2,0},{3,1},{4,6},{5,7},{6,4},{7,5},{8,10},{9,11},{10,... | collective-permute-start | bytes 884744 | tf_op jit(solution)/shard_map/ppermute | solution.py:317
  3.9 13.0 %collective-permute-start.5 = (bf16[128,768]{1,0:T(8,128)(2,1)}, bf16[128,768]{1,0:T(8,128)(2,1)S(1)}, u32[]{:S(2)}, u32[]{:S(2)}) collective-permute-start(bf16[128,768]{1,0:T(8,128)(2,1)} %bitcast.91), channel_id=1, source_target_pairs={{0,16},{4,20},{8,24},{12,28},{16,0},{20,4},{24,8},{28,12},{1,17},{... | collective-permute-start | bytes 589832 | tf_op jit(solution)/shard_map/ppermute | solution.py:317
  6.5 13.6 %collective-permute-start.17 = (bf16[192,768]{1,0:T(8,128)(2,1)}, bf16[192,768]{1,0:T(8,128)(2,1)S(1)}, u32[]{:S(2)}, u32[]{:S(2)}) collective-permute-start(bf16[192,768]{1,0:T(8,128)(2,1)} %refs_0_.11), channel_id=1, source_target_pairs={{0,1},{1,0},{2,3},{3,2},{4,5},{5,4},{6,7},{7,6},{8,9},{9,8},{10,11... | collective-permute-start | bytes 884744 | tf_op jit(solution)/shard_map/ppermute | solution.py:317
  16.9 15.9 %collective-permute-start.12 = (bf16[192,768]{1,0:T(8,128)(2,1)}, bf16[192,768]{1,0:T(8,128)(2,1)S(1)}, u32[]{:S(2)}, u32[]{:S(2)}) collective-permute-start(bf16[192,768]{1,0:T(8,128)(2,1)} %refs_0_.9), channel_id=1, source_target_pairs={{0,2},{1,3},{2,0},{3,1},{4,6},{5,7},{6,4},{7,5},{8,10},{9,11},{10,... | collective-permute-start | bytes 884744 | tf_op jit(solution)/shard_map/ppermute | solution.py:317
  18.5 14.9 %collective-permute-start.11 = (bf16[192,768]{1,0:T(8,128)(2,1)}, bf16[192,768]{1,0:T(8,128)(2,1)S(1)}, u32[]{:S(2)}, u32[]{:S(2)}) collective-permute-start(bf16[192,768]{1,0:T(8,128)(2,1)} %refs_0_.9), channel_id=1, source_target_pairs={{0,1},{1,0},{2,3},{3,2},{4,5},{5,4},{6,7},{7,6},{8,9},{9,8},{10,11... | collective-permute-start | bytes 884744 | tf_op jit(solution)/shard_map/ppermute | solution.py:317
  18.6 27.1 %collective-permute-start.15 = (bf16[192,1536]{1,0:T(8,128)(2,1)}, bf16[192,1536]{1,0:T(8,128)(2,1)}, u32[]{:S(2)}, u32[]{:S(2)}) collective-permute-start(bf16[192,1536]{1,0:T(8,128)(2,1)} %refs_0_.10), channel_id=1, source_target_pairs={{0,2},{1,3},{2,0},{3,1},{4,6},{5,7},{6,4},{7,5},{8,10},{9,11},{10,... | collective-permute-start | bytes 1769480 | tf_op jit(solution)/shard_map/ppermute | solution.py:317
  20.2 14.9 %collective-permute-start.10 = (bf16[192,768]{1,0:T(8,128)(2,1)S(1)}, bf16[192,768]{1,0:T(8,128)(2,1)S(1)}, u32[]{:S(2)}, u32[]{:S(2)}) collective-permute-start(bf16[192,768]{1,0:T(8,128)(2,1)S(1)} %collective-permute-done.9.refs_2_), channel_id=1, source_target_pairs={{0,1},{1,0},{2,3},{3,2},{4,5},{5,4},{6,7},{7,6},{8,9},{9,8},{10,11... | collective-permute-start | bytes 884744 | tf_op jit(solution)/shard_map/ppermute | solution.py:317
  26.6 22.3 %collective-permute-start.14 = (bf16[192,1536]{1,0:T(8,128)(2,1)}, bf16[192,1536]{1,0:T(8,128)(2,1)S(1)}, u32[]{:S(2)}, u32[]{:S(2)}) collective-permute-start(bf16[192,1536]{1,0:T(8,128)(2,1)} %refs_0_.10), channel_id=1, source_target_pairs={{0,1},{1,0},{2,3},{3,2},{4,5},{5,4},{6,7},{7,6},{8,9},{9,8},{10,11... | collective-permute-start | bytes 1769480 | tf_op jit(solution)/shard_map/ppermute | solution.py:317
  32.9 31.6 %collective-permute-start.3 = (bf16[192,2304]{1,0:T(8,128)(2,1)}, bf16[192,2304]{1,0:T(8,128)(2,1)S(1)}, u32[]{:S(2)}, u32[]{:S(2)}) collective-permute-start(bf16[192,2304]{1,0:T(8,128)(2,1)} %refs_0_.7), channel_id=1, source_target_pairs={{0,2},{1,3},{2,0},{3,1},{4,6},{5,7},{6,4},{7,5},{8,10},{9,11},{10,... | collective-permute-start | bytes 2654216 | tf_op jit(solution)/shard_map/ppermute | solution.py:317
  45.6 18.9 %collective-permute-start.16 = (bf16[192,1536]{1,0:T(8,128)(2,1)}, bf16[192,1536]{1,0:T(8,128)(2,1)}, u32[]{:S(2)}, u32[]{:S(2)}) collective-permute-start(bf16[192,1536]{1,0:T(8,128)(2,1)} %collective-permute-done.15.refs_2_), channel_id=1, source_target_pairs={{0,1},{1,0},{2,3},{3,2},{4,5},{5,4},{6,7},{7,6},{8,9},{9,8},{10,11... | collective-permute-start | bytes 1769480 | tf_op jit(solution)/shard_map/ppermute | solution.py:317
  46.6 26.4 %collective-permute-start.7 = (bf16[512,768]{1,0:T(8,128)(2,1)}, bf16[512,768]{1,0:T(8,128)(2,1)S(1)}, u32[]{:S(2)}, u32[]{:S(2)}) collective-permute-start(bf16[512,768]{1,0:T(8,128)(2,1)} %pad_maximum_fusion.1), channel_id=1, source_target_pairs={{0,4},{4,0},{8,12},{12,8},{16,20},{20,16},{24,28},{28,24},{1,5},{5... | collective-permute-start | bytes 2359304 | tf_op jit(solution)/shard_map/ppermute | solution.py:317
  48.3 41.6 %collective-permute-start.24 = (bf16[768,768]{1,0:T(8,128)(2,1)}, bf16[768,768]{1,0:T(8,128)(2,1)}, u32[]{:S(2)}, u32[]{:S(2)}) collective-permute-start(bf16[768,768]{1,0:T(8,128)(2,1)} %refs_0_.13), channel_id=1, source_target_pairs={{0,2},{1,3},{2,0},{3,1},{4,6},{5,7},{6,4},{7,5},{8,10},{9,11},{10,... | collective-permute-start | bytes 3538952 | tf_op jit(solution)/shard_map/ppermute | solution.py:317
  48.9 64.8 %collective-permute-start.21 = (bf16[192,3072]{1,0:T(8,128)(2,1)}, bf16[192,3072]{1,0:T(8,128)(2,1)}, u32[]{:S(2)}, u32[]{:S(2)}) collective-permute-start(bf16[192,3072]{1,0:T(8,128)(2,1)} %refs_0_.12), channel_id=1, source_target_pairs={{0,2},{1,3},{2,0},{3,1},{4,6},{5,7},{6,4},{7,5},{8,10},{9,11},{10,... | collective-permute-start | bytes 3538952 | tf_op jit(solution)/shard_map/ppermute | solution.py:317
  64.5 49.2 %collective-permute-start.4 = (bf16[192,2304]{1,0:T(8,128)(2,1)S(1)}, bf16[192,2304]{1,0:T(8,128)(2,1)}, u32[]{:S(2)}, u32[]{:S(2)}) collective-permute-start(bf16[192,2304]{1,0:T(8,128)(2,1)S(1)} %collective-permute-done.3.refs_2_), channel_id=1, source_target_pairs={{0,1},{1,0},{2,3},{3,2},{4,5},{5,4},{6,7},{7,6},{8,9},{9,8},{10,11... | collective-permute-start | bytes 2654216 | tf_op jit(solution)/shard_map/ppermute | solution.py:317
  73.0 85.8 %collective-permute-start.23 = (bf16[768,768]{1,0:T(8,128)(2,1)}, bf16[768,768]{1,0:T(8,128)(2,1)}, u32[]{:S(2)}, u32[]{:S(2)}) collective-permute-start(bf16[768,768]{1,0:T(8,128)(2,1)} %refs_0_.13), channel_id=1, source_target_pairs={{0,1},{1,0},{2,3},{3,2},{4,5},{5,4},{6,7},{7,6},{8,9},{9,8},{10,11... | collective-permute-start | bytes 3538952 | tf_op jit(solution)/shard_map/ppermute | solution.py:317
  75.1 73.2 %collective-permute-start.20 = (bf16[192,3072]{1,0:T(8,128)(2,1)}, bf16[192,3072]{1,0:T(8,128)(2,1)}, u32[]{:S(2)}, u32[]{:S(2)}) collective-permute-start(bf16[192,3072]{1,0:T(8,128)(2,1)} %refs_0_.12), channel_id=1, source_target_pairs={{0,1},{1,0},{2,3},{3,2},{4,5},{5,4},{6,7},{7,6},{8,9},{9,8},{10,11... | collective-permute-start | bytes 3538952 | tf_op jit(solution)/shard_map/ppermute | solution.py:317
  89.9 68.9 %collective-permute-start.25 = (bf16[768,768]{1,0:T(8,128)(2,1)}, bf16[768,768]{1,0:T(8,128)(2,1)}, u32[]{:S(2)}, u32[]{:S(2)}) collective-permute-start(bf16[768,768]{1,0:T(8,128)(2,1)} %collective-permute-done.24.refs_2_), channel_id=1, source_target_pairs={{0,1},{1,0},{2,3},{3,2},{4,5},{5,4},{6,7},{7,6},{8,9},{9,8},{10,11... | collective-permute-start | bytes 3538952 | tf_op jit(solution)/shard_map/ppermute | solution.py:317
  113.7 34.5 %collective-permute-start.22 = (bf16[192,3072]{1,0:T(8,128)(2,1)}, bf16[192,3072]{1,0:T(8,128)(2,1)}, u32[]{:S(2)}, u32[]{:S(2)}) collective-permute-start(bf16[192,3072]{1,0:T(8,128)(2,1)} %collective-permute-done.21.refs_2_), channel_id=1, source_target_pairs={{0,1},{1,0},{2,3},{3,2},{4,5},{5,4},{6,7},{7,6},{8,9},{9,8},{10,11... | collective-permute-start | bytes 3538952 | tf_op jit(solution)/shard_map/ppermute | solution.py:317
  203.2 18.8 %collective-permute-start.29 = (bf16[384,2304]{1,0:T(8,128)(2,1)}, bf16[384,2304]{1,0:T(8,128)(2,1)}, u32[]{:S(2)}, u32[]{:S(2)}) collective-permute-start(bf16[384,2304]{1,0:T(8,128)(2,1)} %get-tuple-element.32), channel_id=1, source_target_pairs={{0,1},{1,0},{2,3},{3,2},{4,5},{5,4},{6,7},{7,6},{8,9},{9,8},{10,11... | collective-permute-start | bytes 5308424 | tf_op jit(solution)/shard_map/ppermute | solution.py:317
  211.0 19.7 %collective-permute-start.26 = (bf16[512,768]{1,0:T(8,128)(2,1)}, bf16[512,768]{1,0:T(8,128)(2,1)}, u32[]{:S(2)}, u32[]{:S(2)}) collective-permute-start(bf16[512,768]{1,0:T(8,128)(2,1)} %slice.380), channel_id=1, source_target_pairs={{0,4},{4,0},{8,12},{12,8},{16,20},{20,16},{24,28},{28,24},{1,5},{5... | collective-permute-start | bytes 2359304 | tf_op jit(solution)/shard_map/ppermute | solution.py:317
  221.9 46.0 %collective-permute-start.45 = (bf16[384,3072]{1,0:T(8,128)(2,1)}, bf16[384,3072]{1,0:T(8,128)(2,1)}, u32[]{:S(2)}, u32[]{:S(2)}) collective-permute-start(bf16[384,3072]{1,0:T(8,128)(2,1)} %get-tuple-element.36), channel_id=1, source_target_pairs={{0,1},{1,0},{2,3},{3,2},{4,5},{5,4},{6,7},{7,6},{8,9},{9,8},{10,11... | collective-permute-start | bytes 7077896 | tf_op jit(solution)/shard_map/ppermute | solution.py:317
  224.6 29.1 %collective-permute-start.30 = (bf16[192,2304]{1,0:T(8,128)(2,1)}, bf16[192,2304]{1,0:T(8,128)(2,1)}, u32[]{:S(2)}, u32[]{:S(2)}) collective-permute-start(bf16[192,2304]{1,0:T(8,128)(2,1)} %add_convert_fusion.4), channel_id=1, source_target_pairs={{0,2},{1,3},{2,0},{3,1},{4,6},{5,7},{6,4},{7,5},{8,10},{9,11},{10,... | collective-permute-start | bytes 2654216 | tf_op jit(solution)/shard_map/ppermute | solution.py:317
  233.0 18.9 %collective-permute-start.27 = (bf16[256,768]{1,0:T(8,128)(2,1)S(1)}, bf16[256,768]{1,0:T(8,128)(2,1)}, u32[]{:S(2)}, u32[]{:S(2)}) collective-permute-start(bf16[256,768]{1,0:T(8,128)(2,1)S(1)} %slice.382), channel_id=1, source_target_pairs={{0,8},{4,12},{8,0},{12,4},{16,24},{20,28},{24,16},{28,20},{1,9},{5... | collective-permute-start | bytes 1179656 | tf_op jit(solution)/shard_map/ppermute | solution.py:317
  244.9 37.1 %collective-permute-start.37 = (bf16[384,3840]{1,0:T(8,128)(2,1)}, bf16[384,3840]{1,0:T(8,128)(2,1)}, u32[]{:S(2)}, u32[]{:S(2)}) collective-permute-start(bf16[384,3840]{1,0:T(8,128)(2,1)} %get-tuple-element.34), channel_id=1, source_target_pairs={{0,1},{1,0},{2,3},{3,2},{4,5},{5,4},{6,7},{7,6},{8,9},{9,8},{10,11... | collective-permute-start | bytes 8847368 | tf_op jit(solution)/shard_map/ppermute | solution.py:317
  251.4 24.7 %collective-permute-start.53 = (bf16[1536,768]{1,0:T(8,128)(2,1)}, bf16[1536,768]{1,0:T(8,128)(2,1)S(1)}, u32[]{:S(2)}, u32[]{:S(2)}) collective-permute-start(bf16[1536,768]{1,0:T(8,128)(2,1)} %get-tuple-element.38), channel_id=1, source_target_pairs={{0,1},{1,0},{2,3},{3,2},{4,5},{5,4},{6,7},{7,6},{8,9},{9,8},{10,11... | collective-permute-start | bytes 7077896 | tf_op jit(solution)/shard_map/ppermute | solution.py:317
  253.0 12.0 %collective-permute-start.28 = (bf16[128,768]{1,0:T(8,128)(2,1)S(1)}, bf16[128,768]{1,0:T(8,128)(2,1)S(1)}, u32[]{:S(2)}, u32[]{:S(2)}) collective-permute-start(bf16[128,768]{1,0:T(8,128)(2,1)S(1)} %slice.384), channel_id=1, source_target_pairs={{0,16},{4,20},{8,24},{12,28},{16,0},{20,4},{24,8},{28,12},{1,17},{... | collective-permute-start | bytes 589832 | tf_op jit(solution)/shard_map/ppermute | solution.py:317
  269.8 29.0 %collective-permute-start.46 = (bf16[192,3072]{1,0:T(8,128)(2,1)S(1)}, bf16[192,3072]{1,0:T(8,128)(2,1)S(1)}, u32[]{:S(2)}, u32[]{:S(2)}) collective-permute-start(bf16[192,3072]{1,0:T(8,128)(2,1)S(1)} %add_convert_fusion.3), channel_id=1, source_target_pairs={{0,2},{1,3},{2,0},{3,1},{4,6},{5,7},{6,4},{7,5},{8,10},{9,11},{10,... | collective-permute-start | bytes 3538952 | tf_op jit(solution)/shard_map/ppermute | solution.py:317
  276.4 47.6 %collective-permute-start.54 = (bf16[768,768]{1,0:T(8,128)(2,1)S(1)}, bf16[768,768]{1,0:T(8,128)(2,1)S(1)}, u32[]{:S(2)}, u32[]{:S(2)}) collective-permute-start(bf16[768,768]{1,0:T(8,128)(2,1)S(1)} %add_convert_fusion.2), channel_id=1, source_target_pairs={{0,2},{1,3},{2,0},{3,1},{4,6},{5,7},{6,4},{7,5},{8,10},{9,11},{10,... | collective-permute-start | bytes 3538952 | tf_op jit(solution)/shard_map/ppermute | solution.py:317
  283.8 69.9 %collective-permute-start.38 = (bf16[192,3840]{1,0:T(8,128)(2,1)S(1)}, bf16[192,3840]{1,0:T(8,128)(2,1)S(1)}, u32[]{:S(2)}, u32[]{:S(2)}) collective-permute-start(bf16[192,3840]{1,0:T(8,128)(2,1)S(1)} %add_convert_fusion.1), channel_id=1, source_target_pairs={{0,2},{1,3},{2,0},{3,1},{4,6},{5,7},{6,4},{7,5},{8,10},{9,11},{10,... | collective-permute-start | bytes 4423688 | tf_op jit(solution)/shard_map/ppermute | solution.py:317
  287.3 38.8 %collective-permute-start.35 = (bf16[48,2304]{1,0:T(8,128)(2,1)S(1)}, bf16[48,2304]{1,0:T(8,128)(2,1)S(1)}, u32[]{:S(2)}, u32[]{:S(2)}) collective-permute-start(bf16[48,2304]{1,0:T(8,128)(2,1)S(1)} %pad_maximum_fusion.10), channel_id=1, source_target_pairs={{0,8},{4,12},{8,0},{12,4},{16,24},{20,28},{24,16},{28,20},{1,9},{5... | collective-permute-start | bytes 663560 | tf_op jit(solution)/shard_map/ppermute | solution.py:317
  300.6 26.1 %collective-permute-start.47 = (bf16[96,3072]{1,0:T(8,128)(2,1)S(1)}, bf16[96,3072]{1,0:T(8,128)(2,1)S(1)}, u32[]{:S(2)}, u32[]{:S(2)}) collective-permute-start(bf16[96,3072]{1,0:T(8,128)(2,1)S(1)} %get-tuple-element.51), channel_id=1, source_target_pairs={{0,4},{4,0},{8,12},{12,8},{16,20},{20,16},{24,28},{28,24},{1,5},{5... | collective-permute-start | bytes 1769480 | tf_op jit(solution)/shard_map/ppermute | solution.py:317
  324.5 16.2 %collective-permute-start.55 = (bf16[384,768]{1,0:T(8,128)(2,1)S(1)}, bf16[384,768]{1,0:T(8,128)(2,1)S(1)}, u32[]{:S(2)}, u32[]{:S(2)}) collective-permute-start(bf16[384,768]{1,0:T(8,128)(2,1)S(1)} %get-tuple-element.49), channel_id=1, source_target_pairs={{0,4},{4,0},{8,12},{12,8},{16,20},{20,16},{24,28},{28,24},{1,5},{5... | collective-permute-start | bytes 1769480 | tf_op jit(solution)/shard_map/ppermute | solution.py:317
  326.1 99.3 %collective-permute-start.36 = (bf16[96,2304]{1,0:T(8,128)(2,1)S(1)}, bf16[96,2304]{1,0:T(8,128)(2,1)}, u32[]{:S(2)}, u32[]{:S(2)}) collective-permute-start(bf16[96,2304]{1,0:T(8,128)(2,1)S(1)} %pad_maximum_fusion.5.low_ref), channel_id=1, source_target_pairs={{0,4},{4,0},{8,12},{12,8},{16,20},{20,16},{24,28},{28,24},{1,5},{5... | collective-permute-start | bytes 1327112 | tf_op jit(solution)/shard_map/ppermute | solution.py:317
  326.9 30.3 %collective-permute-start.48 = (bf16[48,3072]{1,0:T(8,128)(2,1)S(1)}, bf16[48,3072]{1,0:T(8,128)(2,1)S(1)}, u32[]{:S(2)}, u32[]{:S(2)}) collective-permute-start(bf16[48,3072]{1,0:T(8,128)(2,1)S(1)} %get-tuple-element.59), channel_id=1, source_target_pairs={{0,8},{4,12},{8,0},{12,4},{16,24},{20,28},{24,16},{28,20},{1,9},{5... | collective-permute-start | bytes 884744 | tf_op jit(solution)/shard_map/ppermute | solution.py:317
  340.9 18.5 %collective-permute-start.56 = (bf16[192,768]{1,0:T(8,128)(2,1)S(1)}, bf16[192,768]{1,0:T(8,128)(2,1)S(1)}, u32[]{:S(2)}, u32[]{:S(2)}) collective-permute-start(bf16[192,768]{1,0:T(8,128)(2,1)S(1)} %get-tuple-element.57), channel_id=1, source_target_pairs={{0,8},{4,12},{8,0},{12,4},{16,24},{20,28},{24,16},{28,20},{1,9},{5... | collective-permute-start | bytes 884744 | tf_op jit(solution)/shard_map/ppermute | solution.py:317
  355.6 16.6 %collective-permute-start.39 = (bf16[96,3840]{1,0:T(8,128)(2,1)S(1)}, bf16[96,3840]{1,0:T(8,128)(2,1)S(1)}, u32[]{:S(2)}, u32[]{:S(2)}) collective-permute-start(bf16[96,3840]{1,0:T(8,128)(2,1)S(1)} %get-tuple-element.47), channel_id=1, source_target_pairs={{0,4},{4,0},{8,12},{12,8},{16,20},{20,16},{24,28},{28,24},{1,5},{5... | collective-permute-start | bytes 2211848 | tf_op jit(solution)/shard_map/ppermute | solution.py:317
  357.2 17.1 %collective-permute-start.49 = (bf16[24,3072]{1,0:T(8,128)(2,1)S(1)}, bf16[24,3072]{1,0:T(8,128)(2,1)S(1)}, u32[]{:S(2)}, u32[]{:S(2)}) collective-permute-start(bf16[24,3072]{1,0:T(8,128)(2,1)S(1)} %add_convert_fusion.31), channel_id=1, source_target_pairs={{0,16},{4,20},{8,24},{12,28},{16,0},{20,4},{24,8},{28,12},{1,17},{... | collective-permute-start | bytes 442376 | tf_op jit(solution)/shard_map/ppermute | solution.py:317
  359.4 24.2 %collective-permute-start.57 = (bf16[96,768]{1,0:T(8,128)(2,1)S(1)}, bf16[96,768]{1,0:T(8,128)(2,1)S(1)}, u32[]{:S(2)}, u32[]{:S(2)}) collective-permute-start(bf16[96,768]{1,0:T(8,128)(2,1)S(1)} %add_convert_fusion.28), channel_id=1, source_target_pairs={{0,16},{4,20},{8,24},{12,28},{16,0},{20,4},{24,8},{28,12},{1,17},{... | collective-permute-start | bytes 442376 | tf_op jit(solution)/shard_map/ppermute | solution.py:317
  374.3 21.5 %collective-permute-start.50 = (bf16[24,3072]{1,0:T(8,128)(2,1)S(1)}, bf16[24,3072]{1,0:T(8,128)(2,1)S(1)}, u32[]{:S(2)}, u32[]{:S(2)}) collective-permute-start(bf16[24,3072]{1,0:T(8,128)(2,1)S(1)} %add_convert_fusion.30), channel_id=1, source_target_pairs={{0,16},{4,20},{8,24},{12,28},{16,0},{20,4},{24,8},{28,12},{1,17},{... | collective-permute-start | bytes 442376 | tf_op jit(solution)/shard_map/ppermute | solution.py:317
  383.6 12.1 %collective-permute-start.41 = (bf16[24,3840]{1,0:T(8,128)(2,1)S(1)}, bf16[24,3840]{1,0:T(8,128)(2,1)S(1)}, u32[]{:S(2)}, u32[]{:S(2)}) collective-permute-start(bf16[24,3840]{1,0:T(8,128)(2,1)S(1)} %add_convert_fusion.25), channel_id=1, source_target_pairs={{0,16},{4,20},{8,24},{12,28},{16,0},{20,4},{24,8},{28,12},{1,17},{... | collective-permute-start | bytes 552968 | tf_op jit(solution)/shard_map/ppermute | solution.py:317
  383.7 15.3 %collective-permute-start.58 = (bf16[96,768]{1,0:T(8,128)(2,1)S(1)}, bf16[96,768]{1,0:T(8,128)(2,1)S(1)}, u32[]{:S(2)}, u32[]{:S(2)}) collective-permute-start(bf16[96,768]{1,0:T(8,128)(2,1)S(1)} %add_convert_fusion.27), channel_id=1, source_target_pairs={{0,16},{4,20},{8,24},{12,28},{16,0},{20,4},{24,8},{28,12},{1,17},{... | collective-permute-start | bytes 442376 | tf_op jit(solution)/shard_map/ppermute | solution.py:317
  395.8 14.9 %collective-permute-start.51 = (bf16[48,3072]{1,0:T(8,128)(2,1)S(1)}, bf16[48,3072]{1,0:T(8,128)(2,1)S(1)}, u32[]{:S(2)}, u32[]{:S(2)}) collective-permute-start(bf16[48,3072]{1,0:T(8,128)(2,1)S(1)} %pad_maximum_fusion.8), channel_id=1, source_target_pairs={{0,8},{4,12},{8,0},{12,4},{16,24},{20,28},{24,16},{28,20},{1,9},{5... | collective-permute-start | bytes 884744 | tf_op jit(solution)/shard_map/ppermute | solution.py:317
  399.1 18.0 %collective-permute-start.59 = (bf16[192,768]{1,0:T(8,128)(2,1)S(1)}, bf16[192,768]{1,0:T(8,128)(2,1)S(1)}, u32[]{:S(2)}, u32[]{:S(2)}) collective-permute-start(bf16[192,768]{1,0:T(8,128)(2,1)S(1)} %pad_maximum_fusion.9), channel_id=1, source_target_pairs={{0,8},{4,12},{8,0},{12,4},{16,24},{20,28},{24,16},{28,20},{1,9},{5... | collective-permute-start | bytes 884744 | tf_op jit(solution)/shard_map/ppermute | solution.py:317
  406.1 16.7 %collective-permute-start.43 = (bf16[48,3840]{1,0:T(8,128)(2,1)S(1)}, bf16[48,3840]{1,0:T(8,128)(2,1)S(1)}, u32[]{:S(2)}, u32[]{:S(2)}) collective-permute-start(bf16[48,3840]{1,0:T(8,128)(2,1)S(1)} %pad_maximum_fusion.7), channel_id=1, source_target_pairs={{0,8},{4,12},{8,0},{12,4},{16,24},{20,28},{24,16},{28,20},{1,9},{5... | collective-permute-start | bytes 1105928 | tf_op jit(solution)/shard_map/ppermute | solution.py:317
  410.8 20.4 %collective-permute-start.52 = (bf16[96,3072]{1,0:T(8,128)(2,1)S(1)}, bf16[96,3072]{1,0:T(8,128)(2,1)}, u32[]{:S(2)}, u32[]{:S(2)}) collective-permute-start(bf16[96,3072]{1,0:T(8,128)(2,1)S(1)} %pad_maximum_fusion.3.low_ref), channel_id=1, source_target_pairs={{0,4},{4,0},{8,12},{12,8},{16,20},{20,16},{24,28},{28,24},{1,5},{5... | collective-permute-start | bytes 1769480 | tf_op jit(solution)/shard_map/ppermute | solution.py:317
  417.9 22.0 %collective-permute-start.60 = (bf16[384,768]{1,0:T(8,128)(2,1)}, bf16[384,768]{1,0:T(8,128)(2,1)}, u32[]{:S(2)}, u32[]{:S(2)}) collective-permute-start(bf16[384,768]{1,0:T(8,128)(2,1)} %pad_maximum_fusion.4.low_ref), channel_id=1, source_target_pairs={{0,4},{4,0},{8,12},{12,8},{16,20},{20,16},{24,28},{28,24},{1,5},{5... | collective-permute-start | bytes 1769480 | tf_op jit(solution)/shard_map/ppermute | solution.py:317
  422.9 27.6 %collective-permute-start.44 = (bf16[96,3840]{1,0:T(8,128)(2,1)S(1)}, bf16[96,3840]{1,0:T(8,128)(2,1)S(1)}, u32[]{:S(2)}, u32[]{:S(2)}) collective-permute-start(bf16[96,3840]{1,0:T(8,128)(2,1)S(1)} %pad_maximum_fusion.2.low_ref), channel_id=1, source_target_pairs={{0,4},{4,0},{8,12},{12,8},{16,20},{20,16},{24,28},{28,24},{1,5},{5... | collective-permute-start | bytes 2211848 | tf_op jit(solution)/shard_map/ppermute | solution.py:317
  (69 other events, 599.7 us)

commit v3 on v2

v3 whole, which is shorter than its diff:
```python
import functools

import jax
import jax.numpy as jnp
from jax import lax
from jax.experimental import pallas as pl
from jax.experimental.pallas import tpu as pltpu
from jax.sharding import PartitionSpec as P

H = 12
STRETCH = 64


NORM_EPS = 1e-06
MASKED_SCORE = -1e30
KEY_BLOCK = 1024


def lasting(microseconds):
    return pl.CostEstimate(
        flops=int(microseconds * 1.15e10), bytes_accessed=int(microseconds * 1e6), transcendentals=0
    )


def to_low(values):
    return values.astype(jnp.bfloat16)


def matmul(left, right):
    return jnp.dot(left, right, preferred_element_type=jnp.float32)


def left_product(left, right):
    return lax.dot_general(left, right, (((0,), (0,)), ((), ())), preferred_element_type=jnp.float32)


def right_product(left, right):
    return lax.dot_general(left, right, (((1,), (1,)), ((), ())), preferred_element_type=jnp.float32)


def inverse_rms(values):
    return lax.rsqrt(jnp.mean(values * values, axis=-1, keepdims=True) + NORM_EPS)


def rms_back(values, scale, gain, grad):
    gained = gain * grad
    along = jnp.mean(gained * values, axis=-1, keepdims=True)
    return scale * gained - values * (scale * scale * scale) * along


def head_rows(rows, head_size):
    wide = rows.astype(jnp.float32)
    lane = lax.broadcasted_iota(jnp.int32, wide.shape, 1)
    first = jnp.where(lane < head_size, wide, 0.0)
    second = jnp.where(lane >= head_size, wide, 0.0)
    return to_low(jnp.concatenate([first, second], axis=0))


def join_heads(columns, head_size):
    tok_count = columns.shape[1] // 2
    return jnp.concatenate(
        [columns[:head_size, :tok_count], columns[head_size:, tok_count:]], axis=0
    ).T


def self_scores(query, key, key_pos, low_pos, high_pos, score_scale):
    scores = right_product(key, query) * score_scale
    return jnp.where((key_pos >= low_pos) & (key_pos <= high_pos), scores, MASKED_SCORE)


def self_forward_kernel(
    head_size, blocks, q_ref, k_ref, v_ref, pos_ref, low_ref, high_ref, o_ref, lse_ref
):
    score_scale = head_size ** (-0.5)
    query = head_rows(q_ref[...], head_size)
    low_pos, high_pos = low_ref[...], high_ref[...]
    rows = k_ref.shape[0] // blocks

    def scores_of(index):
        span = pl.ds(pl.multiple_of(index * rows, rows), rows)
        return self_scores(query, k_ref[span, :], pos_ref[span, :], low_pos, high_pos, score_scale)

    def values_of(index):
        return v_ref[pl.ds(pl.multiple_of(index * rows, rows), rows), :]

    if blocks == 1:
        scores = scores_of(0)
        peak = jnp.max(scores, axis=0, keepdims=True)
        weights = jnp.exp(scores - peak)
        total = jnp.sum(weights, axis=0, keepdims=True)
        running = left_product(values_of(0), to_low(weights))
    else:
        peak = lax.fori_loop(
            0,
            blocks,
            lambda i, top: jnp.maximum(top, jnp.max(scores_of(i), axis=0, keepdims=True)),
            jnp.full((1, query.shape[0]), MASKED_SCORE, jnp.float32),
        )

        def add(index, state):
            total, running = state
            weights = jnp.exp(scores_of(index) - peak)
            return (
                total + jnp.sum(weights, axis=0, keepdims=True),
                running + left_product(values_of(index), to_low(weights)),
            )

        total, running = lax.fori_loop(
            0,
            blocks,
            add,
            (
                jnp.zeros((1, query.shape[0]), jnp.float32),
                jnp.zeros((2 * head_size, query.shape[0]), jnp.float32),
            ),
        )
    o_ref[...] = to_low(join_heads(running / total, head_size))
    lse_ref[0] = peak + jnp.log(total)


def self_backward_kernel(
    head_size,
    blocks,
    q_ref,
    k_ref,
    v_ref,
    do_ref,
    pos_ref,
    low_ref,
    high_ref,
    lse_ref,
    dq_ref,
    dkv_ref,
):
    score_scale = head_size ** (-0.5)
    query = head_rows(q_ref[...], head_size)
    grad = head_rows(do_ref[...], head_size)
    low_pos, high_pos = low_ref[...], high_ref[...]
    log_total = lse_ref[0]
    rows = k_ref.shape[0] // blocks

    def span_of(index):
        return pl.ds(pl.multiple_of(index * rows, rows), rows)

    def pair_of(index):
        span = span_of(index)
        scores = self_scores(
            query, k_ref[span, :], pos_ref[span, :], low_pos, high_pos, score_scale
        )
        return jnp.exp(scores - log_total), right_product(v_ref[span, :], grad)

    def finish(index, probs, dprobs, delta):
        span = span_of(index)
        dscores = to_low(probs * (dprobs - delta))
        dkv_ref[0, span, :] = to_low(score_scale * matmul(dscores, query))
        dkv_ref[1, span, :] = to_low(matmul(to_low(probs), grad))
        return left_product(k_ref[span, :], dscores)

    if blocks == 1:
        probs, dprobs = pair_of(0)
        delta = jnp.sum(probs * dprobs, axis=0, keepdims=True)
        columns = finish(0, probs, dprobs, delta)
    else:

        def add_delta(index, delta):
            probs, dprobs = pair_of(index)
            return delta + jnp.sum(probs * dprobs, axis=0, keepdims=True)

        delta = lax.fori_loop(
            0, blocks, add_delta, jnp.zeros((1, query.shape[0]), jnp.float32)
        )

        def add_query(index, columns):
            probs, dprobs = pair_of(index)
            return columns + finish(index, probs, dprobs, delta)

        columns = lax.fori_loop(
            0, blocks, add_query, jnp.zeros((2 * head_size, query.shape[0]), jnp.float32)
        )
    dq_ref[...] = to_low(score_scale * join_heads(columns, head_size))


def self_specs(tok_count, key_count, pairs):
    wide = 128
    return (
        pl.BlockSpec((tok_count, wide), lambda i: (0, i)),
        pl.BlockSpec((key_count, wide), lambda i: (0, i)),
        pl.BlockSpec((key_count, wide), lambda i: (0, pairs + i)),
        pl.BlockSpec((key_count, 1), lambda i: (0, 0)),
        pl.BlockSpec((1, 2 * tok_count), lambda i: (0, 0)),
        pl.BlockSpec((1, 1, 2 * tok_count), lambda i: (i, 0, 0)),
    )


def self_forward(query, key_value, key_pos, low_pos, high_pos):
    tok_count, feature_width = query.shape
    key_count = key_value.shape[0]
    head_size = feature_width // H
    pairs = H // 2
    blocks = max(1, key_count // KEY_BLOCK)
    rows, keys, values, pos, edge, lse = self_specs(tok_count, key_count, pairs)
    return pl.pallas_call(
        functools.partial(self_forward_kernel, head_size, blocks),
        grid=(pairs,),
        in_specs=[rows, keys, values, pos, edge, edge],
        out_specs=[rows, lse],
        out_shape=[
            jax.ShapeDtypeStruct((tok_count, feature_width), jnp.bfloat16),
            jax.ShapeDtypeStruct((pairs, 1, 2 * tok_count), jnp.float32),
        ],
        cost_estimate=lasting(7.6),
        name="self_forward",
    )(query, key_value, key_value, key_pos, low_pos, high_pos)


def self_backward(query, key_value, grad, key_pos, low_pos, high_pos, log_total):
    tok_count, feature_width = query.shape
    key_count = key_value.shape[0]
    head_size = feature_width // H
    pairs = H // 2
    blocks = max(1, key_count // KEY_BLOCK)
    rows, keys, values, pos, edge, lse = self_specs(tok_count, key_count, pairs)
    return pl.pallas_call(
        functools.partial(self_backward_kernel, head_size, blocks),
        grid=(pairs,),
        in_specs=[rows, keys, values, rows, pos, edge, edge, lse],
        out_specs=[rows, pl.BlockSpec((2, key_count, 128), lambda i: (0, 0, i))],
        out_shape=[
            jax.ShapeDtypeStruct((tok_count, feature_width), jnp.bfloat16),
            jax.ShapeDtypeStruct((2, key_count, feature_width), jnp.bfloat16),
        ],
        cost_estimate=lasting(10.2),
        name="self_backward",
    )(query, key_value, key_value, grad, key_pos, low_pos, high_pos, log_total)


WHOLE = ((0, None), (1, None), (2, None), (3, None))
HALVES = ((0, None), (1, None), (2, 0), (2, 1), (3, 0), (3, 1))


def bases_of(pieces):
    return WHOLE if len(pieces) == len(WHOLE) else HALVES


def fill(out_ref, pieces, index_ref, columns=slice(None)):
    rows = pieces[0].shape[0]
    for piece, (j, half) in zip(pieces, bases_of(pieces)):
        place = (index_ref[0] ^ j) * rows
        if half is not None:
            place = place + ((index_ref[1] % 2) ^ half) * (rows // 2)
        part = piece[:, columns].astype(out_ref.dtype)
        out_ref[pl.ds(pl.multiple_of(place, 16), piece.shape[0]), :] = part


def whole(value):
    zeros = (0,) * value.ndim
    return pl.BlockSpec(value.shape, lambda *_: zeros)


def chain_call(kernel, name, grid, index, inputs, outputs, scratch, microseconds):
    return pl.pallas_call(
        kernel,
        grid_spec=pltpu.PrefetchScalarGridSpec(
            num_scalar_prefetch=1,
            grid=grid,
            in_specs=[spec for _, spec in inputs],
            out_specs=[spec for _, _, spec in outputs],
            scratch_shapes=scratch,
        ),
        out_shape=[jax.ShapeDtypeStruct(shape, dtype) for shape, dtype, _ in outputs],
        cost_estimate=lasting(microseconds),
        name=name,
    )(index, *[value for value, _ in inputs])


def const(shape):
    zeros = (0,) * len(shape)
    return pl.BlockSpec(shape, lambda *_: zeros)


def project_kernel(layout, tok, pieces, index_ref, *refs):
    row_refs, refs = refs[: len(layout)], refs[len(layout) :]
    piece_refs, refs = refs[:pieces], refs[pieces:]
    q_ref, kv_ref, norm_ref, w_ref, gain_ref, rows_ref, column_ref = refs
    width = q_ref.shape[1]
    step = pl.program_id(0)

    @pl.when(step == 0)
    def _():
        for row_ref, moves in zip(row_refs, layout):
            for start, place, count in moves:
                rows_ref[pl.ds(place, count), :] = row_ref[pl.ds(start, count), :]
        fill(w_ref, piece_refs, index_ref, slice(0, 3 * width))
        fill(column_ref, piece_refs, index_ref, slice(3 * width, 3 * width + 128))
        gain_ref[...] = column_ref[...].T[: gain_ref.shape[0], :]

    count = norm_ref.shape[0]
    values = rows_ref[pl.ds(pl.multiple_of(step * count, count), count), :].astype(jnp.float32)
    norm = to_low(values * inverse_rms(values) * gain_ref[0:1, :])
    norm_ref[...] = norm
    kv_ref[...] = to_low(matmul(norm, w_ref[:, width:]))

    @pl.when(step == 0)
    def _():
        q_ref[...] = to_low(matmul(norm_ref[pl.ds(0, tok), :], w_ref[:, :width]))


def project(index, row_pieces, layout, pieces, tok):
    width = row_pieces[0].shape[1]
    total = sum(piece.shape[0] for piece in row_pieces)
    block = min(512, total)
    inputs = [(value, whole(value)) for value in (*row_pieces, *pieces)]
    outputs = [
        ((tok, width), jnp.bfloat16, const((tok, width))),
        ((total, 2 * width), jnp.bfloat16, pl.BlockSpec((block, 2 * width), lambda i, _: (i, 0))),
        ((total, width), jnp.bfloat16, pl.BlockSpec((block, width), lambda i, _: (i, 0))),
        ((width, 3 * width), jnp.bfloat16, const((width, 3 * width))),
        ((8, width), jnp.float32, const((8, width))),
    ]
    scratch = [pltpu.VMEM((total, width), jnp.bfloat16), pltpu.VMEM((width, 128), jnp.float32)]
    return chain_call(
        functools.partial(project_kernel, layout, tok, len(pieces)),
        "project",
        (total // block,),
        index,
        inputs,
        outputs,
        scratch,
        9.6,
    )


def attend_out_kernel(pieces, index_ref, att_ref, own_ref, gain_ref, *refs):
    piece_refs, (after_ref, norm_ref, query_ref, w_ref) = refs[:pieces], refs[pieces:]
    width = att_ref.shape[1]
    fill(w_ref, piece_refs, index_ref)
    rows = own_ref[...].astype(jnp.float32) + matmul(att_ref[...], w_ref[:, :width])
    after_ref[...] = rows
    norm = to_low(rows * inverse_rms(rows) * gain_ref[1:2, :])
    norm_ref[...] = norm
    query_ref[...] = to_low(matmul(norm, w_ref[:, width:]))


def attend_out(index, attended, own, gain_rows, pieces):
    tok, width = attended.shape
    inputs = [(value, whole(value)) for value in (attended, own, gain_rows)]
    inputs += [
        (piece, pl.BlockSpec((piece.shape[0], 2 * width), lambda *_: (0, 0))) for piece in pieces
    ]
    outputs = [
        ((tok, width), jnp.float32, const((tok, width))),
        ((tok, width), jnp.bfloat16, const((tok, width))),
        ((tok, width), jnp.bfloat16, const((tok, width))),
        ((width, 2 * width), jnp.bfloat16, const((width, 2 * width))),
    ]
    return chain_call(
        functools.partial(attend_out_kernel, len(pieces)),
        "attend_out",
        (1,),
        index,
        inputs,
        outputs,
        [],
        4.4,
    )


def cross_forward_kernel(head_size, stretches, pieces, index_ref, *refs):
    q_ref, enc_ref, rows_ref, keep_ref, gain_ref = refs[:5]
    refs = refs[5:]
    key_refs, value_refs = refs[:pieces], refs[pieces : 2 * pieces]
    out_refs, refs = refs[2 * pieces : 3 * pieces], refs[3 * pieces :]
    kv_ref, cross_ref, after_ref, norm_ref, wkv_ref, wout_ref = refs
    score_scale = head_size ** (-0.5)
    pair = pl.program_id(0)
    wide = q_ref.shape[1]
    fill(wkv_ref.at[0], key_refs, index_ref)
    fill(wkv_ref.at[1], value_refs, index_ref)
    kv_ref[0] = to_low(matmul(enc_ref[...], wkv_ref[0]))
    kv_ref[1] = to_low(matmul(enc_ref[...], wkv_ref[1]))

    @pl.when(pair == 0)
    def _():
        fill(wout_ref, out_refs, index_ref)

    keys = enc_ref.shape[0] // stretches
    parts = []
    for s in range(stretches):
        span = pl.ds(s * keys, keys)
        query = head_rows(q_ref[pl.ds(s * STRETCH, STRETCH), :], head_size)
        scores = right_product(kv_ref[0, span, :], query) * score_scale
        weights = jnp.exp(scores - jnp.max(scores, axis=0, keepdims=True))
        probs = to_low(weights / jnp.sum(weights, axis=0, keepdims=True))
        parts.append(join_heads(left_product(kv_ref[1, span, :], probs), head_size))
    columns = pl.ds(pl.multiple_of(pair * wide, wide), wide)
    cross_ref[:, columns] = to_low(jnp.concatenate(parts, axis=0))

    @pl.when(pair == pl.num_programs(0) - 1)
    def _():
        rows = rows_ref[...] + keep_ref[...] * matmul(cross_ref[...], wout_ref[...])
        after_ref[...] = rows
        norm_ref[...] = to_low(rows * inverse_rms(rows) * gain_ref[2:3, :])


def cross_forward(index, query, enc_rows, after_attn, keep_rows, gain_rows, pieces, stretches):
    tok, width = query.shape
    pairs = H // 2
    keys = enc_rows.shape[0]
    inputs = [(query, pl.BlockSpec((tok, 128), lambda i, _: (0, i)))]
    inputs += [(value, whole(value)) for value in (enc_rows, after_attn, keep_rows, gain_rows)]
    for first in (0, pairs):
        inputs += [
            (piece, pl.BlockSpec((piece.shape[0], 128), lambda i, _, f=first: (0, f + i)))
            for piece in pieces
        ]
    inputs += [(piece, pl.BlockSpec((piece.shape[0], width), lambda i, _: (0, 2))) for piece in pieces]
    outputs = [
        ((2, keys, width), jnp.bfloat16, pl.BlockSpec((2, keys, 128), lambda i, _: (0, 0, i))),
        ((tok, width), jnp.bfloat16, const((tok, width))),
        ((tok, width), jnp.float32, const((tok, width))),
        ((tok, width), jnp.bfloat16, const((tok, width))),
        ((2, width, width), jnp.bfloat16, pl.BlockSpec((2, width, 128), lambda i, _: (0, 0, i))),
        ((width, width), jnp.bfloat16, const((width, width))),
    ]
    return chain_call(
        functools.partial(cross_forward_kernel, width // H, stretches, len(pieces)),
        "cross_forward",
        (pairs,),
        index,
        inputs,
        outputs,
        [],
        12.3,
    )


ERF_ABOVE = (
    -2.72614225801306e-10, 2.77068142495902e-08, -2.10102402082508e-06, -5.69250639462346e-05,
    -7.34990630326855e-04, -2.95459980854025e-03, -1.60960333262415e-02,
)
ERF_BELOW = (
    -1.45660718464996e-05, -2.13374055278905e-04, -1.68282697438203e-03, -7.37332916720468e-03,
    -1.42647390514189e-02,
)


def erf(values):
    values = jnp.clip(values, -4.0, 4.0)
    square = values * values
    above, below = ERF_ABOVE[0], ERF_BELOW[0]
    for factor in ERF_ABOVE[1:]:
        above = above * square + factor
    for factor in ERF_BELOW[1:]:
        below = below * square + factor
    return values * above / below


def mlp_kernel(tok, chunks, index_ref, *refs):
    norms, cots, pieces, (down_ref,) = refs[:4], refs[4:8], refs[8:12], refs[12:13]
    (
        grad_own_ref, grad_across_ref, grad_send_ref, out_own_ref, out_across_ref, out_send_ref,
        down_share_ref, keep_ref, send_ref, w_ref, held_ref, norm_all, cot_all, act_all, inner_all,
    ) = refs[13:]
    fill(w_ref, pieces, index_ref)
    for k in range(4):
        norm_all[pl.ds(k * tok, tok), :] = norms[k][...]
        cot_all[pl.ds(k * tok, tok), :] = cots[k][...]
    for k in range(2):
        rows = pl.ds(2 * k * tok, 2 * tok)
        inner = matmul(norm_all[rows, :], w_ref[...])
        share_below = 0.5 * (1.0 + erf(inner * (2.0**-0.5)))
        activation = to_low(inner * share_below)
        act_all[rows, :] = activation
        slope = share_below + inner * jnp.exp(-0.5 * inner * inner) * ((2.0 * jnp.pi) ** -0.5)
        grad_inner = to_low(right_product(cot_all[rows, :], down_ref[...]) * slope)
        inner_all[rows, :] = grad_inner
        grad = right_product(grad_inner, w_ref[...])
        out = matmul(activation, down_ref[...])
        for own_ref, across_ref, send_refs, value in (
            (grad_own_ref, grad_across_ref, grad_send_ref, grad),
            (out_own_ref, out_across_ref, out_send_ref, out),
        ):
            if k == 0:
                own_ref[...] = value[:tok]
            else:
                across_ref[...] = value[:tok]
            send_refs[k] = to_low(value[tok:])
    depth = down_ref.shape[0]
    held_ref[...] = left_product(act_all[...], cot_all[...])
    store_chunks(down_share_ref, 0, held_ref, 0, depth, index_ref[2], chunks[1])
    held_ref[...] = left_product(norm_all[...], inner_all[...])
    rows = depth // 4
    for out_ref, order in ((keep_ref, (0, 2)), (send_ref, (1, 3))):
        for k, j in enumerate(order):
            store_chunks(
                out_ref, k * rows, held_ref, (index_ref[0] ^ j) * rows, rows, index_ref[2], chunks[0]
            )


def mlp_share(index, norms, cots, pieces, w_down):
    depth, width = w_down.shape
    tok = norms[0][2]
    chunks = (chunk_count(width // len(WHOLE)), chunk_count(depth))
    inputs = []
    for value, start, count in (*norms, *cots, *pieces):
        inputs.append((value, pl.BlockSpec((count, depth), lambda *_, s=start // count: (s, 0))))
    inputs.append((w_down, whole(w_down)))
    token_f32 = ((tok, width), jnp.float32, const((tok, width)))
    token_send = ((2, tok, width), jnp.bfloat16, const((2, tok, width)))
    rows = ((width // 2, depth), jnp.bfloat16, const((width // 2, depth)))
    outputs = [token_f32, token_f32, token_send, token_f32, token_f32, token_send]
    outputs += [((depth, width), jnp.bfloat16, const((depth, width))), rows, rows]
    scratch = [pltpu.VMEM((width, depth), jnp.bfloat16), pltpu.VMEM((depth, depth), jnp.float32)]
    scratch += [pltpu.VMEM((4 * tok, depth), jnp.bfloat16)] * 4
    return chain_call(
        functools.partial(mlp_kernel, tok, chunks),
        "mlp_share",
        (1,),
        index,
        inputs,
        outputs,
        scratch,
        14.0,
    )


def inner_out_kernel(index_ref, own_ref, far_ref, weight_ref, gain_ref, out_ref, sum_ref):
    half = own_ref.shape[0]
    upper = index_ref[1] % 2
    own = own_ref[...].astype(jnp.float32)
    far = far_ref[...].astype(jnp.float32)
    out_ref[pl.ds(pl.multiple_of(upper * half, 8), half), :] = own
    out_ref[pl.ds(pl.multiple_of((1 - upper) * half, 8), half), :] = far
    part = jnp.sum(weight_ref[...].astype(jnp.float32) * out_ref[...], axis=1, keepdims=True)
    part = part / gain_ref[...]

    @pl.when(pl.program_id(0) == 0)
    def _():
        sum_ref[...] = part

    @pl.when(pl.program_id(0) > 0)
    def _():
        sum_ref[...] = sum_ref[...] + part


def inner_out(index, halves, weight, gain):
    own, far = halves
    rows, full = weight.shape
    depth = full // len(WHOLE)
    block = pl.BlockSpec((rows // 2, depth), lambda t, index_ref: (0, t ^ index_ref[0]))
    column = gain.astype(jnp.float32).reshape(rows, 1)
    inputs = [(own, block), (far, block)]
    inputs += [(weight, pl.BlockSpec((rows, depth), lambda t, _: (0, t))), (column, whole(column))]
    outputs = [
        ((rows, full), jnp.float32, pl.BlockSpec((rows, depth), lambda t, _: (0, t))),
        ((rows, 1), jnp.float32, const((rows, 1))),
    ]
    total, sums = chain_call(
        inner_out_kernel, "inner_out", (len(WHOLE),), index, inputs, outputs, [], 3.0
    )
    return total, sums.reshape(rows)


def cross_backward_kernel(head_size, stretches, index_ref, *refs):
    q_ref, kv_ref, cot_ref, part0, part1, part2, cross_ref, wout_ref, keep_ref = refs[:9]
    w_ref, rows_ref, gain_ref = refs[9:12]
    dq_ref, dkv_ref, out_ref, branch_ref, attended_ref, first_ref, grad_ref, do_ref = refs[12:]
    score_scale = head_size ** (-0.5)
    pair = pl.program_id(0)
    wide = q_ref.shape[1]
    keys = kv_ref.shape[1] // stretches
    columns = pl.ds(pl.multiple_of(pair * wide, wide), wide)

    @pl.when(pair == 0)
    def _():
        values = cross_ref[...]
        grad_norm = (
            part0[...] + part1[...].astype(jnp.float32) + part2[...].astype(jnp.float32)
        )
        grad = cot_ref[...].astype(jnp.float32) + rms_back(
            values, inverse_rms(values), gain_ref[2:3, :], grad_norm
        )
        grad_ref[...] = grad
        branch = to_low(keep_ref[...] * grad)
        first_ref[...] = branch
        do_ref[...] = to_low(right_product(branch, wout_ref[...]))

    parts = []
    for s in range(stretches):
        rows = pl.ds(s * STRETCH, STRETCH)
        span = pl.ds(s * keys, keys)
        query = head_rows(q_ref[rows, :], head_size)
        grad = head_rows(do_ref[rows, columns], head_size)
        scores = right_product(kv_ref[0, span, :], query) * score_scale
        weights = jnp.exp(scores - jnp.max(scores, axis=0, keepdims=True))
        probs = weights / jnp.sum(weights, axis=0, keepdims=True)
        dprobs = right_product(kv_ref[1, span, :], grad)
        delta = jnp.sum(probs * dprobs, axis=0, keepdims=True)
        dscores = to_low(probs * (dprobs - delta))
        dkv_ref[0, span, :] = to_low(score_scale * matmul(dscores, query))
        dkv_ref[1, span, :] = to_low(matmul(to_low(probs), grad))
        parts.append(join_heads(left_product(kv_ref[0, span, :], dscores), head_size))
    dq_ref[:, columns] = to_low(score_scale * jnp.concatenate(parts, axis=0))

    @pl.when(pair == pl.num_programs(0) - 1)
    def _():
        width = rows_ref.shape[1]
        values = rows_ref[...]
        grad_norm = right_product(dq_ref[...], w_ref[:, width:])
        total = grad_ref[...] + rms_back(
            values, inverse_rms(values), gain_ref[1:2, :], grad_norm
        )
        out_ref[...] = total
        branch = to_low(total)
        branch_ref[...] = branch
        attended_ref[...] = to_low(right_product(branch, w_ref[:, :width]))


def cross_backward(
    index, query, key_value, cotangent, terms, after_cross, w_cout, keep_rows, w_pair, after_attn,
    gain_rows, stretches,
):
    tok, width = query.shape
    keys = key_value.shape[1]
    block = pl.BlockSpec((tok, 128), lambda i, _: (0, i))
    planes = pl.BlockSpec((2, keys, 128), lambda i, _: (0, 0, i))
    inputs = [(query, block), (key_value, planes), (cotangent, whole(cotangent))]
    own, sibling, across = terms
    inputs += [
        (own, whole(own)),
        (sibling, pl.BlockSpec((None, tok, width), lambda *_: (0, 0, 0))),
        (across, whole(across)),
    ]
    inputs += [
        (value, whole(value))
        for value in (after_cross, w_cout, keep_rows, w_pair, after_attn, gain_rows)
    ]
    low = ((tok, width), jnp.bfloat16, const((tok, width)))
    outputs = [
        low,
        ((2, keys, width), jnp.bfloat16, planes),
        ((tok, width), jnp.float32, const((tok, width))),
        low,
        low,
        low,
    ]
    return chain_call(
        functools.partial(cross_backward_kernel, width // H, stretches),
        "cross_backward",
        (H // 2,),
        index,
        inputs,
        outputs,
        [pltpu.VMEM((tok, width), jnp.float32), pltpu.VMEM((tok, width), jnp.bfloat16)],
        13.0,
    )


def swap(values, axis, bit):
    count = lax.axis_size(axis)
    return lax.ppermute(values, axis, [(i, i ^ bit) for i in range(count)])


def after(value, *earlier):
    return lax.optimization_barrier((value,) + earlier)[0]


def mirrored(position, count):
    out = 0
    for _ in range(count.bit_length() - 1):
        out, position = 2 * out + position % 2, position // 2
    return out


def positions_kernel(
    stretches, index_ref, deal_ref, lengths_ref, pos_ref, low_ref, high_ref, keep_ref
):
    ctx_index = index_ref[1]
    held = pos_ref.shape[0] // STRETCH
    offset = lax.broadcasted_iota(jnp.int32, (STRETCH, 1), 0)
    for s in range(held):
        device = ctx_index ^ mirrored(s // stretches, held // stretches)
        given = deal_ref[device * stretches + s % stretches]
        pos_ref[pl.ds(s * STRETCH, STRETCH), :] = given * STRETCH + offset
    lane = lax.broadcasted_iota(jnp.int32, low_ref.shape, 1) % (stretches * STRETCH)
    low_pos = jnp.zeros(low_ref.shape, jnp.int32)
    high_pos = jnp.zeros(low_ref.shape, jnp.int32)
    for s in range(stretches):
        given = deal_ref[ctx_index * stretches + s]
        start, end = 0, 0
        for q in range(lengths_ref.shape[0]):
            start = jnp.where(end <= given, end, start)
            end = end + lengths_ref[q]
        here = lane // STRETCH == s
        low_pos = jnp.where(here, start * STRETCH, low_pos)
        high_pos = jnp.where(here, given * STRETCH + lane % STRETCH, high_pos)
        kept = jnp.where(given != start, 1.0, 0.0).astype(jnp.float32)
        keep_ref[pl.ds(s * STRETCH, STRETCH), :] = jnp.full((STRETCH, 1), kept, jnp.float32)
    low_ref[...] = low_pos
    high_ref[...] = high_pos


def positions(index, deal_row, lengths_row, stretches):
    tok_count = stretches * STRETCH
    smem = pl.BlockSpec(memory_space=pltpu.SMEM)
    vmem = pl.BlockSpec(memory_space=pltpu.VMEM)
    return pl.pallas_call(
        functools.partial(positions_kernel, stretches),
        in_specs=[smem] * 3,
        out_specs=[vmem] * 4,
        out_shape=[
            jax.ShapeDtypeStruct((deal_row.shape[0] * STRETCH, 1), jnp.int32),
            jax.ShapeDtypeStruct((1, 2 * tok_count), jnp.int32),
            jax.ShapeDtypeStruct((1, 2 * tok_count), jnp.int32),
            jax.ShapeDtypeStruct((tok_count, 1), jnp.float32),
        ],
        cost_estimate=lasting(1.5),
        name="positions",
    )(index, deal_row, lengths_row)


def chunk_count(rows):
    count = lax.axis_size("ctx")
    return count if count & (count - 1) == 0 and rows % (8 * count) == 0 else 1


def store_chunks(out_ref, start, held_ref, base, rows, own_chunk, chunks):
    size = rows // chunks
    for p in range(chunks):
        place = base + (own_chunk ^ p) * size
        part = held_ref[pl.ds(pl.multiple_of(place, 8), size), :]
        out_ref[pl.ds(start + p * size, size), :] = part.astype(out_ref.dtype)


def products_kernel(tiles, rows, chunks, index_ref, *refs):
    count = len(tiles)
    inputs, (keep_ref, send_ref, held_ref) = refs[:-3], refs[-3:]
    fsdp_index, own_chunk = index_ref[0], index_ref[2]
    width = held_ref.shape[1]
    for t, (left, right, column) in enumerate(tiles):

        @pl.when(pl.program_id(0) == t)
        def _(left=left, right=right, column=column):
            grads = inputs[right][:, pl.ds(column * width, width)]
            held_ref[...] = left_product(inputs[left][...], grads)

    for out_ref, order in ((keep_ref, (0, 2)), (send_ref, (1, 3))):
        for k, j in enumerate(order):
            store_chunks(
                out_ref, k * rows, held_ref, (fsdp_index ^ j) * rows, rows, own_chunk, chunks
            )


def wide_products(index, terms):
    shares = lax.axis_size("fsdp")
    inputs, tiles = [], []
    width = terms[0][0].shape[1]
    for left, right, plane in terms:
        if not inputs or all(left is not value for value, _ in inputs):
            inputs.append((left, None))
        first = next(i for i, (value, _) in enumerate(inputs) if value is left)
        inputs.append((right, plane))
        for column in range(right.shape[-1] // width):
            tiles.append((first, len(inputs) - 1, column))
    rows = width // shares
    chunks = chunk_count(rows)
    specs = []
    for value, plane in inputs:
        if value.ndim == 2:
            specs.append(pl.BlockSpec(value.shape, lambda i, _: (0, 0)))
        else:
            specs.append(
                pl.BlockSpec((None,) + value.shape[1:], lambda i, _, plane=plane: (plane, 0, 0))
            )
    total = len(tiles) * width
    out = jax.ShapeDtypeStruct((2 * rows, total), jnp.bfloat16)
    out_spec = pl.BlockSpec((2 * rows, width), lambda i, _: (0, i))
    return pl.pallas_call(
        functools.partial(products_kernel, tiles, rows, chunks),
        grid_spec=pltpu.PrefetchScalarGridSpec(
            num_scalar_prefetch=1,
            grid=(len(tiles),),
            in_specs=specs,
            out_specs=[out_spec, out_spec],
            scratch_shapes=[pltpu.VMEM((width, width), jnp.float32)],
        ),
        out_shape=[out, out],
        cost_estimate=lasting(8.2),
        name="wide_products",
    )(index, *[value for value, _ in inputs])


def add_low(*parts):
    return to_low(sum(part.astype(jnp.float32) for part in parts))


def reduction(keep, send):
    rows = keep.shape[0] // 2
    token = yield send
    received = after(swap(send, "fsdp", 1), *token)
    sent = add_low(keep[rows:], received[rows:])
    token = yield sent
    across = after(swap(sent, "fsdp", 2), *token)
    return (yield from ctx_reduction((keep[:rows], received[:rows], across)))


def in_order(index, bit, own, far):
    upper = (index & bit) != 0
    return jnp.concatenate([jnp.where(upper, far, own), jnp.where(upper, own, far)], axis=0)


def ctx_reduction(parts):
    index = lax.axis_index("ctx")
    half = parts[0].shape[0] // 2
    chunks = chunk_count(2 * half)
    if chunks == 1:
        share = lax.psum(add_low(*parts), "ctx")
        upper = (index & 1) != 0
        first, second = share[:half], share[half:]
        return jnp.where(upper, second, first), jnp.where(upper, first, second)
    bit = 1
    while bit < chunks:
        sent = add_low(*[part[half:] for part in parts])
        held = add_low(*[part[:half] for part in parts])
        token = yield sent
        parts = (held, after(swap(sent, "ctx", bit), *token))
        half, bit = half // 2, 2 * bit
    gathered = add_low(*parts)
    token = yield gathered
    while bit > 2:
        bit = bit // 2
        far = after(swap(gathered, "ctx", bit), *token)
        gathered = in_order(index, bit, gathered, far)
        token = yield gathered
    return gathered, after(swap(gathered, "ctx", 1), *token)


def finished(halves, offset, width):
    own, far = (half[:, offset : offset + width] for half in halves)
    return in_order(lax.axis_index("ctx"), 1, own, far).astype(jnp.float32)


def sum_to_owner(rows_sum):
    total = to_low(rows_sum)
    bit = 1
    while bit < lax.axis_size("ctx"):
        half = total.shape[0] // 2
        sent = total[half:]
        token = yield sent
        total = add_low(total[:half], after(swap(sent, "ctx", bit), *token))
        bit = 2 * bit
    return total


class Steps:
    def __init__(self, steps):
        self.steps = steps
        self.result = None
        self.advance(None)

    def advance(self, token):
        try:
            return self.steps.send(token)
        except StopIteration as stop:
            self.result = stop.value
            return stop.value[1] if isinstance(stop.value, tuple) else stop.value

    def move(self, *token):
        return token[0] if self.result is not None else self.advance(token)

    def finish(self, *token):
        sent = token[0]
        while self.result is None:
            sent = self.move(sent)
        return sent


def gain_gradient(weight, grad, gain):
    return jnp.sum(weight.astype(jnp.float32) * grad, axis=1) / gain.astype(jnp.float32)


def local(
    hidden,
    neighbours,
    cotangent,
    stretch_deal,
    seq_lengths,
    norm_gains,
    attn_qkv,
    attn_out,
    cross_q,
    cross_kv,
    cross_out,
    mlp_in,
    mlp_out,
):
    shares = lax.axis_size("fsdp")
    fsdp_index = lax.axis_index("fsdp")
    ctx_index = lax.axis_index("ctx")
    ctx_count = lax.axis_size("ctx")
    own_chunk, bit = 0 * ctx_index, 1
    while bit < ctx_count:
        own_chunk = 2 * own_chunk + (ctx_index & bit) // bit
        bit = 2 * bit
    place = jnp.stack([fsdp_index, ctx_index, own_chunk]).astype(jnp.int32)
    feature_width = hidden.shape[2]
    own = hidden[0]
    tok = own.shape[0]
    stretch_count = tok // STRETCH
    enc_rows = neighbours[0].reshape(-1, feature_width)
    cot = cotangent[0]

    key_pos, low_pos, high_pos, keep_rows = positions(
        place, stretch_deal[0], seq_lengths[0], stretch_count
    )

    first_share = jnp.concatenate(
        [attn_qkv, jnp.pad(norm_gains.T, ((0, 0), (0, 128 - norm_gains.shape[0])))], axis=1
    )
    own = after(own, first_share)
    across_qkv = swap(first_share, "fsdp", 2)
    if ctx_count == 8:
        far, last, near = swap(own, "ctx", 4), swap(own, "ctx", 6), swap(own, "ctx", 2)
        beside = swap(own, "ctx", 1)
        second = after(jnp.concatenate([far, near, last], axis=0), key_pos)
        row_pieces = [own, second, beside, swap(second, "ctx", 1)]
        layout = [((0, k * tok, piece.shape[0]),) for k, piece in zip((0, 1, 4, 5), row_pieces)]
        second = after(second, beside)
    else:
        first = own
        bit = ctx_count
        while bit > 2:
            bit = bit // 2
            first = jnp.concatenate([first, swap(first, "ctx", bit)], axis=0)
        row_pieces = [first, swap(first, "ctx", 1)]
        layout = [((0, k * first.shape[0], first.shape[0]),) for k in range(2)]
        second = first
    sibling_qkv = swap(after(first_share, second), "fsdp", 1)
    across_qkv = after(across_qkv, second)
    diagonal_qkv = swap(across_qkv, "fsdp", 1)
    pair_share = jnp.concatenate([attn_out, cross_q], axis=1)
    across_pair = swap(after(pair_share, second), "fsdp", 2)
    cross_share = jnp.concatenate([cross_kv, cross_out], axis=1)
    across_cross = swap(after(cross_share, across_qkv), "fsdp", 2)
    depth = mlp_out.shape[0]
    rows_in = mlp_in.shape[0]

    def block_of(j):
        return lax.dynamic_slice_in_dim(mlp_in, (fsdp_index ^ j) * depth, depth, axis=1)

    block_own = block_of(0)
    exchange_sibling = jnp.concatenate([block_of(1), cot], axis=0)
    exchange_across = jnp.concatenate([block_of(2), block_of(3), cot], axis=0)

    query, key_value, norm_all, w_qkv, gain_rows = project(
        place, row_pieces, layout, [first_share, sibling_qkv, across_qkv, diagonal_qkv], tok
    )
    across_pair = after(across_pair, query)
    diagonal_pair = swap(across_pair, "fsdp", 1)
    sibling_pair = swap(after(pair_share, query), "fsdp", 1)
    from_across = swap(after(exchange_across, across_pair), "fsdp", 2)
    attended, log_total = self_forward(query, key_value, key_pos, low_pos, high_pos)
    sibling_cross = swap(after(cross_share, attended), "fsdp", 1)
    after_attn, norm_two, cross_query, w_pair = attend_out(
        place, attended, own, gain_rows, [pair_share, sibling_pair, across_pair, diagonal_pair]
    )
    across_cross = after(across_cross, cross_query)
    diagonal_cross = swap(across_cross, "fsdp", 1)
    cross_key_value, cross_rows, after_cross, norm_three, w_ckv, w_cout = cross_forward(
        place,
        cross_query,
        enc_rows,
        after_attn,
        keep_rows,
        gain_rows,
        [cross_share, sibling_cross, across_cross, diagonal_cross],
        stretch_count,
    )
    from_sibling = swap(after(exchange_sibling, cross_query), "fsdp", 1)
    norm_across, norm_sibling = swap(norm_three, "fsdp", 2), swap(norm_three, "fsdp", 1)
    from_across = after(from_across, norm_three)
    from_diagonal = swap(from_across[rows_in:], "fsdp", 1)
    norm_diagonal = swap(norm_across, "fsdp", 1)
    cot_across = from_across[2 * rows_in :]
    (
        grad_own, grad_across, grad_send, out_own, out_across, out_send, share_down, keep_in, send_in,
    ) = mlp_share(
        place,
        [(value, 0, tok) for value in (norm_three, norm_sibling, norm_across, norm_diagonal)],
        [
            (value, 0, tok)
            for value in (cot, from_sibling[rows_in:], cot_across, from_diagonal[rows_in:])
        ],
        [
            (block_own, 0, rows_in),
            (from_sibling, 0, rows_in),
            (from_across, 0, rows_in),
            (from_diagonal, 0, rows_in),
        ],
        mlp_out,
    )

    from_sibling = swap(grad_send, "fsdp", 1)
    grad_far = swap(add_low(grad_across, from_sibling[1]), "fsdp", 2)
    down = Steps(ctx_reduction((share_down,)))
    received_in = swap(send_in, "fsdp", 1)
    (
        grad_cross_query, grad_cross_pair, grad_after_attn, grad_attn_branch, grad_attended,
        grad_cross_branch,
    ) = cross_backward(
        place,
        cross_query,
        cross_key_value,
        cot,
        (grad_own, from_sibling, grad_far),
        after_cross,
        w_cout,
        keep_rows,
        w_pair,
        after_attn,
        gain_rows,
        stretch_count,
    )
    received_in = after(received_in, grad_cross_query)
    across_in = swap(
        jnp.concatenate([keep_in[rows_in:], received_in[rows_in:]], axis=1), "fsdp", 2
    )
    ready = down.move(grad_cross_query)
    keep_cross, send_cross = wide_products(
        place,
        [
            (cross_rows, grad_cross_branch, None),
            (norm_two, grad_cross_query, None),
            (enc_rows, grad_cross_pair, 0),
            (enc_rows, grad_cross_pair, 1),
            (attended, grad_attn_branch, None),
        ],
    )
    cross = Steps(reduction(keep_cross, send_cross))
    grad_query, grad_pair = self_backward(
        query,
        key_value,
        after(grad_attended, keep_cross, ready),
        key_pos,
        low_pos,
        high_pos,
        log_total,
    )
    across_in = after(across_in, grad_query)
    inner = Steps(
        ctx_reduction(
            (jnp.concatenate([keep_in[:rows_in], received_in[:rows_in], across_in], axis=1),)
        )
    )
    ready = cross.move(down.move(grad_query))
    keep_attn, send_attn = wide_products(
        place,
        [
            (norm_all[:tok], after(grad_query, ready), None),
            (norm_all, grad_pair, 0),
            (norm_all, grad_pair, 1),
        ],
    )
    attn = Steps(reduction(keep_attn, send_attn))
    grad_pair, grad_query = lax.optimization_barrier((grad_pair, grad_query, keep_attn))[:2]
    grad_norm1_all = right_product(
        grad_pair[0], w_qkv[:, feature_width : 2 * feature_width]
    ) + right_product(grad_pair[1], w_qkv[:, 2 * feature_width :])
    norm1 = Steps(sum_to_owner(grad_norm1_all))
    out_sibling = swap(after(out_send, keep_attn), "fsdp", 1)
    grad_cross_pair = after(grad_cross_pair, grad_norm1_all)
    grad_enc = right_product(grad_cross_pair[0], w_ckv[0]) + right_product(
        grad_cross_pair[1], w_ckv[1]
    )
    out_sibling = after(out_sibling, grad_enc)
    out_far = swap(add_low(out_across, out_sibling[1]), "fsdp", 2)
    ready = grad_enc
    for step in (cross, attn, inner, down, norm1, inner, down, norm1, cross, attn):
        ready = step.move(ready)
    layer_out = after_cross + (
        out_own + out_sibling[0].astype(jnp.float32) + after(out_far, ready).astype(jnp.float32)
    )
    for step in (inner, down, norm1, cross, attn):
        ready = step.move(ready)
    ready = down.finish(ready)
    total_down = finished(down.result, 0, feature_width)
    input_rows = own.astype(jnp.float32)
    ready = norm1.finish(ready)
    grad_norm1 = (
        norm1.result.astype(jnp.float32)
        + right_product(after(grad_query, ready), w_qkv[:, :feature_width])
    )
    grad_input = grad_after_attn + rms_back(
        input_rows, inverse_rms(input_rows), gain_rows[0:1], grad_norm1
    )
    ready = after(ready, grad_input, total_down, layer_out)
    for step in (cross, attn, inner, cross, attn, inner, cross, attn):
        ready = step.move(ready)
    ready = inner.finish(ready)
    total_in, gain_three = inner_out(place, inner.result, mlp_in, norm_gains[2])
    ready = after(ready, total_in)
    while attn.result is None or cross.result is None:
        for step in (cross, attn):
            if step.result is None:
                ready = step.move(ready)
    halves_cross, halves_attn = cross.result, attn.result
    d = feature_width
    total_cout = finished(halves_cross, 0, d)
    total_cq = finished(halves_cross, d, d)
    total_ckv = finished(halves_cross, 2 * d, 2 * d)
    total_out = finished(halves_cross, 4 * d, d)
    total_qkv = finished(halves_attn, 0, 3 * d)
    grad_gains = jnp.stack(
        [
            gain_gradient(attn_qkv, total_qkv, norm_gains[0]),
            gain_gradient(cross_q, total_cq, norm_gains[1]),
            gain_three,
        ]
    )
    return (
        layer_out[None],
        grad_input[None],
        grad_enc.reshape(neighbours.shape),
        grad_gains,
        total_qkv,
        total_out,
        total_cq,
        total_ckv,
        total_cout,
        total_in,
        total_down,
    )


def solution(mesh):
    return jax.shard_map(
        local,
        mesh=mesh,
        in_specs=(
            P("fsdp", "ctx", None),
            P("fsdp", "ctx", None, None),
            P("fsdp", "ctx", None),
            P("fsdp", None),
            P("fsdp", None),
            P(None, "fsdp"),
            P("fsdp", None),
            P("fsdp", None),
            P("fsdp", None),
            P("fsdp", None),
            P("fsdp", None),
            P("fsdp", None),
            P("fsdp", None),
        ),
        out_specs=(
            P("fsdp", "ctx", None),
            P("fsdp", "ctx", None),
            P("fsdp", "ctx", None, None),
            P(None, "fsdp"),
            P("fsdp", None),
            P("fsdp", None),
            P("fsdp", None),
            P("fsdp", None),
            P("fsdp", None),
            P("fsdp", None),
            P("fsdp", None),
        ),
        check_vma=False,
    )
```

time: 469 us -> 332 us (0.71)
  waiting for transfers between devices: 199 us -> 117 us
  matrix products: 45.7 us -> 8.19 us
  Pallas kernels: 113 us -> 89.5 us
  local copies, waits for them, and re-layouts: 8.89 us -> 22.2 us
  other arithmetic: 38.7 us -> 26.8 us
  starting transfers between devices: 57.2 us -> 65.4 us
    ppermute x61 -> x57, waiting for transfers between devices: 199 us -> 117 us  [swap(): return lax.ppermute(values, axis, [(i, i ^ bit) for i in range(count)])]
    dot_general x8 -> x0, matrix products: 23.1 us -> none  [matmul(): return jnp.dot(left, right, preferred_element_type=jnp.float32)]
    pallas_call x17 -> x7, Pallas kernels: 72.5 us -> 55.5 us  [the longest x6 53.8 us: chain_call(): pl.pallas_call(kernel, grid_spec=pltpu.PrefetchScalarGridSpec(num_scalar_...]
    dot_general x10 -> x5, matrix products: 22.6 us -> 8.19 us  [right_product(): lax.dot_general(left, right, (((1,), (1,)), ((), ())), preferred_element_...]
    slice x3 -> x13, local copies, waits for them, and re-layouts: 1 us -> 9.99 us  [the longest x2 2.77 us: ctx_reduction(): sent = add_low(*[part[half:] for part in parts])]
    ppermute x61 -> x57, starting transfers between devices: 57.2 us -> 65.4 us  [swap(): return lax.ppermute(values, axis, [(i, i ^ bit) for i in range(count)])]
    convert_element_type x28 -> x21, other arithmetic: 20.3 us -> 12.5 us  [to_low(): return values.astype(jnp.bfloat16)]
    pallas_call x3 -> x2, Pallas kernels: 22.4 us -> 16.4 us  [wide_products(): pl.pallas_call(functools.partial(products_kernel, tiles, rows, chunks), g...]
  transfers between devices with their start and end apart: 61 -> 57, of which waited for: 27 -> 20; matrix products, arithmetic and copies ran while one was open for 16% -> 14% of each run, Pallas kernels for 15% -> 24%
where the time goes in v3:
time: 332 us; the launch traced here: 331 us
  waiting for transfers between devices  117 us (35%)
  Pallas kernels  89.5 us (27%)
  starting transfers between devices  65.4 us (20%)
  other arithmetic  26.8 us (8%)
  local copies, waits for them, and re-layouts  22.2 us (7%)
  matrix products  8.19 us (2%)
    ppermute x57, waiting for transfers between devices, swap(): return lax.ppermute(values, axis, [(i, i ^ bit) for i in range(count)])  117 us
    ppermute x57, starting transfers between devices, swap(): return lax.ppermute(values, axis, [(i, i ^ bit) for i in range(count)])  65.4 us
    pallas_call x6, Pallas kernels, chain_call(): pl.pallas_call(kernel, grid_spec=pltpu.PrefetchScalarGridSpec(num_scalar_...  53.8 us
    pallas_call x2, Pallas kernels, wide_products(): pl.pallas_call(functools.partial(products_kernel, tiles, rows, chunks), g...  16.4 us
    convert_element_type x21, other arithmetic, to_low(): return values.astype(jnp.bfloat16)  12.5 us
    pallas_call x1, Pallas kernels, self_backward(): pl.pallas_call(functools.partial(self_backward_kernel, head_size, blocks)...  10.2 us
    unnamed x109, local copies, waits for them, and re-layouts  9.84 us
    dot_general x5, matrix products, right_product(): lax.dot_general(left, right, (((1,), (1,)), ((), ())), preferred_element_...  8.19 us
  transfers between devices with their start and end apart: 57, of which 20 were waited for; matrix products, arithmetic and copies ran while one was open for 14% of the time, Pallas kernels for 24%

profile of v3, /device:TPU:0, one launch (start us, length us, event | category | flops | bytes accessed | tf_op | source)
XLA Modules:
  0.0 331.1 jit_solution(12651651992353092984)
XLA Ops:
  2.8 5.1 %collective-permute-start.2 = (bf16[128,768]{1,0:T(8,128)(2,1)S(1)}, bf16[128,768]{1,0:T(8,128)(2,1)S(1)}, u32[]{:S(2)}, u32[]{:S(2)}) collective-permute-start(bf16[128,768]{1,0:T(8,128)(2,1)S(1)} %bitcast.57), channel_id=1, source_target_pairs={{0,24},{4,28},{8,16},{12,20},{16,8},{20,12},{24,0},{28,4},{1,25},{... | collective-permute-start | bytes 589832 | tf_op jit(solution)/shard_map/ppermute | solution.py:661
  8.5 1.6 collective-permute-start.3
  12.3 1.7 positions.1
  14.0 4.1 %collective-permute-done.1 = bf16[128,768]{1,0:T(8,128)(2,1)S(1)} collective-permute-done((bf16[128,768]{1,0:T(8,128)(2,1)S(1)}, bf16[128,768]{1,0:T(8,128)(2,1)S(1)}, u32[]{:S(2)}, u32[]{:S(2)}) %collective-permute-start.1) | collective-permute-done | bytes 196640 | tf_op jit(solution)/shard_map/ppermute | solution.py:661
  18.1 6.5 %collective-permute-done = bf16[128,768]{1,0:T(8,128)(2,1)S(1)} collective-permute-done((bf16[128,768]{1,0:T(8,128)(2,1)S(1)}, bf16[128,768]{1,0:T(8,128)(2,1)S(1)}, u32[]{:S(2)}, u32[]{:S(2)}) %collective-permute-start) | collective-permute-done | bytes 196640 | tf_op jit(solution)/shard_map/ppermute | solution.py:661
  24.7 6.9 %collective-permute-done.6.refs_6_ = bf16[192,2432]{1,0:T(8,128)(2,1)S(1)} collective-permute-done((bf16[192,2432]{1,0:T(8,128)(2,1)S(1)}, bf16[192,2432]{1,0:T(8,128)(2,1)S(1)}, u32[]{:S(2)}, u32[]{:S(2)}) %collective-permute-start.6) | collective-permute-done | bytes 933920 | tf_op jit(solution)/shard_map/ppermute | solution.py:661
  36.0 11.4 %collective-permute-done.4.refs_3_ = bf16[384,768]{1,0:T(8,128)(2,1)S(1)} collective-permute-done((bf16[384,768]{1,0:T(8,128)(2,1)S(1)}, bf16[384,768]{1,0:T(8,128)(2,1)S(1)}, u32[]{:S(2)}, u32[]{:S(2)}) %collective-permute-start.4) | collective-permute-done | bytes 589856 | tf_op jit(solution)/shard_map/ppermute | solution.py:661
  49.1 9.6 %project.1 = (bf16[128,768]{1,0:T(8,128)(2,1)}, bf16[1024,1536]{1,0:T(8,128)(2,1)}, bf16[1024,768]{1,0:T(8,128)(2,1)}, bf16[768,2304]{1,0:T(8,128)(2,1)}, f32[8,768]{1,0:T(8,128)}) custom-call(s32[3]{0:T(128)} %pad_add_fusion.index_ref, bf16[128,768]{1,0:T(8,128)(2,1)} %bitcast.55, bf16[384,768]{1,0:T(8,128)(2,1)} %copy-done.19, ...), custom_call_target="tpu_custom_call" | custom-call | flops 110399995904 | bytes 9600000 | tf_op jit(solution)/shard_map/project/pallas_call | solution.py:261
  59.3 7.5 %self_forward.1 = (bf16[128,768]{1,0:T(8,128)(2,1)}, f32[6,1,256]{2,1,0:T(1,128)}) custom-call(bf16[128,768]{1,0:T(8,128)(2,1)} %get-tuple-element.115.q_ref, bf16[1024,1536]{1,0:T(8,128)(2,1)} %get-tuple-element.116.k_ref.v_ref, bf16[1024,1536]{1,0:T(8,128)(2,1)} %get-tuple-element.116.k_ref.v_ref, s32[1024,1]{1,0:T(8,128)} %get-tuple-element.110.pos_ref, ...), custom_call_target="tpu_custom_call" | custom-call | flops 87399997440 | bytes 7600000 | tf_op jit(solution)/shard_map/self_forward/pallas_call | solution.py:202
  68.0 4.4 %attend_out.1 = (f32[128,768]{1,0:T(8,128)}, bf16[128,768]{1,0:T(8,128)(2,1)}, bf16[128,768]{1,0:T(8,128)(2,1)}, bf16[768,1536]{1,0:T(8,128)(2,1)}) custom-call(s32[3]{0:T(128)} %pad_add_fusion.index_ref, bf16[128,768]{1,0:T(8,128)(2,1)} %get-tuple-element.119.att_ref.refs_7_, bf16[128,768]{1,0:T(8,128)(2,1)} %bitcast.56, ...), custom_call_target="tpu_custom_call" | custom-call | flops 50600001536 | bytes 4400000 | tf_op jit(solution)/shard_map/attend_out/pallas_call | solution.py:261
  76.3 12.2 %cross_forward.1 = (bf16[2,512,768]{2,1,0:T(8,128)(2,1)}, bf16[128,768]{1,0:T(8,128)(2,1)}, f32[128,768]{1,0:T(8,128)}, bf16[128,768]{1,0:T(8,128)(2,1)}, bf16[2...) custom-call(s32[3]{0:T(128)} %pad_add_fusion.index_ref, bf16[128,768]{1,0:T(8,128)(2,1)} %get-tuple-element.124.refs_0_, ...), custom_call_target="tpu_custom_call" | custom-call | flops 141450002432 | bytes 12300000 | tf_op jit(solution)/shard_map/cross_forward/pallas_call | solution.py:261
  88.5 4.8 %collective-permute-done.18.refs_10_ = bf16[512,768]{1,0:T(8,128)(2,1)S(1)} collective-permute-done((bf16[512,768]{1,0:T(8,128)(2,1)S(1)}, bf16[512,768]{1,0:T(8,128)(2,1)S(1)}, u32[]{:S(2)}, u32[]{:S(2)}) %collective-permute-start.18) | collective-permute-done | bytes 786464 | tf_op jit(solution)/shard_map/ppermute | solution.py:661
  95.2 5.8 %collective-permute-done.15.refs_2_ = bf16[128,768]{1,0:T(8,128)(2,1)S(1)} collective-permute-done((bf16[128,768]{1,0:T(8,128)(2,1)}, bf16[128,768]{1,0:T(8,128)(2,1)S(1)}, u32[]{:S(2)}, u32[]{:S(2)}) %collective-permute-start.15) | collective-permute-done | bytes 196640 | tf_op jit(solution)/shard_map/ppermute | solution.py:661
  104.0 10.1 %mlp_share.1 = (f32[128,768]{1,0:T(8,128)}, f32[128,768]{1,0:T(8,128)}, bf16[2,128,768]{2,1,0:T(8,128)(2,1)}, f32[128,768]{1,0:T(8,128)}, f32[128,768]{1,0:T(8,1...) custom-call(s32[3]{0:T(128)} %pad_add_fusion.index_ref, ...), custom_call_target="tpu_custom_call" | custom-call | flops 160999997440 | bytes 14000000 | tf_op jit(solution)/shard_map/mlp_share/pallas_call | solution.py:261
  115.4 1.6 slice.289.refs_0_
  118.4 1.9 slice.292
  123.3 4.9 %collective-permute-done.21.refs_5_ = bf16[128,768]{1,0:T(8,128)(2,1)S(1)} collective-permute-done((bf16[128,768]{1,0:T(8,128)(2,1)S(1)}, bf16[128,768]{1,0:T(8,128)(2,1)S(1)}, u32[]{:S(2)}, u32[]{:S(2)}) %collective-permute-start.21) | collective-permute-done | bytes 196640 | tf_op jit(solution)/shard_map/ppermute | solution.py:661
  129.0 12.4 %cross_backward.1 = (bf16[128,768]{1,0:T(8,128)(2,1)}, bf16[2,512,768]{2,1,0:T(8,128)(2,1)}, f32[128,768]{1,0:T(8,128)}, bf16[128,768]{1,0:T(8,128)(2,1)}, bf16[...) custom-call(s32[3]{0:T(128)} %pad_add_fusion.index_ref, bf16[128,768]{1,0:T(8,128)(2,1)} %get-tuple-element.124.refs_0_, ...), custom_call_target="tpu_custom_call" | custom-call | flops 149500002304 | bytes 13000000 | tf_op jit(solution)/shard_map/cross_backward/pallas_call | solution.py:261
  141.4 2.0 add_convert_fusion.12
  144.8 8.3 %wide_products.2 = (bf16[384,3840]{1,0:T(8,128)(2,1)}, bf16[384,3840]{1,0:T(8,128)(2,1)}) custom-call(s32[3]{0:T(128)} %pad_add_fusion.index_ref, bf16[128,768]{1,0:T(8,128)(2,1)} %get-tuple-element.145.refs_0_, bf16[128,768]{1,0:T(8,128)(2,1)} %get-tuple-element.146.refs_1_, bf16[128,768]{1,0:T(8,128)(2,1)} %get-tuple-element.147.refs_2_, ...), custom_call_target="tpu_custom_call" | custom-call | flops 94299996160 | bytes 8199999 | tf_op jit(solution)/shard_map/wide_products/pallas_call | solution.py:778
  155.9 10.2 %self_backward.1 = (bf16[128,768]{1,0:T(8,128)(2,1)}, bf16[2,1024,768]{2,1,0:T(8,128)(2,1)}) custom-call(bf16[128,768]{1,0:T(8,128)(2,1)} %get-tuple-element.115.q_ref, bf16[1024,1536]{1,0:T(8,128)(2,1)} %get-tuple-element.116.k_ref.v_ref, bf16[1024,1536]{1,0:T(8,128)(2,1)} %get-tuple-element.116.k_ref.v_ref, bf16[128,768]{1,0:T(8,128)(2,1)} %get-tuple-element.154.do_ref, ...), custom_call_target="tpu_custom_call" | custom-call | flops 117300002816 | bytes 10200000 | tf_op jit(solution)/shard_map/self_backward/pallas_call | solution.py:223
  166.1 1.6 add_convert_fusion.25
  167.7 2.6 collective-permute-start.32
  174.8 2.9 add_convert_fusion
  179.0 8.0 %wide_products.3 = (bf16[384,2304]{1,0:T(8,128)(2,1)}, bf16[384,2304]{1,0:T(8,128)(2,1)}) custom-call(s32[3]{0:T(128)} %pad_add_fusion.index_ref, bf16[128,768]{1,0:T(8,128)(2,1)} %slice.289.refs_0_, bf16[128,768]{1,0:T(8,128)(2,1)} %get-tuple-element.194.refs_1_, bf16[1024,768]{1,0:T(8,128)(2,1)} %get-tuple-element.137.refs_2_, ...), custom_call_target="tpu_custom_call" | custom-call | flops 94299996160 | bytes 8199999 | tf_op jit(solution)/shard_map/wide_products/pallas_call | solution.py:778
  187.0 3.3 %fusion.1 = f32[1024,768]{1,0:T(8,128)S(1)} fusion(bf16[2,1024,768]{2,1,0:T(8,128)(2,1)} %get-tuple-element.164.refs_3_.refs_4_, bf16[768,2304]{1,0:T(8,128)(2,1)} %get-tuple-element.165), kind=kOutput, calls=%fused_computation.6 | convolution fusion | flops 1207959552 | bytes 5898240 | tf_op jit(solution)/shard_map/dot_general | solution.py:38
  194.3 2.0 convolution_add_fusion.1
  196.9 15.0 %collective-permute-done.28 = bf16[192,3840]{1,0:T(8,128)(2,1)} collective-permute-done((bf16[192,3840]{1,0:T(8,128)(2,1)}, bf16[192,3840]{1,0:T(8,128)(2,1)}, u32[]{:S(2)}, u32[]{:S(2)}) %collective-permute-start.28) | collective-permute-done | bytes 1474592 | tf_op jit(solution)/shard_map/ppermute | solution.py:661
  212.9 2.3 add_convert_fusion.3
  219.7 2.2 collective-permute-start.37
  222.2 8.5 %collective-permute-done.38 = bf16[48,3072]{1,0:T(8,128)(2,1)S(1)} collective-permute-done((bf16[48,3072]{1,0:T(8,128)(2,1)S(1)}, bf16[48,3072]{1,0:T(8,128)(2,1)S(1)}, u32[]{:S(2)}, u32[]{:S(2)}) %collective-permute-start.38) | collective-permute-done | bytes 294944 | tf_op jit(solution)/shard_map/ppermute | solution.py:661
  230.7 3.4 %collective-permute-start.41 = (bf16[24,3072]{1,0:T(8,128)(2,1)S(1)}, bf16[24,3072]{1,0:T(8,128)(2,1)S(1)}, u32[]{:S(2)}, u32[]{:S(2)}) collective-permute-start(bf16[24,3072]{1,0:T(8,128)(2,1)S(1)} %add_convert_fusion.22), channel_id=1, source_target_pairs={{0,16},{4,20},{8,24},{12,28},{16,0},{20,4},{24,8},{28,12},{1,17},{... | collective-permute-start | bytes 442376 | tf_op jit(solution)/shard_map/ppermute | solution.py:661
  234.1 10.2 %collective-permute-done.36 = bf16[256,768]{1,0:T(8,128)(2,1)S(1)} collective-permute-done((bf16[256,768]{1,0:T(8,128)(2,1)S(1)}, bf16[256,768]{1,0:T(8,128)(2,1)S(1)}, u32[]{:S(2)}, u32[]{:S(2)}) %collective-permute-start.36) | collective-permute-done | bytes 393248 | tf_op jit(solution)/shard_map/ppermute | solution.py:661
  244.5 4.2 %collective-permute-start.39 = (bf16[128,768]{1,0:T(8,128)(2,1)S(1)}, bf16[128,768]{1,0:T(8,128)(2,1)S(1)}, u32[]{:S(2)}, u32[]{:S(2)}) collective-permute-start(bf16[128,768]{1,0:T(8,128)(2,1)S(1)} %slice.386), channel_id=1, source_target_pairs={{0,16},{4,20},{8,24},{12,28},{16,0},{20,4},{24,8},{28,12},{1,17},{... | collective-permute-start | bytes 589832 | tf_op jit(solution)/shard_map/ppermute | solution.py:661
  249.3 1.7 collective-permute-start.43
  251.1 5.0 %collective-permute-done.40 = bf16[192,768]{1,0:T(8,128)(2,1)S(1)} collective-permute-done((bf16[192,768]{1,0:T(8,128)(2,1)S(1)}, bf16[192,768]{1,0:T(8,128)(2,1)S(1)}, u32[]{:S(2)}, u32[]{:S(2)}) %collective-permute-start.40) | collective-permute-done | bytes 294944 | tf_op jit(solution)/shard_map/ppermute | solution.py:661
  257.9 5.6 %collective-permute-done.44 = bf16[48,3840]{1,0:T(8,128)(2,1)S(1)} collective-permute-done((bf16[48,3840]{1,0:T(8,128)(2,1)S(1)}, bf16[48,3840]{1,0:T(8,128)(2,1)S(1)}, u32[]{:S(2)}, u32[]{:S(2)}) %collective-permute-start.44) | collective-permute-done | bytes 368672 | tf_op jit(solution)/shard_map/ppermute | solution.py:661
  263.6 2.1 collective-permute-start.46
  266.6 6.4 %collective-permute-done.46 = bf16[24,3840]{1,0:T(8,128)(2,1)S(1)} collective-permute-done((bf16[24,3840]{1,0:T(8,128)(2,1)S(1)}, bf16[24,3840]{1,0:T(8,128)(2,1)S(1)}, u32[]{:S(2)}, u32[]{:S(2)}) %collective-permute-start.46) | collective-permute-done | bytes 184352 | tf_op jit(solution)/shard_map/ppermute | solution.py:661
  273.4 5.6 %collective-permute-start.45 = (bf16[48,2304]{1,0:T(8,128)(2,1)S(1)}, bf16[48,2304]{1,0:T(8,128)(2,1)S(1)}, u32[]{:S(2)}, u32[]{:S(2)}) collective-permute-start(bf16[48,2304]{1,0:T(8,128)(2,1)S(1)} %get-tuple-element.240), channel_id=1, source_target_pairs={{0,8},{4,12},{8,0},{12,4},{16,24},{20,28},{24,16},{28,20},{1,9},{5... | collective-permute-start | bytes 663560 | tf_op jit(solution)/shard_map/ppermute | solution.py:661
  282.5 3.6 %collective-permute-done.45 = bf16[48,2304]{1,0:T(8,128)(2,1)S(1)} collective-permute-done((bf16[48,2304]{1,0:T(8,128)(2,1)S(1)}, bf16[48,2304]{1,0:T(8,128)(2,1)S(1)}, u32[]{:S(2)}, u32[]{:S(2)}) %collective-permute-start.45) | collective-permute-done | bytes 221216 | tf_op jit(solution)/shard_map/ppermute | solution.py:661
  286.1 2.9 collective-permute-start.47
  292.5 3.4 %collective-permute-start.50 = (bf16[24,2304]{1,0:T(8,128)(2,1)S(1)}, bf16[24,2304]{1,0:T(8,128)(2,1)S(1)}, u32[]{:S(2)}, u32[]{:S(2)}) collective-permute-start(bf16[24,2304]{1,0:T(8,128)(2,1)S(1)} %add_convert_fusion.26), channel_id=1, source_target_pairs={{0,16},{4,20},{8,24},{12,28},{16,0},{20,4},{24,8},{28,12},{1,17},{... | collective-permute-start | bytes 331784 | tf_op jit(solution)/shard_map/ppermute | solution.py:661
  297.5 1.9 collective-permute-start.56
  299.4 3.0 collective-permute-done.51
  304.0 8.2 %collective-permute-done.56.far_ref = bf16[96,3072]{1,0:T(8,128)(2,1)S(1)} collective-permute-done((bf16[96,3072]{1,0:T(8,128)(2,1)S(1)}, bf16[96,3072]{1,0:T(8,128)(2,1)S(1)}, u32[]{:S(2)}, u32[]{:S(2)}) %collective-permute-start.56) | collective-permute-done | bytes 589856 | tf_op jit(solution)/shard_map/ppermute | solution.py:661
  313.0 5.1 %inner_out.1 = (f32[192,3072]{1,0:T(8,128)}, f32[192,1]{1,0:T(8,128)}) custom-call(s32[3]{0:T(128)} %pad_add_fusion.index_ref, bf16[96,3072]{1,0:T(8,128)(2,1)} %copy-done.20, bf16[96,3072]{1,0:T(8,128)(2,1)} %copy-done.42, bf16[192,3072]{1,0:T(8,128)(2,1)} %weight_ref.1, f32[192,1]{1,0:T(8,128)} %copy.30.gain_ref), custom_call_target="tpu_custom_call" | custom-call | flops 34500001792 | bytes 3000000 | tf_op jit(solution)/shard_map/inner_out/pallas_call | solution.py:261
  325.0 3.9 %collective-permute-done.55 = bf16[96,2304]{1,0:T(8,128)(2,1)S(1)} collective-permute-done((bf16[96,2304]{1,0:T(8,128)(2,1)S(1)}, bf16[96,2304]{1,0:T(8,128)(2,1)S(1)}, u32[]{:S(2)}, u32[]{:S(2)}) %collective-permute-start.55) | collective-permute-done | bytes 442400 | tf_op jit(solution)/shard_map/ppermute | solution.py:661
  (268 shorter events, 71.6 us)
Async XLA Ops:
  2.8 11.2 %collective-permute-start.2 = (bf16[128,768]{1,0:T(8,128)(2,1)S(1)}, bf16[128,768]{1,0:T(8,128)(2,1)S(1)}, u32[]{:S(2)}, u32[]{:S(2)}) collective-permute-start(bf16[128,768]{1,0:T(8,128)(2,1)S(1)} %bitcast.57), channel_id=1, source_target_pairs={{0,24},{4,28},{8,16},{12,20},{16,8},{20,12},{24,0},{28,4},{1,25},{... | collective-permute-start | bytes 589832 | tf_op jit(solution)/shard_map/ppermute | solution.py:661
  7.9 10.2 %collective-permute-start.1 = (bf16[128,768]{1,0:T(8,128)(2,1)S(1)}, bf16[128,768]{1,0:T(8,128)(2,1)S(1)}, u32[]{:S(2)}, u32[]{:S(2)}) collective-permute-start(bf16[128,768]{1,0:T(8,128)(2,1)S(1)} %bitcast.58), channel_id=1, source_target_pairs={{0,8},{4,12},{8,0},{12,4},{16,24},{20,28},{24,16},{28,20},{1,9},{5... | collective-permute-start | bytes 589832 | tf_op jit(solution)/shard_map/ppermute | solution.py:661
  7.9 16.7 %collective-permute-start = (bf16[128,768]{1,0:T(8,128)(2,1)S(1)}, bf16[128,768]{1,0:T(8,128)(2,1)S(1)}, u32[]{:S(2)}, u32[]{:S(2)}) collective-permute-start(bf16[128,768]{1,0:T(8,128)(2,1)S(1)} %bitcast.59), channel_id=1, source_target_pairs={{0,16},{4,20},{8,24},{12,28},{16,0},{20,4},{24,8},{28,12},{1,17},{... | collective-permute-start | bytes 589832 | tf_op jit(solution)/shard_map/ppermute | solution.py:661
  8.5 16.1 %collective-permute-start.3 = (bf16[128,768]{1,0:T(8,128)(2,1)S(1)}, bf16[128,768]{1,0:T(8,128)(2,1)}, u32[]{:S(2)}, u32[]{:S(2)}) collective-permute-start(bf16[128,768]{1,0:T(8,128)(2,1)S(1)} %bitcast.60), channel_id=1, source_target_pairs={{0,4},{4,0},{8,12},{12,8},{16,20},{20,16},{24,28},{28,24},{1,5},{5... | collective-permute-start | bytes 589832 | tf_op jit(solution)/shard_map/ppermute | solution.py:661
  10.2 21.5 %collective-permute-start.6 = (bf16[192,2432]{1,0:T(8,128)(2,1)S(1)}, bf16[192,2432]{1,0:T(8,128)(2,1)S(1)}, u32[]{:S(2)}, u32[]{:S(2)}) collective-permute-start(bf16[192,2432]{1,0:T(8,128)(2,1)S(1)} %fusion.14.refs_4_), channel_id=1, source_target_pairs={{0,2},{1,3},{2,0},{3,1},{4,6},{5,7},{6,4},{7,5},{8,10},{9,11},{10,... | collective-permute-start | bytes 2801672 | tf_op jit(solution)/shard_map/ppermute | solution.py:661
  24.7 22.7 %collective-permute-start.5 = (bf16[192,2432]{1,0:T(8,128)(2,1)S(1)}, bf16[192,2432]{1,0:T(8,128)(2,1)S(1)}, u32[]{:S(2)}, u32[]{:S(2)}) collective-permute-start(bf16[192,2432]{1,0:T(8,128)(2,1)S(1)} %fusion.14.refs_4_), channel_id=1, source_target_pairs={{0,1},{1,0},{2,3},{3,2},{4,5},{5,4},{6,7},{7,6},{8,9},{9,8},{10,11... | collective-permute-start | bytes 2801672 | tf_op jit(solution)/shard_map/ppermute | solution.py:661
  31.6 17.5 %collective-permute-start.7 = (bf16[192,2432]{1,0:T(8,128)(2,1)S(1)}, bf16[192,2432]{1,0:T(8,128)(2,1)}, u32[]{:S(2)}, u32[]{:S(2)}) collective-permute-start(bf16[192,2432]{1,0:T(8,128)(2,1)S(1)} %collective-permute-done.6.refs_6_), channel_id=1, source_target_pairs={{0,1},{1,0},{2,3},{3,2},{4,5},{5,4},{6,7},{7,6},{8,9},{9,8},{10,11... | collective-permute-start | bytes 2801672 | tf_op jit(solution)/shard_map/ppermute | solution.py:661
  31.6 15.7 %collective-permute-start.4 = (bf16[384,768]{1,0:T(8,128)(2,1)S(1)}, bf16[384,768]{1,0:T(8,128)(2,1)S(1)}, u32[]{:S(2)}, u32[]{:S(2)}) collective-permute-start(bf16[384,768]{1,0:T(8,128)(2,1)S(1)} %pad_maximum_fusion.3.refs_1_), channel_id=1, source_target_pairs={{0,4},{4,0},{8,12},{12,8},{16,20},{20,16},{24,28},{28,24},{1,5},{5... | collective-permute-start | bytes 1769480 | tf_op jit(solution)/shard_map/ppermute | solution.py:661
  34.0 24.9 %collective-permute-start.9 = (bf16[192,1536]{1,0:T(8,128)(2,1)S(1)}, bf16[192,1536]{1,0:T(8,128)(2,1)}, u32[]{:S(2)}, u32[]{:S(2)}) collective-permute-start(bf16[192,1536]{1,0:T(8,128)(2,1)S(1)} %constant_dynamic-update-slice_fusion.refs_0_), channel_id=1, source_target_pairs={{0,2},{1,3},{2,0},{3,1},{4,6},{5,7},{6,4},{7,5},{8,10},{9,11},{10,... | collective-permute-start | bytes 1769480 | tf_op jit(solution)/shard_map/ppermute | solution.py:661
  35.5 36.8 %collective-permute-start.12 = (bf16[192,2304]{1,0:T(8,128)(2,1)}, bf16[192,2304]{1,0:T(8,128)(2,1)}, u32[]{:S(2)}, u32[]{:S(2)}) collective-permute-start(bf16[192,2304]{1,0:T(8,128)(2,1)} %constant_dynamic-update-slice_fusion.2.refs_5_.refs_9_.refs_13_), channel_id=1, source_target_pairs={{0,2},{1,3},{2,0},{3,1},{4,6},{5,7},{6,4},{7,5},{8,10},{9,11},{10,... | collective-permute-start | bytes 2654216 | tf_op jit(solution)/shard_map/ppermute | solution.py:661
  66.9 8.5 %collective-permute-start.11 = (bf16[192,2304]{1,0:T(8,128)(2,1)}, bf16[192,2304]{1,0:T(8,128)(2,1)S(1)}, u32[]{:S(2)}, u32[]{:S(2)}) collective-permute-start(bf16[192,2304]{1,0:T(8,128)(2,1)} %constant_dynamic-update-slice_fusion.2.refs_5_.refs_9_.refs_13_), channel_id=1, source_target_pairs={{0,1},{1,0},{2,3},{3,2},{4,5},{5,4},{6,7},{7,6},{8,9},{9,8},{10,11... | collective-permute-start | bytes 2654216 | tf_op jit(solution)/shard_map/ppermute | solution.py:661
  73.8 19.6 %collective-permute-start.18 = (bf16[512,768]{1,0:T(8,128)(2,1)S(1)}, bf16[512,768]{1,0:T(8,128)(2,1)S(1)}, u32[]{:S(2)}, u32[]{:S(2)}) collective-permute-start(bf16[512,768]{1,0:T(8,128)(2,1)S(1)} %pad_maximum_fusion.2), channel_id=1, source_target_pairs={{0,2},{1,3},{2,0},{3,1},{4,6},{5,7},{6,4},{7,5},{8,10},{9,11},{10,... | collective-permute-start | bytes 2359304 | tf_op jit(solution)/shard_map/ppermute | solution.py:661
  75.4 25.7 %collective-permute-start.17 = (bf16[320,768]{1,0:T(8,128)(2,1)S(1)}, bf16[320,768]{1,0:T(8,128)(2,1)S(1)}, u32[]{:S(2)}, u32[]{:S(2)}) collective-permute-start(bf16[320,768]{1,0:T(8,128)(2,1)S(1)} %pad_maximum_fusion.7), channel_id=1, source_target_pairs={{0,1},{1,0},{2,3},{3,2},{4,5},{5,4},{6,7},{7,6},{8,9},{9,8},{10,11... | collective-permute-start | bytes 1474568 | tf_op jit(solution)/shard_map/ppermute | solution.py:661
  93.4 9.1 %collective-permute-start.19 = (bf16[320,768]{1,0:T(8,128)(2,1)S(1)}, bf16[320,768]{1,0:T(8,128)(2,1)S(1)}, u32[]{:S(2)}, u32[]{:S(2)}) collective-permute-start(bf16[320,768]{1,0:T(8,128)(2,1)S(1)} %slice.287), channel_id=1, source_target_pairs={{0,1},{1,0},{2,3},{3,2},{4,5},{5,4},{6,7},{7,6},{8,9},{9,8},{10,11... | collective-permute-start | bytes 1474568 | tf_op jit(solution)/shard_map/ppermute | solution.py:661
  120.3 21.1 %collective-permute-start.22 = (bf16[384,768]{1,0:T(8,128)(2,1)}, bf16[384,768]{1,0:T(8,128)(2,1)}, u32[]{:S(2)}, u32[]{:S(2)}) collective-permute-start(bf16[384,768]{1,0:T(8,128)(2,1)} %slice.292), channel_id=1, source_target_pairs={{0,4},{4,0},{8,12},{12,8},{16,20},{20,16},{24,28},{28,24},{1,5},{5... | collective-permute-start | bytes 1769480 | tf_op jit(solution)/shard_map/ppermute | solution.py:661
  120.8 32.3 %collective-permute-start.33 = (bf16[384,768]{1,0:T(8,128)(2,1)}, bf16[384,768]{1,0:T(8,128)(2,1)}, u32[]{:S(2)}, u32[]{:S(2)}) collective-permute-start(bf16[384,768]{1,0:T(8,128)(2,1)} %get-tuple-element.174), channel_id=1, source_target_pairs={{0,1},{1,0},{2,3},{3,2},{4,5},{5,4},{6,7},{7,6},{8,9},{9,8},{10,11... | collective-permute-start | bytes 1769480 | tf_op jit(solution)/shard_map/ppermute | solution.py:661
  143.4 22.7 %collective-permute-start.24 = (bf16[192,768]{1,0:T(8,128)(2,1)}, bf16[192,768]{1,0:T(8,128)(2,1)}, u32[]{:S(2)}, u32[]{:S(2)}) collective-permute-start(bf16[192,768]{1,0:T(8,128)(2,1)} %get-tuple-element.220), channel_id=1, source_target_pairs={{0,8},{4,12},{8,0},{12,4},{16,24},{20,28},{24,16},{28,20},{1,9},{5... | collective-permute-start | bytes 884744 | tf_op jit(solution)/shard_map/ppermute | solution.py:661
  153.1 21.7 %collective-permute-start.23 = (bf16[384,3840]{1,0:T(8,128)(2,1)}, bf16[384,3840]{1,0:T(8,128)(2,1)}, u32[]{:S(2)}, u32[]{:S(2)}) collective-permute-start(bf16[384,3840]{1,0:T(8,128)(2,1)} %get-tuple-element.157), channel_id=1, source_target_pairs={{0,1},{1,0},{2,3},{3,2},{4,5},{5,4},{6,7},{7,6},{8,9},{9,8},{10,11... | collective-permute-start | bytes 8847368 | tf_op jit(solution)/shard_map/ppermute | solution.py:661
  154.3 16.1 %collective-permute-start.34 = (bf16[192,1536]{1,0:T(8,128)(2,1)S(1)}, bf16[192,1536]{1,0:T(8,128)(2,1)S(1)}, u32[]{:S(2)}, u32[]{:S(2)}) collective-permute-start(bf16[192,1536]{1,0:T(8,128)(2,1)S(1)} %pad_maximum_fusion.4), channel_id=1, source_target_pairs={{0,2},{1,3},{2,0},{3,1},{4,6},{5,7},{6,4},{7,5},{8,10},{9,11},{10,... | collective-permute-start | bytes 1769480 | tf_op jit(solution)/shard_map/ppermute | solution.py:661
  167.7 50.6 %collective-permute-start.32 = (bf16[96,768]{1,0:T(8,128)(2,1)}, bf16[96,768]{1,0:T(8,128)(2,1)}, u32[]{:S(2)}, u32[]{:S(2)}) collective-permute-start(bf16[96,768]{1,0:T(8,128)(2,1)} %add_convert_fusion.25), channel_id=1, source_target_pairs={{0,16},{4,20},{8,24},{12,28},{16,0},{20,4},{24,8},{28,12},{1,17},{... | collective-permute-start | bytes 442376 | tf_op jit(solution)/shard_map/ppermute | solution.py:661
  173.3 42.7 %collective-permute-start.35 = (bf16[96,3072]{1,0:T(8,128)(2,1)}, bf16[96,3072]{1,0:T(8,128)(2,1)}, u32[]{:S(2)}, u32[]{:S(2)}) collective-permute-start(bf16[96,3072]{1,0:T(8,128)(2,1)} %slice.382), channel_id=1, source_target_pairs={{0,4},{4,0},{8,12},{12,8},{16,20},{20,16},{24,28},{28,24},{1,5},{5... | collective-permute-start | bytes 1769480 | tf_op jit(solution)/shard_map/ppermute | solution.py:661
  177.7 34.2 %collective-permute-start.28 = (bf16[192,3840]{1,0:T(8,128)(2,1)}, bf16[192,3840]{1,0:T(8,128)(2,1)}, u32[]{:S(2)}, u32[]{:S(2)}) collective-permute-start(bf16[192,3840]{1,0:T(8,128)(2,1)} %add_convert_fusion), channel_id=1, source_target_pairs={{0,2},{1,3},{2,0},{3,1},{4,6},{5,7},{6,4},{7,5},{8,10},{9,11},{10,... | collective-permute-start | bytes 4423688 | tf_op jit(solution)/shard_map/ppermute | solution.py:661
  187.0 9.3 %collective-permute-start.25 = (bf16[2,128,768]{2,1,0:T(8,128)(2,1)}, bf16[2,128,768]{2,1,0:T(8,128)(2,1)S(1)}, u32[]{:S(2)}, u32[]{:S(2)}) collective-permute-start(bf16[2,128,768]{2,1,0:T(8,128)(2,1)} %get-tuple-element.163), channel_id=1, source_target_pairs={{0,1},{1,0},{2,3},{3,2},{4,5},{5,4},{6,7},{7,6},{8,9},{9,8},{10,11... | collective-permute-start | bytes 1179656 | tf_op jit(solution)/shard_map/ppermute | solution.py:661
  192.3 23.0 %collective-permute-start.27 = (bf16[384,2304]{1,0:T(8,128)(2,1)S(1)}, bf16[384,2304]{1,0:T(8,128)(2,1)S(1)}, u32[]{:S(2)}, u32[]{:S(2)}) collective-permute-start(bf16[384,2304]{1,0:T(8,128)(2,1)S(1)} %copy-done.38), channel_id=1, source_target_pairs={{0,1},{1,0},{2,3},{3,2},{4,5},{5,4},{6,7},{7,6},{8,9},{9,8},{10,11... | collective-permute-start | bytes 5308424 | tf_op jit(solution)/shard_map/ppermute | solution.py:661
  196.3 23.4 %collective-permute-start.31 = (bf16[512,768]{1,0:T(8,128)(2,1)S(1)}, bf16[512,768]{1,0:T(8,128)(2,1)S(1)}, u32[]{:S(2)}, u32[]{:S(2)}) collective-permute-start(bf16[512,768]{1,0:T(8,128)(2,1)S(1)} %slice.380), channel_id=1, source_target_pairs={{0,4},{4,0},{8,12},{12,8},{16,20},{20,16},{24,28},{28,24},{1,5},{5... | collective-permute-start | bytes 2359304 | tf_op jit(solution)/shard_map/ppermute | solution.py:661
  211.9 44.4 %collective-permute-start.26 = (bf16[128,768]{1,0:T(8,128)(2,1)S(1)}, bf16[128,768]{1,0:T(8,128)(2,1)S(1)}, u32[]{:S(2)}, u32[]{:S(2)}) collective-permute-start(bf16[128,768]{1,0:T(8,128)(2,1)S(1)} %fusion.25), channel_id=1, source_target_pairs={{0,2},{1,3},{2,0},{3,1},{4,6},{5,7},{6,4},{7,5},{8,10},{9,11},{10,... | collective-permute-start | bytes 589832 | tf_op jit(solution)/shard_map/ppermute | solution.py:661
  215.3 29.2 %collective-permute-start.30 = (bf16[96,3840]{1,0:T(8,128)(2,1)S(1)}, bf16[96,3840]{1,0:T(8,128)(2,1)S(1)}, u32[]{:S(2)}, u32[]{:S(2)}) collective-permute-start(bf16[96,3840]{1,0:T(8,128)(2,1)S(1)} %get-tuple-element.214), channel_id=1, source_target_pairs={{0,4},{4,0},{8,12},{12,8},{16,20},{20,16},{24,28},{28,24},{1,5},{5... | collective-permute-start | bytes 2211848 | tf_op jit(solution)/shard_map/ppermute | solution.py:661
  216.1 32.8 %collective-permute-start.29 = (bf16[192,2304]{1,0:T(8,128)(2,1)S(1)}, bf16[192,2304]{1,0:T(8,128)(2,1)S(1)}, u32[]{:S(2)}, u32[]{:S(2)}) collective-permute-start(bf16[192,2304]{1,0:T(8,128)(2,1)S(1)} %add_convert_fusion.1), channel_id=1, source_target_pairs={{0,2},{1,3},{2,0},{3,1},{4,6},{5,7},{6,4},{7,5},{8,10},{9,11},{10,... | collective-permute-start | bytes 2654216 | tf_op jit(solution)/shard_map/ppermute | solution.py:661
  218.3 12.3 %collective-permute-start.38 = (bf16[48,3072]{1,0:T(8,128)(2,1)S(1)}, bf16[48,3072]{1,0:T(8,128)(2,1)S(1)}, u32[]{:S(2)}, u32[]{:S(2)}) collective-permute-start(bf16[48,3072]{1,0:T(8,128)(2,1)S(1)} %get-tuple-element.218), channel_id=1, source_target_pairs={{0,8},{4,12},{8,0},{12,4},{16,24},{20,28},{24,16},{28,20},{1,9},{5... | collective-permute-start | bytes 884744 | tf_op jit(solution)/shard_map/ppermute | solution.py:661
  219.7 11.0 %collective-permute-start.37 = (bf16[96,768]{1,0:T(8,128)(2,1)S(1)}, bf16[96,768]{1,0:T(8,128)(2,1)S(1)}, u32[]{:S(2)}, u32[]{:S(2)}) collective-permute-start(bf16[96,768]{1,0:T(8,128)(2,1)S(1)} %add_convert_fusion.23), channel_id=1, source_target_pairs={{0,16},{4,20},{8,24},{12,28},{16,0},{20,4},{24,8},{28,12},{1,17},{... | collective-permute-start | bytes 442376 | tf_op jit(solution)/shard_map/ppermute | solution.py:661
  230.7 13.7 %collective-permute-start.36 = (bf16[256,768]{1,0:T(8,128)(2,1)S(1)}, bf16[256,768]{1,0:T(8,128)(2,1)S(1)}, u32[]{:S(2)}, u32[]{:S(2)}) collective-permute-start(bf16[256,768]{1,0:T(8,128)(2,1)S(1)} %slice.384), channel_id=1, source_target_pairs={{0,8},{4,12},{8,0},{12,4},{16,24},{20,28},{24,16},{28,20},{1,9},{5... | collective-permute-start | bytes 1179656 | tf_op jit(solution)/shard_map/ppermute | solution.py:661
  230.7 18.6 %collective-permute-start.41 = (bf16[24,3072]{1,0:T(8,128)(2,1)S(1)}, bf16[24,3072]{1,0:T(8,128)(2,1)S(1)}, u32[]{:S(2)}, u32[]{:S(2)}) collective-permute-start(bf16[24,3072]{1,0:T(8,128)(2,1)S(1)} %add_convert_fusion.22), channel_id=1, source_target_pairs={{0,16},{4,20},{8,24},{12,28},{16,0},{20,4},{24,8},{28,12},{1,17},{... | collective-permute-start | bytes 442376 | tf_op jit(solution)/shard_map/ppermute | solution.py:661
  244.3 11.8 %collective-permute-start.40 = (bf16[192,768]{1,0:T(8,128)(2,1)S(1)}, bf16[192,768]{1,0:T(8,128)(2,1)S(1)}, u32[]{:S(2)}, u32[]{:S(2)}) collective-permute-start(bf16[192,768]{1,0:T(8,128)(2,1)S(1)} %pad_maximum_fusion.10), channel_id=1, source_target_pairs={{0,8},{4,12},{8,0},{12,4},{16,24},{20,28},{24,16},{28,20},{1,9},{5... | collective-permute-start | bytes 884744 | tf_op jit(solution)/shard_map/ppermute | solution.py:661
  244.5 13.4 %collective-permute-start.39 = (bf16[128,768]{1,0:T(8,128)(2,1)S(1)}, bf16[128,768]{1,0:T(8,128)(2,1)S(1)}, u32[]{:S(2)}, u32[]{:S(2)}) collective-permute-start(bf16[128,768]{1,0:T(8,128)(2,1)S(1)} %slice.386), channel_id=1, source_target_pairs={{0,16},{4,20},{8,24},{12,28},{16,0},{20,4},{24,8},{28,12},{1,17},{... | collective-permute-start | bytes 589832 | tf_op jit(solution)/shard_map/ppermute | solution.py:661
  248.9 14.7 %collective-permute-start.44 = (bf16[48,3840]{1,0:T(8,128)(2,1)S(1)}, bf16[48,3840]{1,0:T(8,128)(2,1)S(1)}, u32[]{:S(2)}, u32[]{:S(2)}) collective-permute-start(bf16[48,3840]{1,0:T(8,128)(2,1)S(1)} %get-tuple-element.230), channel_id=1, source_target_pairs={{0,8},{4,12},{8,0},{12,4},{16,24},{20,28},{24,16},{28,20},{1,9},{5... | collective-permute-start | bytes 1105928 | tf_op jit(solution)/shard_map/ppermute | solution.py:661
  249.3 23.9 %collective-permute-start.43 = (bf16[96,2304]{1,0:T(8,128)(2,1)S(1)}, bf16[96,2304]{1,0:T(8,128)(2,1)S(1)}, u32[]{:S(2)}, u32[]{:S(2)}) collective-permute-start(bf16[96,2304]{1,0:T(8,128)(2,1)S(1)} %get-tuple-element.216), channel_id=1, source_target_pairs={{0,4},{4,0},{8,12},{12,8},{16,20},{20,16},{24,28},{28,24},{1,5},{5... | collective-permute-start | bytes 1327112 | tf_op jit(solution)/shard_map/ppermute | solution.py:661
  256.1 32.9 %collective-permute-start.49 = (bf16[24,3072]{1,0:T(8,128)(2,1)S(1)}, bf16[24,3072]{1,0:T(8,128)(2,1)S(1)}, u32[]{:S(2)}, u32[]{:S(2)}) collective-permute-start(bf16[24,3072]{1,0:T(8,128)(2,1)S(1)} %add_convert_fusion.20), channel_id=1, source_target_pairs={{0,16},{4,20},{8,24},{12,28},{16,0},{20,4},{24,8},{28,12},{1,17},{... | collective-permute-start | bytes 442376 | tf_op jit(solution)/shard_map/ppermute | solution.py:661
  256.4 22.7 %collective-permute-start.42 = (bf16[384,768]{1,0:T(8,128)(2,1)S(1)}, bf16[384,768]{1,0:T(8,128)(2,1)S(1)}, u32[]{:S(2)}, u32[]{:S(2)}) collective-permute-start(bf16[384,768]{1,0:T(8,128)(2,1)S(1)} %pad_maximum_fusion.5), channel_id=1, source_target_pairs={{0,4},{4,0},{8,12},{12,8},{16,20},{20,16},{24,28},{28,24},{1,5},{5... | collective-permute-start | bytes 1769480 | tf_op jit(solution)/shard_map/ppermute | solution.py:661
  263.6 9.4 %collective-permute-start.46 = (bf16[24,3840]{1,0:T(8,128)(2,1)S(1)}, bf16[24,3840]{1,0:T(8,128)(2,1)S(1)}, u32[]{:S(2)}, u32[]{:S(2)}) collective-permute-start(bf16[24,3840]{1,0:T(8,128)(2,1)S(1)} %add_convert_fusion.19), channel_id=1, source_target_pairs={{0,16},{4,20},{8,24},{12,28},{16,0},{20,4},{24,8},{28,12},{1,17},{... | collective-permute-start | bytes 552968 | tf_op jit(solution)/shard_map/ppermute | solution.py:661
  273.1 17.4 %collective-permute-start.48 = (bf16[24,3840]{1,0:T(8,128)(2,1)S(1)}, bf16[24,3840]{1,0:T(8,128)(2,1)S(1)}, u32[]{:S(2)}, u32[]{:S(2)}) collective-permute-start(bf16[24,3840]{1,0:T(8,128)(2,1)S(1)} %add_convert_fusion.17), channel_id=1, source_target_pairs={{0,16},{4,20},{8,24},{12,28},{16,0},{20,4},{24,8},{28,12},{1,17},{... | collective-permute-start | bytes 552968 | tf_op jit(solution)/shard_map/ppermute | solution.py:661
  273.4 12.6 %collective-permute-start.45 = (bf16[48,2304]{1,0:T(8,128)(2,1)S(1)}, bf16[48,2304]{1,0:T(8,128)(2,1)S(1)}, u32[]{:S(2)}, u32[]{:S(2)}) collective-permute-start(bf16[48,2304]{1,0:T(8,128)(2,1)S(1)} %get-tuple-element.240), channel_id=1, source_target_pairs={{0,8},{4,12},{8,0},{12,4},{16,24},{20,28},{24,16},{28,20},{1,9},{5... | collective-permute-start | bytes 663560 | tf_op jit(solution)/shard_map/ppermute | solution.py:661
  289.1 8.3 %collective-permute-start.52 = (bf16[48,3072]{1,0:T(8,128)(2,1)S(1)}, bf16[48,3072]{1,0:T(8,128)(2,1)S(1)}, u32[]{:S(2)}, u32[]{:S(2)}) collective-permute-start(bf16[48,3072]{1,0:T(8,128)(2,1)S(1)} %pad_maximum_fusion.11), channel_id=1, source_target_pairs={{0,8},{4,12},{8,0},{12,4},{16,24},{20,28},{24,16},{28,20},{1,9},{5... | collective-permute-start | bytes 884744 | tf_op jit(solution)/shard_map/ppermute | solution.py:661
  290.6 11.8 %collective-permute-start.51 = (bf16[48,3840]{1,0:T(8,128)(2,1)S(1)}, bf16[48,3840]{1,0:T(8,128)(2,1)S(1)}, u32[]{:S(2)}, u32[]{:S(2)}) collective-permute-start(bf16[48,3840]{1,0:T(8,128)(2,1)S(1)} %pad_maximum_fusion.9), channel_id=1, source_target_pairs={{0,8},{4,12},{8,0},{12,4},{16,24},{20,28},{24,16},{28,20},{1,9},{5... | collective-permute-start | bytes 1105928 | tf_op jit(solution)/shard_map/ppermute | solution.py:661
  292.5 10.9 %collective-permute-start.50 = (bf16[24,2304]{1,0:T(8,128)(2,1)S(1)}, bf16[24,2304]{1,0:T(8,128)(2,1)S(1)}, u32[]{:S(2)}, u32[]{:S(2)}) collective-permute-start(bf16[24,2304]{1,0:T(8,128)(2,1)S(1)} %add_convert_fusion.26), channel_id=1, source_target_pairs={{0,16},{4,20},{8,24},{12,28},{16,0},{20,4},{24,8},{28,12},{1,17},{... | collective-permute-start | bytes 331784 | tf_op jit(solution)/shard_map/ppermute | solution.py:661
  297.5 14.7 %collective-permute-start.56 = (bf16[96,3072]{1,0:T(8,128)(2,1)S(1)}, bf16[96,3072]{1,0:T(8,128)(2,1)S(1)}, u32[]{:S(2)}, u32[]{:S(2)}) collective-permute-start(bf16[96,3072]{1,0:T(8,128)(2,1)S(1)} %pad_maximum_fusion.6.own_ref), channel_id=1, source_target_pairs={{0,4},{4,0},{8,12},{12,8},{16,20},{20,16},{24,28},{28,24},{1,5},{5... | collective-permute-start | bytes 1769480 | tf_op jit(solution)/shard_map/ppermute | solution.py:661
  302.6 17.4 %collective-permute-start.54 = (bf16[96,3840]{1,0:T(8,128)(2,1)S(1)}, bf16[96,3840]{1,0:T(8,128)(2,1)S(1)}, u32[]{:S(2)}, u32[]{:S(2)}) collective-permute-start(bf16[96,3840]{1,0:T(8,128)(2,1)S(1)} %pad_maximum_fusion.1), channel_id=1, source_target_pairs={{0,4},{4,0},{8,12},{12,8},{16,20},{20,16},{24,28},{28,24},{1,5},{5... | collective-permute-start | bytes 2211848 | tf_op jit(solution)/shard_map/ppermute | solution.py:661
  303.4 16.9 %collective-permute-start.53 = (bf16[48,2304]{1,0:T(8,128)(2,1)S(1)}, bf16[48,2304]{1,0:T(8,128)(2,1)S(1)}, u32[]{:S(2)}, u32[]{:S(2)}) collective-permute-start(bf16[48,2304]{1,0:T(8,128)(2,1)S(1)} %pad_maximum_fusion.12), channel_id=1, source_target_pairs={{0,8},{4,12},{8,0},{12,4},{16,24},{20,28},{24,16},{28,20},{1,9},{5... | collective-permute-start | bytes 663560 | tf_op jit(solution)/shard_map/ppermute | solution.py:661
  320.5 8.4 %collective-permute-start.55 = (bf16[96,2304]{1,0:T(8,128)(2,1)S(1)}, bf16[96,2304]{1,0:T(8,128)(2,1)S(1)}, u32[]{:S(2)}, u32[]{:S(2)}) collective-permute-start(bf16[96,2304]{1,0:T(8,128)(2,1)S(1)} %pad_maximum_fusion.8), channel_id=1, source_target_pairs={{0,4},{4,0},{8,12},{12,8},{16,20},{20,16},{24,28},{28,24},{1,5},{5... | collective-permute-start | bytes 1327112 | tf_op jit(solution)/shard_map/ppermute | solution.py:661
  (62 other events, 442.6 us)

commit v4 on v3

--- a/solution.py
+++ b/solution.py
@@ -278,25 +278,45 @@
     return pl.BlockSpec(shape, lambda *_: zeros)
 
 
-def project_kernel(layout, tok, pieces, index_ref, *refs):
-    row_refs, refs = refs[: len(layout)], refs[len(layout) :]
-    piece_refs, refs = refs[:pieces], refs[pieces:]
-    q_ref, kv_ref, norm_ref, w_ref, gain_ref, rows_ref, column_ref = refs
+def rows_kernel(layout, *refs):
+    row_refs, (rows_ref, scale_ref) = refs[: len(layout)], refs[len(layout) :]
+    for row_ref, places in zip(row_refs, layout):
+        count = row_ref.shape[0] // len(places)
+        for k, place in enumerate(places):
+            rows = row_ref[pl.ds(k * count, count), :]
+            rows_ref[pl.ds(place, count), :] = rows
+            scale_ref[pl.ds(place, count), :] = inverse_rms(rows.astype(jnp.float32))
+
+
+def held_rows(row_pieces, layout):
+    total = sum(piece.shape[0] for piece in row_pieces)
+    width = row_pieces[0].shape[1]
+    return pl.pallas_call(
+        functools.partial(rows_kernel, layout),
+        out_shape=[
+            jax.ShapeDtypeStruct((total, width), jnp.bfloat16),
+            jax.ShapeDtypeStruct((total, 1), jnp.float32),
+        ],
+        cost_estimate=lasting(2.0),
+        name="held_rows",
+    )(*row_pieces)
+
+
+def project_kernel(tok, pieces, index_ref, rows_ref, scale_ref, *refs):
+    piece_refs, (q_ref, kv_ref, norm_ref, w_ref, gain_ref, column_ref) = (
+        refs[:pieces],
+        refs[pieces:],
+    )
     width = q_ref.shape[1]
     step = pl.program_id(0)
 
     @pl.when(step == 0)
     def _():
-        for row_ref, moves in zip(row_refs, layout):
-            for start, place, count in moves:
-                rows_ref[pl.ds(place, count), :] = row_ref[pl.ds(start, count), :]
         fill(w_ref, piece_refs, index_ref, slice(0, 3 * width))
         fill(column_ref, piece_refs, index_ref, slice(3 * width, 3 * width + 128))
         gain_ref[...] = column_ref[...].T[: gain_ref.shape[0], :]
 
-    count = norm_ref.shape[0]
-    values = rows_ref[pl.ds(pl.multiple_of(step * count, count), count), :].astype(jnp.float32)
-    norm = to_low(values * inverse_rms(values) * gain_ref[0:1, :])
+    norm = to_low(rows_ref[...].astype(jnp.float32) * scale_ref[...] * gain_ref[0:1, :])
     norm_ref[...] = norm
     kv_ref[...] = to_low(matmul(norm, w_ref[:, width:]))
 
@@ -305,28 +325,78 @@
         q_ref[...] = to_low(matmul(norm_ref[pl.ds(0, tok), :], w_ref[:, :width]))
 
 
-def project(index, row_pieces, layout, pieces, tok):
-    width = row_pieces[0].shape[1]
-    total = sum(piece.shape[0] for piece in row_pieces)
+def project(index, rows, scale, pieces, tok):
+    total, width = rows.shape
     block = min(512, total)
-    inputs = [(value, whole(value)) for value in (*row_pieces, *pieces)]
+
+    def rows_of(columns):
+        return pl.BlockSpec((block, columns), lambda i, _: (i, 0))
+
+    inputs = [(rows, rows_of(width)), (scale, rows_of(1))]
+    inputs += [(value, whole(value)) for value in pieces]
     outputs = [
         ((tok, width), jnp.bfloat16, const((tok, width))),
-        ((total, 2 * width), jnp.bfloat16, pl.BlockSpec((block, 2 * width), lambda i, _: (i, 0))),
-        ((total, width), jnp.bfloat16, pl.BlockSpec((block, width), lambda i, _: (i, 0))),
+        ((total, 2 * width), jnp.bfloat16, rows_of(2 * width)),
+        ((total, width), jnp.bfloat16, rows_of(width)),
         ((width, 3 * width), jnp.bfloat16, const((width, 3 * width))),
         ((8, width), jnp.float32, const((8, width))),
     ]
-    scratch = [pltpu.VMEM((total, width), jnp.bfloat16), pltpu.VMEM((width, 128), jnp.float32)]
     return chain_call(
-        functools.partial(project_kernel, layout, tok, len(pieces)),
+        functools.partial(project_kernel, tok, len(pieces)),
         "project",
         (total // block,),
         index,
         inputs,
         outputs,
-        scratch,
-        9.6,
+        [pltpu.VMEM((width, 128), jnp.float32)],
+        9.0,
+    )
+
+
+def enc_terms_kernel(index_ref, pair_ref, w_ref, out_ref):
+    out_ref[...] = right_product(pair_ref[0], w_ref[0]) + right_product(pair_ref[1], w_ref[1])
+
+
+def enc_terms(index, grad_pair, w_pair):
+    _, total, width = grad_pair.shape
+    block = min(256, total)
+    inputs = [
+        (grad_pair, pl.BlockSpec((2, block, width), lambda i, _: (0, i, 0))),
+        (w_pair, whole(w_pair)),
+    ]
+    outputs = [((total, width), jnp.float32, pl.BlockSpec((block, width), lambda i, _: (i, 0)))]
+    return chain_call(
+        enc_terms_kernel, "enc_terms", (total // block,), index, inputs, outputs, [], 4.0
+    )[0]
+
+
+def norm_terms_kernel(index_ref, pair_ref, query_ref, w_ref, out_ref, own_ref):
+    width = out_ref.shape[1]
+    out_ref[...] = to_low(
+        right_product(pair_ref[0], w_ref[:, width : 2 * width])
+        + right_product(pair_ref[1], w_ref[:, 2 * width :])
+    )
+
+    @pl.when(pl.program_id(0) == 0)
+    def _():
+        own_ref[...] = right_product(query_ref[...], w_ref[:, :width])
+
+
+def norm_terms(index, grad_pair, grad_query, w_qkv):
+    _, total, width = grad_pair.shape
+    tok = grad_query.shape[0]
+    block = min(512, total)
+    inputs = [
+        (grad_pair, pl.BlockSpec((2, block, width), lambda i, _: (0, i, 0))),
+        (grad_query, whole(grad_query)),
+        (w_qkv, whole(w_qkv)),
+    ]
+    outputs = [
+        ((total, width), jnp.bfloat16, pl.BlockSpec((block, width), lambda i, _: (i, 0))),
+        ((tok, width), jnp.float32, const((tok, width))),
+    ]
+    return chain_call(
+        norm_terms_kernel, "norm_terms", (total // block,), index, inputs, outputs, [], 0.01
     )
 
 
@@ -456,15 +526,21 @@
 
 
 def mlp_kernel(tok, chunks, index_ref, *refs):
-    norms, cots, pieces, (down_ref,) = refs[:4], refs[4:8], refs[8:12], refs[12:13]
-    (
-        grad_own_ref, grad_across_ref, grad_send_ref, out_own_ref, out_across_ref, out_send_ref,
-        down_share_ref, keep_ref, send_ref, w_ref, held_ref, norm_all, cot_all, act_all, inner_all,
-    ) = refs[13:]
-    fill(w_ref, pieces, index_ref)
+    norms, cot_ref, block_ref, exchanged, down_ref = refs[:4], refs[4], refs[5], refs[6:9], refs[9]
+    grad_refs, out_own_ref, out_across_ref, out_send_ref = refs[10:14], refs[14], refs[15], refs[16]
+    down_share_ref, keep_ref, send_ref, w_ref, held_ref, norm_all, cot_all, act_all, inner_all = refs[
+        17:
+    ]
+    rows_in = block_ref.shape[0]
+    starts = (0, 0, rows_in)
+    blocks = [ref.at[pl.ds(start, rows_in), :] for ref, start in zip(exchanged, starts)]
+    fill(w_ref, [block_ref, *blocks], index_ref)
+    cot_all[pl.ds(0, tok), :] = cot_ref[...]
+    for k, ref in enumerate(exchanged):
+        start = ref.shape[0] - tok
+        cot_all[pl.ds((k + 1) * tok, tok), :] = ref[pl.ds(start, tok), :]
     for k in range(4):
         norm_all[pl.ds(k * tok, tok), :] = norms[k][...]
-        cot_all[pl.ds(k * tok, tok), :] = cots[k][...]
     for k in range(2):
         rows = pl.ds(2 * k * tok, 2 * tok)
         inner = matmul(norm_all[rows, :], w_ref[...])
@@ -476,15 +552,13 @@
         inner_all[rows, :] = grad_inner
         grad = right_product(grad_inner, w_ref[...])
         out = matmul(activation, down_ref[...])
-        for own_ref, across_ref, send_refs, value in (
-            (grad_own_ref, grad_across_ref, grad_send_ref, grad),
-            (out_own_ref, out_across_ref, out_send_ref, out),
-        ):
-            if k == 0:
-                own_ref[...] = value[:tok]
-            else:
-                across_ref[...] = value[:tok]
-            send_refs[k] = to_low(value[tok:])
+        grad_refs[2 * k][...] = grad[:tok].astype(grad_refs[2 * k].dtype)
+        grad_refs[2 * k + 1][...] = to_low(grad[tok:])
+        if k == 0:
+            out_own_ref[...] = out[:tok]
+        else:
+            out_across_ref[...] = out[:tok]
+        out_send_ref[k] = to_low(out[tok:])
     depth = down_ref.shape[0]
     held_ref[...] = left_product(act_all[...], cot_all[...])
     store_chunks(down_share_ref, 0, held_ref, 0, depth, index_ref[2], chunks[1])
@@ -497,18 +571,16 @@
             )
 
 
-def mlp_share(index, norms, cots, pieces, w_down):
+def mlp_share(index, norms, cot, block_own, exchanged, w_down):
     depth, width = w_down.shape
-    tok = norms[0][2]
+    tok = cot.shape[0]
     chunks = (chunk_count(width // len(WHOLE)), chunk_count(depth))
-    inputs = []
-    for value, start, count in (*norms, *cots, *pieces):
-        inputs.append((value, pl.BlockSpec((count, depth), lambda *_, s=start // count: (s, 0))))
-    inputs.append((w_down, whole(w_down)))
+    inputs = [(value, whole(value)) for value in (*norms, cot, block_own, *exchanged, w_down)]
     token_f32 = ((tok, width), jnp.float32, const((tok, width)))
+    token_low = ((tok, width), jnp.bfloat16, const((tok, width)))
     token_send = ((2, tok, width), jnp.bfloat16, const((2, tok, width)))
     rows = ((width // 2, depth), jnp.bfloat16, const((width // 2, depth)))
-    outputs = [token_f32, token_f32, token_send, token_f32, token_f32, token_send]
+    outputs = [token_f32, token_low, token_low, token_low, token_f32, token_f32, token_send]
     outputs += [((depth, width), jnp.bfloat16, const((depth, width))), rows, rows]
     scratch = [pltpu.VMEM((width, depth), jnp.bfloat16), pltpu.VMEM((depth, depth), jnp.float32)]
     scratch += [pltpu.VMEM((4 * tok, depth), jnp.bfloat16)] * 4
@@ -520,7 +592,7 @@
         inputs,
         outputs,
         scratch,
-        14.0,
+        11.0,
     )
 
 
@@ -562,9 +634,9 @@
 
 
 def cross_backward_kernel(head_size, stretches, index_ref, *refs):
-    q_ref, kv_ref, cot_ref, part0, part1, part2, cross_ref, wout_ref, keep_ref = refs[:9]
-    w_ref, rows_ref, gain_ref = refs[9:12]
-    dq_ref, dkv_ref, out_ref, branch_ref, attended_ref, first_ref, grad_ref, do_ref = refs[12:]
+    q_ref, kv_ref, cot_ref, cross_ref, wout_ref, keep_ref, w_ref, rows_ref, gain_ref = refs[:9]
+    terms = refs[9:13]
+    dq_ref, dkv_ref, out_ref, branch_ref, attended_ref, first_ref, grad_ref, do_ref = refs[13:]
     score_scale = head_size ** (-0.5)
     pair = pl.program_id(0)
     wide = q_ref.shape[1]
@@ -574,9 +646,7 @@
     @pl.when(pair == 0)
     def _():
         values = cross_ref[...]
-        grad_norm = (
-            part0[...] + part1[...].astype(jnp.float32) + part2[...].astype(jnp.float32)
-        )
+        grad_norm = sum(term[...].astype(jnp.float32) for term in terms)
         grad = cot_ref[...].astype(jnp.float32) + rms_back(
             values, inverse_rms(values), gain_ref[2:3, :], grad_norm
         )
@@ -625,15 +695,9 @@
     block = pl.BlockSpec((tok, 128), lambda i, _: (0, i))
     planes = pl.BlockSpec((2, keys, 128), lambda i, _: (0, 0, i))
     inputs = [(query, block), (key_value, planes), (cotangent, whole(cotangent))]
-    own, sibling, across = terms
-    inputs += [
-        (own, whole(own)),
-        (sibling, pl.BlockSpec((None, tok, width), lambda *_: (0, 0, 0))),
-        (across, whole(across)),
-    ]
     inputs += [
         (value, whole(value))
-        for value in (after_cross, w_cout, keep_rows, w_pair, after_attn, gain_rows)
+        for value in (after_cross, w_cout, keep_rows, w_pair, after_attn, gain_rows, *terms)
     ]
     low = ((tok, width), jnp.bfloat16, const((tok, width)))
     outputs = [
@@ -751,14 +815,15 @@
             )
 
 
-def wide_products(index, terms):
+def wide_products(index, terms, microseconds):
     shares = lax.axis_size("fsdp")
     inputs, tiles = [], []
     width = terms[0][0].shape[1]
     for left, right, plane in terms:
-        if not inputs or all(left is not value for value, _ in inputs):
-            inputs.append((left, None))
-        first = next(i for i, (value, _) in enumerate(inputs) if value is left)
+        count = right.shape[-2]
+        if not any(left is value and count == held for value, held in inputs):
+            inputs.append((left, count))
+        first = next(i for i, (v, held) in enumerate(inputs) if v is left and held == count)
         inputs.append((right, plane))
         for column in range(right.shape[-1] // width):
             tiles.append((first, len(inputs) - 1, column))
@@ -767,7 +832,7 @@
     specs = []
     for value, plane in inputs:
         if value.ndim == 2:
-            specs.append(pl.BlockSpec(value.shape, lambda i, _: (0, 0)))
+            specs.append(pl.BlockSpec((plane or value.shape[0], value.shape[1]), lambda i, _: (0, 0)))
         else:
             specs.append(
                 pl.BlockSpec((None,) + value.shape[1:], lambda i, _, plane=plane: (plane, 0, 0))
@@ -785,7 +850,7 @@
             scratch_shapes=[pltpu.VMEM((width, width), jnp.float32)],
         ),
         out_shape=[out, out],
-        cost_estimate=lasting(8.2),
+        cost_estimate=lasting(microseconds),
         name="wide_products",
     )(index, *[value for value, _ in inputs])
 
@@ -796,11 +861,11 @@
 
 def reduction(keep, send):
     rows = keep.shape[0] // 2
-    token = yield send
-    received = after(swap(send, "fsdp", 1), *token)
+    received = swap(send, "fsdp", 1)
+    received = yield send, received
     sent = add_low(keep[rows:], received[rows:])
-    token = yield sent
-    across = after(swap(sent, "fsdp", 2), *token)
+    across = swap(sent, "fsdp", 2)
+    across = yield sent, across
     return (yield from ctx_reduction((keep[:rows], received[:rows], across)))
 
 
@@ -822,17 +887,18 @@
     while bit < chunks:
         sent = add_low(*[part[half:] for part in parts])
         held = add_low(*[part[:half] for part in parts])
-        token = yield sent
-        parts = (held, after(swap(sent, "ctx", bit), *token))
+        far = swap(sent, "ctx", bit)
+        parts = (held, (yield sent, far))
         half, bit = half // 2, 2 * bit
     gathered = add_low(*parts)
-    token = yield gathered
     while bit > 2:
         bit = bit // 2
-        far = after(swap(gathered, "ctx", bit), *token)
+        far = swap(gathered, "ctx", bit)
+        far = yield gathered, far
         gathered = in_order(index, bit, gathered, far)
-        token = yield gathered
-    return gathered, after(swap(gathered, "ctx", 1), *token)
+    far = swap(gathered, "ctx", 1)
+    far = yield gathered, far
+    return gathered, far
 
 
 def finished(halves, offset, width):
@@ -840,14 +906,14 @@
     return in_order(lax.axis_index("ctx"), 1, own, far).astype(jnp.float32)
 
 
-def sum_to_owner(rows_sum):
-    total = to_low(rows_sum)
+def sum_to_owner(total):
     bit = 1
     while bit < lax.axis_size("ctx"):
         half = total.shape[0] // 2
         sent = total[half:]
-        token = yield sent
-        total = add_low(total[:half], after(swap(sent, "ctx", bit), *token))
+        far = swap(sent, "ctx", bit)
+        far = yield sent, far
+        total = add_low(total[:half], far)
         bit = 2 * bit
     return total
 
@@ -858,15 +924,22 @@
         self.result = None
         self.advance(None)
 
-    def advance(self, token):
+    def advance(self, arrived):
         try:
-            return self.steps.send(token)
+            sent, self.arriving = self.steps.send(arrived)
+            return sent
         except StopIteration as stop:
             self.result = stop.value
             return stop.value[1] if isinstance(stop.value, tuple) else stop.value
 
+    def hold(self, *token):
+        if self.result is not None:
+            return token[0]
+        self.arriving = after(self.arriving, *token)
+        return self.arriving
+
     def move(self, *token):
-        return token[0] if self.result is not None else self.advance(token)
+        return token[0] if self.result is not None else self.advance(self.hold(*token))
 
     def finish(self, *token):
         sent = token[0]
@@ -917,14 +990,14 @@
     first_share = jnp.concatenate(
         [attn_qkv, jnp.pad(norm_gains.T, ((0, 0), (0, 128 - norm_gains.shape[0])))], axis=1
     )
-    own = after(own, first_share)
     across_qkv = swap(first_share, "fsdp", 2)
     if ctx_count == 8:
         far, last, near = swap(own, "ctx", 4), swap(own, "ctx", 6), swap(own, "ctx", 2)
         beside = swap(own, "ctx", 1)
-        second = after(jnp.concatenate([far, near, last], axis=0), key_pos)
-        row_pieces = [own, second, beside, swap(second, "ctx", 1)]
-        layout = [((0, k * tok, piece.shape[0]),) for k, piece in zip((0, 1, 4, 5), row_pieces)]
+        beside_near = swap(near, "ctx", 1)
+        second = after(jnp.concatenate([far, last], axis=0), near)
+        row_pieces = [own, near, second, beside, beside_near, swap(second, "ctx", 1)]
+        layout = [[k * tok for k in ks] for ks in ((0,), (2,), (1, 3), (4,), (6,), (5, 7))]
         second = after(second, beside)
     else:
         first = own
@@ -933,7 +1006,7 @@
             bit = bit // 2
             first = jnp.concatenate([first, swap(first, "ctx", bit)], axis=0)
         row_pieces = [first, swap(first, "ctx", 1)]
-        layout = [((0, k * first.shape[0], first.shape[0]),) for k in range(2)]
+        layout = [[k * first.shape[0]] for k in range(2)]
         second = first
     sibling_qkv = swap(after(first_share, second), "fsdp", 1)
     across_qkv = after(across_qkv, second)
@@ -941,7 +1014,7 @@
     pair_share = jnp.concatenate([attn_out, cross_q], axis=1)
     across_pair = swap(after(pair_share, second), "fsdp", 2)
     cross_share = jnp.concatenate([cross_kv, cross_out], axis=1)
-    across_cross = swap(after(cross_share, across_qkv), "fsdp", 2)
+    across_cross = swap(after(cross_share, second), "fsdp", 2)
     depth = mlp_out.shape[0]
     rows_in = mlp_in.shape[0]
 
@@ -952,8 +1025,13 @@
     exchange_sibling = jnp.concatenate([block_of(1), cot], axis=0)
     exchange_across = jnp.concatenate([block_of(2), block_of(3), cot], axis=0)
 
+    rows_all, scale_all = held_rows(row_pieces, layout)
     query, key_value, norm_all, w_qkv, gain_rows = project(
-        place, row_pieces, layout, [first_share, sibling_qkv, across_qkv, diagonal_qkv], tok
+        place,
+        rows_all,
+        scale_all,
+        [first_share, sibling_qkv, across_qkv, after(diagonal_qkv, scale_all)],
+        tok,
     )
     across_pair = after(across_pair, query)
     diagonal_pair = swap(across_pair, "fsdp", 1)
@@ -961,10 +1039,10 @@
     from_across = swap(after(exchange_across, across_pair), "fsdp", 2)
     attended, log_total = self_forward(query, key_value, key_pos, low_pos, high_pos)
     sibling_cross = swap(after(cross_share, attended), "fsdp", 1)
+    across_cross = after(across_cross, attended)
     after_attn, norm_two, cross_query, w_pair = attend_out(
         place, attended, own, gain_rows, [pair_share, sibling_pair, across_pair, diagonal_pair]
     )
-    across_cross = after(across_cross, cross_query)
     diagonal_cross = swap(across_cross, "fsdp", 1)
     cross_key_value, cross_rows, after_cross, norm_three, w_ckv, w_cout = cross_forward(
         place,
@@ -979,31 +1057,31 @@
     from_sibling = swap(after(exchange_sibling, cross_query), "fsdp", 1)
     norm_across, norm_sibling = swap(norm_three, "fsdp", 2), swap(norm_three, "fsdp", 1)
     from_across = after(from_across, norm_three)
-    from_diagonal = swap(from_across[rows_in:], "fsdp", 1)
+    from_diagonal = swap(from_across, "fsdp", 1)
     norm_diagonal = swap(norm_across, "fsdp", 1)
-    cot_across = from_across[2 * rows_in :]
     (
-        grad_own, grad_across, grad_send, out_own, out_across, out_send, share_down, keep_in, send_in,
+        grad_own, grad_sibling, grad_across, grad_diagonal, out_own, out_across, out_send, share_down,
+        keep_in, send_in,
     ) = mlp_share(
         place,
-        [(value, 0, tok) for value in (norm_three, norm_sibling, norm_across, norm_diagonal)],
-        [
-            (value, 0, tok)
-            for value in (cot, from_sibling[rows_in:], cot_across, from_diagonal[rows_in:])
-        ],
-        [
-            (block_own, 0, rows_in),
-            (from_sibling, 0, rows_in),
-            (from_across, 0, rows_in),
-            (from_diagonal, 0, rows_in),
-        ],
+        [norm_three, norm_sibling, norm_across, norm_diagonal],
+        cot,
+        block_own,
+        [from_sibling, from_across, from_diagonal],
         mlp_out,
     )
 
-    from_sibling = swap(grad_send, "fsdp", 1)
-    grad_far = swap(add_low(grad_across, from_sibling[1]), "fsdp", 2)
+    terms = (
+        grad_own,
+        swap(grad_sibling, "fsdp", 1),
+        swap(grad_across, "fsdp", 2),
+        swap(grad_diagonal, "fsdp", 3),
+    )
+    received_in = swap(send_in, "fsdp", 1)
+    across_in = swap(
+        jnp.concatenate([keep_in[rows_in:], received_in[rows_in:]], axis=1), "fsdp", 2
+    )
     down = Steps(ctx_reduction((share_down,)))
-    received_in = swap(send_in, "fsdp", 1)
     (
         grad_cross_query, grad_cross_pair, grad_after_attn, grad_attn_branch, grad_attended,
         grad_cross_branch,
@@ -1012,7 +1090,7 @@
         cross_query,
         cross_key_value,
         cot,
-        (grad_own, from_sibling, grad_far),
+        terms,
         after_cross,
         w_cout,
         keep_rows,
@@ -1021,88 +1099,79 @@
         gain_rows,
         stretch_count,
     )
-    received_in = after(received_in, grad_cross_query)
-    across_in = swap(
-        jnp.concatenate([keep_in[rows_in:], received_in[rows_in:]], axis=1), "fsdp", 2
-    )
-    ready = down.move(grad_cross_query)
+    across_in = after(across_in, grad_attended)
+    arrived = down.hold(grad_attended)
     keep_cross, send_cross = wide_products(
         place,
         [
             (cross_rows, grad_cross_branch, None),
             (norm_two, grad_cross_query, None),
-            (enc_rows, grad_cross_pair, 0),
+            (enc_rows, after(grad_cross_pair, across_in, arrived), 0),
             (enc_rows, grad_cross_pair, 1),
             (attended, grad_attn_branch, None),
         ],
+        8.2,
     )
     cross = Steps(reduction(keep_cross, send_cross))
+    ready = down.move(keep_cross)
+    share_in = jnp.concatenate(
+        [keep_in[:rows_in], received_in[:rows_in], after(across_in, ready)], axis=1
+    )
+    inner = Steps(ctx_reduction((share_in,)))
+    ready = cross.move(share_in)
     grad_query, grad_pair = self_backward(
         query,
         key_value,
-        after(grad_attended, keep_cross, ready),
+        after(grad_attended, ready),
         key_pos,
         low_pos,
         high_pos,
         log_total,
     )
-    across_in = after(across_in, grad_query)
-    inner = Steps(
-        ctx_reduction(
-            (jnp.concatenate([keep_in[:rows_in], received_in[:rows_in], across_in], axis=1),)
-        )
-    )
-    ready = cross.move(down.move(grad_query))
+    ready = inner.move(down.move(grad_query))
     keep_attn, send_attn = wide_products(
         place,
         [
-            (norm_all[:tok], after(grad_query, ready), None),
+            (norm_all, after(grad_query, ready), None),
             (norm_all, grad_pair, 0),
             (norm_all, grad_pair, 1),
         ],
+        0.01,
     )
     attn = Steps(reduction(keep_attn, send_attn))
-    grad_pair, grad_query = lax.optimization_barrier((grad_pair, grad_query, keep_attn))[:2]
-    grad_norm1_all = right_product(
-        grad_pair[0], w_qkv[:, feature_width : 2 * feature_width]
-    ) + right_product(grad_pair[1], w_qkv[:, 2 * feature_width :])
-    norm1 = Steps(sum_to_owner(grad_norm1_all))
-    out_sibling = swap(after(out_send, keep_attn), "fsdp", 1)
-    grad_cross_pair = after(grad_cross_pair, grad_norm1_all)
-    grad_enc = right_product(grad_cross_pair[0], w_ckv[0]) + right_product(
-        grad_cross_pair[1], w_ckv[1]
-    )
-    out_sibling = after(out_sibling, grad_enc)
+    norm1_all, norm1_query = norm_terms(place, after(grad_pair, keep_attn), grad_query, w_qkv)
+    ready = cross.move(norm1_all)
+    norm1 = Steps(sum_to_owner(after(norm1_all, ready)))
+    grad_enc = enc_terms(place, after(grad_cross_pair, ready), w_ckv)
+    out_sibling = swap(after(out_send, grad_enc), "fsdp", 1)
+    ready = grad_enc
+    for step in (attn, down, inner, cross, down, inner, attn, norm1):
+        ready = step.move(ready)
+    out_sibling = after(out_sibling, ready)
     out_far = swap(add_low(out_across, out_sibling[1]), "fsdp", 2)
-    ready = grad_enc
-    for step in (cross, attn, inner, down, norm1, inner, down, norm1, cross, attn):
+    for step in (cross, attn, norm1, inner, down):
         ready = step.move(ready)
     layer_out = after_cross + (
         out_own + out_sibling[0].astype(jnp.float32) + after(out_far, ready).astype(jnp.float32)
     )
-    for step in (inner, down, norm1, cross, attn):
+    for step in (cross, attn, inner):
         ready = step.move(ready)
-    ready = down.finish(ready)
+    ready = down.finish(norm1.finish(ready))
+    input_rows = own.astype(jnp.float32)
+    grad_norm1 = norm1.result.astype(jnp.float32) + norm1_query
+    grad_input = grad_after_attn + rms_back(
+        input_rows, inverse_rms(input_rows), after(gain_rows, ready)[0:1], grad_norm1
+    )
     total_down = finished(down.result, 0, feature_width)
-    input_rows = own.astype(jnp.float32)
-    ready = norm1.finish(ready)
-    grad_norm1 = (
-        norm1.result.astype(jnp.float32)
-        + right_product(after(grad_query, ready), w_qkv[:, :feature_width])
-    )
-    grad_input = grad_after_attn + rms_back(
-        input_rows, inverse_rms(input_rows), gain_rows[0:1], grad_norm1
-    )
-    ready = after(ready, grad_input, total_down, layer_out)
-    for step in (cross, attn, inner, cross, attn, inner, cross, attn):
+    ready = after(ready, total_down, grad_input, layer_out)
+    for step in (cross, attn):
         ready = step.move(ready)
     ready = inner.finish(ready)
     total_in, gain_three = inner_out(place, inner.result, mlp_in, norm_gains[2])
     ready = after(ready, total_in)
     while attn.result is None or cross.result is None:
         for step in (cross, attn):
-            if step.result is None:
-                ready = step.move(ready)
+            ready = step.move(ready)
     halves_cross, halves_attn = cross.result, attn.result
     d = feature_width
     total_cout = finished(halves_cross, 0, d)

time: 332 us -> 310 us (0.934)
  waiting for transfers between devices: 117 us -> 85.4 us
  Pallas kernels: 89.5 us -> 105 us
  matrix products: 8.19 us -> 0 us
  local copies, waits for them, and re-layouts: 22.2 us -> 14.8 us
  other arithmetic: 26.8 us -> 32.4 us
  starting transfers between devices: 65.4 us -> 69.9 us
    ppermute x57 -> x59, waiting for transfers between devices: 117 us -> 85.4 us  [swap(): return lax.ppermute(values, axis, [(i, i ^ bit) for i in range(count)])]
    pallas_call x6 -> x8, Pallas kernels: 53.8 us -> 66.6 us  [chain_call(): pl.pallas_call(kernel, grid_spec=pltpu.PrefetchScalarGridSpec(num_scalar_...]
    dot_general x5 -> x0, matrix products: 8.19 us -> none  [right_product(): lax.dot_general(left, right, (((1,), (1,)), ((), ())), preferred_element_...]
    ppermute x57 -> x59, starting transfers between devices: 65.4 us -> 69.9 us  [swap(): return lax.ppermute(values, axis, [(i, i ^ bit) for i in range(count)])]
    slice x6 -> x1, local copies, waits for them, and re-layouts: 5.18 us -> 0.75 us  [local(): after(gain_rows, ready)[0:1]]
    convert_element_type x21 -> x20, other arithmetic: 12.5 us -> 16.2 us  [to_low(): return values.astype(jnp.bfloat16)]
    unnamed x109 -> x105, local copies, waits for them, and re-layouts: 9.84 us -> 7.93 us
  transfers between devices with their start and end apart: 57 -> 59, of which waited for: 20 -> 24; matrix products, arithmetic and copies ran while one was open for 14% -> 13% of each run, Pallas kernels for 24% -> 28%
where the time goes in v4:
time: 310 us; the launch traced here: 309 us
  Pallas kernels  105 us (34%)
  waiting for transfers between devices  85.4 us (28%)
  starting transfers between devices  69.9 us (23%)
  other arithmetic  32.4 us (10%)
  local copies, waits for them, and re-layouts  14.8 us (5%)
    ppermute x59, waiting for transfers between devices, swap(): return lax.ppermute(values, axis, [(i, i ^ bit) for i in range(count)])  85.4 us
    ppermute x59, starting transfers between devices, swap(): return lax.ppermute(values, axis, [(i, i ^ bit) for i in range(count)])  69.9 us
    pallas_call x8, Pallas kernels, chain_call(): pl.pallas_call(kernel, grid_spec=pltpu.PrefetchScalarGridSpec(num_scalar_...  66.6 us
    pallas_call x2, Pallas kernels, wide_products(): pl.pallas_call(functools.partial(products_kernel, tiles, rows, chunks), g...  16.4 us
    convert_element_type x20, other arithmetic, to_low(): return values.astype(jnp.bfloat16)  16.2 us
    pallas_call x1, Pallas kernels, self_backward(): pl.pallas_call(functools.partial(self_backward_kernel, head_size, blocks)...  10.1 us
    unnamed x105, local copies, waits for them, and re-layouts  7.93 us
    pallas_call x1, Pallas kernels, self_forward(): pl.pallas_call(functools.partial(self_forward_kernel, head_size, blocks),...  7.52 us
  transfers between devices with their start and end apart: 59, of which 24 were waited for; matrix products, arithmetic and copies ran while one was open for 13% of the time, Pallas kernels for 28%

profile of v4, /device:TPU:0, one launch (start us, length us, event | category | flops | bytes accessed | tf_op | source)
XLA Modules:
  0.0 309.2 jit_solution(2780579719303402970)
XLA Ops:
  0.6 3.1 collective-permute-start
  3.7 2.5 collective-permute-start.2
  9.9 1.6 collective-permute-start.7
  12.1 1.7 positions.1
  14.8 1.7 collective-permute-done.2
  16.5 7.3 %collective-permute-done.1 = bf16[128,768]{1,0:T(8,128)(2,1)S(1)} collective-permute-done((bf16[128,768]{1,0:T(8,128)(2,1)}, bf16[128,768]{1,0:T(8,128)(2,1)S(1)}, u32[]{:S(2)}, u32[]{:S(2)}) %collective-permute-start.1) | collective-permute-done | bytes 196640 | tf_op jit(solution)/shard_map/ppermute | solution.py:725
  33.1 5.1 %collective-permute-done.4.refs_4_ = bf16[128,768]{1,0:T(8,128)(2,1)S(1)} collective-permute-done((bf16[128,768]{1,0:T(8,128)(2,1)}, bf16[128,768]{1,0:T(8,128)(2,1)S(1)}, u32[]{:S(2)}, u32[]{:S(2)}) %collective-permute-start.4) | collective-permute-done | bytes 196640 | tf_op jit(solution)/shard_map/ppermute | solution.py:725
  39.6 3.0 held_rows.1
  42.6 9.4 %project.1 = (bf16[128,768]{1,0:T(8,128)(2,1)}, bf16[1024,1536]{1,0:T(8,128)(2,1)}, bf16[1024,768]{1,0:T(8,128)(2,1)}, bf16[768,2304]{1,0:T(8,128)(2,1)}, f32[8,768]{1,0:T(8,128)}) custom-call(s32[3]{0:T(128)} %pad_add_fusion.index_ref, bf16[1024,768]{1,0:T(8,128)(2,1)} %get-tuple-element.117.rows_ref, f32[1024,1]{1,0:T(8,128)} %get-tuple-element.118.scale_ref, ...), custom_call_target="tpu_custom_call" | custom-call | flops 103499997184 | bytes 9000000 | tf_op jit(solution)/shard_map/project/pallas_call | solution.py:261
  52.6 7.5 %self_forward.1 = (bf16[128,768]{1,0:T(8,128)(2,1)}, f32[6,1,256]{2,1,0:T(1,128)}) custom-call(bf16[128,768]{1,0:T(8,128)(2,1)} %get-tuple-element.123.q_ref, bf16[1024,1536]{1,0:T(8,128)(2,1)} %get-tuple-element.124.k_ref.v_ref, bf16[1024,1536]{1,0:T(8,128)(2,1)} %get-tuple-element.124.k_ref.v_ref, s32[1024,1]{1,0:T(8,128)} %get-tuple-element.125.pos_ref, ...), custom_call_target="tpu_custom_call" | custom-call | flops 87399997440 | bytes 7600000 | tf_op jit(solution)/shard_map/self_forward/pallas_call | solution.py:202
  60.2 3.4 %collective-permute-done.13.refs_7_.refs_11_.refs_15_ = bf16[192,2304]{1,0:T(8,128)(2,1)} collective-permute-done((bf16[192,2304]{1,0:T(8,128)(2,1)}, bf16[192,2304]{1,0:T(8,128)(2,1)}, u32[]{:S(2)}, u32[]{:S(2)}) %collective-permute-start.13) | collective-permute-done | bytes 884768 | tf_op jit(solution)/shard_map/ppermute | solution.py:725
  65.9 4.2 %attend_out.1 = (f32[128,768]{1,0:T(8,128)}, bf16[128,768]{1,0:T(8,128)(2,1)}, bf16[128,768]{1,0:T(8,128)(2,1)}, bf16[768,1536]{1,0:T(8,128)(2,1)}) custom-call(s32[3]{0:T(128)} %pad_add_fusion.index_ref, bf16[128,768]{1,0:T(8,128)(2,1)} %get-tuple-element.128.att_ref.refs_7_, bf16[128,768]{1,0:T(8,128)(2,1)} %bitcast.34, ...), custom_call_target="tpu_custom_call" | custom-call | flops 50600001536 | bytes 4400000 | tf_op jit(solution)/shard_map/attend_out/pallas_call | solution.py:261
  71.4 12.4 %cross_forward.1 = (bf16[2,512,768]{2,1,0:T(8,128)(2,1)}, bf16[128,768]{1,0:T(8,128)(2,1)}, f32[128,768]{1,0:T(8,128)}, bf16[128,768]{1,0:T(8,128)(2,1)}, bf16[2...) custom-call(s32[3]{0:T(128)} %pad_add_fusion.index_ref, bf16[128,768]{1,0:T(8,128)(2,1)} %get-tuple-element.133.refs_0_, ...), custom_call_target="tpu_custom_call" | custom-call | flops 141450002432 | bytes 12300000 | tf_op jit(solution)/shard_map/cross_forward/pallas_call | solution.py:261
  86.0 5.7 %collective-permute-done.16.refs_2_ = bf16[128,768]{1,0:T(8,128)(2,1)S(1)} collective-permute-done((bf16[128,768]{1,0:T(8,128)(2,1)}, bf16[128,768]{1,0:T(8,128)(2,1)S(1)}, u32[]{:S(2)}, u32[]{:S(2)}) %collective-permute-start.16) | collective-permute-done | bytes 196640 | tf_op jit(solution)/shard_map/ppermute | solution.py:725
  94.2 9.9 %mlp_share.1 = (f32[128,768]{1,0:T(8,128)}, bf16[128,768]{1,0:T(8,128)(2,1)}, bf16[128,768]{1,0:T(8,128)(2,1)}, bf16[128,768]{1,0:T(8,128)(2,1)}, f32[128,768]{1...) custom-call(s32[3]{0:T(128)} %pad_add_fusion.index_ref, ...), custom_call_target="tpu_custom_call" | custom-call | flops 126500003840 | bytes 11000000 | tf_op jit(solution)/shard_map/mlp_share/pallas_call | solution.py:261
  106.2 1.9 slice.242
  113.4 2.5 collective-permute-done.23.refs_12_
  116.6 12.3 %cross_backward.1 = (bf16[128,768]{1,0:T(8,128)(2,1)}, bf16[2,512,768]{2,1,0:T(8,128)(2,1)}, f32[128,768]{1,0:T(8,128)}, bf16[128,768]{1,0:T(8,128)(2,1)}, bf16[...) custom-call(s32[3]{0:T(128)} %pad_add_fusion.index_ref, bf16[128,768]{1,0:T(8,128)(2,1)} %get-tuple-element.133.refs_0_, ...), custom_call_target="tpu_custom_call" | custom-call | flops 149500002304 | bytes 13000000 | tf_op jit(solution)/shard_map/cross_backward/pallas_call | solution.py:261
  128.9 8.3 %wide_products.2 = (bf16[384,3840]{1,0:T(8,128)(2,1)}, bf16[384,3840]{1,0:T(8,128)(2,1)}) custom-call(s32[3]{0:T(128)} %pad_add_fusion.index_ref, bf16[128,768]{1,0:T(8,128)(2,1)} %get-tuple-element.154.refs_0_, bf16[128,768]{1,0:T(8,128)(2,1)} %get-tuple-element.155.refs_1_, bf16[128,768]{1,0:T(8,128)(2,1)} %get-tuple-element.156.refs_2_, ...), custom_call_target="tpu_custom_call" | custom-call | flops 94299996160 | bytes 8199999 | tf_op jit(solution)/shard_map/wide_products/pallas_call | solution.py:843
  143.9 2.9 add_convert_fusion
  148.2 10.1 %self_backward.1 = (bf16[128,768]{1,0:T(8,128)(2,1)}, bf16[2,1024,768]{2,1,0:T(8,128)(2,1)}) custom-call(bf16[128,768]{1,0:T(8,128)(2,1)} %get-tuple-element.123.q_ref, bf16[1024,1536]{1,0:T(8,128)(2,1)} %get-tuple-element.124.k_ref.v_ref, bf16[1024,1536]{1,0:T(8,128)(2,1)} %get-tuple-element.124.k_ref.v_ref, bf16[128,768]{1,0:T(8,128)(2,1)} %get-tuple-element.171.do_ref, ...), custom_call_target="tpu_custom_call" | custom-call | flops 117300002816 | bytes 10200000 | tf_op jit(solution)/shard_map/self_backward/pallas_call | solution.py:223
  159.3 1.7 collective-permute-start.35
  162.5 8.0 %wide_products.3 = (bf16[384,2304]{1,0:T(8,128)(2,1)}, bf16[384,2304]{1,0:T(8,128)(2,1)}) custom-call(s32[3]{0:T(128)} %pad_add_fusion.index_ref, bf16[1024,768]{1,0:T(8,128)(2,1)} %get-tuple-element.174.refs_0_.refs_2_, bf16[128,768]{1,0:T(8,128)(2,1)} %get-tuple-element.178.refs_1_.query_ref, bf16[1024,768]{1,0:T(8,128)(2,1)} %get-tuple-element.174.refs_0_.refs_2_, ...), custom_call_target="tpu_custom_call" | custom-call | flops 115000000 | bytes 10000 | tf_op jit(solution)/shard_map/wide_products/pallas_call | solution.py:843
  170.5 7.8 %norm_terms.1 = (bf16[1024,768]{1,0:T(8,128)(2,1)}, f32[128,768]{1,0:T(8,128)}) custom-call(s32[3]{0:T(128)} %pad_add_fusion.index_ref, bf16[2,1024,768]{2,1,0:T(8,128)(2,1)} %get-tuple-element.180.refs_3_.refs_4_.pair_ref, bf16[128,768]{1,0:T(8,128)(2,1)} %get-tuple-element.178.refs_1_.query_ref, bf16[768,2304]{1,0:T(8,128)(2,1)} %get-tuple-element.181.w_ref), custom_call_target="tpu_custom_call" | custom-call | flops 115000000 | bytes 10000 | tf_op jit(solution)/shard_map/norm_terms/pallas_call | solution.py:261
  178.3 3.3 %collective-permute-done.28 = bf16[192,3840]{1,0:T(8,128)(2,1)} collective-permute-done((bf16[192,3840]{1,0:T(8,128)(2,1)}, bf16[192,3840]{1,0:T(8,128)(2,1)}, u32[]{:S(2)}, u32[]{:S(2)}) %collective-permute-start.28) | collective-permute-done | bytes 1474592 | tf_op jit(solution)/shard_map/ppermute | solution.py:725
  181.6 3.4 %add_convert_fusion.3 = (bf16[96,3840]{1,0:T(8,128)(2,1)}, bf16[96,3840]{1,0:T(8,128)(2,1)}) fusion(bf16[192,3840]{1,0:T(8,128)(2,1)} %collective-permute-done.28, bf16[384,3840]{1,0:T(8,128)(2,1)} %collective-permute-done.27, bf16[384,3840]{1,0:T(8,128)(2,1)S(1)} %copy-done.2), kind=kLoop, calls=%fused_computation.6 | loop fusion | flops 4423680 | bytes 5898240 | tf_op jit(solution)/shard_map/convert_element_type | solution.py:26
  186.6 5.5 %enc_terms.1 = f32[512,768]{1,0:T(8,128)} custom-call(s32[3]{0:T(128)} %pad_add_fusion.index_ref, bf16[2,512,768]{2,1,0:T(8,128)(2,1)} %get-tuple-element.184.refs_5_.refs_6_.pair_ref, bf16[2,768,768]{2,1,0:T(8,128)(2,1)} %get-tuple-element.185.w_ref), custom_call_target="tpu_custom_call" | custom-call | flops 46000001024 | bytes 4000000 | tf_op jit(solution)/shard_map/enc_terms/pallas_call | solution.py:261
  196.6 2.3 collective-permute-start.38
  199.8 5.0 %collective-permute-done.39 = bf16[96,3840]{1,0:T(8,128)(2,1)} collective-permute-done((bf16[96,3840]{1,0:T(8,128)(2,1)}, bf16[96,3840]{1,0:T(8,128)(2,1)}, u32[]{:S(2)}, u32[]{:S(2)}) %collective-permute-start.39) | collective-permute-done | bytes 737312 | tf_op jit(solution)/shard_map/ppermute | solution.py:725
  204.8 2.2 collective-permute-start.37
  209.4 3.6 %collective-permute-done.37 = bf16[24,3072]{1,0:T(8,128)(2,1)S(1)} collective-permute-done((bf16[24,3072]{1,0:T(8,128)(2,1)S(1)}, bf16[24,3072]{1,0:T(8,128)(2,1)S(1)}, u32[]{:S(2)}, u32[]{:S(2)}) %collective-permute-start.37) | collective-permute-done | bytes 147488 | tf_op jit(solution)/shard_map/ppermute | solution.py:725
  213.9 2.1 collective-permute-done.34
  216.1 2.1 collective-permute-start.42
  224.6 6.3 %collective-permute-done.44 = bf16[96,2304]{1,0:T(8,128)(2,1)S(1)} collective-permute-done((bf16[96,2304]{1,0:T(8,128)(2,1)S(1)}, bf16[96,2304]{1,0:T(8,128)(2,1)S(1)}, u32[]{:S(2)}, u32[]{:S(2)}) %collective-permute-start.44) | collective-permute-done | bytes 442400 | tf_op jit(solution)/shard_map/ppermute | solution.py:725
  232.0 9.2 %collective-permute-done.43 = bf16[256,768]{1,0:T(8,128)(2,1)S(1)} collective-permute-done((bf16[256,768]{1,0:T(8,128)(2,1)S(1)}, bf16[256,768]{1,0:T(8,128)(2,1)S(1)}, u32[]{:S(2)}, u32[]{:S(2)}) %collective-permute-start.43) | collective-permute-done | bytes 393248 | tf_op jit(solution)/shard_map/ppermute | solution.py:725
  241.4 3.3 %collective-permute-start.47 = (bf16[128,768]{1,0:T(8,128)(2,1)S(1)}, bf16[128,768]{1,0:T(8,128)(2,1)S(1)}, u32[]{:S(2)}, u32[]{:S(2)}) collective-permute-start(bf16[128,768]{1,0:T(8,128)(2,1)S(1)} %slice.329), channel_id=1, source_target_pairs={{0,16},{4,20},{8,24},{12,28},{16,0},{20,4},{24,8},{28,12},{1,17},{... | collective-permute-start | bytes 589832 | tf_op jit(solution)/shard_map/ppermute | solution.py:725
  245.0 2.0 collective-permute-start.46
  247.2 2.4 collective-permute-start.52
  250.4 9.0 %collective-permute-done.52 = bf16[24,3840]{1,0:T(8,128)(2,1)S(1)} collective-permute-done((bf16[24,3840]{1,0:T(8,128)(2,1)S(1)}, bf16[24,3840]{1,0:T(8,128)(2,1)S(1)}, u32[]{:S(2)}, u32[]{:S(2)}) %collective-permute-start.52) | collective-permute-done | bytes 184352 | tf_op jit(solution)/shard_map/ppermute | solution.py:725
  259.5 4.3 %collective-permute-start.54 = (bf16[48,3840]{1,0:T(8,128)(2,1)S(1)}, bf16[48,3840]{1,0:T(8,128)(2,1)S(1)}, u32[]{:S(2)}, u32[]{:S(2)}) collective-permute-start(bf16[48,3840]{1,0:T(8,128)(2,1)S(1)} %pad_maximum_fusion.9), channel_id=1, source_target_pairs={{0,8},{4,12},{8,0},{12,4},{16,24},{20,28},{24,16},{28,20},{1,9},{5... | collective-permute-start | bytes 1105928 | tf_op jit(solution)/shard_map/ppermute | solution.py:725
  264.1 3.3 %collective-permute-start.58 = (bf16[96,3072]{1,0:T(8,128)(2,1)S(1)}, bf16[96,3072]{1,0:T(8,128)(2,1)S(1)}, u32[]{:S(2)}, u32[]{:S(2)}) collective-permute-start(bf16[96,3072]{1,0:T(8,128)(2,1)S(1)} %pad_maximum_fusion.5.own_ref), channel_id=1, source_target_pairs={{0,4},{4,0},{8,12},{12,8},{16,20},{20,16},{24,28},{28,24},{1,5},{5... | collective-permute-start | bytes 1769480 | tf_op jit(solution)/shard_map/ppermute | solution.py:725
  267.5 5.2 %collective-permute-done.51 = bf16[24,2304]{1,0:T(8,128)(2,1)S(1)} collective-permute-done((bf16[24,2304]{1,0:T(8,128)(2,1)S(1)}, bf16[24,2304]{1,0:T(8,128)(2,1)S(1)}, u32[]{:S(2)}, u32[]{:S(2)}) %collective-permute-start.51) | collective-permute-done | bytes 110624 | tf_op jit(solution)/shard_map/ppermute | solution.py:725
  272.8 3.5 %collective-permute-start.53 = (bf16[24,2304]{1,0:T(8,128)(2,1)S(1)}, bf16[24,2304]{1,0:T(8,128)(2,1)S(1)}, u32[]{:S(2)}, u32[]{:S(2)}) collective-permute-start(bf16[24,2304]{1,0:T(8,128)(2,1)S(1)} %add_convert_fusion.26), channel_id=1, source_target_pairs={{0,16},{4,20},{8,24},{12,28},{16,0},{20,4},{24,8},{28,12},{1,17},{... | collective-permute-start | bytes 331784 | tf_op jit(solution)/shard_map/ppermute | solution.py:725
  276.5 3.2 %collective-permute-start.56 = (bf16[96,3840]{1,0:T(8,128)(2,1)S(1)}, bf16[96,3840]{1,0:T(8,128)(2,1)S(1)}, u32[]{:S(2)}, u32[]{:S(2)}) collective-permute-start(bf16[96,3840]{1,0:T(8,128)(2,1)S(1)} %pad_maximum_fusion.1), channel_id=1, source_target_pairs={{0,4},{4,0},{8,12},{12,8},{16,20},{20,16},{24,28},{28,24},{1,5},{5... | collective-permute-start | bytes 2211848 | tf_op jit(solution)/shard_map/ppermute | solution.py:725
  285.2 5.1 %inner_out.1 = (f32[192,3072]{1,0:T(8,128)}, f32[192,1]{1,0:T(8,128)}) custom-call(s32[3]{0:T(128)} %pad_add_fusion.index_ref, bf16[96,3072]{1,0:T(8,128)(2,1)} %copy-done.22, bf16[96,3072]{1,0:T(8,128)(2,1)} %copy-done.40, bf16[192,3072]{1,0:T(8,128)(2,1)} %weight_ref.1, f32[192,1]{1,0:T(8,128)} %copy.26.gain_ref), custom_call_target="tpu_custom_call" | custom-call | flops 34500001792 | bytes 3000000 | tf_op jit(solution)/shard_map/inner_out/pallas_call | solution.py:261
  291.3 4.6 %collective-permute-done.56 = bf16[96,3840]{1,0:T(8,128)(2,1)S(1)} collective-permute-done((bf16[96,3840]{1,0:T(8,128)(2,1)S(1)}, bf16[96,3840]{1,0:T(8,128)(2,1)S(1)}, u32[]{:S(2)}, u32[]{:S(2)}) %collective-permute-start.56) | collective-permute-done | bytes 737312 | tf_op jit(solution)/shard_map/ppermute | solution.py:725
  296.3 1.8 collective-permute-start.57
  301.2 5.7 %collective-permute-done.57 = bf16[96,2304]{1,0:T(8,128)(2,1)S(1)} collective-permute-done((bf16[96,2304]{1,0:T(8,128)(2,1)S(1)}, bf16[96,2304]{1,0:T(8,128)(2,1)S(1)}, u32[]{:S(2)}, u32[]{:S(2)}) %collective-permute-start.57) | collective-permute-done | bytes 442400 | tf_op jit(solution)/shard_map/ppermute | solution.py:725
  (261 shorter events, 75.2 us)
Async XLA Ops:
  0.6 23.2 %collective-permute-start = (bf16[128,768]{1,0:T(8,128)(2,1)}, bf16[128,768]{1,0:T(8,128)(2,1)}, u32[]{:S(2)}, u32[]{:S(2)}) collective-permute-start(bf16[128,768]{1,0:T(8,128)(2,1)} %bitcast.29), channel_id=1, source_target_pairs={{0,8},{4,12},{8,0},{12,4},{16,24},{20,28},{24,16},{28,20},{1,9},{5... | collective-permute-start | bytes 589832 | tf_op jit(solution)/shard_map/ppermute | solution.py:725
  3.7 12.8 %collective-permute-start.2 = (bf16[128,768]{1,0:T(8,128)(2,1)}, bf16[128,768]{1,0:T(8,128)(2,1)S(1)}, u32[]{:S(2)}, u32[]{:S(2)}) collective-permute-start(bf16[128,768]{1,0:T(8,128)(2,1)} %bitcast.30), channel_id=1, source_target_pairs={{0,24},{4,28},{8,16},{12,20},{16,8},{20,12},{24,0},{28,4},{1,25},{... | collective-permute-start | bytes 589832 | tf_op jit(solution)/shard_map/ppermute | solution.py:725
  6.2 17.6 %collective-permute-start.1 = (bf16[128,768]{1,0:T(8,128)(2,1)}, bf16[128,768]{1,0:T(8,128)(2,1)S(1)}, u32[]{:S(2)}, u32[]{:S(2)}) collective-permute-start(bf16[128,768]{1,0:T(8,128)(2,1)} %bitcast.31), channel_id=1, source_target_pairs={{0,16},{4,20},{8,24},{12,28},{16,0},{20,4},{24,8},{28,12},{1,17},{... | collective-permute-start | bytes 589832 | tf_op jit(solution)/shard_map/ppermute | solution.py:725
  6.3 22.4 %collective-permute-start.3 = (bf16[128,768]{1,0:T(8,128)(2,1)}, bf16[128,768]{1,0:T(8,128)(2,1)}, u32[]{:S(2)}, u32[]{:S(2)}) collective-permute-start(bf16[128,768]{1,0:T(8,128)(2,1)} %bitcast.32), channel_id=1, source_target_pairs={{0,4},{4,0},{8,12},{12,8},{16,20},{20,16},{24,28},{28,24},{1,5},{5... | collective-permute-start | bytes 589832 | tf_op jit(solution)/shard_map/ppermute | solution.py:725
  9.9 21.7 %collective-permute-start.7 = (bf16[192,2432]{1,0:T(8,128)(2,1)S(1)}, bf16[192,2432]{1,0:T(8,128)(2,1)S(1)}, u32[]{:S(2)}, u32[]{:S(2)}) collective-permute-start(bf16[192,2432]{1,0:T(8,128)(2,1)S(1)} %fusion.1.refs_0_), channel_id=1, source_target_pairs={{0,2},{1,3},{2,0},{3,1},{4,6},{5,7},{6,4},{7,5},{8,10},{9,11},{10,... | collective-permute-start | bytes 2801672 | tf_op jit(solution)/shard_map/ppermute | solution.py:725
  23.9 14.3 %collective-permute-start.5 = (bf16[256,768]{1,0:T(8,128)(2,1)S(1)}, bf16[256,768]{1,0:T(8,128)(2,1)S(1)}, u32[]{:S(2)}, u32[]{:S(2)}) collective-permute-start(bf16[256,768]{1,0:T(8,128)(2,1)S(1)} %pad_maximum_fusion.8.refs_2_), channel_id=1, source_target_pairs={{0,4},{4,0},{8,12},{12,8},{16,20},{20,16},{24,28},{28,24},{1,5},{5... | collective-permute-start | bytes 1179656 | tf_op jit(solution)/shard_map/ppermute | solution.py:725
  26.4 11.7 %collective-permute-start.4 = (bf16[128,768]{1,0:T(8,128)(2,1)}, bf16[128,768]{1,0:T(8,128)(2,1)S(1)}, u32[]{:S(2)}, u32[]{:S(2)}) collective-permute-start(bf16[128,768]{1,0:T(8,128)(2,1)} %collective-permute-done.refs_1_), channel_id=1, source_target_pairs={{0,4},{4,0},{8,12},{12,8},{16,20},{20,16},{24,28},{28,24},{1,5},{5... | collective-permute-start | bytes 589832 | tf_op jit(solution)/shard_map/ppermute | solution.py:725
  28.7 13.9 %collective-permute-start.6 = (bf16[192,2432]{1,0:T(8,128)(2,1)S(1)}, bf16[192,2432]{1,0:T(8,128)(2,1)}, u32[]{:S(2)}, u32[]{:S(2)}) collective-permute-start(bf16[192,2432]{1,0:T(8,128)(2,1)S(1)} %fusion.1.refs_0_), channel_id=1, source_target_pairs={{0,1},{1,0},{2,3},{3,2},{4,5},{5,4},{6,7},{7,6},{8,9},{9,8},{10,11... | collective-permute-start | bytes 2801672 | tf_op jit(solution)/shard_map/ppermute | solution.py:725
  28.8 23.3 %collective-permute-start.10 = (bf16[192,1536]{1,0:T(8,128)(2,1)S(1)}, bf16[192,1536]{1,0:T(8,128)(2,1)}, u32[]{:S(2)}, u32[]{:S(2)}) collective-permute-start(bf16[192,1536]{1,0:T(8,128)(2,1)S(1)} %constant_dynamic-update-slice_fusion.refs_0_), channel_id=1, source_target_pairs={{0,2},{1,3},{2,0},{3,1},{4,6},{5,7},{6,4},{7,5},{8,10},{9,11},{10,... | collective-permute-start | bytes 1769480 | tf_op jit(solution)/shard_map/ppermute | solution.py:725
  31.6 32.0 %collective-permute-start.13 = (bf16[192,2304]{1,0:T(8,128)(2,1)}, bf16[192,2304]{1,0:T(8,128)(2,1)}, u32[]{:S(2)}, u32[]{:S(2)}) collective-permute-start(bf16[192,2304]{1,0:T(8,128)(2,1)} %constant_dynamic-update-slice_fusion.2.refs_5_.refs_9_.refs_13_), channel_id=1, source_target_pairs={{0,2},{1,3},{2,0},{3,1},{4,6},{5,7},{6,4},{7,5},{8,10},{9,11},{10,... | collective-permute-start | bytes 2654216 | tf_op jit(solution)/shard_map/ppermute | solution.py:725
  52.0 13.1 %collective-permute-start.9 = (bf16[192,1536]{1,0:T(8,128)(2,1)S(1)}, bf16[192,1536]{1,0:T(8,128)(2,1)S(1)}, u32[]{:S(2)}, u32[]{:S(2)}) collective-permute-start(bf16[192,1536]{1,0:T(8,128)(2,1)S(1)} %constant_dynamic-update-slice_fusion.refs_0_), channel_id=1, source_target_pairs={{0,1},{1,0},{2,3},{3,2},{4,5},{5,4},{6,7},{7,6},{8,9},{9,8},{10,11... | collective-permute-start | bytes 1769480 | tf_op jit(solution)/shard_map/ppermute | solution.py:725
  52.1 13.0 %collective-permute-start.11 = (bf16[192,1536]{1,0:T(8,128)(2,1)}, bf16[192,1536]{1,0:T(8,128)(2,1)}, u32[]{:S(2)}, u32[]{:S(2)}) collective-permute-start(bf16[192,1536]{1,0:T(8,128)(2,1)} %collective-permute-done.10.refs_2_), channel_id=1, source_target_pairs={{0,1},{1,0},{2,3},{3,2},{4,5},{5,4},{6,7},{7,6},{8,9},{9,8},{10,11... | collective-permute-start | bytes 1769480 | tf_op jit(solution)/shard_map/ppermute | solution.py:725
  60.1 10.0 %collective-permute-start.12 = (bf16[192,2304]{1,0:T(8,128)(2,1)}, bf16[192,2304]{1,0:T(8,128)(2,1)S(1)}, u32[]{:S(2)}, u32[]{:S(2)}) collective-permute-start(bf16[192,2304]{1,0:T(8,128)(2,1)} %constant_dynamic-update-slice_fusion.2.refs_5_.refs_9_.refs_13_), channel_id=1, source_target_pairs={{0,1},{1,0},{2,3},{3,2},{4,5},{5,4},{6,7},{7,6},{8,9},{9,8},{10,11... | collective-permute-start | bytes 2654216 | tf_op jit(solution)/shard_map/ppermute | solution.py:725
  63.6 20.3 %collective-permute-start.19 = (bf16[512,768]{1,0:T(8,128)(2,1)}, bf16[512,768]{1,0:T(8,128)(2,1)}, u32[]{:S(2)}, u32[]{:S(2)}) collective-permute-start(bf16[512,768]{1,0:T(8,128)(2,1)} %pad_maximum_fusion.2), channel_id=1, source_target_pairs={{0,2},{1,3},{2,0},{3,1},{4,6},{5,7},{6,4},{7,5},{8,10},{9,11},{10,... | collective-permute-start | bytes 2359304 | tf_op jit(solution)/shard_map/ppermute | solution.py:725
  83.9 9.3 %collective-permute-start.20 = (bf16[512,768]{1,0:T(8,128)(2,1)}, bf16[512,768]{1,0:T(8,128)(2,1)S(1)}, u32[]{:S(2)}, u32[]{:S(2)}) collective-permute-start(bf16[512,768]{1,0:T(8,128)(2,1)} %collective-permute-done.19.refs_7_), channel_id=1, source_target_pairs={{0,1},{1,0},{2,3},{3,2},{4,5},{5,4},{6,7},{7,6},{8,9},{9,8},{10,11... | collective-permute-start | bytes 2359304 | tf_op jit(solution)/shard_map/ppermute | solution.py:725
  104.3 9.1 %collective-permute-start.21 = (bf16[128,768]{1,0:T(8,128)(2,1)}, bf16[128,768]{1,0:T(8,128)(2,1)S(1)}, u32[]{:S(2)}, u32[]{:S(2)}) collective-permute-start(bf16[128,768]{1,0:T(8,128)(2,1)} %get-tuple-element.150), channel_id=1, source_target_pairs={{0,1},{1,0},{2,3},{3,2},{4,5},{5,4},{6,7},{7,6},{8,9},{9,8},{10,11... | collective-permute-start | bytes 589832 | tf_op jit(solution)/shard_map/ppermute | solution.py:725
  106.1 9.8 %collective-permute-start.23 = (bf16[128,768]{1,0:T(8,128)(2,1)}, bf16[128,768]{1,0:T(8,128)(2,1)S(1)}, u32[]{:S(2)}, u32[]{:S(2)}) collective-permute-start(bf16[128,768]{1,0:T(8,128)(2,1)} %get-tuple-element.152), channel_id=1, source_target_pairs={{0,3},{1,2},{2,1},{3,0},{4,7},{5,6},{6,5},{7,4},{8,11},{9,10},{10,... | collective-permute-start | bytes 589832 | tf_op jit(solution)/shard_map/ppermute | solution.py:725
  108.1 20.8 %collective-permute-start.26 = (bf16[384,768]{1,0:T(8,128)(2,1)}, bf16[384,768]{1,0:T(8,128)(2,1)}, u32[]{:S(2)}, u32[]{:S(2)}) collective-permute-start(bf16[384,768]{1,0:T(8,128)(2,1)} %slice.242), channel_id=1, source_target_pairs={{0,4},{4,0},{8,12},{12,8},{16,20},{20,16},{24,28},{28,24},{1,5},{5... | collective-permute-start | bytes 1769480 | tf_op jit(solution)/shard_map/ppermute | solution.py:725
  112.0 16.9 %collective-permute-start.25 = (bf16[192,1536]{1,0:T(8,128)(2,1)}, bf16[192,1536]{1,0:T(8,128)(2,1)}, u32[]{:S(2)}, u32[]{:S(2)}) collective-permute-start(bf16[192,1536]{1,0:T(8,128)(2,1)} %pad_maximum_fusion.3), channel_id=1, source_target_pairs={{0,2},{1,3},{2,0},{3,1},{4,6},{5,7},{6,4},{7,5},{8,10},{9,11},{10,... | collective-permute-start | bytes 1769480 | tf_op jit(solution)/shard_map/ppermute | solution.py:725
  140.5 17.7 %collective-permute-start.30 = (bf16[192,768]{1,0:T(8,128)(2,1)S(1)}, bf16[192,768]{1,0:T(8,128)(2,1)S(1)}, u32[]{:S(2)}, u32[]{:S(2)}) collective-permute-start(bf16[192,768]{1,0:T(8,128)(2,1)S(1)} %get-tuple-element.234), channel_id=1, source_target_pairs={{0,8},{4,12},{8,0},{12,4},{16,24},{20,28},{24,16},{28,20},{1,9},{5... | collective-permute-start | bytes 884744 | tf_op jit(solution)/shard_map/ppermute | solution.py:725
  143.2 15.2 %collective-permute-start.29 = (bf16[96,3072]{1,0:T(8,128)(2,1)S(1)}, bf16[96,3072]{1,0:T(8,128)(2,1)S(1)}, u32[]{:S(2)}, u32[]{:S(2)}) collective-permute-start(bf16[96,3072]{1,0:T(8,128)(2,1)S(1)} %slice.317), channel_id=1, source_target_pairs={{0,4},{4,0},{8,12},{12,8},{16,20},{20,16},{24,28},{28,24},{1,5},{5... | collective-permute-start | bytes 1769480 | tf_op jit(solution)/shard_map/ppermute | solution.py:725
  146.7 34.9 %collective-permute-start.28 = (bf16[192,3840]{1,0:T(8,128)(2,1)}, bf16[192,3840]{1,0:T(8,128)(2,1)}, u32[]{:S(2)}, u32[]{:S(2)}) collective-permute-start(bf16[192,3840]{1,0:T(8,128)(2,1)} %add_convert_fusion), channel_id=1, source_target_pairs={{0,2},{1,3},{2,0},{3,1},{4,6},{5,7},{6,4},{7,5},{8,10},{9,11},{10,... | collective-permute-start | bytes 4423688 | tf_op jit(solution)/shard_map/ppermute | solution.py:725
  159.3 37.2 %collective-permute-start.35 = (bf16[48,3072]{1,0:T(8,128)(2,1)}, bf16[48,3072]{1,0:T(8,128)(2,1)}, u32[]{:S(2)}, u32[]{:S(2)}) collective-permute-start(bf16[48,3072]{1,0:T(8,128)(2,1)} %get-tuple-element.232), channel_id=1, source_target_pairs={{0,8},{4,12},{8,0},{12,4},{16,24},{20,28},{24,16},{28,20},{1,9},{5... | collective-permute-start | bytes 884744 | tf_op jit(solution)/shard_map/ppermute | solution.py:725
  161.0 33.1 %collective-permute-start.36 = (bf16[96,768]{1,0:T(8,128)(2,1)S(1)}, bf16[96,768]{1,0:T(8,128)(2,1)}, u32[]{:S(2)}, u32[]{:S(2)}) collective-permute-start(bf16[96,768]{1,0:T(8,128)(2,1)S(1)} %add_convert_fusion.25), channel_id=1, source_target_pairs={{0,16},{4,20},{8,24},{12,28},{16,0},{20,4},{24,8},{28,12},{1,17},{... | collective-permute-start | bytes 442376 | tf_op jit(solution)/shard_map/ppermute | solution.py:725
  170.5 21.6 %collective-permute-start.33 = (bf16[384,2304]{1,0:T(8,128)(2,1)}, bf16[384,2304]{1,0:T(8,128)(2,1)}, u32[]{:S(2)}, u32[]{:S(2)}) collective-permute-start(bf16[384,2304]{1,0:T(8,128)(2,1)} %get-tuple-element.188), channel_id=1, source_target_pairs={{0,1},{1,0},{2,3},{3,2},{4,5},{5,4},{6,7},{7,6},{8,9},{9,8},{10,11... | collective-permute-start | bytes 5308424 | tf_op jit(solution)/shard_map/ppermute | solution.py:725
  185.1 19.7 %collective-permute-start.39 = (bf16[96,3840]{1,0:T(8,128)(2,1)}, bf16[96,3840]{1,0:T(8,128)(2,1)}, u32[]{:S(2)}, u32[]{:S(2)}) collective-permute-start(bf16[96,3840]{1,0:T(8,128)(2,1)} %get-tuple-element.228), channel_id=1, source_target_pairs={{0,4},{4,0},{8,12},{12,8},{16,20},{20,16},{24,28},{28,24},{1,5},{5... | collective-permute-start | bytes 2211848 | tf_op jit(solution)/shard_map/ppermute | solution.py:725
  192.0 29.8 %collective-permute-start.31 = (bf16[2,128,768]{2,1,0:T(8,128)(2,1)}, bf16[2,128,768]{2,1,0:T(8,128)(2,1)S(1)}, u32[]{:S(2)}, u32[]{:S(2)}) collective-permute-start(bf16[2,128,768]{2,1,0:T(8,128)(2,1)} %get-tuple-element.186), channel_id=1, source_target_pairs={{0,1},{1,0},{2,3},{3,2},{4,5},{5,4},{6,7},{7,6},{8,9},{9,8},{10,11... | collective-permute-start | bytes 1179656 | tf_op jit(solution)/shard_map/ppermute | solution.py:725
  192.1 27.9 %collective-permute-start.32 = (bf16[512,768]{1,0:T(8,128)(2,1)S(1)}, bf16[512,768]{1,0:T(8,128)(2,1)S(1)}, u32[]{:S(2)}, u32[]{:S(2)}) collective-permute-start(bf16[512,768]{1,0:T(8,128)(2,1)S(1)} %slice.260), channel_id=1, source_target_pairs={{0,4},{4,0},{8,12},{12,8},{16,20},{20,16},{24,28},{28,24},{1,5},{5... | collective-permute-start | bytes 2359304 | tf_op jit(solution)/shard_map/ppermute | solution.py:725
  194.1 22.0 %collective-permute-start.34 = (bf16[192,2304]{1,0:T(8,128)(2,1)S(1)}, bf16[192,2304]{1,0:T(8,128)(2,1)S(1)}, u32[]{:S(2)}, u32[]{:S(2)}) collective-permute-start(bf16[192,2304]{1,0:T(8,128)(2,1)S(1)} %add_convert_fusion.1), channel_id=1, source_target_pairs={{0,2},{1,3},{2,0},{3,1},{4,6},{5,7},{6,4},{7,5},{8,10},{9,11},{10,... | collective-permute-start | bytes 2654216 | tf_op jit(solution)/shard_map/ppermute | solution.py:725
  196.6 12.1 %collective-permute-start.38 = (bf16[96,768]{1,0:T(8,128)(2,1)S(1)}, bf16[96,768]{1,0:T(8,128)(2,1)S(1)}, u32[]{:S(2)}, u32[]{:S(2)}) collective-permute-start(bf16[96,768]{1,0:T(8,128)(2,1)S(1)} %add_convert_fusion.23), channel_id=1, source_target_pairs={{0,16},{4,20},{8,24},{12,28},{16,0},{20,4},{24,8},{28,12},{1,17},{... | collective-permute-start | bytes 442376 | tf_op jit(solution)/shard_map/ppermute | solution.py:725
  208.7 15.4 %collective-permute-start.45 = (bf16[48,3840]{1,0:T(8,128)(2,1)S(1)}, bf16[48,3840]{1,0:T(8,128)(2,1)S(1)}, u32[]{:S(2)}, u32[]{:S(2)}) collective-permute-start(bf16[48,3840]{1,0:T(8,128)(2,1)S(1)} %get-tuple-element.244), channel_id=1, source_target_pairs={{0,8},{4,12},{8,0},{12,4},{16,24},{20,28},{24,16},{28,20},{1,9},{5... | collective-permute-start | bytes 1105928 | tf_op jit(solution)/shard_map/ppermute | solution.py:725
  213.0 31.8 %collective-permute-start.41 = (bf16[192,768]{1,0:T(8,128)(2,1)S(1)}, bf16[192,768]{1,0:T(8,128)(2,1)S(1)}, u32[]{:S(2)}, u32[]{:S(2)}) collective-permute-start(bf16[192,768]{1,0:T(8,128)(2,1)S(1)} %pad_maximum_fusion.10), channel_id=1, source_target_pairs={{0,8},{4,12},{8,0},{12,4},{16,24},{20,28},{24,16},{28,20},{1,9},{5... | collective-permute-start | bytes 884744 | tf_op jit(solution)/shard_map/ppermute | solution.py:725
  216.1 25.3 %collective-permute-start.42 = (bf16[24,3072]{1,0:T(8,128)(2,1)S(1)}, bf16[24,3072]{1,0:T(8,128)(2,1)S(1)}, u32[]{:S(2)}, u32[]{:S(2)}) collective-permute-start(bf16[24,3072]{1,0:T(8,128)(2,1)S(1)} %add_convert_fusion.20), channel_id=1, source_target_pairs={{0,16},{4,20},{8,24},{12,28},{16,0},{20,4},{24,8},{28,12},{1,17},{... | collective-permute-start | bytes 442376 | tf_op jit(solution)/shard_map/ppermute | solution.py:725
  220.1 10.9 %collective-permute-start.44 = (bf16[96,2304]{1,0:T(8,128)(2,1)S(1)}, bf16[96,2304]{1,0:T(8,128)(2,1)S(1)}, u32[]{:S(2)}, u32[]{:S(2)}) collective-permute-start(bf16[96,2304]{1,0:T(8,128)(2,1)S(1)} %get-tuple-element.230), channel_id=1, source_target_pairs={{0,4},{4,0},{8,12},{12,8},{16,20},{20,16},{24,28},{28,24},{1,5},{5... | collective-permute-start | bytes 1327112 | tf_op jit(solution)/shard_map/ppermute | solution.py:725
  221.8 19.4 %collective-permute-start.43 = (bf16[256,768]{1,0:T(8,128)(2,1)S(1)}, bf16[256,768]{1,0:T(8,128)(2,1)S(1)}, u32[]{:S(2)}, u32[]{:S(2)}) collective-permute-start(bf16[256,768]{1,0:T(8,128)(2,1)S(1)} %slice.324), channel_id=1, source_target_pairs={{0,8},{4,12},{8,0},{12,4},{16,24},{20,28},{24,16},{28,20},{1,9},{5... | collective-permute-start | bytes 1179656 | tf_op jit(solution)/shard_map/ppermute | solution.py:725
  224.1 20.9 %collective-permute-start.40 = (bf16[128,768]{1,0:T(8,128)(2,1)S(1)}, bf16[128,768]{1,0:T(8,128)(2,1)S(1)}, u32[]{:S(2)}, u32[]{:S(2)}) collective-permute-start(bf16[128,768]{1,0:T(8,128)(2,1)S(1)} %fusion.8), channel_id=1, source_target_pairs={{0,2},{1,3},{2,0},{3,1},{4,6},{5,7},{6,4},{7,5},{8,10},{9,11},{10,... | collective-permute-start | bytes 589832 | tf_op jit(solution)/shard_map/ppermute | solution.py:725
  231.0 16.1 %collective-permute-start.50 = (bf16[24,3840]{1,0:T(8,128)(2,1)S(1)}, bf16[24,3840]{1,0:T(8,128)(2,1)S(1)}, u32[]{:S(2)}, u32[]{:S(2)}) collective-permute-start(bf16[24,3840]{1,0:T(8,128)(2,1)S(1)} %add_convert_fusion.19), channel_id=1, source_target_pairs={{0,16},{4,20},{8,24},{12,28},{16,0},{20,4},{24,8},{28,12},{1,17},{... | collective-permute-start | bytes 552968 | tf_op jit(solution)/shard_map/ppermute | solution.py:725
  241.2 22.6 %collective-permute-start.49 = (bf16[48,2304]{1,0:T(8,128)(2,1)S(1)}, bf16[48,2304]{1,0:T(8,128)(2,1)S(1)}, u32[]{:S(2)}, u32[]{:S(2)}) collective-permute-start(bf16[48,2304]{1,0:T(8,128)(2,1)S(1)} %get-tuple-element.254), channel_id=1, source_target_pairs={{0,8},{4,12},{8,0},{12,4},{16,24},{20,28},{24,16},{28,20},{1,9},{5... | collective-permute-start | bytes 663560 | tf_op jit(solution)/shard_map/ppermute | solution.py:725
  241.4 26.1 %collective-permute-start.47 = (bf16[128,768]{1,0:T(8,128)(2,1)S(1)}, bf16[128,768]{1,0:T(8,128)(2,1)S(1)}, u32[]{:S(2)}, u32[]{:S(2)}) collective-permute-start(bf16[128,768]{1,0:T(8,128)(2,1)S(1)} %slice.329), channel_id=1, source_target_pairs={{0,16},{4,20},{8,24},{12,28},{16,0},{20,4},{24,8},{28,12},{1,17},{... | collective-permute-start | bytes 589832 | tf_op jit(solution)/shard_map/ppermute | solution.py:725
  244.8 19.1 %collective-permute-start.48 = (bf16[48,3072]{1,0:T(8,128)(2,1)S(1)}, bf16[48,3072]{1,0:T(8,128)(2,1)S(1)}, u32[]{:S(2)}, u32[]{:S(2)}) collective-permute-start(bf16[48,3072]{1,0:T(8,128)(2,1)S(1)} %pad_maximum_fusion.11), channel_id=1, source_target_pairs={{0,8},{4,12},{8,0},{12,4},{16,24},{20,28},{24,16},{28,20},{1,9},{5... | collective-permute-start | bytes 884744 | tf_op jit(solution)/shard_map/ppermute | solution.py:725
  245.0 35.6 %collective-permute-start.46 = (bf16[384,768]{1,0:T(8,128)(2,1)S(1)}, bf16[384,768]{1,0:T(8,128)(2,1)S(1)}, u32[]{:S(2)}, u32[]{:S(2)}) collective-permute-start(bf16[384,768]{1,0:T(8,128)(2,1)S(1)} %pad_maximum_fusion.4), channel_id=1, source_target_pairs={{0,4},{4,0},{8,12},{12,8},{16,20},{20,16},{24,28},{28,24},{1,5},{5... | collective-permute-start | bytes 1769480 | tf_op jit(solution)/shard_map/ppermute | solution.py:725
  247.2 12.3 %collective-permute-start.52 = (bf16[24,3840]{1,0:T(8,128)(2,1)S(1)}, bf16[24,3840]{1,0:T(8,128)(2,1)S(1)}, u32[]{:S(2)}, u32[]{:S(2)}) collective-permute-start(bf16[24,3840]{1,0:T(8,128)(2,1)S(1)} %add_convert_fusion.17), channel_id=1, source_target_pairs={{0,16},{4,20},{8,24},{12,28},{16,0},{20,4},{24,8},{28,12},{1,17},{... | collective-permute-start | bytes 552968 | tf_op jit(solution)/shard_map/ppermute | solution.py:725
  259.5 16.7 %collective-permute-start.54 = (bf16[48,3840]{1,0:T(8,128)(2,1)S(1)}, bf16[48,3840]{1,0:T(8,128)(2,1)S(1)}, u32[]{:S(2)}, u32[]{:S(2)}) collective-permute-start(bf16[48,3840]{1,0:T(8,128)(2,1)S(1)} %pad_maximum_fusion.9), channel_id=1, source_target_pairs={{0,8},{4,12},{8,0},{12,4},{16,24},{20,28},{24,16},{28,20},{1,9},{5... | collective-permute-start | bytes 1105928 | tf_op jit(solution)/shard_map/ppermute | solution.py:725
  263.8 8.9 %collective-permute-start.51 = (bf16[24,2304]{1,0:T(8,128)(2,1)S(1)}, bf16[24,2304]{1,0:T(8,128)(2,1)S(1)}, u32[]{:S(2)}, u32[]{:S(2)}) collective-permute-start(bf16[24,2304]{1,0:T(8,128)(2,1)S(1)} %add_convert_fusion.28), channel_id=1, source_target_pairs={{0,16},{4,20},{8,24},{12,28},{16,0},{20,4},{24,8},{28,12},{1,17},{... | collective-permute-start | bytes 331784 | tf_op jit(solution)/shard_map/ppermute | solution.py:725
  264.1 20.3 %collective-permute-start.58 = (bf16[96,3072]{1,0:T(8,128)(2,1)S(1)}, bf16[96,3072]{1,0:T(8,128)(2,1)S(1)}, u32[]{:S(2)}, u32[]{:S(2)}) collective-permute-start(bf16[96,3072]{1,0:T(8,128)(2,1)S(1)} %pad_maximum_fusion.5.own_ref), channel_id=1, source_target_pairs={{0,4},{4,0},{8,12},{12,8},{16,20},{20,16},{24,28},{28,24},{1,5},{5... | collective-permute-start | bytes 1769480 | tf_op jit(solution)/shard_map/ppermute | solution.py:725
  276.5 19.4 %collective-permute-start.56 = (bf16[96,3840]{1,0:T(8,128)(2,1)S(1)}, bf16[96,3840]{1,0:T(8,128)(2,1)S(1)}, u32[]{:S(2)}, u32[]{:S(2)}) collective-permute-start(bf16[96,3840]{1,0:T(8,128)(2,1)S(1)} %pad_maximum_fusion.1), channel_id=1, source_target_pairs={{0,4},{4,0},{8,12},{12,8},{16,20},{20,16},{24,28},{28,24},{1,5},{5... | collective-permute-start | bytes 2211848 | tf_op jit(solution)/shard_map/ppermute | solution.py:725
  280.3 15.8 %collective-permute-start.55 = (bf16[48,2304]{1,0:T(8,128)(2,1)S(1)}, bf16[48,2304]{1,0:T(8,128)(2,1)S(1)}, u32[]{:S(2)}, u32[]{:S(2)}) collective-permute-start(bf16[48,2304]{1,0:T(8,128)(2,1)S(1)} %pad_maximum_fusion.12), channel_id=1, source_target_pairs={{0,8},{4,12},{8,0},{12,4},{16,24},{20,28},{24,16},{28,20},{1,9},{5... | collective-permute-start | bytes 663560 | tf_op jit(solution)/shard_map/ppermute | solution.py:725
  296.3 10.6 %collective-permute-start.57 = (bf16[96,2304]{1,0:T(8,128)(2,1)S(1)}, bf16[96,2304]{1,0:T(8,128)(2,1)S(1)}, u32[]{:S(2)}, u32[]{:S(2)}) collective-permute-start(bf16[96,2304]{1,0:T(8,128)(2,1)S(1)} %pad_maximum_fusion.7), channel_id=1, source_target_pairs={{0,4},{4,0},{8,12},{12,8},{16,20},{20,16},{24,28},{28,24},{1,5},{5... | collective-permute-start | bytes 1327112 | tf_op jit(solution)/shard_map/ppermute | solution.py:725
  (62 other events, 375.7 us)

commit v5 on v4

--- a/solution.py
+++ b/solution.py
@@ -48,8 +48,12 @@
     return scale * gained - values * (scale * scale * scale) * along
 
 
-def head_rows(rows, head_size):
-    wide = rows.astype(jnp.float32)
+PAIR = 128
+STEP = 256
+
+
+def head_rows(rows, head_size, scale=1.0):
+    wide = rows.astype(jnp.float32) * scale
     lane = lax.broadcasted_iota(jnp.int32, wide.shape, 1)
     first = jnp.where(lane < head_size, wide, 0.0)
     second = jnp.where(lane >= head_size, wide, 0.0)
@@ -63,59 +67,63 @@
     ).T
 
 
-def self_scores(query, key, key_pos, low_pos, high_pos, score_scale):
-    scores = right_product(key, query) * score_scale
-    return jnp.where((key_pos >= low_pos) & (key_pos <= high_pos), scores, MASKED_SCORE)
-
-
 def self_forward_kernel(
     head_size, blocks, q_ref, k_ref, v_ref, pos_ref, low_ref, high_ref, o_ref, lse_ref
 ):
     score_scale = head_size ** (-0.5)
-    query = head_rows(q_ref[...], head_size)
     low_pos, high_pos = low_ref[...], high_ref[...]
     rows = k_ref.shape[0] // blocks
 
-    def scores_of(index):
-        span = pl.ds(pl.multiple_of(index * rows, rows), rows)
-        return self_scores(query, k_ref[span, :], pos_ref[span, :], low_pos, high_pos, score_scale)
-
-    def values_of(index):
-        return v_ref[pl.ds(pl.multiple_of(index * rows, rows), rows), :]
-
-    if blocks == 1:
-        scores = scores_of(0)
-        peak = jnp.max(scores, axis=0, keepdims=True)
-        weights = jnp.exp(scores - peak)
-        total = jnp.sum(weights, axis=0, keepdims=True)
-        running = left_product(values_of(0), to_low(weights))
-    else:
-        peak = lax.fori_loop(
-            0,
-            blocks,
-            lambda i, top: jnp.maximum(top, jnp.max(scores_of(i), axis=0, keepdims=True)),
-            jnp.full((1, query.shape[0]), MASKED_SCORE, jnp.float32),
-        )
-
-        def add(index, state):
-            total, running = state
-            weights = jnp.exp(scores_of(index) - peak)
-            return (
-                total + jnp.sum(weights, axis=0, keepdims=True),
-                running + left_product(values_of(index), to_low(weights)),
+    def span_of(index):
+        return pl.ds(pl.multiple_of(index * rows, rows), rows)
+
+    def visible(index):
+        key_pos = pos_ref[span_of(index), :]
+        return (key_pos >= low_pos) & (key_pos <= high_pos)
+
+    once = visible(0) if blocks == 1 else None
+    for p in range(q_ref.shape[1] // PAIR):
+        columns = pl.ds(p * PAIR, PAIR)
+        query = head_rows(q_ref[:, columns], head_size, score_scale)
+
+        def scores_of(index, query=query, columns=columns):
+            seen = visible(index) if once is None else once
+            scores = right_product(k_ref[span_of(index), columns], query)
+            return jnp.where(seen, scores, MASKED_SCORE)
+
+        if blocks == 1:
+            scores = scores_of(0)
+            peak = jnp.max(scores, axis=0, keepdims=True)
+            weights = jnp.exp(scores - peak)
+            total = jnp.sum(weights, axis=0, keepdims=True)
+            running = left_product(v_ref[:, columns], to_low(weights))
+        else:
+            peak = lax.fori_loop(
+                0,
+                blocks,
+                lambda i, top: jnp.maximum(top, jnp.max(scores_of(i), axis=0, keepdims=True)),
+                jnp.full((1, query.shape[0]), MASKED_SCORE, jnp.float32),
             )
 
-        total, running = lax.fori_loop(
-            0,
-            blocks,
-            add,
-            (
-                jnp.zeros((1, query.shape[0]), jnp.float32),
-                jnp.zeros((2 * head_size, query.shape[0]), jnp.float32),
-            ),
-        )
-    o_ref[...] = to_low(join_heads(running / total, head_size))
-    lse_ref[0] = peak + jnp.log(total)
+            def add(index, state, peak=peak, columns=columns, scores_of=scores_of):
+                total, running = state
+                weights = jnp.exp(scores_of(index) - peak)
+                return (
+                    total + jnp.sum(weights, axis=0, keepdims=True),
+                    running + left_product(v_ref[span_of(index), columns], to_low(weights)),
+                )
+
+            total, running = lax.fori_loop(
+                0,
+                blocks,
+                add,
+                (
+                    jnp.zeros((1, query.shape[0]), jnp.float32),
+                    jnp.zeros((2 * head_size, query.shape[0]), jnp.float32),
+                ),
+            )
+        o_ref[:, columns] = to_low(join_heads(running / total, head_size))
+        lse_ref[p] = peak + jnp.log(total)
 
 
 def self_backward_kernel(
@@ -133,62 +141,68 @@
     dkv_ref,
 ):
     score_scale = head_size ** (-0.5)
-    query = head_rows(q_ref[...], head_size)
-    grad = head_rows(do_ref[...], head_size)
     low_pos, high_pos = low_ref[...], high_ref[...]
-    log_total = lse_ref[0]
     rows = k_ref.shape[0] // blocks
 
     def span_of(index):
         return pl.ds(pl.multiple_of(index * rows, rows), rows)
 
-    def pair_of(index):
-        span = span_of(index)
-        scores = self_scores(
-            query, k_ref[span, :], pos_ref[span, :], low_pos, high_pos, score_scale
-        )
-        return jnp.exp(scores - log_total), right_product(v_ref[span, :], grad)
-
-    def finish(index, probs, dprobs, delta):
-        span = span_of(index)
-        dscores = to_low(probs * (dprobs - delta))
-        dkv_ref[0, span, :] = to_low(score_scale * matmul(dscores, query))
-        dkv_ref[1, span, :] = to_low(matmul(to_low(probs), grad))
-        return left_product(k_ref[span, :], dscores)
-
-    if blocks == 1:
-        probs, dprobs = pair_of(0)
-        delta = jnp.sum(probs * dprobs, axis=0, keepdims=True)
-        columns = finish(0, probs, dprobs, delta)
-    else:
-
-        def add_delta(index, delta):
-            probs, dprobs = pair_of(index)
-            return delta + jnp.sum(probs * dprobs, axis=0, keepdims=True)
-
-        delta = lax.fori_loop(
-            0, blocks, add_delta, jnp.zeros((1, query.shape[0]), jnp.float32)
-        )
-
-        def add_query(index, columns):
-            probs, dprobs = pair_of(index)
-            return columns + finish(index, probs, dprobs, delta)
-
-        columns = lax.fori_loop(
-            0, blocks, add_query, jnp.zeros((2 * head_size, query.shape[0]), jnp.float32)
-        )
-    dq_ref[...] = to_low(score_scale * join_heads(columns, head_size))
-
-
-def self_specs(tok_count, key_count, pairs):
-    wide = 128
+    def visible(index):
+        key_pos = pos_ref[span_of(index), :]
+        return (key_pos >= low_pos) & (key_pos <= high_pos)
+
+    once = visible(0) if blocks == 1 else None
+    for p in range(q_ref.shape[1] // PAIR):
+        columns = pl.ds(p * PAIR, PAIR)
+        query = head_rows(q_ref[:, columns], head_size, score_scale)
+        grad = head_rows(do_ref[:, columns], head_size)
+        log_total = lse_ref[p]
+
+        def pair_of(index, query=query, grad=grad, log_total=log_total, columns=columns):
+            span = span_of(index)
+            seen = visible(index) if once is None else once
+            scores = jnp.where(seen, right_product(k_ref[span, columns], query), MASKED_SCORE)
+            return jnp.exp(scores - log_total), right_product(v_ref[span, columns], grad)
+
+        def finish(index, probs, dprobs, delta, query=query, grad=grad, columns=columns):
+            span = span_of(index)
+            dscores = to_low(probs * (dprobs - delta))
+            dkv_ref[0, span, columns] = to_low(matmul(dscores, query))
+            dkv_ref[1, span, columns] = to_low(matmul(to_low(probs), grad))
+            return left_product(k_ref[span, columns], dscores)
+
+        if blocks == 1:
+            probs, dprobs = pair_of(0)
+            delta = jnp.sum(probs * dprobs, axis=0, keepdims=True)
+            turned = finish(0, probs, dprobs, delta)
+        else:
+
+            def add_delta(index, delta, pair_of=pair_of):
+                probs, dprobs = pair_of(index)
+                return delta + jnp.sum(probs * dprobs, axis=0, keepdims=True)
+
+            delta = lax.fori_loop(
+                0, blocks, add_delta, jnp.zeros((1, query.shape[0]), jnp.float32)
+            )
+
+            def add_query(index, turned, delta=delta, pair_of=pair_of, finish=finish):
+                probs, dprobs = pair_of(index)
+                return turned + finish(index, probs, dprobs, delta)
+
+            turned = lax.fori_loop(
+                0, blocks, add_query, jnp.zeros((2 * head_size, query.shape[0]), jnp.float32)
+            )
+        dq_ref[:, columns] = to_low(score_scale * join_heads(turned, head_size))
+
+
+def self_specs(tok_count, key_count, steps):
     return (
-        pl.BlockSpec((tok_count, wide), lambda i: (0, i)),
-        pl.BlockSpec((key_count, wide), lambda i: (0, i)),
-        pl.BlockSpec((key_count, wide), lambda i: (0, pairs + i)),
+        pl.BlockSpec((tok_count, STEP), lambda i: (0, i)),
+        pl.BlockSpec((key_count, STEP), lambda i: (0, i)),
+        pl.BlockSpec((key_count, STEP), lambda i: (0, steps + i)),
         pl.BlockSpec((key_count, 1), lambda i: (0, 0)),
         pl.BlockSpec((1, 2 * tok_count), lambda i: (0, 0)),
-        pl.BlockSpec((1, 1, 2 * tok_count), lambda i: (i, 0, 0)),
+        pl.BlockSpec((STEP // PAIR, 1, 2 * tok_count), lambda i: (i, 0, 0)),
     )
 
 
@@ -196,17 +210,17 @@
     tok_count, feature_width = query.shape
     key_count = key_value.shape[0]
     head_size = feature_width // H
-    pairs = H // 2
+    steps = feature_width // STEP
     blocks = max(1, key_count // KEY_BLOCK)
-    rows, keys, values, pos, edge, lse = self_specs(tok_count, key_count, pairs)
+    rows, keys, values, pos, edge, lse = self_specs(tok_count, key_count, steps)
     return pl.pallas_call(
         functools.partial(self_forward_kernel, head_size, blocks),
-        grid=(pairs,),
+        grid=(steps,),
         in_specs=[rows, keys, values, pos, edge, edge],
         out_specs=[rows, lse],
         out_shape=[
             jax.ShapeDtypeStruct((tok_count, feature_width), jnp.bfloat16),
-            jax.ShapeDtypeStruct((pairs, 1, 2 * tok_count), jnp.float32),
+            jax.ShapeDtypeStruct((H // 2, 1, 2 * tok_count), jnp.float32),
         ],
         cost_estimate=lasting(7.6),
         name="self_forward",
@@ -217,14 +231,14 @@
     tok_count, feature_width = query.shape
     key_count = key_value.shape[0]
     head_size = feature_width // H
-    pairs = H // 2
+    steps = feature_width // STEP
     blocks = max(1, key_count // KEY_BLOCK)
-    rows, keys, values, pos, edge, lse = self_specs(tok_count, key_count, pairs)
+    rows, keys, values, pos, edge, lse = self_specs(tok_count, key_count, steps)
     return pl.pallas_call(
         functools.partial(self_backward_kernel, head_size, blocks),
-        grid=(pairs,),
+        grid=(steps,),
         in_specs=[rows, keys, values, rows, pos, edge, edge, lse],
-        out_specs=[rows, pl.BlockSpec((2, key_count, 128), lambda i: (0, 0, i))],
+        out_specs=[rows, pl.BlockSpec((2, key_count, STEP), lambda i: (0, 0, i))],
         out_shape=[
             jax.ShapeDtypeStruct((tok_count, feature_width), jnp.bfloat16),
             jax.ShapeDtypeStruct((2, key_count, feature_width), jnp.bfloat16),
@@ -454,16 +468,20 @@
         fill(wout_ref, out_refs, index_ref)
 
     keys = enc_ref.shape[0] // stretches
-    parts = []
-    for s in range(stretches):
-        span = pl.ds(s * keys, keys)
-        query = head_rows(q_ref[pl.ds(s * STRETCH, STRETCH), :], head_size)
-        scores = right_product(kv_ref[0, span, :], query) * score_scale
-        weights = jnp.exp(scores - jnp.max(scores, axis=0, keepdims=True))
-        probs = to_low(weights / jnp.sum(weights, axis=0, keepdims=True))
-        parts.append(join_heads(left_product(kv_ref[1, span, :], probs), head_size))
+    sides = []
+    for p in range(wide // PAIR):
+        part = pl.ds(p * PAIR, PAIR)
+        parts = []
+        for s in range(stretches):
+            span = pl.ds(s * keys, keys)
+            query = head_rows(q_ref[pl.ds(s * STRETCH, STRETCH), part], head_size, score_scale)
+            scores = right_product(kv_ref[0, span, part], query)
+            weights = jnp.exp(scores - jnp.max(scores, axis=0, keepdims=True))
+            probs = to_low(weights / jnp.sum(weights, axis=0, keepdims=True))
+            parts.append(join_heads(left_product(kv_ref[1, span, part], probs), head_size))
+        sides.append(jnp.concatenate(parts, axis=0))
     columns = pl.ds(pl.multiple_of(pair * wide, wide), wide)
-    cross_ref[:, columns] = to_low(jnp.concatenate(parts, axis=0))
+    cross_ref[:, columns] = to_low(jnp.concatenate(sides, axis=1))
 
     @pl.when(pair == pl.num_programs(0) - 1)
     def _():
@@ -474,22 +492,22 @@
 
 def cross_forward(index, query, enc_rows, after_attn, keep_rows, gain_rows, pieces, stretches):
     tok, width = query.shape
-    pairs = H // 2
+    pairs = width // STEP
     keys = enc_rows.shape[0]
-    inputs = [(query, pl.BlockSpec((tok, 128), lambda i, _: (0, i)))]
+    inputs = [(query, pl.BlockSpec((tok, STEP), lambda i, _: (0, i)))]
     inputs += [(value, whole(value)) for value in (enc_rows, after_attn, keep_rows, gain_rows)]
     for first in (0, pairs):
         inputs += [
-            (piece, pl.BlockSpec((piece.shape[0], 128), lambda i, _, f=first: (0, f + i)))
+            (piece, pl.BlockSpec((piece.shape[0], STEP), lambda i, _, f=first: (0, f + i)))
             for piece in pieces
         ]
     inputs += [(piece, pl.BlockSpec((piece.shape[0], width), lambda i, _: (0, 2))) for piece in pieces]
     outputs = [
-        ((2, keys, width), jnp.bfloat16, pl.BlockSpec((2, keys, 128), lambda i, _: (0, 0, i))),
+        ((2, keys, width), jnp.bfloat16, pl.BlockSpec((2, keys, STEP), lambda i, _: (0, 0, i))),
         ((tok, width), jnp.bfloat16, const((tok, width))),
         ((tok, width), jnp.float32, const((tok, width))),
         ((tok, width), jnp.bfloat16, const((tok, width))),
-        ((2, width, width), jnp.bfloat16, pl.BlockSpec((2, width, 128), lambda i, _: (0, 0, i))),
+        ((2, width, width), jnp.bfloat16, pl.BlockSpec((2, width, STEP), lambda i, _: (0, 0, i))),
         ((width, width), jnp.bfloat16, const((width, width))),
     ]
     return chain_call(
@@ -641,7 +659,6 @@
     pair = pl.program_id(0)
     wide = q_ref.shape[1]
     keys = kv_ref.shape[1] // stretches
-    columns = pl.ds(pl.multiple_of(pair * wide, wide), wide)
 
     @pl.when(pair == 0)
     def _():
@@ -655,22 +672,28 @@
         first_ref[...] = branch
         do_ref[...] = to_low(right_product(branch, wout_ref[...]))
 
-    parts = []
-    for s in range(stretches):
-        rows = pl.ds(s * STRETCH, STRETCH)
-        span = pl.ds(s * keys, keys)
-        query = head_rows(q_ref[rows, :], head_size)
-        grad = head_rows(do_ref[rows, columns], head_size)
-        scores = right_product(kv_ref[0, span, :], query) * score_scale
-        weights = jnp.exp(scores - jnp.max(scores, axis=0, keepdims=True))
-        probs = weights / jnp.sum(weights, axis=0, keepdims=True)
-        dprobs = right_product(kv_ref[1, span, :], grad)
-        delta = jnp.sum(probs * dprobs, axis=0, keepdims=True)
-        dscores = to_low(probs * (dprobs - delta))
-        dkv_ref[0, span, :] = to_low(score_scale * matmul(dscores, query))
-        dkv_ref[1, span, :] = to_low(matmul(to_low(probs), grad))
-        parts.append(join_heads(left_product(kv_ref[0, span, :], dscores), head_size))
-    dq_ref[:, columns] = to_low(score_scale * jnp.concatenate(parts, axis=0))
+    sides = []
+    for p in range(wide // PAIR):
+        part = pl.ds(p * PAIR, PAIR)
+        place = pl.ds(pl.multiple_of(pair * wide + p * PAIR, PAIR), PAIR)
+        parts = []
+        for s in range(stretches):
+            rows = pl.ds(s * STRETCH, STRETCH)
+            span = pl.ds(s * keys, keys)
+            query = head_rows(q_ref[rows, part], head_size, score_scale)
+            grad = head_rows(do_ref[rows, place], head_size)
+            scores = right_product(kv_ref[0, span, part], query)
+            weights = jnp.exp(scores - jnp.max(scores, axis=0, keepdims=True))
+            probs = weights / jnp.sum(weights, axis=0, keepdims=True)
+            dprobs = right_product(kv_ref[1, span, part], grad)
+            delta = jnp.sum(probs * dprobs, axis=0, keepdims=True)
+            dscores = to_low(probs * (dprobs - delta))
+            dkv_ref[0, span, part] = to_low(matmul(dscores, query))
+            dkv_ref[1, span, part] = to_low(matmul(to_low(probs), grad))
+            parts.append(join_heads(left_product(kv_ref[0, span, part], dscores), head_size))
+        sides.append(jnp.concatenate(parts, axis=0))
+    columns = pl.ds(pl.multiple_of(pair * wide, wide), wide)
+    dq_ref[:, columns] = to_low(score_scale * jnp.concatenate(sides, axis=1))
 
     @pl.when(pair == pl.num_programs(0) - 1)
     def _():
@@ -692,8 +715,8 @@
 ):
     tok, width = query.shape
     keys = key_value.shape[1]
-    block = pl.BlockSpec((tok, 128), lambda i, _: (0, i))
-    planes = pl.BlockSpec((2, keys, 128), lambda i, _: (0, 0, i))
+    block = pl.BlockSpec((tok, STEP), lambda i, _: (0, i))
+    planes = pl.BlockSpec((2, keys, STEP), lambda i, _: (0, 0, i))
     inputs = [(query, block), (key_value, planes), (cotangent, whole(cotangent))]
     inputs += [
         (value, whole(value))
@@ -711,7 +734,7 @@
     return chain_call(
         functools.partial(cross_backward_kernel, width // H, stretches),
         "cross_backward",
-        (H // 2,),
+        (width // STEP,),
         index,
         inputs,
         outputs,
@@ -778,7 +801,7 @@
             jax.ShapeDtypeStruct((1, 2 * tok_count), jnp.int32),
             jax.ShapeDtypeStruct((tok_count, 1), jnp.float32),
         ],
-        cost_estimate=lasting(1.5),
+        cost_estimate=lasting(0.01),
         name="positions",
     )(index, deal_row, lengths_row)
 
@@ -1100,6 +1123,7 @@
         stretch_count,
     )
     across_in = after(across_in, grad_attended)
+    out_sibling = swap(after(out_send, grad_attended), "fsdp", 1)
     arrived = down.hold(grad_attended)
     keep_cross, send_cross = wide_products(
         place,
@@ -1128,6 +1152,8 @@
         high_pos,
         log_total,
     )
+    out_sibling = after(out_sibling, grad_query)
+    out_far = swap(add_low(out_across, out_sibling[1]), "fsdp", 2)
     ready = inner.move(down.move(grad_query))
     keep_attn, send_attn = wide_products(
         place,
@@ -1143,17 +1169,13 @@
     ready = cross.move(norm1_all)
     norm1 = Steps(sum_to_owner(after(norm1_all, ready)))
     grad_enc = enc_terms(place, after(grad_cross_pair, ready), w_ckv)
-    out_sibling = swap(after(out_send, grad_enc), "fsdp", 1)
-    ready = grad_enc
-    for step in (attn, down, inner, cross, down, inner, attn, norm1):
-        ready = step.move(ready)
-    out_sibling = after(out_sibling, ready)
-    out_far = swap(add_low(out_across, out_sibling[1]), "fsdp", 2)
-    for step in (cross, attn, norm1, inner, down):
-        ready = step.move(ready)
+    ready = attn.move(grad_enc)
     layer_out = after_cross + (
         out_own + out_sibling[0].astype(jnp.float32) + after(out_far, ready).astype(jnp.float32)
     )
+    ready = down.move(ready, layer_out)
+    for step in (inner, cross, down, inner, attn, norm1, cross, attn, down, inner, norm1):
+        ready = step.move(ready)
     for step in (cross, attn, inner):
         ready = step.move(ready)
     ready = down.finish(norm1.finish(ready))
@@ -1163,29 +1185,25 @@
         input_rows, inverse_rms(input_rows), after(gain_rows, ready)[0:1], grad_norm1
     )
     total_down = finished(down.result, 0, feature_width)
-    ready = after(ready, total_down, grad_input, layer_out)
-    for step in (cross, attn):
-        ready = step.move(ready)
+    ready = cross.move(ready, total_down, grad_input)
+    ready = attn.move(ready)
+    ready = cross.move(ready)
+    ready = attn.move(ready)
     ready = inner.finish(ready)
     total_in, gain_three = inner_out(place, inner.result, mlp_in, norm_gains[2])
-    ready = after(ready, total_in)
-    while attn.result is None or cross.result is None:
-        for step in (cross, attn):
-            ready = step.move(ready)
-    halves_cross, halves_attn = cross.result, attn.result
+    cross.move(ready, total_in)
+    ready = cross.finish(ready)
     d = feature_width
-    total_cout = finished(halves_cross, 0, d)
-    total_cq = finished(halves_cross, d, d)
-    total_ckv = finished(halves_cross, 2 * d, 2 * d)
-    total_out = finished(halves_cross, 4 * d, d)
-    total_qkv = finished(halves_attn, 0, 3 * d)
-    grad_gains = jnp.stack(
-        [
-            gain_gradient(attn_qkv, total_qkv, norm_gains[0]),
-            gain_gradient(cross_q, total_cq, norm_gains[1]),
-            gain_three,
-        ]
-    )
+    total_cout = finished(cross.result, 0, d)
+    total_cq = finished(cross.result, d, d)
+    total_ckv = finished(cross.result, 2 * d, 2 * d)
+    total_out = finished(cross.result, 4 * d, d)
+    gain_two = gain_gradient(cross_q, total_cq, norm_gains[1])
+    attn.move(ready, total_cout, total_ckv, total_out, gain_two)
+    attn.finish(ready)
+    total_qkv = finished(attn.result, 0, 3 * d)
+    gain_one = gain_gradient(attn_qkv, total_qkv, norm_gains[0])
+    grad_gains = jnp.stack([gain_one, gain_two, gain_three])
     return (
         layer_out[None],
         grad_input[None],

time: 310 us -> 305 us (0.984)
  starting transfers between devices: 69.9 us -> 58.8 us
  waiting for transfers between devices: 85.4 us -> 95.4 us
  Pallas kernels: 105 us -> 99.9 us
    ppermute x59, starting transfers between devices: 69.9 us -> 58.8 us  [swap(): return lax.ppermute(values, axis, [(i, i ^ bit) for i in range(count)])]
    ppermute x59, waiting for transfers between devices: 85.4 us -> 95.4 us  [swap(): return lax.ppermute(values, axis, [(i, i ^ bit) for i in range(count)])]
    pallas_call x8, Pallas kernels: 66.6 us -> 62.5 us  [chain_call(): pl.pallas_call(kernel, grid_spec=pltpu.PrefetchScalarGridSpec(num_scalar_...]
    unnamed x105 -> x103, local copies, waits for them, and re-layouts: 7.93 us -> 6.86 us
  transfers between devices with their start and end apart: 59 -> 59, of which waited for: 24 -> 26; matrix products, arithmetic and copies ran while one was open for 13% -> 13% of each run, Pallas kernels for 28% -> 27%
where the time goes in v5:
time: 305 us; the launch traced here: 304 us
  Pallas kernels  99.9 us (33%)
  waiting for transfers between devices  95.4 us (31%)
  starting transfers between devices  58.8 us (19%)
  other arithmetic  34.8 us (11%)
  local copies, waits for them, and re-layouts  13.7 us (4%)
    ppermute x59, waiting for transfers between devices, swap(): return lax.ppermute(values, axis, [(i, i ^ bit) for i in range(count)])  95.4 us
    pallas_call x8, Pallas kernels, chain_call(): pl.pallas_call(kernel, grid_spec=pltpu.PrefetchScalarGridSpec(num_scalar_...  62.5 us
    ppermute x59, starting transfers between devices, swap(): return lax.ppermute(values, axis, [(i, i ^ bit) for i in range(count)])  58.8 us
    convert_element_type x20, other arithmetic, to_low(): return values.astype(jnp.bfloat16)  18.6 us
    pallas_call x2, Pallas kernels, wide_products(): pl.pallas_call(functools.partial(products_kernel, tiles, rows, chunks), g...  16.3 us
    pallas_call x1, Pallas kernels, self_backward(): pl.pallas_call(functools.partial(self_backward_kernel, head_size, blocks)...  9.34 us
    pallas_call x1, Pallas kernels, self_forward(): pl.pallas_call(functools.partial(self_forward_kernel, head_size, blocks),...  7.13 us
    unnamed x103, local copies, waits for them, and re-layouts  6.86 us
  transfers between devices with their start and end apart: 59, of which 26 were waited for; matrix products, arithmetic and copies ran while one was open for 13% of the time, Pallas kernels for 27%

profile of v5, /device:TPU:0, one launch (start us, length us, event | category | flops | bytes accessed | tf_op | source)
XLA Modules:
  0.0 304.1 jit_solution(11120427317938589727)
XLA Ops:
  0.7 3.1 %collective-permute-start = (bf16[128,768]{1,0:T(8,128)(2,1)}, bf16[128,768]{1,0:T(8,128)(2,1)}, u32[]{:S(2)}, u32[]{:S(2)}) collective-permute-start(bf16[128,768]{1,0:T(8,128)(2,1)} %bitcast.27), channel_id=1, source_target_pairs={{0,8},{4,12},{8,0},{12,4},{16,24},{20,28},{24,16},{28,20},{1,9},{5... | collective-permute-start | bytes 589832 | tf_op jit(solution)/shard_map/ppermute | solution.py:748
  3.7 2.5 collective-permute-start.2
  13.3 3.2 %collective-permute-done.2 = bf16[128,768]{1,0:T(8,128)(2,1)S(1)} collective-permute-done((bf16[128,768]{1,0:T(8,128)(2,1)}, bf16[128,768]{1,0:T(8,128)(2,1)S(1)}, u32[]{:S(2)}, u32[]{:S(2)}) %collective-permute-start.2) | collective-permute-done | bytes 196640 | tf_op jit(solution)/shard_map/ppermute | solution.py:748
  16.5 7.4 %collective-permute-done.1 = bf16[128,768]{1,0:T(8,128)(2,1)} collective-permute-done((bf16[128,768]{1,0:T(8,128)(2,1)}, bf16[128,768]{1,0:T(8,128)(2,1)}, u32[]{:S(2)}, u32[]{:S(2)}) %collective-permute-start.1) | collective-permute-done | bytes 196640 | tf_op jit(solution)/shard_map/ppermute | solution.py:748
  33.3 5.9 %collective-permute-done.4.refs_4_ = bf16[128,768]{1,0:T(8,128)(2,1)S(1)} collective-permute-done((bf16[128,768]{1,0:T(8,128)(2,1)}, bf16[128,768]{1,0:T(8,128)(2,1)S(1)}, u32[]{:S(2)}, u32[]{:S(2)}) %collective-permute-start.4) | collective-permute-done | bytes 196640 | tf_op jit(solution)/shard_map/ppermute | solution.py:748
  39.9 3.0 held_rows.1
  42.9 9.4 %project.1 = (bf16[128,768]{1,0:T(8,128)(2,1)}, bf16[1024,1536]{1,0:T(8,128)(2,1)}, bf16[1024,768]{1,0:T(8,128)(2,1)}, bf16[768,2304]{1,0:T(8,128)(2,1)}, f32[8,768]{1,0:T(8,128)}) custom-call(s32[3]{0:T(128)} %pad_add_fusion.index_ref, bf16[1024,768]{1,0:T(8,128)(2,1)} %get-tuple-element.119.rows_ref, f32[1024,1]{1,0:T(8,128)} %get-tuple-element.120.scale_ref, ...), custom_call_target="tpu_custom_call" | custom-call | flops 103499997184 | bytes 9000000 | tf_op jit(solution)/shard_map/project/pallas_call | solution.py:275
  52.9 7.1 %self_forward.1 = (bf16[128,768]{1,0:T(8,128)(2,1)}, f32[6,1,256]{2,1,0:T(1,128)}) custom-call(bf16[128,768]{1,0:T(8,128)(2,1)} %get-tuple-element.125.q_ref, bf16[1024,1536]{1,0:T(8,128)(2,1)} %get-tuple-element.126.k_ref.v_ref, bf16[1024,1536]{1,0:T(8,128)(2,1)} %get-tuple-element.126.k_ref.v_ref, s32[1024,1]{1,0:T(8,128)} %get-tuple-element.127.pos_ref, ...), custom_call_target="tpu_custom_call" | custom-call | flops 87399997440 | bytes 7600000 | tf_op jit(solution)/shard_map/self_forward/pallas_call | solution.py:216
  60.1 5.9 %collective-permute-done.13.refs_7_.refs_11_.refs_15_ = bf16[192,2304]{1,0:T(8,128)(2,1)} collective-permute-done((bf16[192,2304]{1,0:T(8,128)(2,1)}, bf16[192,2304]{1,0:T(8,128)(2,1)}, u32[]{:S(2)}, u32[]{:S(2)}) %collective-permute-start.13) | collective-permute-done | bytes 884768 | tf_op jit(solution)/shard_map/ppermute | solution.py:748
  68.3 4.2 %attend_out.1 = (f32[128,768]{1,0:T(8,128)}, bf16[128,768]{1,0:T(8,128)(2,1)}, bf16[128,768]{1,0:T(8,128)(2,1)}, bf16[768,1536]{1,0:T(8,128)(2,1)}) custom-call(s32[3]{0:T(128)} %pad_add_fusion.index_ref, bf16[128,768]{1,0:T(8,128)(2,1)} %get-tuple-element.130.att_ref.refs_7_, bf16[128,768]{1,0:T(8,128)(2,1)} %bitcast.32, ...), custom_call_target="tpu_custom_call" | custom-call | flops 50600001536 | bytes 4400000 | tf_op jit(solution)/shard_map/attend_out/pallas_call | solution.py:275
  73.8 9.5 %cross_forward.1 = (bf16[2,512,768]{2,1,0:T(8,128)(2,1)}, bf16[128,768]{1,0:T(8,128)(2,1)}, f32[128,768]{1,0:T(8,128)}, bf16[128,768]{1,0:T(8,128)(2,1)}, bf16[2...) custom-call(s32[3]{0:T(128)} %pad_add_fusion.index_ref, bf16[128,768]{1,0:T(8,128)(2,1)} %get-tuple-element.135.refs_0_, ...), custom_call_target="tpu_custom_call" | custom-call | flops 141450002432 | bytes 12300000 | tf_op jit(solution)/shard_map/cross_forward/pallas_call | solution.py:275
  83.4 2.9 collective-permute-done.19.refs_7_
  88.4 5.6 %collective-permute-done.16.refs_2_ = bf16[128,768]{1,0:T(8,128)(2,1)S(1)} collective-permute-done((bf16[128,768]{1,0:T(8,128)(2,1)}, bf16[128,768]{1,0:T(8,128)(2,1)S(1)}, u32[]{:S(2)}, u32[]{:S(2)}) %collective-permute-start.16) | collective-permute-done | bytes 196640 | tf_op jit(solution)/shard_map/ppermute | solution.py:748
  96.5 9.9 %mlp_share.1 = (f32[128,768]{1,0:T(8,128)}, bf16[128,768]{1,0:T(8,128)(2,1)}, bf16[128,768]{1,0:T(8,128)(2,1)}, bf16[128,768]{1,0:T(8,128)(2,1)}, f32[128,768]{1...) custom-call(s32[3]{0:T(128)} %pad_add_fusion.index_ref, ...), custom_call_target="tpu_custom_call" | custom-call | flops 126500003840 | bytes 11000000 | tf_op jit(solution)/shard_map/mlp_share/pallas_call | solution.py:275
  108.5 1.9 slice.242
  115.8 2.5 collective-permute-done.23.refs_12_
  119.0 10.9 %cross_backward.1 = (bf16[128,768]{1,0:T(8,128)(2,1)}, bf16[2,512,768]{2,1,0:T(8,128)(2,1)}, f32[128,768]{1,0:T(8,128)}, bf16[128,768]{1,0:T(8,128)(2,1)}, bf16[...) custom-call(s32[3]{0:T(128)} %pad_add_fusion.index_ref, bf16[128,768]{1,0:T(8,128)(2,1)} %get-tuple-element.135.refs_0_, ...), custom_call_target="tpu_custom_call" | custom-call | flops 149500002304 | bytes 13000000 | tf_op jit(solution)/shard_map/cross_backward/pallas_call | solution.py:275
  131.1 8.3 %wide_products.2 = (bf16[384,3840]{1,0:T(8,128)(2,1)}, bf16[384,3840]{1,0:T(8,128)(2,1)}) custom-call(s32[3]{0:T(128)} %pad_add_fusion.index_ref, bf16[128,768]{1,0:T(8,128)(2,1)} %get-tuple-element.157.refs_0_, bf16[128,768]{1,0:T(8,128)(2,1)} %get-tuple-element.158.refs_1_, bf16[128,768]{1,0:T(8,128)(2,1)} %get-tuple-element.159.refs_2_, ...), custom_call_target="tpu_custom_call" | custom-call | flops 94299996160 | bytes 8199999 | tf_op jit(solution)/shard_map/wide_products/pallas_call | solution.py:866
  145.2 2.9 add_convert_fusion
  149.6 9.3 %self_backward.1 = (bf16[128,768]{1,0:T(8,128)(2,1)}, bf16[2,1024,768]{2,1,0:T(8,128)(2,1)}) custom-call(bf16[128,768]{1,0:T(8,128)(2,1)} %get-tuple-element.125.q_ref, bf16[1024,1536]{1,0:T(8,128)(2,1)} %get-tuple-element.126.k_ref.v_ref, bf16[1024,1536]{1,0:T(8,128)(2,1)} %get-tuple-element.126.k_ref.v_ref, bf16[128,768]{1,0:T(8,128)(2,1)} %get-tuple-element.174.do_ref, ...), custom_call_target="tpu_custom_call" | custom-call | flops 117300002816 | bytes 10200000 | tf_op jit(solution)/shard_map/self_backward/pallas_call | solution.py:237
  158.9 1.6 add_convert_fusion.25
  161.5 1.8 collective-permute-start.37
  166.0 8.0 %wide_products.3 = (bf16[384,2304]{1,0:T(8,128)(2,1)}, bf16[384,2304]{1,0:T(8,128)(2,1)}) custom-call(s32[3]{0:T(128)} %pad_add_fusion.index_ref, bf16[1024,768]{1,0:T(8,128)(2,1)} %get-tuple-element.179.refs_0_.refs_2_, bf16[128,768]{1,0:T(8,128)(2,1)} %get-tuple-element.182.refs_1_.query_ref, bf16[1024,768]{1,0:T(8,128)(2,1)} %get-tuple-element.179.refs_0_.refs_2_, ...), custom_call_target="tpu_custom_call" | custom-call | flops 115000000 | bytes 10000 | tf_op jit(solution)/shard_map/wide_products/pallas_call | solution.py:866
  174.0 8.0 %norm_terms.1 = (bf16[1024,768]{1,0:T(8,128)(2,1)}, f32[128,768]{1,0:T(8,128)}) custom-call(s32[3]{0:T(128)} %pad_add_fusion.index_ref, bf16[2,1024,768]{2,1,0:T(8,128)(2,1)} %get-tuple-element.186.refs_3_.refs_4_.pair_ref, bf16[128,768]{1,0:T(8,128)(2,1)} %get-tuple-element.182.refs_1_.query_ref, bf16[768,2304]{1,0:T(8,128)(2,1)} %get-tuple-element.187.w_ref), custom_call_target="tpu_custom_call" | custom-call | flops 115000000 | bytes 10000 | tf_op jit(solution)/shard_map/norm_terms/pallas_call | solution.py:275
  183.5 3.4 %add_convert_fusion.3 = (bf16[96,3840]{1,0:T(8,128)(2,1)}, bf16[96,3840]{1,0:T(8,128)(2,1)}) fusion(bf16[192,3840]{1,0:T(8,128)(2,1)} %collective-permute-done.33, bf16[384,3840]{1,0:T(8,128)(2,1)} %collective-permute-done.28, bf16[384,3840]{1,0:T(8,128)(2,1)S(1)} %copy-done.2), kind=kLoop, calls=%fused_computation.6 | loop fusion | flops 4423680 | bytes 5898240 | tf_op jit(solution)/shard_map/convert_element_type | solution.py:26
  188.4 5.4 %enc_terms.1 = f32[512,768]{1,0:T(8,128)} custom-call(s32[3]{0:T(128)} %pad_add_fusion.index_ref, bf16[2,512,768]{2,1,0:T(8,128)(2,1)} %get-tuple-element.190.refs_5_.refs_6_.pair_ref, bf16[2,768,768]{2,1,0:T(8,128)(2,1)} %get-tuple-element.191.w_ref), custom_call_target="tpu_custom_call" | custom-call | flops 46000001024 | bytes 4000000 | tf_op jit(solution)/shard_map/enc_terms/pallas_call | solution.py:275
  199.4 3.1 %collective-permute-start.35 = (bf16[96,768]{1,0:T(8,128)(2,1)S(1)}, bf16[96,768]{1,0:T(8,128)(2,1)S(1)}, u32[]{:S(2)}, u32[]{:S(2)}) collective-permute-start(bf16[96,768]{1,0:T(8,128)(2,1)S(1)} %add_convert_fusion.23), channel_id=1, source_target_pairs={{0,16},{4,20},{8,24},{12,28},{16,0},{20,4},{24,8},{28,12},{1,17},{... | collective-permute-start | bytes 442376 | tf_op jit(solution)/shard_map/ppermute | solution.py:748
  203.6 3.1 %collective-permute-done.36 = bf16[96,3840]{1,0:T(8,128)(2,1)} collective-permute-done((bf16[96,3840]{1,0:T(8,128)(2,1)}, bf16[96,3840]{1,0:T(8,128)(2,1)}, u32[]{:S(2)}, u32[]{:S(2)}) %collective-permute-start.36) | collective-permute-done | bytes 737312 | tf_op jit(solution)/shard_map/ppermute | solution.py:748
  207.9 2.0 collective-permute-start.42
  209.9 2.3 collective-permute-done.35
  212.3 1.7 collective-permute-done.40
  219.1 4.3 %collective-permute-done.43 = bf16[512,768]{1,0:T(8,128)(2,1)S(1)} collective-permute-done((bf16[512,768]{1,0:T(8,128)(2,1)S(1)}, bf16[512,768]{1,0:T(8,128)(2,1)S(1)}, u32[]{:S(2)}, u32[]{:S(2)}) %collective-permute-start.43) | collective-permute-done | bytes 786464 | tf_op jit(solution)/shard_map/ppermute | solution.py:748
  223.7 2.0 collective-permute-start.45
  227.4 3.6 %collective-permute-done.41 = bf16[96,2304]{1,0:T(8,128)(2,1)S(1)} collective-permute-done((bf16[96,2304]{1,0:T(8,128)(2,1)S(1)}, bf16[96,2304]{1,0:T(8,128)(2,1)S(1)}, u32[]{:S(2)}, u32[]{:S(2)}) %collective-permute-start.41) | collective-permute-done | bytes 442400 | tf_op jit(solution)/shard_map/ppermute | solution.py:748
  231.0 1.8 collective-permute-start.49
  232.9 2.5 collective-permute-done.38
  237.1 10.2 %collective-permute-done.45 = bf16[256,768]{1,0:T(8,128)(2,1)S(1)} collective-permute-done((bf16[256,768]{1,0:T(8,128)(2,1)S(1)}, bf16[256,768]{1,0:T(8,128)(2,1)S(1)}, u32[]{:S(2)}, u32[]{:S(2)}) %collective-permute-start.45) | collective-permute-done | bytes 393248 | tf_op jit(solution)/shard_map/ppermute | solution.py:748
  248.3 2.2 collective-permute-start.52
  250.6 3.3 %collective-permute-done.49 = bf16[48,2304]{1,0:T(8,128)(2,1)S(1)} collective-permute-done((bf16[48,2304]{1,0:T(8,128)(2,1)S(1)}, bf16[48,2304]{1,0:T(8,128)(2,1)S(1)}, u32[]{:S(2)}, u32[]{:S(2)}) %collective-permute-start.49) | collective-permute-done | bytes 221216 | tf_op jit(solution)/shard_map/ppermute | solution.py:748
  254.0 3.9 %collective-permute-done.48 = bf16[48,3072]{1,0:T(8,128)(2,1)S(1)} collective-permute-done((bf16[48,3072]{1,0:T(8,128)(2,1)S(1)}, bf16[48,3072]{1,0:T(8,128)(2,1)S(1)}, u32[]{:S(2)}, u32[]{:S(2)}) %collective-permute-start.48) | collective-permute-done | bytes 294944 | tf_op jit(solution)/shard_map/ppermute | solution.py:748
  259.5 2.8 collective-permute-done.47
  266.9 3.0 collective-permute-start.53
  269.9 6.4 %collective-permute-done.54 = bf16[48,3840]{1,0:T(8,128)(2,1)S(1)} collective-permute-done((bf16[48,3840]{1,0:T(8,128)(2,1)S(1)}, bf16[48,3840]{1,0:T(8,128)(2,1)S(1)}, u32[]{:S(2)}, u32[]{:S(2)}) %collective-permute-start.54) | collective-permute-done | bytes 368672 | tf_op jit(solution)/shard_map/ppermute | solution.py:748
  276.5 2.4 collective-permute-start.57
  279.1 5.1 %inner_out.1 = (f32[192,3072]{1,0:T(8,128)}, f32[192,1]{1,0:T(8,128)}) custom-call(s32[3]{0:T(128)} %pad_add_fusion.index_ref, bf16[96,3072]{1,0:T(8,128)(2,1)} %copy-done.22, bf16[96,3072]{1,0:T(8,128)(2,1)} %collective-permute-done.56.far_ref, bf16[192,3072]{1,0:T(8,128)(2,1)} %weight_ref.1, f32[192,1]{1,0:T(8,128)} %copy.26.gain_ref), custom_call_target="tpu_custom_call" | custom-call | flops 34500001792 | bytes 3000000 | tf_op jit(solution)/shard_map/inner_out/pallas_call | solution.py:275
  284.1 6.7 %collective-permute-done.57 = bf16[96,3840]{1,0:T(8,128)(2,1)S(1)} collective-permute-done((bf16[96,3840]{1,0:T(8,128)(2,1)S(1)}, bf16[96,3840]{1,0:T(8,128)(2,1)S(1)}, u32[]{:S(2)}, u32[]{:S(2)}) %collective-permute-start.57) | collective-permute-done | bytes 737312 | tf_op jit(solution)/shard_map/ppermute | solution.py:748
  293.5 2.1 collective-permute-start.58
  296.6 5.3 %collective-permute-done.58 = bf16[96,2304]{1,0:T(8,128)(2,1)S(1)} collective-permute-done((bf16[96,2304]{1,0:T(8,128)(2,1)S(1)}, bf16[96,2304]{1,0:T(8,128)(2,1)S(1)}, u32[]{:S(2)}, u32[]{:S(2)}) %collective-permute-start.58) | collective-permute-done | bytes 442400 | tf_op jit(solution)/shard_map/ppermute | solution.py:748
  (260 shorter events, 79.1 us)
Async XLA Ops:
  0.7 24.3 %collective-permute-start = (bf16[128,768]{1,0:T(8,128)(2,1)}, bf16[128,768]{1,0:T(8,128)(2,1)}, u32[]{:S(2)}, u32[]{:S(2)}) collective-permute-start(bf16[128,768]{1,0:T(8,128)(2,1)} %bitcast.27), channel_id=1, source_target_pairs={{0,8},{4,12},{8,0},{12,4},{16,24},{20,28},{24,16},{28,20},{1,9},{5... | collective-permute-start | bytes 589832 | tf_op jit(solution)/shard_map/ppermute | solution.py:748
  3.7 12.8 %collective-permute-start.2 = (bf16[128,768]{1,0:T(8,128)(2,1)}, bf16[128,768]{1,0:T(8,128)(2,1)S(1)}, u32[]{:S(2)}, u32[]{:S(2)}) collective-permute-start(bf16[128,768]{1,0:T(8,128)(2,1)} %bitcast.28), channel_id=1, source_target_pairs={{0,24},{4,28},{8,16},{12,20},{16,8},{20,12},{24,0},{28,4},{1,25},{... | collective-permute-start | bytes 589832 | tf_op jit(solution)/shard_map/ppermute | solution.py:748
  6.2 17.7 %collective-permute-start.1 = (bf16[128,768]{1,0:T(8,128)(2,1)}, bf16[128,768]{1,0:T(8,128)(2,1)}, u32[]{:S(2)}, u32[]{:S(2)}) collective-permute-start(bf16[128,768]{1,0:T(8,128)(2,1)} %bitcast.29), channel_id=1, source_target_pairs={{0,16},{4,20},{8,24},{12,28},{16,0},{20,4},{24,8},{28,12},{1,17},{... | collective-permute-start | bytes 589832 | tf_op jit(solution)/shard_map/ppermute | solution.py:748
  6.3 24.7 %collective-permute-start.3 = (bf16[128,768]{1,0:T(8,128)(2,1)}, bf16[128,768]{1,0:T(8,128)(2,1)}, u32[]{:S(2)}, u32[]{:S(2)}) collective-permute-start(bf16[128,768]{1,0:T(8,128)(2,1)} %bitcast.30), channel_id=1, source_target_pairs={{0,4},{4,0},{8,12},{12,8},{16,20},{20,16},{24,28},{28,24},{1,5},{5... | collective-permute-start | bytes 589832 | tf_op jit(solution)/shard_map/ppermute | solution.py:748
  10.0 22.8 %collective-permute-start.7 = (bf16[192,2432]{1,0:T(8,128)(2,1)S(1)}, bf16[192,2432]{1,0:T(8,128)(2,1)}, u32[]{:S(2)}, u32[]{:S(2)}) collective-permute-start(bf16[192,2432]{1,0:T(8,128)(2,1)S(1)} %fusion.1.refs_0_), channel_id=1, source_target_pairs={{0,2},{1,3},{2,0},{3,1},{4,6},{5,7},{6,4},{7,5},{8,10},{9,11},{10,... | collective-permute-start | bytes 2801672 | tf_op jit(solution)/shard_map/ppermute | solution.py:748
  24.9 14.3 %collective-permute-start.5 = (bf16[256,768]{1,0:T(8,128)(2,1)S(1)}, bf16[256,768]{1,0:T(8,128)(2,1)}, u32[]{:S(2)}, u32[]{:S(2)}) collective-permute-start(bf16[256,768]{1,0:T(8,128)(2,1)S(1)} %pad_maximum_fusion.8.refs_2_), channel_id=1, source_target_pairs={{0,4},{4,0},{8,12},{12,8},{16,20},{20,16},{24,28},{28,24},{1,5},{5... | collective-permute-start | bytes 1179656 | tf_op jit(solution)/shard_map/ppermute | solution.py:748
  27.5 11.7 %collective-permute-start.4 = (bf16[128,768]{1,0:T(8,128)(2,1)}, bf16[128,768]{1,0:T(8,128)(2,1)S(1)}, u32[]{:S(2)}, u32[]{:S(2)}) collective-permute-start(bf16[128,768]{1,0:T(8,128)(2,1)} %collective-permute-done.refs_1_), channel_id=1, source_target_pairs={{0,4},{4,0},{8,12},{12,8},{16,20},{20,16},{24,28},{28,24},{1,5},{5... | collective-permute-start | bytes 589832 | tf_op jit(solution)/shard_map/ppermute | solution.py:748
  31.1 11.8 %collective-permute-start.6 = (bf16[192,2432]{1,0:T(8,128)(2,1)S(1)}, bf16[192,2432]{1,0:T(8,128)(2,1)}, u32[]{:S(2)}, u32[]{:S(2)}) collective-permute-start(bf16[192,2432]{1,0:T(8,128)(2,1)S(1)} %fusion.1.refs_0_), channel_id=1, source_target_pairs={{0,1},{1,0},{2,3},{3,2},{4,5},{5,4},{6,7},{7,6},{8,9},{9,8},{10,11... | collective-permute-start | bytes 2801672 | tf_op jit(solution)/shard_map/ppermute | solution.py:748
  31.2 21.2 %collective-permute-start.10 = (bf16[192,1536]{1,0:T(8,128)(2,1)S(1)}, bf16[192,1536]{1,0:T(8,128)(2,1)}, u32[]{:S(2)}, u32[]{:S(2)}) collective-permute-start(bf16[192,1536]{1,0:T(8,128)(2,1)S(1)} %copy-done.34), channel_id=1, source_target_pairs={{0,2},{1,3},{2,0},{3,1},{4,6},{5,7},{6,4},{7,5},{8,10},{9,11},{10,... | collective-permute-start | bytes 1769480 | tf_op jit(solution)/shard_map/ppermute | solution.py:748
  32.8 33.2 %collective-permute-start.13 = (bf16[192,2304]{1,0:T(8,128)(2,1)}, bf16[192,2304]{1,0:T(8,128)(2,1)}, u32[]{:S(2)}, u32[]{:S(2)}) collective-permute-start(bf16[192,2304]{1,0:T(8,128)(2,1)} %constant_dynamic-update-slice_fusion.2.refs_5_.refs_9_.refs_13_), channel_id=1, source_target_pairs={{0,2},{1,3},{2,0},{3,1},{4,6},{5,7},{6,4},{7,5},{8,10},{9,11},{10,... | collective-permute-start | bytes 2654216 | tf_op jit(solution)/shard_map/ppermute | solution.py:748
  52.3 15.2 %collective-permute-start.9 = (bf16[192,1536]{1,0:T(8,128)(2,1)S(1)}, bf16[192,1536]{1,0:T(8,128)(2,1)S(1)}, u32[]{:S(2)}, u32[]{:S(2)}) collective-permute-start(bf16[192,1536]{1,0:T(8,128)(2,1)S(1)} %copy-done.34), channel_id=1, source_target_pairs={{0,1},{1,0},{2,3},{3,2},{4,5},{5,4},{6,7},{7,6},{8,9},{9,8},{10,11... | collective-permute-start | bytes 1769480 | tf_op jit(solution)/shard_map/ppermute | solution.py:748
  52.4 15.1 %collective-permute-start.11 = (bf16[192,1536]{1,0:T(8,128)(2,1)}, bf16[192,1536]{1,0:T(8,128)(2,1)}, u32[]{:S(2)}, u32[]{:S(2)}) collective-permute-start(bf16[192,1536]{1,0:T(8,128)(2,1)} %collective-permute-done.10.refs_2_), channel_id=1, source_target_pairs={{0,1},{1,0},{2,3},{3,2},{4,5},{5,4},{6,7},{7,6},{8,9},{9,8},{10,11... | collective-permute-start | bytes 1769480 | tf_op jit(solution)/shard_map/ppermute | solution.py:748
  60.0 12.5 %collective-permute-start.12 = (bf16[192,2304]{1,0:T(8,128)(2,1)}, bf16[192,2304]{1,0:T(8,128)(2,1)S(1)}, u32[]{:S(2)}, u32[]{:S(2)}) collective-permute-start(bf16[192,2304]{1,0:T(8,128)(2,1)} %constant_dynamic-update-slice_fusion.2.refs_5_.refs_9_.refs_13_), channel_id=1, source_target_pairs={{0,1},{1,0},{2,3},{3,2},{4,5},{5,4},{6,7},{7,6},{8,9},{9,8},{10,11... | collective-permute-start | bytes 2654216 | tf_op jit(solution)/shard_map/ppermute | solution.py:748
  66.0 20.3 %collective-permute-start.19 = (bf16[512,768]{1,0:T(8,128)(2,1)}, bf16[512,768]{1,0:T(8,128)(2,1)}, u32[]{:S(2)}, u32[]{:S(2)}) collective-permute-start(bf16[512,768]{1,0:T(8,128)(2,1)} %pad_maximum_fusion.2), channel_id=1, source_target_pairs={{0,2},{1,3},{2,0},{3,1},{4,6},{5,7},{6,4},{7,5},{8,10},{9,11},{10,... | collective-permute-start | bytes 2359304 | tf_op jit(solution)/shard_map/ppermute | solution.py:748
  106.6 9.2 %collective-permute-start.21 = (bf16[128,768]{1,0:T(8,128)(2,1)}, bf16[128,768]{1,0:T(8,128)(2,1)S(1)}, u32[]{:S(2)}, u32[]{:S(2)}) collective-permute-start(bf16[128,768]{1,0:T(8,128)(2,1)} %get-tuple-element.152), channel_id=1, source_target_pairs={{0,1},{1,0},{2,3},{3,2},{4,5},{5,4},{6,7},{7,6},{8,9},{9,8},{10,11... | collective-permute-start | bytes 589832 | tf_op jit(solution)/shard_map/ppermute | solution.py:748
  108.5 9.8 %collective-permute-start.23 = (bf16[128,768]{1,0:T(8,128)(2,1)}, bf16[128,768]{1,0:T(8,128)(2,1)S(1)}, u32[]{:S(2)}, u32[]{:S(2)}) collective-permute-start(bf16[128,768]{1,0:T(8,128)(2,1)} %get-tuple-element.154), channel_id=1, source_target_pairs={{0,3},{1,2},{2,1},{3,0},{4,7},{5,6},{6,5},{7,4},{8,11},{9,10},{10,... | collective-permute-start | bytes 589832 | tf_op jit(solution)/shard_map/ppermute | solution.py:748
  110.4 19.5 %collective-permute-start.27 = (bf16[384,768]{1,0:T(8,128)(2,1)}, bf16[384,768]{1,0:T(8,128)(2,1)}, u32[]{:S(2)}, u32[]{:S(2)}) collective-permute-start(bf16[384,768]{1,0:T(8,128)(2,1)} %slice.242), channel_id=1, source_target_pairs={{0,4},{4,0},{8,12},{12,8},{16,20},{20,16},{24,28},{28,24},{1,5},{5... | collective-permute-start | bytes 1769480 | tf_op jit(solution)/shard_map/ppermute | solution.py:748
  114.3 16.8 %collective-permute-start.26 = (bf16[192,1536]{1,0:T(8,128)(2,1)}, bf16[192,1536]{1,0:T(8,128)(2,1)}, u32[]{:S(2)}, u32[]{:S(2)}) collective-permute-start(bf16[192,1536]{1,0:T(8,128)(2,1)} %pad_maximum_fusion.3), channel_id=1, source_target_pairs={{0,2},{1,3},{2,0},{3,1},{4,6},{5,7},{6,4},{7,5},{8,10},{9,11},{10,... | collective-permute-start | bytes 1769480 | tf_op jit(solution)/shard_map/ppermute | solution.py:748
  140.3 24.4 %collective-permute-start.24 = (bf16[2,128,768]{2,1,0:T(8,128)(2,1)}, bf16[2,128,768]{2,1,0:T(8,128)(2,1)S(1)}, u32[]{:S(2)}, u32[]{:S(2)}) collective-permute-start(bf16[2,128,768]{2,1,0:T(8,128)(2,1)} %get-tuple-element.156), channel_id=1, source_target_pairs={{0,1},{1,0},{2,3},{3,2},{4,5},{5,4},{6,7},{7,6},{8,9},{9,8},{10,11... | collective-permute-start | bytes 1179656 | tf_op jit(solution)/shard_map/ppermute | solution.py:748
  141.9 17.0 %collective-permute-start.31 = (bf16[192,768]{1,0:T(8,128)(2,1)S(1)}, bf16[192,768]{1,0:T(8,128)(2,1)}, u32[]{:S(2)}, u32[]{:S(2)}) collective-permute-start(bf16[192,768]{1,0:T(8,128)(2,1)S(1)} %get-tuple-element.238), channel_id=1, source_target_pairs={{0,8},{4,12},{8,0},{12,4},{16,24},{20,28},{24,16},{28,20},{1,9},{5... | collective-permute-start | bytes 884744 | tf_op jit(solution)/shard_map/ppermute | solution.py:748
  143.4 17.1 %collective-permute-start.30 = (bf16[96,3072]{1,0:T(8,128)(2,1)S(1)}, bf16[96,3072]{1,0:T(8,128)(2,1)S(1)}, u32[]{:S(2)}, u32[]{:S(2)}) collective-permute-start(bf16[96,3072]{1,0:T(8,128)(2,1)S(1)} %slice.317), channel_id=1, source_target_pairs={{0,4},{4,0},{8,12},{12,8},{16,20},{20,16},{24,28},{28,24},{1,5},{5... | collective-permute-start | bytes 1769480 | tf_op jit(solution)/shard_map/ppermute | solution.py:748
  148.0 35.4 %collective-permute-start.33 = (bf16[192,3840]{1,0:T(8,128)(2,1)}, bf16[192,3840]{1,0:T(8,128)(2,1)}, u32[]{:S(2)}, u32[]{:S(2)}) collective-permute-start(bf16[192,3840]{1,0:T(8,128)(2,1)} %add_convert_fusion), channel_id=1, source_target_pairs={{0,2},{1,3},{2,0},{3,1},{4,6},{5,7},{6,4},{7,5},{8,10},{9,11},{10,... | collective-permute-start | bytes 4423688 | tf_op jit(solution)/shard_map/ppermute | solution.py:748
  161.5 41.0 %collective-permute-start.37 = (bf16[48,3072]{1,0:T(8,128)(2,1)}, bf16[48,3072]{1,0:T(8,128)(2,1)}, u32[]{:S(2)}, u32[]{:S(2)}) collective-permute-start(bf16[48,3072]{1,0:T(8,128)(2,1)} %get-tuple-element.236), channel_id=1, source_target_pairs={{0,8},{4,12},{8,0},{12,4},{16,24},{20,28},{24,16},{28,20},{1,9},{5... | collective-permute-start | bytes 884744 | tf_op jit(solution)/shard_map/ppermute | solution.py:748
  163.3 35.1 %collective-permute-start.34 = (bf16[96,768]{1,0:T(8,128)(2,1)}, bf16[96,768]{1,0:T(8,128)(2,1)}, u32[]{:S(2)}, u32[]{:S(2)}) collective-permute-start(bf16[96,768]{1,0:T(8,128)(2,1)} %add_convert_fusion.25), channel_id=1, source_target_pairs={{0,16},{4,20},{8,24},{12,28},{16,0},{20,4},{24,8},{28,12},{1,17},{... | collective-permute-start | bytes 442376 | tf_op jit(solution)/shard_map/ppermute | solution.py:748
  165.5 30.5 %collective-permute-start.29 = (bf16[128,768]{1,0:T(8,128)(2,1)}, bf16[128,768]{1,0:T(8,128)(2,1)S(1)}, u32[]{:S(2)}, u32[]{:S(2)}) collective-permute-start(bf16[128,768]{1,0:T(8,128)(2,1)} %fusion.7), channel_id=1, source_target_pairs={{0,2},{1,3},{2,0},{3,1},{4,6},{5,7},{6,4},{7,5},{8,10},{9,11},{10,... | collective-permute-start | bytes 589832 | tf_op jit(solution)/shard_map/ppermute | solution.py:748
  174.0 19.9 %collective-permute-start.32 = (bf16[384,2304]{1,0:T(8,128)(2,1)}, bf16[384,2304]{1,0:T(8,128)(2,1)}, u32[]{:S(2)}, u32[]{:S(2)}) collective-permute-start(bf16[384,2304]{1,0:T(8,128)(2,1)} %get-tuple-element.185), channel_id=1, source_target_pairs={{0,1},{1,0},{2,3},{3,2},{4,5},{5,4},{6,7},{7,6},{8,9},{9,8},{10,11... | collective-permute-start | bytes 5308424 | tf_op jit(solution)/shard_map/ppermute | solution.py:748
  186.9 19.7 %collective-permute-start.36 = (bf16[96,3840]{1,0:T(8,128)(2,1)}, bf16[96,3840]{1,0:T(8,128)(2,1)}, u32[]{:S(2)}, u32[]{:S(2)}) collective-permute-start(bf16[96,3840]{1,0:T(8,128)(2,1)} %get-tuple-element.232), channel_id=1, source_target_pairs={{0,4},{4,0},{8,12},{12,8},{16,20},{20,16},{24,28},{28,24},{1,5},{5... | collective-permute-start | bytes 2211848 | tf_op jit(solution)/shard_map/ppermute | solution.py:748
  193.9 29.5 %collective-permute-start.43 = (bf16[512,768]{1,0:T(8,128)(2,1)S(1)}, bf16[512,768]{1,0:T(8,128)(2,1)S(1)}, u32[]{:S(2)}, u32[]{:S(2)}) collective-permute-start(bf16[512,768]{1,0:T(8,128)(2,1)S(1)} %slice.287), channel_id=1, source_target_pairs={{0,4},{4,0},{8,12},{12,8},{16,20},{20,16},{24,28},{28,24},{1,5},{5... | collective-permute-start | bytes 2359304 | tf_op jit(solution)/shard_map/ppermute | solution.py:748
  196.0 20.2 %collective-permute-start.39 = (bf16[192,2304]{1,0:T(8,128)(2,1)S(1)}, bf16[192,2304]{1,0:T(8,128)(2,1)S(1)}, u32[]{:S(2)}, u32[]{:S(2)}) collective-permute-start(bf16[192,2304]{1,0:T(8,128)(2,1)S(1)} %add_convert_fusion.1), channel_id=1, source_target_pairs={{0,2},{1,3},{2,0},{3,1},{4,6},{5,7},{6,4},{7,5},{8,10},{9,11},{10,... | collective-permute-start | bytes 2654216 | tf_op jit(solution)/shard_map/ppermute | solution.py:748
  199.4 12.7 %collective-permute-start.35 = (bf16[96,768]{1,0:T(8,128)(2,1)S(1)}, bf16[96,768]{1,0:T(8,128)(2,1)S(1)}, u32[]{:S(2)}, u32[]{:S(2)}) collective-permute-start(bf16[96,768]{1,0:T(8,128)(2,1)S(1)} %add_convert_fusion.23), channel_id=1, source_target_pairs={{0,16},{4,20},{8,24},{12,28},{16,0},{20,4},{24,8},{28,12},{1,17},{... | collective-permute-start | bytes 442376 | tf_op jit(solution)/shard_map/ppermute | solution.py:748
  203.5 10.5 %collective-permute-start.40 = (bf16[24,3072]{1,0:T(8,128)(2,1)S(1)}, bf16[24,3072]{1,0:T(8,128)(2,1)S(1)}, u32[]{:S(2)}, u32[]{:S(2)}) collective-permute-start(bf16[24,3072]{1,0:T(8,128)(2,1)S(1)} %add_convert_fusion.22), channel_id=1, source_target_pairs={{0,16},{4,20},{8,24},{12,28},{16,0},{20,4},{24,8},{28,12},{1,17},{... | collective-permute-start | bytes 442376 | tf_op jit(solution)/shard_map/ppermute | solution.py:748
  207.9 19.2 %collective-permute-start.42 = (bf16[48,3840]{1,0:T(8,128)(2,1)S(1)}, bf16[48,3840]{1,0:T(8,128)(2,1)S(1)}, u32[]{:S(2)}, u32[]{:S(2)}) collective-permute-start(bf16[48,3840]{1,0:T(8,128)(2,1)S(1)} %get-tuple-element.248), channel_id=1, source_target_pairs={{0,8},{4,12},{8,0},{12,4},{16,24},{20,28},{24,16},{28,20},{1,9},{5... | collective-permute-start | bytes 1105928 | tf_op jit(solution)/shard_map/ppermute | solution.py:748
  212.2 23.2 %collective-permute-start.38 = (bf16[192,768]{1,0:T(8,128)(2,1)S(1)}, bf16[192,768]{1,0:T(8,128)(2,1)S(1)}, u32[]{:S(2)}, u32[]{:S(2)}) collective-permute-start(bf16[192,768]{1,0:T(8,128)(2,1)S(1)} %pad_maximum_fusion.10), channel_id=1, source_target_pairs={{0,8},{4,12},{8,0},{12,4},{16,24},{20,28},{24,16},{28,20},{1,9},{5... | collective-permute-start | bytes 884744 | tf_op jit(solution)/shard_map/ppermute | solution.py:748
  215.0 22.0 %collective-permute-start.46 = (bf16[24,3072]{1,0:T(8,128)(2,1)S(1)}, bf16[24,3072]{1,0:T(8,128)(2,1)S(1)}, u32[]{:S(2)}, u32[]{:S(2)}) collective-permute-start(bf16[24,3072]{1,0:T(8,128)(2,1)S(1)} %add_convert_fusion.20), channel_id=1, source_target_pairs={{0,16},{4,20},{8,24},{12,28},{16,0},{20,4},{24,8},{28,12},{1,17},{... | collective-permute-start | bytes 442376 | tf_op jit(solution)/shard_map/ppermute | solution.py:748
  217.6 13.3 %collective-permute-start.41 = (bf16[96,2304]{1,0:T(8,128)(2,1)S(1)}, bf16[96,2304]{1,0:T(8,128)(2,1)S(1)}, u32[]{:S(2)}, u32[]{:S(2)}) collective-permute-start(bf16[96,2304]{1,0:T(8,128)(2,1)S(1)} %get-tuple-element.234), channel_id=1, source_target_pairs={{0,4},{4,0},{8,12},{12,8},{16,20},{20,16},{24,28},{28,24},{1,5},{5... | collective-permute-start | bytes 1327112 | tf_op jit(solution)/shard_map/ppermute | solution.py:748
  223.7 23.6 %collective-permute-start.45 = (bf16[256,768]{1,0:T(8,128)(2,1)S(1)}, bf16[256,768]{1,0:T(8,128)(2,1)S(1)}, u32[]{:S(2)}, u32[]{:S(2)}) collective-permute-start(bf16[256,768]{1,0:T(8,128)(2,1)S(1)} %slice.327), channel_id=1, source_target_pairs={{0,8},{4,12},{8,0},{12,4},{16,24},{20,28},{24,16},{28,20},{1,9},{5... | collective-permute-start | bytes 1179656 | tf_op jit(solution)/shard_map/ppermute | solution.py:748
  227.2 21.1 %collective-permute-start.50 = (bf16[24,3840]{1,0:T(8,128)(2,1)S(1)}, bf16[24,3840]{1,0:T(8,128)(2,1)S(1)}, u32[]{:S(2)}, u32[]{:S(2)}) collective-permute-start(bf16[24,3840]{1,0:T(8,128)(2,1)S(1)} %add_convert_fusion.19), channel_id=1, source_target_pairs={{0,16},{4,20},{8,24},{12,28},{16,0},{20,4},{24,8},{28,12},{1,17},{... | collective-permute-start | bytes 552968 | tf_op jit(solution)/shard_map/ppermute | solution.py:748
  231.0 22.8 %collective-permute-start.49 = (bf16[48,2304]{1,0:T(8,128)(2,1)S(1)}, bf16[48,2304]{1,0:T(8,128)(2,1)S(1)}, u32[]{:S(2)}, u32[]{:S(2)}) collective-permute-start(bf16[48,2304]{1,0:T(8,128)(2,1)S(1)} %get-tuple-element.258), channel_id=1, source_target_pairs={{0,8},{4,12},{8,0},{12,4},{16,24},{20,28},{24,16},{28,20},{1,9},{5... | collective-permute-start | bytes 663560 | tf_op jit(solution)/shard_map/ppermute | solution.py:748
  235.5 26.9 %collective-permute-start.44 = (bf16[384,768]{1,0:T(8,128)(2,1)S(1)}, bf16[384,768]{1,0:T(8,128)(2,1)S(1)}, u32[]{:S(2)}, u32[]{:S(2)}) collective-permute-start(bf16[384,768]{1,0:T(8,128)(2,1)S(1)} %pad_maximum_fusion.4), channel_id=1, source_target_pairs={{0,4},{4,0},{8,12},{12,8},{16,20},{20,16},{24,28},{28,24},{1,5},{5... | collective-permute-start | bytes 1769480 | tf_op jit(solution)/shard_map/ppermute | solution.py:748
  237.1 20.8 %collective-permute-start.48 = (bf16[48,3072]{1,0:T(8,128)(2,1)S(1)}, bf16[48,3072]{1,0:T(8,128)(2,1)S(1)}, u32[]{:S(2)}, u32[]{:S(2)}) collective-permute-start(bf16[48,3072]{1,0:T(8,128)(2,1)S(1)} %pad_maximum_fusion.11), channel_id=1, source_target_pairs={{0,8},{4,12},{8,0},{12,4},{16,24},{20,28},{24,16},{28,20},{1,9},{5... | collective-permute-start | bytes 884744 | tf_op jit(solution)/shard_map/ppermute | solution.py:748
  247.4 14.9 %collective-permute-start.47 = (bf16[128,768]{1,0:T(8,128)(2,1)S(1)}, bf16[128,768]{1,0:T(8,128)(2,1)S(1)}, u32[]{:S(2)}, u32[]{:S(2)}) collective-permute-start(bf16[128,768]{1,0:T(8,128)(2,1)S(1)} %slice.330), channel_id=1, source_target_pairs={{0,16},{4,20},{8,24},{12,28},{16,0},{20,4},{24,8},{28,12},{1,17},{... | collective-permute-start | bytes 589832 | tf_op jit(solution)/shard_map/ppermute | solution.py:748
  248.3 18.4 %collective-permute-start.52 = (bf16[24,3840]{1,0:T(8,128)(2,1)S(1)}, bf16[24,3840]{1,0:T(8,128)(2,1)S(1)}, u32[]{:S(2)}, u32[]{:S(2)}) collective-permute-start(bf16[24,3840]{1,0:T(8,128)(2,1)S(1)} %add_convert_fusion.17), channel_id=1, source_target_pairs={{0,16},{4,20},{8,24},{12,28},{16,0},{20,4},{24,8},{28,12},{1,17},{... | collective-permute-start | bytes 552968 | tf_op jit(solution)/shard_map/ppermute | solution.py:748
  253.9 13.0 %collective-permute-start.51 = (bf16[24,2304]{1,0:T(8,128)(2,1)S(1)}, bf16[24,2304]{1,0:T(8,128)(2,1)S(1)}, u32[]{:S(2)}, u32[]{:S(2)}) collective-permute-start(bf16[24,2304]{1,0:T(8,128)(2,1)S(1)} %add_convert_fusion.28), channel_id=1, source_target_pairs={{0,16},{4,20},{8,24},{12,28},{16,0},{20,4},{24,8},{28,12},{1,17},{... | collective-permute-start | bytes 331784 | tf_op jit(solution)/shard_map/ppermute | solution.py:748
  258.0 21.0 %collective-permute-start.56 = (bf16[96,3072]{1,0:T(8,128)(2,1)S(1)}, bf16[96,3072]{1,0:T(8,128)(2,1)}, u32[]{:S(2)}, u32[]{:S(2)}) collective-permute-start(bf16[96,3072]{1,0:T(8,128)(2,1)S(1)} %pad_maximum_fusion.5.own_ref), channel_id=1, source_target_pairs={{0,4},{4,0},{8,12},{12,8},{16,20},{20,16},{24,28},{28,24},{1,5},{5... | collective-permute-start | bytes 1769480 | tf_op jit(solution)/shard_map/ppermute | solution.py:748
  266.8 9.5 %collective-permute-start.54 = (bf16[48,3840]{1,0:T(8,128)(2,1)S(1)}, bf16[48,3840]{1,0:T(8,128)(2,1)S(1)}, u32[]{:S(2)}, u32[]{:S(2)}) collective-permute-start(bf16[48,3840]{1,0:T(8,128)(2,1)S(1)} %pad_maximum_fusion.9), channel_id=1, source_target_pairs={{0,8},{4,12},{8,0},{12,4},{16,24},{20,28},{24,16},{28,20},{1,9},{5... | collective-permute-start | bytes 1105928 | tf_op jit(solution)/shard_map/ppermute | solution.py:748
  266.9 12.0 %collective-permute-start.53 = (bf16[24,2304]{1,0:T(8,128)(2,1)S(1)}, bf16[24,2304]{1,0:T(8,128)(2,1)S(1)}, u32[]{:S(2)}, u32[]{:S(2)}) collective-permute-start(bf16[24,2304]{1,0:T(8,128)(2,1)S(1)} %add_convert_fusion.26), channel_id=1, source_target_pairs={{0,16},{4,20},{8,24},{12,28},{16,0},{20,4},{24,8},{28,12},{1,17},{... | collective-permute-start | bytes 331784 | tf_op jit(solution)/shard_map/ppermute | solution.py:748
  276.5 14.4 %collective-permute-start.57 = (bf16[96,3840]{1,0:T(8,128)(2,1)S(1)}, bf16[96,3840]{1,0:T(8,128)(2,1)S(1)}, u32[]{:S(2)}, u32[]{:S(2)}) collective-permute-start(bf16[96,3840]{1,0:T(8,128)(2,1)S(1)} %pad_maximum_fusion.1), channel_id=1, source_target_pairs={{0,4},{4,0},{8,12},{12,8},{16,20},{20,16},{24,28},{28,24},{1,5},{5... | collective-permute-start | bytes 2211848 | tf_op jit(solution)/shard_map/ppermute | solution.py:748
  279.0 14.4 %collective-permute-start.55 = (bf16[48,2304]{1,0:T(8,128)(2,1)S(1)}, bf16[48,2304]{1,0:T(8,128)(2,1)S(1)}, u32[]{:S(2)}, u32[]{:S(2)}) collective-permute-start(bf16[48,2304]{1,0:T(8,128)(2,1)S(1)} %pad_maximum_fusion.12), channel_id=1, source_target_pairs={{0,8},{4,12},{8,0},{12,4},{16,24},{20,28},{24,16},{28,20},{1,9},{5... | collective-permute-start | bytes 663560 | tf_op jit(solution)/shard_map/ppermute | solution.py:748
  (61 other events, 354.6 us)

commit v6 on v5

--- a/solution.py
+++ b/solution.py
@@ -1167,29 +1167,28 @@
     attn = Steps(reduction(keep_attn, send_attn))
     norm1_all, norm1_query = norm_terms(place, after(grad_pair, keep_attn), grad_query, w_qkv)
     ready = cross.move(norm1_all)
-    norm1 = Steps(sum_to_owner(after(norm1_all, ready)))
     grad_enc = enc_terms(place, after(grad_cross_pair, ready), w_ckv)
     ready = attn.move(grad_enc)
     layer_out = after_cross + (
         out_own + out_sibling[0].astype(jnp.float32) + after(out_far, ready).astype(jnp.float32)
     )
     ready = down.move(ready, layer_out)
-    for step in (inner, cross, down, inner, attn, norm1, cross, attn, down, inner, norm1):
+    for step in (inner, cross, down, inner, attn):
         ready = step.move(ready)
-    for step in (cross, attn, inner):
+    norm1 = Steps(sum_to_owner(after(norm1_all, ready)))
+    for step in (cross, attn, down, inner, cross, norm1, attn, inner, cross, norm1, attn):
         ready = step.move(ready)
-    ready = down.finish(norm1.finish(ready))
+    ready = norm1.finish(ready)
     input_rows = own.astype(jnp.float32)
     grad_norm1 = norm1.result.astype(jnp.float32) + norm1_query
     grad_input = grad_after_attn + rms_back(
         input_rows, inverse_rms(input_rows), after(gain_rows, ready)[0:1], grad_norm1
     )
+    ready = cross.move(ready)
+    ready = attn.move(down.finish(ready), grad_input)
     total_down = finished(down.result, 0, feature_width)
-    ready = cross.move(ready, total_down, grad_input)
+    ready = inner.finish(after(ready, total_down))
     ready = attn.move(ready)
-    ready = cross.move(ready)
-    ready = attn.move(ready)
-    ready = inner.finish(ready)
     total_in, gain_three = inner_out(place, inner.result, mlp_in, norm_gains[2])
     cross.move(ready, total_in)
     ready = cross.finish(ready)

time: 305 us -> 303 us (level)
  waiting for transfers between devices: 95.4 us -> 85.3 us
  other arithmetic: 34.8 us -> 40.3 us
    ppermute x59, waiting for transfers between devices: 95.4 us -> 85.3 us  [swap(): return lax.ppermute(values, axis, [(i, i ^ bit) for i in range(count)])]
    unnamed x103 -> x101, local copies, waits for them, and re-layouts: 6.86 us -> 8.9 us
  transfers between devices with their start and end apart: 59 -> 59, of which waited for: 26 -> 22; matrix products, arithmetic and copies ran while one was open for 13% -> 15% of each run, Pallas kernels for 27% -> 27%
where the time goes in v6:
time: 303 us; the launch traced here: 301 us
  Pallas kernels  99.7 us (33%)
  waiting for transfers between devices  85.3 us (28%)
  starting transfers between devices  58.8 us (19%)
  other arithmetic  40.3 us (13%)
  local copies, waits for them, and re-layouts  15.7 us (5%)
    ppermute x59, waiting for transfers between devices, swap(): return lax.ppermute(values, axis, [(i, i ^ bit) for i in range(count)])  85.3 us
    pallas_call x8, Pallas kernels, chain_call(): pl.pallas_call(kernel, grid_spec=pltpu.PrefetchScalarGridSpec(num_scalar_...  62.4 us
    ppermute x59, starting transfers between devices, swap(): return lax.ppermute(values, axis, [(i, i ^ bit) for i in range(count)])  58.8 us
    convert_element_type x20, other arithmetic, to_low(): return values.astype(jnp.bfloat16)  18.7 us
    pallas_call x2, Pallas kernels, wide_products(): pl.pallas_call(functools.partial(products_kernel, tiles, rows, chunks), g...  16.3 us
    pallas_call x1, Pallas kernels, self_backward(): pl.pallas_call(functools.partial(self_backward_kernel, head_size, blocks)...  9.33 us
    unnamed x101, local copies, waits for them, and re-layouts  8.9 us
    pallas_call x1, Pallas kernels, self_forward(): pl.pallas_call(functools.partial(self_forward_kernel, head_size, blocks),...  7.14 us
  transfers between devices with their start and end apart: 59, of which 22 were waited for; matrix products, arithmetic and copies ran while one was open for 15% of the time, Pallas kernels for 27%

profile of v6, /device:TPU:0, one launch (start us, length us, event | category | flops | bytes accessed | tf_op | source)
XLA Modules:
  0.0 301.4 jit_solution(7517622957316272214)
XLA Ops:
  0.7 3.1 %collective-permute-start = (bf16[128,768]{1,0:T(8,128)(2,1)}, bf16[128,768]{1,0:T(8,128)(2,1)}, u32[]{:S(2)}, u32[]{:S(2)}) collective-permute-start(bf16[128,768]{1,0:T(8,128)(2,1)} %bitcast.27), channel_id=1, source_target_pairs={{0,8},{4,12},{8,0},{12,4},{16,24},{20,28},{24,16},{28,20},{1,9},{5... | collective-permute-start | bytes 589832 | tf_op jit(solution)/shard_map/ppermute | solution.py:748
  3.7 2.5 collective-permute-start.2
  10.0 1.6 collective-permute-start.7
  13.3 3.2 %collective-permute-done.2 = bf16[128,768]{1,0:T(8,128)(2,1)S(1)} collective-permute-done((bf16[128,768]{1,0:T(8,128)(2,1)}, bf16[128,768]{1,0:T(8,128)(2,1)S(1)}, u32[]{:S(2)}, u32[]{:S(2)}) %collective-permute-start.2) | collective-permute-done | bytes 196640 | tf_op jit(solution)/shard_map/ppermute | solution.py:748
  16.5 7.4 %collective-permute-done.1 = bf16[128,768]{1,0:T(8,128)(2,1)} collective-permute-done((bf16[128,768]{1,0:T(8,128)(2,1)}, bf16[128,768]{1,0:T(8,128)(2,1)}, u32[]{:S(2)}, u32[]{:S(2)}) %collective-permute-start.1) | collective-permute-done | bytes 196640 | tf_op jit(solution)/shard_map/ppermute | solution.py:748
  31.3 1.6 collective-permute-start.10
  33.4 5.8 %collective-permute-done.4.refs_4_ = bf16[128,768]{1,0:T(8,128)(2,1)S(1)} collective-permute-done((bf16[128,768]{1,0:T(8,128)(2,1)}, bf16[128,768]{1,0:T(8,128)(2,1)S(1)}, u32[]{:S(2)}, u32[]{:S(2)}) %collective-permute-start.4) | collective-permute-done | bytes 196640 | tf_op jit(solution)/shard_map/ppermute | solution.py:748
  39.9 3.0 %held_rows.1 = (bf16[1024,768]{1,0:T(8,128)(2,1)}, f32[1024,1]{1,0:T(8,128)}) custom-call(bf16[128,768]{1,0:T(8,128)(2,1)} %bitcast.31, bf16[128,768]{1,0:T(8,128)(2,1)} %collective-permute-done.refs_1_, bf16[256,768]{1,0:T(8,128)(2,1)} %copy-done.25, bf16[128,768]{1,0:T(8,128)(2,1)} %collective-permute-done.3.refs_3_, bf16[128,768]{1,0:T(8,128)(2,1)} %copy-done.45, ...), custom_call_target="tpu_custom_call" | custom-call | flops 23000000512 | bytes 2000000 | tf_op jit(solution)/shard_map/held_rows/pallas_call | solution.py:308
  43.8 9.4 %project.1 = (bf16[128,768]{1,0:T(8,128)(2,1)}, bf16[1024,1536]{1,0:T(8,128)(2,1)}, bf16[1024,768]{1,0:T(8,128)(2,1)}, bf16[768,2304]{1,0:T(8,128)(2,1)}, f32[8,768]{1,0:T(8,128)}) custom-call(s32[3]{0:T(128)} %pad_add_fusion.index_ref, bf16[1024,768]{1,0:T(8,128)(2,1)} %get-tuple-element.118.rows_ref, f32[1024,1]{1,0:T(8,128)} %get-tuple-element.119.scale_ref, ...), custom_call_target="tpu_custom_call" | custom-call | flops 103499997184 | bytes 9000000 | tf_op jit(solution)/shard_map/project/pallas_call | solution.py:275
  53.8 7.1 %self_forward.1 = (bf16[128,768]{1,0:T(8,128)(2,1)}, f32[6,1,256]{2,1,0:T(1,128)}) custom-call(bf16[128,768]{1,0:T(8,128)(2,1)} %get-tuple-element.124.q_ref, bf16[1024,1536]{1,0:T(8,128)(2,1)} %get-tuple-element.125.k_ref.v_ref, bf16[1024,1536]{1,0:T(8,128)(2,1)} %get-tuple-element.125.k_ref.v_ref, s32[1024,1]{1,0:T(8,128)} %get-tuple-element.126.pos_ref, ...), custom_call_target="tpu_custom_call" | custom-call | flops 87399997440 | bytes 7600000 | tf_op jit(solution)/shard_map/self_forward/pallas_call | solution.py:216
  61.1 5.0 %collective-permute-done.13.refs_7_.refs_11_.refs_15_ = bf16[192,2304]{1,0:T(8,128)(2,1)} collective-permute-done((bf16[192,2304]{1,0:T(8,128)(2,1)}, bf16[192,2304]{1,0:T(8,128)(2,1)}, u32[]{:S(2)}, u32[]{:S(2)}) %collective-permute-start.13) | collective-permute-done | bytes 884768 | tf_op jit(solution)/shard_map/ppermute | solution.py:748
  68.4 4.2 %attend_out.1 = (f32[128,768]{1,0:T(8,128)}, bf16[128,768]{1,0:T(8,128)(2,1)}, bf16[128,768]{1,0:T(8,128)(2,1)}, bf16[768,1536]{1,0:T(8,128)(2,1)}) custom-call(s32[3]{0:T(128)} %pad_add_fusion.index_ref, bf16[128,768]{1,0:T(8,128)(2,1)} %get-tuple-element.129.att_ref.refs_7_, bf16[128,768]{1,0:T(8,128)(2,1)} %bitcast.32, ...), custom_call_target="tpu_custom_call" | custom-call | flops 50600001536 | bytes 4400000 | tf_op jit(solution)/shard_map/attend_out/pallas_call | solution.py:275
  74.0 9.5 %cross_forward.1 = (bf16[2,512,768]{2,1,0:T(8,128)(2,1)}, bf16[128,768]{1,0:T(8,128)(2,1)}, f32[128,768]{1,0:T(8,128)}, bf16[128,768]{1,0:T(8,128)(2,1)}, bf16[2...) custom-call(s32[3]{0:T(128)} %pad_add_fusion.index_ref, bf16[128,768]{1,0:T(8,128)(2,1)} %get-tuple-element.134.refs_0_, ...), custom_call_target="tpu_custom_call" | custom-call | flops 141450002432 | bytes 12300000 | tf_op jit(solution)/shard_map/cross_forward/pallas_call | solution.py:275
  83.5 2.8 collective-permute-done.19.refs_7_
  88.5 5.6 %collective-permute-done.16.refs_2_ = bf16[128,768]{1,0:T(8,128)(2,1)S(1)} collective-permute-done((bf16[128,768]{1,0:T(8,128)(2,1)}, bf16[128,768]{1,0:T(8,128)(2,1)S(1)}, u32[]{:S(2)}, u32[]{:S(2)}) %collective-permute-start.16) | collective-permute-done | bytes 196640 | tf_op jit(solution)/shard_map/ppermute | solution.py:748
  96.5 9.9 %mlp_share.1 = (f32[128,768]{1,0:T(8,128)}, bf16[128,768]{1,0:T(8,128)(2,1)}, bf16[128,768]{1,0:T(8,128)(2,1)}, bf16[128,768]{1,0:T(8,128)(2,1)}, f32[128,768]{1...) custom-call(s32[3]{0:T(128)} %pad_add_fusion.index_ref, ...), custom_call_target="tpu_custom_call" | custom-call | flops 126500003840 | bytes 11000000 | tf_op jit(solution)/shard_map/mlp_share/pallas_call | solution.py:275
  108.6 1.9 slice.242
  115.9 2.5 collective-permute-done.23.refs_12_
  119.1 11.0 %cross_backward.1 = (bf16[128,768]{1,0:T(8,128)(2,1)}, bf16[2,512,768]{2,1,0:T(8,128)(2,1)}, f32[128,768]{1,0:T(8,128)}, bf16[128,768]{1,0:T(8,128)(2,1)}, bf16[...) custom-call(s32[3]{0:T(128)} %pad_add_fusion.index_ref, bf16[128,768]{1,0:T(8,128)(2,1)} %get-tuple-element.134.refs_0_, ...), custom_call_target="tpu_custom_call" | custom-call | flops 149500002304 | bytes 13000000 | tf_op jit(solution)/shard_map/cross_backward/pallas_call | solution.py:275
  131.2 8.3 %wide_products.2 = (bf16[384,3840]{1,0:T(8,128)(2,1)}, bf16[384,3840]{1,0:T(8,128)(2,1)}) custom-call(s32[3]{0:T(128)} %pad_add_fusion.index_ref, bf16[128,768]{1,0:T(8,128)(2,1)} %get-tuple-element.156.refs_0_, bf16[128,768]{1,0:T(8,128)(2,1)} %get-tuple-element.157.refs_1_, bf16[128,768]{1,0:T(8,128)(2,1)} %get-tuple-element.158.refs_2_, ...), custom_call_target="tpu_custom_call" | custom-call | flops 94299996160 | bytes 8199999 | tf_op jit(solution)/shard_map/wide_products/pallas_call | solution.py:866
  145.3 2.9 add_convert_fusion
  149.6 9.3 %self_backward.1 = (bf16[128,768]{1,0:T(8,128)(2,1)}, bf16[2,1024,768]{2,1,0:T(8,128)(2,1)}) custom-call(bf16[128,768]{1,0:T(8,128)(2,1)} %get-tuple-element.124.q_ref, bf16[1024,1536]{1,0:T(8,128)(2,1)} %get-tuple-element.125.k_ref.v_ref, bf16[1024,1536]{1,0:T(8,128)(2,1)} %get-tuple-element.125.k_ref.v_ref, bf16[128,768]{1,0:T(8,128)(2,1)} %get-tuple-element.173.do_ref, ...), custom_call_target="tpu_custom_call" | custom-call | flops 117300002816 | bytes 10200000 | tf_op jit(solution)/shard_map/self_backward/pallas_call | solution.py:237
  159.0 1.6 add_convert_fusion.25
  161.5 1.8 collective-permute-start.35
  166.0 8.0 %wide_products.3 = (bf16[384,2304]{1,0:T(8,128)(2,1)}, bf16[384,2304]{1,0:T(8,128)(2,1)}) custom-call(s32[3]{0:T(128)} %pad_add_fusion.index_ref, bf16[1024,768]{1,0:T(8,128)(2,1)} %get-tuple-element.178.refs_0_.refs_2_, bf16[128,768]{1,0:T(8,128)(2,1)} %get-tuple-element.181.refs_1_.query_ref, bf16[1024,768]{1,0:T(8,128)(2,1)} %get-tuple-element.178.refs_0_.refs_2_, ...), custom_call_target="tpu_custom_call" | custom-call | flops 115000000 | bytes 10000 | tf_op jit(solution)/shard_map/wide_products/pallas_call | solution.py:866
  174.0 8.0 %norm_terms.1 = (bf16[1024,768]{1,0:T(8,128)(2,1)}, f32[128,768]{1,0:T(8,128)}) custom-call(s32[3]{0:T(128)} %pad_add_fusion.index_ref, bf16[2,1024,768]{2,1,0:T(8,128)(2,1)} %get-tuple-element.185.refs_3_.refs_4_.pair_ref, bf16[128,768]{1,0:T(8,128)(2,1)} %get-tuple-element.181.refs_1_.query_ref, bf16[768,2304]{1,0:T(8,128)(2,1)} %get-tuple-element.186.w_ref), custom_call_target="tpu_custom_call" | custom-call | flops 115000000 | bytes 10000 | tf_op jit(solution)/shard_map/norm_terms/pallas_call | solution.py:275
  182.0 1.6 collective-permute-done.33
  183.6 3.4 %add_convert_fusion.3 = (bf16[96,3840]{1,0:T(8,128)(2,1)}, bf16[96,3840]{1,0:T(8,128)(2,1)}) fusion(bf16[192,3840]{1,0:T(8,128)(2,1)} %collective-permute-done.33, bf16[384,3840]{1,0:T(8,128)(2,1)} %collective-permute-done.28, bf16[384,3840]{1,0:T(8,128)(2,1)S(1)} %copy-done.2), kind=kLoop, calls=%fused_computation.6 | loop fusion | flops 4423680 | bytes 5898240 | tf_op jit(solution)/shard_map/convert_element_type | solution.py:26
  188.5 5.2 %enc_terms.1 = f32[512,768]{1,0:T(8,128)} custom-call(s32[3]{0:T(128)} %pad_add_fusion.index_ref, bf16[2,512,768]{2,1,0:T(8,128)(2,1)} %get-tuple-element.189.refs_5_.refs_6_.pair_ref, bf16[2,768,768]{2,1,0:T(8,128)(2,1)} %get-tuple-element.190.w_ref), custom_call_target="tpu_custom_call" | custom-call | flops 46000001024 | bytes 4000000 | tf_op jit(solution)/shard_map/enc_terms/pallas_call | solution.py:275
  195.2 1.6 collective-permute-start.34
  196.9 1.8 fusion.9
  199.7 2.1 collective-permute-start.38
  205.9 1.9 collective-permute-start.41
  207.8 4.4 %collective-permute-done.38 = bf16[96,768]{1,0:T(8,128)(2,1)S(1)} collective-permute-done((bf16[96,768]{1,0:T(8,128)(2,1)S(1)}, bf16[96,768]{1,0:T(8,128)(2,1)S(1)}, u32[]{:S(2)}, u32[]{:S(2)}) %collective-permute-start.38) | collective-permute-done | bytes 147488 | tf_op jit(solution)/shard_map/ppermute | solution.py:748
  212.4 2.0 collective-permute-done.37
  219.8 6.8 %collective-permute-done.41 = bf16[48,3840]{1,0:T(8,128)(2,1)S(1)} collective-permute-done((bf16[48,3840]{1,0:T(8,128)(2,1)S(1)}, bf16[48,3840]{1,0:T(8,128)(2,1)S(1)}, u32[]{:S(2)}, u32[]{:S(2)}) %collective-permute-start.41) | collective-permute-done | bytes 368672 | tf_op jit(solution)/shard_map/ppermute | solution.py:748
  227.2 3.5 %collective-permute-done.45 = bf16[96,2304]{1,0:T(8,128)(2,1)S(1)} collective-permute-done((bf16[96,2304]{1,0:T(8,128)(2,1)S(1)}, bf16[96,2304]{1,0:T(8,128)(2,1)S(1)}, u32[]{:S(2)}, u32[]{:S(2)}) %collective-permute-start.45) | collective-permute-done | bytes 442400 | tf_op jit(solution)/shard_map/ppermute | solution.py:748
  230.9 1.6 collective-permute-start.49
  232.5 2.2 collective-permute-done.44
  236.0 5.5 %collective-permute-start.47 = (bf16[24,3840]{1,0:T(8,128)(2,1)S(1)}, bf16[24,3840]{1,0:T(8,128)(2,1)S(1)}, u32[]{:S(2)}, u32[]{:S(2)}) collective-permute-start(bf16[24,3840]{1,0:T(8,128)(2,1)S(1)} %add_convert_fusion.17), channel_id=1, source_target_pairs={{0,16},{4,20},{8,24},{12,28},{16,0},{20,4},{24,8},{28,12},{1,17},{... | collective-permute-start | bytes 552968 | tf_op jit(solution)/shard_map/ppermute | solution.py:748
  241.5 6.1 %collective-permute-done.40 = bf16[512,768]{1,0:T(8,128)(2,1)S(1)} collective-permute-done((bf16[512,768]{1,0:T(8,128)(2,1)S(1)}, bf16[512,768]{1,0:T(8,128)(2,1)S(1)}, u32[]{:S(2)}, u32[]{:S(2)}) %collective-permute-start.40) | collective-permute-done | bytes 786464 | tf_op jit(solution)/shard_map/ppermute | solution.py:748
  247.9 1.6 collective-permute-start.46
  253.2 9.3 %collective-permute-done.46 = bf16[256,768]{1,0:T(8,128)(2,1)S(1)} collective-permute-done((bf16[256,768]{1,0:T(8,128)(2,1)S(1)}, bf16[256,768]{1,0:T(8,128)(2,1)S(1)}, u32[]{:S(2)}, u32[]{:S(2)}) %collective-permute-start.46) | collective-permute-done | bytes 393248 | tf_op jit(solution)/shard_map/ppermute | solution.py:748
  262.8 3.0 collective-permute-start.52
  265.8 7.3 %collective-permute-done.50 = bf16[128,768]{1,0:T(8,128)(2,1)S(1)} collective-permute-done((bf16[128,768]{1,0:T(8,128)(2,1)S(1)}, bf16[128,768]{1,0:T(8,128)(2,1)S(1)}, u32[]{:S(2)}, u32[]{:S(2)}) %collective-permute-start.50) | collective-permute-done | bytes 196640 | tf_op jit(solution)/shard_map/ppermute | solution.py:748
  279.8 5.1 %inner_out.1 = (f32[192,3072]{1,0:T(8,128)}, f32[192,1]{1,0:T(8,128)}) custom-call(s32[3]{0:T(128)} %pad_add_fusion.index_ref, bf16[96,3072]{1,0:T(8,128)(2,1)} %copy-done.20, bf16[96,3072]{1,0:T(8,128)(2,1)} %copy-done.39, bf16[192,3072]{1,0:T(8,128)(2,1)} %weight_ref.1, f32[192,1]{1,0:T(8,128)} %copy.26.gain_ref), custom_call_target="tpu_custom_call" | custom-call | flops 34500001792 | bytes 3000000 | tf_op jit(solution)/shard_map/inner_out/pallas_call | solution.py:275
  287.2 1.6 maximum_convert_fusion
  293.1 5.1 %collective-permute-done.57 = bf16[96,2304]{1,0:T(8,128)(2,1)S(1)} collective-permute-done((bf16[96,2304]{1,0:T(8,128)(2,1)S(1)}, bf16[96,2304]{1,0:T(8,128)(2,1)S(1)}, u32[]{:S(2)}, u32[]{:S(2)}) %collective-permute-start.57) | collective-permute-done | bytes 442400 | tf_op jit(solution)/shard_map/ppermute | solution.py:748
  (258 shorter events, 79.9 us)
Async XLA Ops:
  0.7 24.3 %collective-permute-start = (bf16[128,768]{1,0:T(8,128)(2,1)}, bf16[128,768]{1,0:T(8,128)(2,1)}, u32[]{:S(2)}, u32[]{:S(2)}) collective-permute-start(bf16[128,768]{1,0:T(8,128)(2,1)} %bitcast.27), channel_id=1, source_target_pairs={{0,8},{4,12},{8,0},{12,4},{16,24},{20,28},{24,16},{28,20},{1,9},{5... | collective-permute-start | bytes 589832 | tf_op jit(solution)/shard_map/ppermute | solution.py:748
  3.7 12.8 %collective-permute-start.2 = (bf16[128,768]{1,0:T(8,128)(2,1)}, bf16[128,768]{1,0:T(8,128)(2,1)S(1)}, u32[]{:S(2)}, u32[]{:S(2)}) collective-permute-start(bf16[128,768]{1,0:T(8,128)(2,1)} %bitcast.28), channel_id=1, source_target_pairs={{0,24},{4,28},{8,16},{12,20},{16,8},{20,12},{24,0},{28,4},{1,25},{... | collective-permute-start | bytes 589832 | tf_op jit(solution)/shard_map/ppermute | solution.py:748
  6.2 17.7 %collective-permute-start.1 = (bf16[128,768]{1,0:T(8,128)(2,1)}, bf16[128,768]{1,0:T(8,128)(2,1)}, u32[]{:S(2)}, u32[]{:S(2)}) collective-permute-start(bf16[128,768]{1,0:T(8,128)(2,1)} %bitcast.29), channel_id=1, source_target_pairs={{0,16},{4,20},{8,24},{12,28},{16,0},{20,4},{24,8},{28,12},{1,17},{... | collective-permute-start | bytes 589832 | tf_op jit(solution)/shard_map/ppermute | solution.py:748
  6.3 24.8 %collective-permute-start.3 = (bf16[128,768]{1,0:T(8,128)(2,1)}, bf16[128,768]{1,0:T(8,128)(2,1)}, u32[]{:S(2)}, u32[]{:S(2)}) collective-permute-start(bf16[128,768]{1,0:T(8,128)(2,1)} %bitcast.30), channel_id=1, source_target_pairs={{0,4},{4,0},{8,12},{12,8},{16,20},{20,16},{24,28},{28,24},{1,5},{5... | collective-permute-start | bytes 589832 | tf_op jit(solution)/shard_map/ppermute | solution.py:748
  10.0 22.9 %collective-permute-start.7 = (bf16[192,2432]{1,0:T(8,128)(2,1)S(1)}, bf16[192,2432]{1,0:T(8,128)(2,1)}, u32[]{:S(2)}, u32[]{:S(2)}) collective-permute-start(bf16[192,2432]{1,0:T(8,128)(2,1)S(1)} %fusion.1.refs_0_), channel_id=1, source_target_pairs={{0,2},{1,3},{2,0},{3,1},{4,6},{5,7},{6,4},{7,5},{8,10},{9,11},{10,... | collective-permute-start | bytes 2801672 | tf_op jit(solution)/shard_map/ppermute | solution.py:748
  24.9 14.3 %collective-permute-start.5 = (bf16[256,768]{1,0:T(8,128)(2,1)S(1)}, bf16[256,768]{1,0:T(8,128)(2,1)}, u32[]{:S(2)}, u32[]{:S(2)}) collective-permute-start(bf16[256,768]{1,0:T(8,128)(2,1)S(1)} %pad_maximum_fusion.8.refs_2_), channel_id=1, source_target_pairs={{0,4},{4,0},{8,12},{12,8},{16,20},{20,16},{24,28},{28,24},{1,5},{5... | collective-permute-start | bytes 1179656 | tf_op jit(solution)/shard_map/ppermute | solution.py:748
  27.4 11.8 %collective-permute-start.4 = (bf16[128,768]{1,0:T(8,128)(2,1)}, bf16[128,768]{1,0:T(8,128)(2,1)S(1)}, u32[]{:S(2)}, u32[]{:S(2)}) collective-permute-start(bf16[128,768]{1,0:T(8,128)(2,1)} %collective-permute-done.refs_1_), channel_id=1, source_target_pairs={{0,4},{4,0},{8,12},{12,8},{16,20},{20,16},{24,28},{28,24},{1,5},{5... | collective-permute-start | bytes 589832 | tf_op jit(solution)/shard_map/ppermute | solution.py:748
  31.2 11.7 %collective-permute-start.6 = (bf16[192,2432]{1,0:T(8,128)(2,1)S(1)}, bf16[192,2432]{1,0:T(8,128)(2,1)S(1)}, u32[]{:S(2)}, u32[]{:S(2)}) collective-permute-start(bf16[192,2432]{1,0:T(8,128)(2,1)S(1)} %fusion.1.refs_0_), channel_id=1, source_target_pairs={{0,1},{1,0},{2,3},{3,2},{4,5},{5,4},{6,7},{7,6},{8,9},{9,8},{10,11... | collective-permute-start | bytes 2801672 | tf_op jit(solution)/shard_map/ppermute | solution.py:748
  31.3 22.1 %collective-permute-start.10 = (bf16[192,1536]{1,0:T(8,128)(2,1)S(1)}, bf16[192,1536]{1,0:T(8,128)(2,1)}, u32[]{:S(2)}, u32[]{:S(2)}) collective-permute-start(bf16[192,1536]{1,0:T(8,128)(2,1)S(1)} %copy-done.32), channel_id=1, source_target_pairs={{0,2},{1,3},{2,0},{3,1},{4,6},{5,7},{6,4},{7,5},{8,10},{9,11},{10,... | collective-permute-start | bytes 1769480 | tf_op jit(solution)/shard_map/ppermute | solution.py:748
  32.9 33.2 %collective-permute-start.13 = (bf16[192,2304]{1,0:T(8,128)(2,1)}, bf16[192,2304]{1,0:T(8,128)(2,1)}, u32[]{:S(2)}, u32[]{:S(2)}) collective-permute-start(bf16[192,2304]{1,0:T(8,128)(2,1)} %constant_dynamic-update-slice_fusion.2.refs_5_.refs_9_.refs_13_), channel_id=1, source_target_pairs={{0,2},{1,3},{2,0},{3,1},{4,6},{5,7},{6,4},{7,5},{8,10},{9,11},{10,... | collective-permute-start | bytes 2654216 | tf_op jit(solution)/shard_map/ppermute | solution.py:748
  53.2 14.3 %collective-permute-start.9 = (bf16[192,1536]{1,0:T(8,128)(2,1)S(1)}, bf16[192,1536]{1,0:T(8,128)(2,1)S(1)}, u32[]{:S(2)}, u32[]{:S(2)}) collective-permute-start(bf16[192,1536]{1,0:T(8,128)(2,1)S(1)} %copy-done.32), channel_id=1, source_target_pairs={{0,1},{1,0},{2,3},{3,2},{4,5},{5,4},{6,7},{7,6},{8,9},{9,8},{10,11... | collective-permute-start | bytes 1769480 | tf_op jit(solution)/shard_map/ppermute | solution.py:748
  53.3 14.3 %collective-permute-start.11 = (bf16[192,1536]{1,0:T(8,128)(2,1)}, bf16[192,1536]{1,0:T(8,128)(2,1)}, u32[]{:S(2)}, u32[]{:S(2)}) collective-permute-start(bf16[192,1536]{1,0:T(8,128)(2,1)} %collective-permute-done.10.refs_2_), channel_id=1, source_target_pairs={{0,1},{1,0},{2,3},{3,2},{4,5},{5,4},{6,7},{7,6},{8,9},{9,8},{10,11... | collective-permute-start | bytes 1769480 | tf_op jit(solution)/shard_map/ppermute | solution.py:748
  61.0 11.7 %collective-permute-start.12 = (bf16[192,2304]{1,0:T(8,128)(2,1)}, bf16[192,2304]{1,0:T(8,128)(2,1)S(1)}, u32[]{:S(2)}, u32[]{:S(2)}) collective-permute-start(bf16[192,2304]{1,0:T(8,128)(2,1)} %constant_dynamic-update-slice_fusion.2.refs_5_.refs_9_.refs_13_), channel_id=1, source_target_pairs={{0,1},{1,0},{2,3},{3,2},{4,5},{5,4},{6,7},{7,6},{8,9},{9,8},{10,11... | collective-permute-start | bytes 2654216 | tf_op jit(solution)/shard_map/ppermute | solution.py:748
  66.1 20.3 %collective-permute-start.19 = (bf16[512,768]{1,0:T(8,128)(2,1)}, bf16[512,768]{1,0:T(8,128)(2,1)}, u32[]{:S(2)}, u32[]{:S(2)}) collective-permute-start(bf16[512,768]{1,0:T(8,128)(2,1)} %pad_maximum_fusion.2), channel_id=1, source_target_pairs={{0,2},{1,3},{2,0},{3,1},{4,6},{5,7},{6,4},{7,5},{8,10},{9,11},{10,... | collective-permute-start | bytes 2359304 | tf_op jit(solution)/shard_map/ppermute | solution.py:748
  106.7 9.2 %collective-permute-start.21 = (bf16[128,768]{1,0:T(8,128)(2,1)}, bf16[128,768]{1,0:T(8,128)(2,1)S(1)}, u32[]{:S(2)}, u32[]{:S(2)}) collective-permute-start(bf16[128,768]{1,0:T(8,128)(2,1)} %get-tuple-element.151), channel_id=1, source_target_pairs={{0,1},{1,0},{2,3},{3,2},{4,5},{5,4},{6,7},{7,6},{8,9},{9,8},{10,11... | collective-permute-start | bytes 589832 | tf_op jit(solution)/shard_map/ppermute | solution.py:748
  108.6 9.8 %collective-permute-start.23 = (bf16[128,768]{1,0:T(8,128)(2,1)}, bf16[128,768]{1,0:T(8,128)(2,1)S(1)}, u32[]{:S(2)}, u32[]{:S(2)}) collective-permute-start(bf16[128,768]{1,0:T(8,128)(2,1)} %get-tuple-element.153), channel_id=1, source_target_pairs={{0,3},{1,2},{2,1},{3,0},{4,7},{5,6},{6,5},{7,4},{8,11},{9,10},{10,... | collective-permute-start | bytes 589832 | tf_op jit(solution)/shard_map/ppermute | solution.py:748
  110.5 19.5 %collective-permute-start.27 = (bf16[384,768]{1,0:T(8,128)(2,1)}, bf16[384,768]{1,0:T(8,128)(2,1)}, u32[]{:S(2)}, u32[]{:S(2)}) collective-permute-start(bf16[384,768]{1,0:T(8,128)(2,1)} %slice.242), channel_id=1, source_target_pairs={{0,4},{4,0},{8,12},{12,8},{16,20},{20,16},{24,28},{28,24},{1,5},{5... | collective-permute-start | bytes 1769480 | tf_op jit(solution)/shard_map/ppermute | solution.py:748
  114.4 16.8 %collective-permute-start.26 = (bf16[192,1536]{1,0:T(8,128)(2,1)}, bf16[192,1536]{1,0:T(8,128)(2,1)}, u32[]{:S(2)}, u32[]{:S(2)}) collective-permute-start(bf16[192,1536]{1,0:T(8,128)(2,1)} %pad_maximum_fusion.3), channel_id=1, source_target_pairs={{0,2},{1,3},{2,0},{3,1},{4,6},{5,7},{6,4},{7,5},{8,10},{9,11},{10,... | collective-permute-start | bytes 1769480 | tf_op jit(solution)/shard_map/ppermute | solution.py:748
  140.4 24.3 %collective-permute-start.24 = (bf16[2,128,768]{2,1,0:T(8,128)(2,1)}, bf16[2,128,768]{2,1,0:T(8,128)(2,1)S(1)}, u32[]{:S(2)}, u32[]{:S(2)}) collective-permute-start(bf16[2,128,768]{2,1,0:T(8,128)(2,1)} %get-tuple-element.155), channel_id=1, source_target_pairs={{0,1},{1,0},{2,3},{3,2},{4,5},{5,4},{6,7},{7,6},{8,9},{9,8},{10,11... | collective-permute-start | bytes 1179656 | tf_op jit(solution)/shard_map/ppermute | solution.py:748
  142.0 16.9 %collective-permute-start.31 = (bf16[192,768]{1,0:T(8,128)(2,1)S(1)}, bf16[192,768]{1,0:T(8,128)(2,1)}, u32[]{:S(2)}, u32[]{:S(2)}) collective-permute-start(bf16[192,768]{1,0:T(8,128)(2,1)S(1)} %get-tuple-element.236), channel_id=1, source_target_pairs={{0,8},{4,12},{8,0},{12,4},{16,24},{20,28},{24,16},{28,20},{1,9},{5... | collective-permute-start | bytes 884744 | tf_op jit(solution)/shard_map/ppermute | solution.py:748
  143.5 17.1 %collective-permute-start.30 = (bf16[96,3072]{1,0:T(8,128)(2,1)S(1)}, bf16[96,3072]{1,0:T(8,128)(2,1)S(1)}, u32[]{:S(2)}, u32[]{:S(2)}) collective-permute-start(bf16[96,3072]{1,0:T(8,128)(2,1)S(1)} %slice.317), channel_id=1, source_target_pairs={{0,4},{4,0},{8,12},{12,8},{16,20},{20,16},{24,28},{28,24},{1,5},{5... | collective-permute-start | bytes 1769480 | tf_op jit(solution)/shard_map/ppermute | solution.py:748
  148.1 35.4 %collective-permute-start.33 = (bf16[192,3840]{1,0:T(8,128)(2,1)}, bf16[192,3840]{1,0:T(8,128)(2,1)}, u32[]{:S(2)}, u32[]{:S(2)}) collective-permute-start(bf16[192,3840]{1,0:T(8,128)(2,1)} %add_convert_fusion), channel_id=1, source_target_pairs={{0,2},{1,3},{2,0},{3,1},{4,6},{5,7},{6,4},{7,5},{8,10},{9,11},{10,... | collective-permute-start | bytes 4423688 | tf_op jit(solution)/shard_map/ppermute | solution.py:748
  161.5 40.4 %collective-permute-start.35 = (bf16[48,3072]{1,0:T(8,128)(2,1)}, bf16[48,3072]{1,0:T(8,128)(2,1)}, u32[]{:S(2)}, u32[]{:S(2)}) collective-permute-start(bf16[48,3072]{1,0:T(8,128)(2,1)} %get-tuple-element.234), channel_id=1, source_target_pairs={{0,8},{4,12},{8,0},{12,4},{16,24},{20,28},{24,16},{28,20},{1,9},{5... | collective-permute-start | bytes 884744 | tf_op jit(solution)/shard_map/ppermute | solution.py:748
  163.3 35.4 %collective-permute-start.36 = (bf16[96,768]{1,0:T(8,128)(2,1)}, bf16[96,768]{1,0:T(8,128)(2,1)}, u32[]{:S(2)}, u32[]{:S(2)}) collective-permute-start(bf16[96,768]{1,0:T(8,128)(2,1)} %add_convert_fusion.25), channel_id=1, source_target_pairs={{0,16},{4,20},{8,24},{12,28},{16,0},{20,4},{24,8},{28,12},{1,17},{... | collective-permute-start | bytes 442376 | tf_op jit(solution)/shard_map/ppermute | solution.py:748
  165.5 31.4 %collective-permute-start.29 = (bf16[128,768]{1,0:T(8,128)(2,1)}, bf16[128,768]{1,0:T(8,128)(2,1)}, u32[]{:S(2)}, u32[]{:S(2)}) collective-permute-start(bf16[128,768]{1,0:T(8,128)(2,1)} %fusion.7), channel_id=1, source_target_pairs={{0,2},{1,3},{2,0},{3,1},{4,6},{5,7},{6,4},{7,5},{8,10},{9,11},{10,... | collective-permute-start | bytes 589832 | tf_op jit(solution)/shard_map/ppermute | solution.py:748
  174.0 19.7 %collective-permute-start.32 = (bf16[384,2304]{1,0:T(8,128)(2,1)}, bf16[384,2304]{1,0:T(8,128)(2,1)}, u32[]{:S(2)}, u32[]{:S(2)}) collective-permute-start(bf16[384,2304]{1,0:T(8,128)(2,1)} %get-tuple-element.184), channel_id=1, source_target_pairs={{0,1},{1,0},{2,3},{3,2},{4,5},{5,4},{6,7},{7,6},{8,9},{9,8},{10,11... | collective-permute-start | bytes 5308424 | tf_op jit(solution)/shard_map/ppermute | solution.py:748
  187.0 17.6 %collective-permute-start.39 = (bf16[96,3840]{1,0:T(8,128)(2,1)}, bf16[96,3840]{1,0:T(8,128)(2,1)}, u32[]{:S(2)}, u32[]{:S(2)}) collective-permute-start(bf16[96,3840]{1,0:T(8,128)(2,1)} %get-tuple-element.230), channel_id=1, source_target_pairs={{0,4},{4,0},{8,12},{12,8},{16,20},{20,16},{24,28},{28,24},{1,5},{5... | collective-permute-start | bytes 2211848 | tf_op jit(solution)/shard_map/ppermute | solution.py:748
  195.2 20.8 %collective-permute-start.34 = (bf16[192,2304]{1,0:T(8,128)(2,1)S(1)}, bf16[192,2304]{1,0:T(8,128)(2,1)S(1)}, u32[]{:S(2)}, u32[]{:S(2)}) collective-permute-start(bf16[192,2304]{1,0:T(8,128)(2,1)S(1)} %add_convert_fusion.1), channel_id=1, source_target_pairs={{0,2},{1,3},{2,0},{3,1},{4,6},{5,7},{6,4},{7,5},{8,10},{9,11},{10,... | collective-permute-start | bytes 2654216 | tf_op jit(solution)/shard_map/ppermute | solution.py:748
  199.7 12.5 %collective-permute-start.38 = (bf16[96,768]{1,0:T(8,128)(2,1)S(1)}, bf16[96,768]{1,0:T(8,128)(2,1)S(1)}, u32[]{:S(2)}, u32[]{:S(2)}) collective-permute-start(bf16[96,768]{1,0:T(8,128)(2,1)S(1)} %add_convert_fusion.23), channel_id=1, source_target_pairs={{0,16},{4,20},{8,24},{12,28},{16,0},{20,4},{24,8},{28,12},{1,17},{... | collective-permute-start | bytes 442376 | tf_op jit(solution)/shard_map/ppermute | solution.py:748
  202.8 11.5 %collective-permute-start.37 = (bf16[24,3072]{1,0:T(8,128)(2,1)S(1)}, bf16[24,3072]{1,0:T(8,128)(2,1)S(1)}, u32[]{:S(2)}, u32[]{:S(2)}) collective-permute-start(bf16[24,3072]{1,0:T(8,128)(2,1)S(1)} %add_convert_fusion.21), channel_id=1, source_target_pairs={{0,16},{4,20},{8,24},{12,28},{16,0},{20,4},{24,8},{28,12},{1,17},{... | collective-permute-start | bytes 442376 | tf_op jit(solution)/shard_map/ppermute | solution.py:748
  205.9 20.7 %collective-permute-start.41 = (bf16[48,3840]{1,0:T(8,128)(2,1)S(1)}, bf16[48,3840]{1,0:T(8,128)(2,1)S(1)}, u32[]{:S(2)}, u32[]{:S(2)}) collective-permute-start(bf16[48,3840]{1,0:T(8,128)(2,1)S(1)} %get-tuple-element.246), channel_id=1, source_target_pairs={{0,8},{4,12},{8,0},{12,4},{16,24},{20,28},{24,16},{28,20},{1,9},{5... | collective-permute-start | bytes 1105928 | tf_op jit(solution)/shard_map/ppermute | solution.py:748
  212.3 22.4 %collective-permute-start.44 = (bf16[192,768]{1,0:T(8,128)(2,1)S(1)}, bf16[192,768]{1,0:T(8,128)(2,1)S(1)}, u32[]{:S(2)}, u32[]{:S(2)}) collective-permute-start(bf16[192,768]{1,0:T(8,128)(2,1)S(1)} %pad_maximum_fusion.10), channel_id=1, source_target_pairs={{0,8},{4,12},{8,0},{12,4},{16,24},{20,28},{24,16},{28,20},{1,9},{5... | collective-permute-start | bytes 884744 | tf_op jit(solution)/shard_map/ppermute | solution.py:748
  215.3 20.4 %collective-permute-start.43 = (bf16[24,3072]{1,0:T(8,128)(2,1)S(1)}, bf16[24,3072]{1,0:T(8,128)(2,1)S(1)}, u32[]{:S(2)}, u32[]{:S(2)}) collective-permute-start(bf16[24,3072]{1,0:T(8,128)(2,1)S(1)} %add_convert_fusion.20), channel_id=1, source_target_pairs={{0,16},{4,20},{8,24},{12,28},{16,0},{20,4},{24,8},{28,12},{1,17},{... | collective-permute-start | bytes 442376 | tf_op jit(solution)/shard_map/ppermute | solution.py:748
  217.6 13.2 %collective-permute-start.45 = (bf16[96,2304]{1,0:T(8,128)(2,1)S(1)}, bf16[96,2304]{1,0:T(8,128)(2,1)S(1)}, u32[]{:S(2)}, u32[]{:S(2)}) collective-permute-start(bf16[96,2304]{1,0:T(8,128)(2,1)S(1)} %get-tuple-element.232), channel_id=1, source_target_pairs={{0,4},{4,0},{8,12},{12,8},{16,20},{20,16},{24,28},{28,24},{1,5},{5... | collective-permute-start | bytes 1327112 | tf_op jit(solution)/shard_map/ppermute | solution.py:748
  218.3 29.3 %collective-permute-start.40 = (bf16[512,768]{1,0:T(8,128)(2,1)S(1)}, bf16[512,768]{1,0:T(8,128)(2,1)S(1)}, u32[]{:S(2)}, u32[]{:S(2)}) collective-permute-start(bf16[512,768]{1,0:T(8,128)(2,1)S(1)} %slice.280), channel_id=1, source_target_pairs={{0,4},{4,0},{8,12},{12,8},{16,20},{20,16},{24,28},{28,24},{1,5},{5... | collective-permute-start | bytes 2359304 | tf_op jit(solution)/shard_map/ppermute | solution.py:748
  226.7 9.2 %collective-permute-start.42 = (bf16[24,3840]{1,0:T(8,128)(2,1)S(1)}, bf16[24,3840]{1,0:T(8,128)(2,1)S(1)}, u32[]{:S(2)}, u32[]{:S(2)}) collective-permute-start(bf16[24,3840]{1,0:T(8,128)(2,1)S(1)} %add_convert_fusion.18), channel_id=1, source_target_pairs={{0,16},{4,20},{8,24},{12,28},{16,0},{20,4},{24,8},{28,12},{1,17},{... | collective-permute-start | bytes 552968 | tf_op jit(solution)/shard_map/ppermute | solution.py:748
  230.9 18.6 %collective-permute-start.49 = (bf16[48,2304]{1,0:T(8,128)(2,1)S(1)}, bf16[48,2304]{1,0:T(8,128)(2,1)S(1)}, u32[]{:S(2)}, u32[]{:S(2)}) collective-permute-start(bf16[48,2304]{1,0:T(8,128)(2,1)S(1)} %get-tuple-element.256), channel_id=1, source_target_pairs={{0,8},{4,12},{8,0},{12,4},{16,24},{20,28},{24,16},{28,20},{1,9},{5... | collective-permute-start | bytes 663560 | tf_op jit(solution)/shard_map/ppermute | solution.py:748
  234.8 42.6 %collective-permute-start.53 = (bf16[384,768]{1,0:T(8,128)(2,1)S(1)}, bf16[384,768]{1,0:T(8,128)(2,1)S(1)}, u32[]{:S(2)}, u32[]{:S(2)}) collective-permute-start(bf16[384,768]{1,0:T(8,128)(2,1)S(1)} %pad_maximum_fusion.4), channel_id=1, source_target_pairs={{0,4},{4,0},{8,12},{12,8},{16,20},{20,16},{24,28},{28,24},{1,5},{5... | collective-permute-start | bytes 1769480 | tf_op jit(solution)/shard_map/ppermute | solution.py:748
  235.8 15.3 %collective-permute-start.48 = (bf16[48,3072]{1,0:T(8,128)(2,1)S(1)}, bf16[48,3072]{1,0:T(8,128)(2,1)S(1)}, u32[]{:S(2)}, u32[]{:S(2)}) collective-permute-start(bf16[48,3072]{1,0:T(8,128)(2,1)S(1)} %pad_maximum_fusion.11), channel_id=1, source_target_pairs={{0,8},{4,12},{8,0},{12,4},{16,24},{20,28},{24,16},{28,20},{1,9},{5... | collective-permute-start | bytes 884744 | tf_op jit(solution)/shard_map/ppermute | solution.py:748
  236.0 16.0 %collective-permute-start.47 = (bf16[24,3840]{1,0:T(8,128)(2,1)S(1)}, bf16[24,3840]{1,0:T(8,128)(2,1)S(1)}, u32[]{:S(2)}, u32[]{:S(2)}) collective-permute-start(bf16[24,3840]{1,0:T(8,128)(2,1)S(1)} %add_convert_fusion.17), channel_id=1, source_target_pairs={{0,16},{4,20},{8,24},{12,28},{16,0},{20,4},{24,8},{28,12},{1,17},{... | collective-permute-start | bytes 552968 | tf_op jit(solution)/shard_map/ppermute | solution.py:748
  247.9 14.7 %collective-permute-start.46 = (bf16[256,768]{1,0:T(8,128)(2,1)S(1)}, bf16[256,768]{1,0:T(8,128)(2,1)S(1)}, u32[]{:S(2)}, u32[]{:S(2)}) collective-permute-start(bf16[256,768]{1,0:T(8,128)(2,1)S(1)} %slice.329), channel_id=1, source_target_pairs={{0,8},{4,12},{8,0},{12,4},{16,24},{20,28},{24,16},{28,20},{1,9},{5... | collective-permute-start | bytes 1179656 | tf_op jit(solution)/shard_map/ppermute | solution.py:748
  249.5 13.2 %collective-permute-start.51 = (bf16[24,2304]{1,0:T(8,128)(2,1)S(1)}, bf16[24,2304]{1,0:T(8,128)(2,1)S(1)}, u32[]{:S(2)}, u32[]{:S(2)}) collective-permute-start(bf16[24,2304]{1,0:T(8,128)(2,1)S(1)} %add_convert_fusion.28), channel_id=1, source_target_pairs={{0,16},{4,20},{8,24},{12,28},{16,0},{20,4},{24,8},{28,12},{1,17},{... | collective-permute-start | bytes 331784 | tf_op jit(solution)/shard_map/ppermute | solution.py:748
  251.3 27.7 %collective-permute-start.56 = (bf16[96,3072]{1,0:T(8,128)(2,1)S(1)}, bf16[96,3072]{1,0:T(8,128)(2,1)S(1)}, u32[]{:S(2)}, u32[]{:S(2)}) collective-permute-start(bf16[96,3072]{1,0:T(8,128)(2,1)S(1)} %pad_maximum_fusion.5.own_ref), channel_id=1, source_target_pairs={{0,4},{4,0},{8,12},{12,8},{16,20},{20,16},{24,28},{28,24},{1,5},{5... | collective-permute-start | bytes 1769480 | tf_op jit(solution)/shard_map/ppermute | solution.py:748
  252.0 21.9 %collective-permute-start.54 = (bf16[48,3840]{1,0:T(8,128)(2,1)S(1)}, bf16[48,3840]{1,0:T(8,128)(2,1)S(1)}, u32[]{:S(2)}, u32[]{:S(2)}) collective-permute-start(bf16[48,3840]{1,0:T(8,128)(2,1)S(1)} %pad_maximum_fusion.9), channel_id=1, source_target_pairs={{0,8},{4,12},{8,0},{12,4},{16,24},{20,28},{24,16},{28,20},{1,9},{5... | collective-permute-start | bytes 1105928 | tf_op jit(solution)/shard_map/ppermute | solution.py:748
  262.7 10.4 %collective-permute-start.50 = (bf16[128,768]{1,0:T(8,128)(2,1)S(1)}, bf16[128,768]{1,0:T(8,128)(2,1)S(1)}, u32[]{:S(2)}, u32[]{:S(2)}) collective-permute-start(bf16[128,768]{1,0:T(8,128)(2,1)S(1)} %slice.333), channel_id=1, source_target_pairs={{0,16},{4,20},{8,24},{12,28},{16,0},{20,4},{24,8},{28,12},{1,17},{... | collective-permute-start | bytes 589832 | tf_op jit(solution)/shard_map/ppermute | solution.py:748
  262.8 15.4 %collective-permute-start.52 = (bf16[24,2304]{1,0:T(8,128)(2,1)S(1)}, bf16[24,2304]{1,0:T(8,128)(2,1)S(1)}, u32[]{:S(2)}, u32[]{:S(2)}) collective-permute-start(bf16[24,2304]{1,0:T(8,128)(2,1)S(1)} %add_convert_fusion.26), channel_id=1, source_target_pairs={{0,16},{4,20},{8,24},{12,28},{16,0},{20,4},{24,8},{28,12},{1,17},{... | collective-permute-start | bytes 331784 | tf_op jit(solution)/shard_map/ppermute | solution.py:748
  275.2 15.4 %collective-permute-start.58 = (bf16[96,3840]{1,0:T(8,128)(2,1)}, bf16[96,3840]{1,0:T(8,128)(2,1)S(1)}, u32[]{:S(2)}, u32[]{:S(2)}) collective-permute-start(bf16[96,3840]{1,0:T(8,128)(2,1)} %pad_maximum_fusion.1), channel_id=1, source_target_pairs={{0,4},{4,0},{8,12},{12,8},{16,20},{20,16},{24,28},{28,24},{1,5},{5... | collective-permute-start | bytes 2211848 | tf_op jit(solution)/shard_map/ppermute | solution.py:748
  279.0 9.8 %collective-permute-start.55 = (bf16[48,2304]{1,0:T(8,128)(2,1)}, bf16[48,2304]{1,0:T(8,128)(2,1)}, u32[]{:S(2)}, u32[]{:S(2)}) collective-permute-start(bf16[48,2304]{1,0:T(8,128)(2,1)} %pad_maximum_fusion.12), channel_id=1, source_target_pairs={{0,8},{4,12},{8,0},{12,4},{16,24},{20,28},{24,16},{28,20},{1,9},{5... | collective-permute-start | bytes 663560 | tf_op jit(solution)/shard_map/ppermute | solution.py:748
  (60 other events, 328.5 us)

commit v7 on v6

--- a/solution.py
+++ b/solution.py
@@ -477,7 +477,7 @@
             query = head_rows(q_ref[pl.ds(s * STRETCH, STRETCH), part], head_size, score_scale)
             scores = right_product(kv_ref[0, span, part], query)
             weights = jnp.exp(scores - jnp.max(scores, axis=0, keepdims=True))
-            probs = to_low(weights / jnp.sum(weights, axis=0, keepdims=True))
+            probs = to_low(weights * (1.0 / jnp.sum(weights, axis=0, keepdims=True)))
             parts.append(join_heads(left_product(kv_ref[1, span, part], probs), head_size))
         sides.append(jnp.concatenate(parts, axis=0))
     columns = pl.ds(pl.multiple_of(pair * wide, wide), wide)
@@ -684,7 +684,7 @@
             grad = head_rows(do_ref[rows, place], head_size)
             scores = right_product(kv_ref[0, span, part], query)
             weights = jnp.exp(scores - jnp.max(scores, axis=0, keepdims=True))
-            probs = weights / jnp.sum(weights, axis=0, keepdims=True)
+            probs = weights * (1.0 / jnp.sum(weights, axis=0, keepdims=True))
             dprobs = right_product(kv_ref[1, span, part], grad)
             delta = jnp.sum(probs * dprobs, axis=0, keepdims=True)
             dscores = to_low(probs * (dprobs - delta))

time: 303 us -> 303 us (level)
  no operation moved by 1% of the time
where the time goes in v7:
time: 303 us; the launch traced here: 301 us
  Pallas kernels  99.7 us (33%)
  waiting for transfers between devices  85.3 us (28%)
  starting transfers between devices  58.8 us (19%)
  other arithmetic  40.3 us (13%)
  local copies, waits for them, and re-layouts  15.7 us (5%)
    ppermute x59, waiting for transfers between devices, swap(): return lax.ppermute(values, axis, [(i, i ^ bit) for i in range(count)])  85.3 us
    pallas_call x8, Pallas kernels, chain_call(): pl.pallas_call(kernel, grid_spec=pltpu.PrefetchScalarGridSpec(num_scalar_...  62.4 us
    ppermute x59, starting transfers between devices, swap(): return lax.ppermute(values, axis, [(i, i ^ bit) for i in range(count)])  58.8 us
    convert_element_type x20, other arithmetic, to_low(): return values.astype(jnp.bfloat16)  18.7 us
    pallas_call x2, Pallas kernels, wide_products(): pl.pallas_call(functools.partial(products_kernel, tiles, rows, chunks), g...  16.3 us
    pallas_call x1, Pallas kernels, self_backward(): pl.pallas_call(functools.partial(self_backward_kernel, head_size, blocks)...  9.33 us
    unnamed x101, local copies, waits for them, and re-layouts  8.9 us
    pallas_call x1, Pallas kernels, self_forward(): pl.pallas_call(functools.partial(self_forward_kernel, head_size, blocks),...  7.14 us
  transfers between devices with their start and end apart: 59, of which 22 were waited for; matrix products, arithmetic and copies ran while one was open for 15% of the time, Pallas kernels for 27%

profile of v7, /device:TPU:0, one launch (start us, length us, event | category | flops | bytes accessed | tf_op | source)
XLA Modules:
  0.0 301.4 jit_solution(7517622957316272214)
XLA Ops:
  0.7 3.1 %collective-permute-start = (bf16[128,768]{1,0:T(8,128)(2,1)}, bf16[128,768]{1,0:T(8,128)(2,1)}, u32[]{:S(2)}, u32[]{:S(2)}) collective-permute-start(bf16[128,768]{1,0:T(8,128)(2,1)} %bitcast.27), channel_id=1, source_target_pairs={{0,8},{4,12},{8,0},{12,4},{16,24},{20,28},{24,16},{28,20},{1,9},{5... | collective-permute-start | bytes 589832 | tf_op jit(solution)/shard_map/ppermute | solution.py:748
  3.7 2.5 collective-permute-start.2
  10.0 1.6 collective-permute-start.7
  13.3 3.2 %collective-permute-done.2 = bf16[128,768]{1,0:T(8,128)(2,1)S(1)} collective-permute-done((bf16[128,768]{1,0:T(8,128)(2,1)}, bf16[128,768]{1,0:T(8,128)(2,1)S(1)}, u32[]{:S(2)}, u32[]{:S(2)}) %collective-permute-start.2) | collective-permute-done | bytes 196640 | tf_op jit(solution)/shard_map/ppermute | solution.py:748
  16.5 7.4 %collective-permute-done.1 = bf16[128,768]{1,0:T(8,128)(2,1)} collective-permute-done((bf16[128,768]{1,0:T(8,128)(2,1)}, bf16[128,768]{1,0:T(8,128)(2,1)}, u32[]{:S(2)}, u32[]{:S(2)}) %collective-permute-start.1) | collective-permute-done | bytes 196640 | tf_op jit(solution)/shard_map/ppermute | solution.py:748
  31.3 1.6 collective-permute-start.10
  33.4 5.8 %collective-permute-done.4.refs_4_ = bf16[128,768]{1,0:T(8,128)(2,1)S(1)} collective-permute-done((bf16[128,768]{1,0:T(8,128)(2,1)}, bf16[128,768]{1,0:T(8,128)(2,1)S(1)}, u32[]{:S(2)}, u32[]{:S(2)}) %collective-permute-start.4) | collective-permute-done | bytes 196640 | tf_op jit(solution)/shard_map/ppermute | solution.py:748
  39.9 3.0 %held_rows.1 = (bf16[1024,768]{1,0:T(8,128)(2,1)}, f32[1024,1]{1,0:T(8,128)}) custom-call(bf16[128,768]{1,0:T(8,128)(2,1)} %bitcast.31, bf16[128,768]{1,0:T(8,128)(2,1)} %collective-permute-done.refs_1_, bf16[256,768]{1,0:T(8,128)(2,1)} %copy-done.25, bf16[128,768]{1,0:T(8,128)(2,1)} %collective-permute-done.3.refs_3_, bf16[128,768]{1,0:T(8,128)(2,1)} %copy-done.45, ...), custom_call_target="tpu_custom_call" | custom-call | flops 23000000512 | bytes 2000000 | tf_op jit(solution)/shard_map/held_rows/pallas_call | solution.py:308
  43.8 9.4 %project.1 = (bf16[128,768]{1,0:T(8,128)(2,1)}, bf16[1024,1536]{1,0:T(8,128)(2,1)}, bf16[1024,768]{1,0:T(8,128)(2,1)}, bf16[768,2304]{1,0:T(8,128)(2,1)}, f32[8,768]{1,0:T(8,128)}) custom-call(s32[3]{0:T(128)} %pad_add_fusion.index_ref, bf16[1024,768]{1,0:T(8,128)(2,1)} %get-tuple-element.118.rows_ref, f32[1024,1]{1,0:T(8,128)} %get-tuple-element.119.scale_ref, ...), custom_call_target="tpu_custom_call" | custom-call | flops 103499997184 | bytes 9000000 | tf_op jit(solution)/shard_map/project/pallas_call | solution.py:275
  53.8 7.1 %self_forward.1 = (bf16[128,768]{1,0:T(8,128)(2,1)}, f32[6,1,256]{2,1,0:T(1,128)}) custom-call(bf16[128,768]{1,0:T(8,128)(2,1)} %get-tuple-element.124.q_ref, bf16[1024,1536]{1,0:T(8,128)(2,1)} %get-tuple-element.125.k_ref.v_ref, bf16[1024,1536]{1,0:T(8,128)(2,1)} %get-tuple-element.125.k_ref.v_ref, s32[1024,1]{1,0:T(8,128)} %get-tuple-element.126.pos_ref, ...), custom_call_target="tpu_custom_call" | custom-call | flops 87399997440 | bytes 7600000 | tf_op jit(solution)/shard_map/self_forward/pallas_call | solution.py:216
  61.1 5.0 %collective-permute-done.13.refs_7_.refs_11_.refs_15_ = bf16[192,2304]{1,0:T(8,128)(2,1)} collective-permute-done((bf16[192,2304]{1,0:T(8,128)(2,1)}, bf16[192,2304]{1,0:T(8,128)(2,1)}, u32[]{:S(2)}, u32[]{:S(2)}) %collective-permute-start.13) | collective-permute-done | bytes 884768 | tf_op jit(solution)/shard_map/ppermute | solution.py:748
  68.4 4.2 %attend_out.1 = (f32[128,768]{1,0:T(8,128)}, bf16[128,768]{1,0:T(8,128)(2,1)}, bf16[128,768]{1,0:T(8,128)(2,1)}, bf16[768,1536]{1,0:T(8,128)(2,1)}) custom-call(s32[3]{0:T(128)} %pad_add_fusion.index_ref, bf16[128,768]{1,0:T(8,128)(2,1)} %get-tuple-element.129.att_ref.refs_7_, bf16[128,768]{1,0:T(8,128)(2,1)} %bitcast.32, ...), custom_call_target="tpu_custom_call" | custom-call | flops 50600001536 | bytes 4400000 | tf_op jit(solution)/shard_map/attend_out/pallas_call | solution.py:275
  74.0 9.5 %cross_forward.1 = (bf16[2,512,768]{2,1,0:T(8,128)(2,1)}, bf16[128,768]{1,0:T(8,128)(2,1)}, f32[128,768]{1,0:T(8,128)}, bf16[128,768]{1,0:T(8,128)(2,1)}, bf16[2...) custom-call(s32[3]{0:T(128)} %pad_add_fusion.index_ref, bf16[128,768]{1,0:T(8,128)(2,1)} %get-tuple-element.134.refs_0_, ...), custom_call_target="tpu_custom_call" | custom-call | flops 141450002432 | bytes 12300000 | tf_op jit(solution)/shard_map/cross_forward/pallas_call | solution.py:275
  83.5 2.8 collective-permute-done.19.refs_7_
  88.5 5.6 %collective-permute-done.16.refs_2_ = bf16[128,768]{1,0:T(8,128)(2,1)S(1)} collective-permute-done((bf16[128,768]{1,0:T(8,128)(2,1)}, bf16[128,768]{1,0:T(8,128)(2,1)S(1)}, u32[]{:S(2)}, u32[]{:S(2)}) %collective-permute-start.16) | collective-permute-done | bytes 196640 | tf_op jit(solution)/shard_map/ppermute | solution.py:748
  96.5 9.9 %mlp_share.1 = (f32[128,768]{1,0:T(8,128)}, bf16[128,768]{1,0:T(8,128)(2,1)}, bf16[128,768]{1,0:T(8,128)(2,1)}, bf16[128,768]{1,0:T(8,128)(2,1)}, f32[128,768]{1...) custom-call(s32[3]{0:T(128)} %pad_add_fusion.index_ref, ...), custom_call_target="tpu_custom_call" | custom-call | flops 126500003840 | bytes 11000000 | tf_op jit(solution)/shard_map/mlp_share/pallas_call | solution.py:275
  108.6 1.9 slice.242
  115.9 2.5 collective-permute-done.23.refs_12_
  119.1 11.0 %cross_backward.1 = (bf16[128,768]{1,0:T(8,128)(2,1)}, bf16[2,512,768]{2,1,0:T(8,128)(2,1)}, f32[128,768]{1,0:T(8,128)}, bf16[128,768]{1,0:T(8,128)(2,1)}, bf16[...) custom-call(s32[3]{0:T(128)} %pad_add_fusion.index_ref, bf16[128,768]{1,0:T(8,128)(2,1)} %get-tuple-element.134.refs_0_, ...), custom_call_target="tpu_custom_call" | custom-call | flops 149500002304 | bytes 13000000 | tf_op jit(solution)/shard_map/cross_backward/pallas_call | solution.py:275
  131.2 8.3 %wide_products.2 = (bf16[384,3840]{1,0:T(8,128)(2,1)}, bf16[384,3840]{1,0:T(8,128)(2,1)}) custom-call(s32[3]{0:T(128)} %pad_add_fusion.index_ref, bf16[128,768]{1,0:T(8,128)(2,1)} %get-tuple-element.156.refs_0_, bf16[128,768]{1,0:T(8,128)(2,1)} %get-tuple-element.157.refs_1_, bf16[128,768]{1,0:T(8,128)(2,1)} %get-tuple-element.158.refs_2_, ...), custom_call_target="tpu_custom_call" | custom-call | flops 94299996160 | bytes 8199999 | tf_op jit(solution)/shard_map/wide_products/pallas_call | solution.py:866
  145.3 2.9 add_convert_fusion
  149.6 9.3 %self_backward.1 = (bf16[128,768]{1,0:T(8,128)(2,1)}, bf16[2,1024,768]{2,1,0:T(8,128)(2,1)}) custom-call(bf16[128,768]{1,0:T(8,128)(2,1)} %get-tuple-element.124.q_ref, bf16[1024,1536]{1,0:T(8,128)(2,1)} %get-tuple-element.125.k_ref.v_ref, bf16[1024,1536]{1,0:T(8,128)(2,1)} %get-tuple-element.125.k_ref.v_ref, bf16[128,768]{1,0:T(8,128)(2,1)} %get-tuple-element.173.do_ref, ...), custom_call_target="tpu_custom_call" | custom-call | flops 117300002816 | bytes 10200000 | tf_op jit(solution)/shard_map/self_backward/pallas_call | solution.py:237
  159.0 1.6 add_convert_fusion.25
  161.5 1.8 collective-permute-start.35
  166.0 8.0 %wide_products.3 = (bf16[384,2304]{1,0:T(8,128)(2,1)}, bf16[384,2304]{1,0:T(8,128)(2,1)}) custom-call(s32[3]{0:T(128)} %pad_add_fusion.index_ref, bf16[1024,768]{1,0:T(8,128)(2,1)} %get-tuple-element.178.refs_0_.refs_2_, bf16[128,768]{1,0:T(8,128)(2,1)} %get-tuple-element.181.refs_1_.query_ref, bf16[1024,768]{1,0:T(8,128)(2,1)} %get-tuple-element.178.refs_0_.refs_2_, ...), custom_call_target="tpu_custom_call" | custom-call | flops 115000000 | bytes 10000 | tf_op jit(solution)/shard_map/wide_products/pallas_call | solution.py:866
  174.0 8.0 %norm_terms.1 = (bf16[1024,768]{1,0:T(8,128)(2,1)}, f32[128,768]{1,0:T(8,128)}) custom-call(s32[3]{0:T(128)} %pad_add_fusion.index_ref, bf16[2,1024,768]{2,1,0:T(8,128)(2,1)} %get-tuple-element.185.refs_3_.refs_4_.pair_ref, bf16[128,768]{1,0:T(8,128)(2,1)} %get-tuple-element.181.refs_1_.query_ref, bf16[768,2304]{1,0:T(8,128)(2,1)} %get-tuple-element.186.w_ref), custom_call_target="tpu_custom_call" | custom-call | flops 115000000 | bytes 10000 | tf_op jit(solution)/shard_map/norm_terms/pallas_call | solution.py:275
  182.0 1.6 collective-permute-done.33
  183.6 3.4 %add_convert_fusion.3 = (bf16[96,3840]{1,0:T(8,128)(2,1)}, bf16[96,3840]{1,0:T(8,128)(2,1)}) fusion(bf16[192,3840]{1,0:T(8,128)(2,1)} %collective-permute-done.33, bf16[384,3840]{1,0:T(8,128)(2,1)} %collective-permute-done.28, bf16[384,3840]{1,0:T(8,128)(2,1)S(1)} %copy-done.2), kind=kLoop, calls=%fused_computation.6 | loop fusion | flops 4423680 | bytes 5898240 | tf_op jit(solution)/shard_map/convert_element_type | solution.py:26
  188.5 5.2 %enc_terms.1 = f32[512,768]{1,0:T(8,128)} custom-call(s32[3]{0:T(128)} %pad_add_fusion.index_ref, bf16[2,512,768]{2,1,0:T(8,128)(2,1)} %get-tuple-element.189.refs_5_.refs_6_.pair_ref, bf16[2,768,768]{2,1,0:T(8,128)(2,1)} %get-tuple-element.190.w_ref), custom_call_target="tpu_custom_call" | custom-call | flops 46000001024 | bytes 4000000 | tf_op jit(solution)/shard_map/enc_terms/pallas_call | solution.py:275
  195.2 1.6 collective-permute-start.34
  196.9 1.8 fusion.9
  199.7 2.1 collective-permute-start.38
  205.9 1.9 collective-permute-start.41
  207.8 4.4 %collective-permute-done.38 = bf16[96,768]{1,0:T(8,128)(2,1)S(1)} collective-permute-done((bf16[96,768]{1,0:T(8,128)(2,1)S(1)}, bf16[96,768]{1,0:T(8,128)(2,1)S(1)}, u32[]{:S(2)}, u32[]{:S(2)}) %collective-permute-start.38) | collective-permute-done | bytes 147488 | tf_op jit(solution)/shard_map/ppermute | solution.py:748
  212.4 2.0 collective-permute-done.37
  219.8 6.8 %collective-permute-done.41 = bf16[48,3840]{1,0:T(8,128)(2,1)S(1)} collective-permute-done((bf16[48,3840]{1,0:T(8,128)(2,1)S(1)}, bf16[48,3840]{1,0:T(8,128)(2,1)S(1)}, u32[]{:S(2)}, u32[]{:S(2)}) %collective-permute-start.41) | collective-permute-done | bytes 368672 | tf_op jit(solution)/shard_map/ppermute | solution.py:748
  227.2 3.5 %collective-permute-done.45 = bf16[96,2304]{1,0:T(8,128)(2,1)S(1)} collective-permute-done((bf16[96,2304]{1,0:T(8,128)(2,1)S(1)}, bf16[96,2304]{1,0:T(8,128)(2,1)S(1)}, u32[]{:S(2)}, u32[]{:S(2)}) %collective-permute-start.45) | collective-permute-done | bytes 442400 | tf_op jit(solution)/shard_map/ppermute | solution.py:748
  230.9 1.6 collective-permute-start.49
  232.5 2.2 collective-permute-done.44
  236.0 5.5 %collective-permute-start.47 = (bf16[24,3840]{1,0:T(8,128)(2,1)S(1)}, bf16[24,3840]{1,0:T(8,128)(2,1)S(1)}, u32[]{:S(2)}, u32[]{:S(2)}) collective-permute-start(bf16[24,3840]{1,0:T(8,128)(2,1)S(1)} %add_convert_fusion.17), channel_id=1, source_target_pairs={{0,16},{4,20},{8,24},{12,28},{16,0},{20,4},{24,8},{28,12},{1,17},{... | collective-permute-start | bytes 552968 | tf_op jit(solution)/shard_map/ppermute | solution.py:748
  241.5 6.1 %collective-permute-done.40 = bf16[512,768]{1,0:T(8,128)(2,1)S(1)} collective-permute-done((bf16[512,768]{1,0:T(8,128)(2,1)S(1)}, bf16[512,768]{1,0:T(8,128)(2,1)S(1)}, u32[]{:S(2)}, u32[]{:S(2)}) %collective-permute-start.40) | collective-permute-done | bytes 786464 | tf_op jit(solution)/shard_map/ppermute | solution.py:748
  247.9 1.6 collective-permute-start.46
  253.2 9.3 %collective-permute-done.46 = bf16[256,768]{1,0:T(8,128)(2,1)S(1)} collective-permute-done((bf16[256,768]{1,0:T(8,128)(2,1)S(1)}, bf16[256,768]{1,0:T(8,128)(2,1)S(1)}, u32[]{:S(2)}, u32[]{:S(2)}) %collective-permute-start.46) | collective-permute-done | bytes 393248 | tf_op jit(solution)/shard_map/ppermute | solution.py:748
  262.8 3.0 collective-permute-start.52
  265.8 7.3 %collective-permute-done.50 = bf16[128,768]{1,0:T(8,128)(2,1)S(1)} collective-permute-done((bf16[128,768]{1,0:T(8,128)(2,1)S(1)}, bf16[128,768]{1,0:T(8,128)(2,1)S(1)}, u32[]{:S(2)}, u32[]{:S(2)}) %collective-permute-start.50) | collective-permute-done | bytes 196640 | tf_op jit(solution)/shard_map/ppermute | solution.py:748
  279.8 5.1 %inner_out.1 = (f32[192,3072]{1,0:T(8,128)}, f32[192,1]{1,0:T(8,128)}) custom-call(s32[3]{0:T(128)} %pad_add_fusion.index_ref, bf16[96,3072]{1,0:T(8,128)(2,1)} %copy-done.20, bf16[96,3072]{1,0:T(8,128)(2,1)} %copy-done.39, bf16[192,3072]{1,0:T(8,128)(2,1)} %weight_ref.1, f32[192,1]{1,0:T(8,128)} %copy.26.gain_ref), custom_call_target="tpu_custom_call" | custom-call | flops 34500001792 | bytes 3000000 | tf_op jit(solution)/shard_map/inner_out/pallas_call | solution.py:275
  287.2 1.6 maximum_convert_fusion
  293.1 5.1 %collective-permute-done.57 = bf16[96,2304]{1,0:T(8,128)(2,1)S(1)} collective-permute-done((bf16[96,2304]{1,0:T(8,128)(2,1)S(1)}, bf16[96,2304]{1,0:T(8,128)(2,1)S(1)}, u32[]{:S(2)}, u32[]{:S(2)}) %collective-permute-start.57) | collective-permute-done | bytes 442400 | tf_op jit(solution)/shard_map/ppermute | solution.py:748
  (258 shorter events, 79.9 us)
Async XLA Ops:
  0.7 24.3 %collective-permute-start = (bf16[128,768]{1,0:T(8,128)(2,1)}, bf16[128,768]{1,0:T(8,128)(2,1)}, u32[]{:S(2)}, u32[]{:S(2)}) collective-permute-start(bf16[128,768]{1,0:T(8,128)(2,1)} %bitcast.27), channel_id=1, source_target_pairs={{0,8},{4,12},{8,0},{12,4},{16,24},{20,28},{24,16},{28,20},{1,9},{5... | collective-permute-start | bytes 589832 | tf_op jit(solution)/shard_map/ppermute | solution.py:748
  3.7 12.8 %collective-permute-start.2 = (bf16[128,768]{1,0:T(8,128)(2,1)}, bf16[128,768]{1,0:T(8,128)(2,1)S(1)}, u32[]{:S(2)}, u32[]{:S(2)}) collective-permute-start(bf16[128,768]{1,0:T(8,128)(2,1)} %bitcast.28), channel_id=1, source_target_pairs={{0,24},{4,28},{8,16},{12,20},{16,8},{20,12},{24,0},{28,4},{1,25},{... | collective-permute-start | bytes 589832 | tf_op jit(solution)/shard_map/ppermute | solution.py:748
  6.2 17.7 %collective-permute-start.1 = (bf16[128,768]{1,0:T(8,128)(2,1)}, bf16[128,768]{1,0:T(8,128)(2,1)}, u32[]{:S(2)}, u32[]{:S(2)}) collective-permute-start(bf16[128,768]{1,0:T(8,128)(2,1)} %bitcast.29), channel_id=1, source_target_pairs={{0,16},{4,20},{8,24},{12,28},{16,0},{20,4},{24,8},{28,12},{1,17},{... | collective-permute-start | bytes 589832 | tf_op jit(solution)/shard_map/ppermute | solution.py:748
  6.3 24.8 %collective-permute-start.3 = (bf16[128,768]{1,0:T(8,128)(2,1)}, bf16[128,768]{1,0:T(8,128)(2,1)}, u32[]{:S(2)}, u32[]{:S(2)}) collective-permute-start(bf16[128,768]{1,0:T(8,128)(2,1)} %bitcast.30), channel_id=1, source_target_pairs={{0,4},{4,0},{8,12},{12,8},{16,20},{20,16},{24,28},{28,24},{1,5},{5... | collective-permute-start | bytes 589832 | tf_op jit(solution)/shard_map/ppermute | solution.py:748
  10.0 22.9 %collective-permute-start.7 = (bf16[192,2432]{1,0:T(8,128)(2,1)S(1)}, bf16[192,2432]{1,0:T(8,128)(2,1)}, u32[]{:S(2)}, u32[]{:S(2)}) collective-permute-start(bf16[192,2432]{1,0:T(8,128)(2,1)S(1)} %fusion.1.refs_0_), channel_id=1, source_target_pairs={{0,2},{1,3},{2,0},{3,1},{4,6},{5,7},{6,4},{7,5},{8,10},{9,11},{10,... | collective-permute-start | bytes 2801672 | tf_op jit(solution)/shard_map/ppermute | solution.py:748
  24.9 14.3 %collective-permute-start.5 = (bf16[256,768]{1,0:T(8,128)(2,1)S(1)}, bf16[256,768]{1,0:T(8,128)(2,1)}, u32[]{:S(2)}, u32[]{:S(2)}) collective-permute-start(bf16[256,768]{1,0:T(8,128)(2,1)S(1)} %pad_maximum_fusion.8.refs_2_), channel_id=1, source_target_pairs={{0,4},{4,0},{8,12},{12,8},{16,20},{20,16},{24,28},{28,24},{1,5},{5... | collective-permute-start | bytes 1179656 | tf_op jit(solution)/shard_map/ppermute | solution.py:748
  27.4 11.8 %collective-permute-start.4 = (bf16[128,768]{1,0:T(8,128)(2,1)}, bf16[128,768]{1,0:T(8,128)(2,1)S(1)}, u32[]{:S(2)}, u32[]{:S(2)}) collective-permute-start(bf16[128,768]{1,0:T(8,128)(2,1)} %collective-permute-done.refs_1_), channel_id=1, source_target_pairs={{0,4},{4,0},{8,12},{12,8},{16,20},{20,16},{24,28},{28,24},{1,5},{5... | collective-permute-start | bytes 589832 | tf_op jit(solution)/shard_map/ppermute | solution.py:748
  31.2 11.7 %collective-permute-start.6 = (bf16[192,2432]{1,0:T(8,128)(2,1)S(1)}, bf16[192,2432]{1,0:T(8,128)(2,1)S(1)}, u32[]{:S(2)}, u32[]{:S(2)}) collective-permute-start(bf16[192,2432]{1,0:T(8,128)(2,1)S(1)} %fusion.1.refs_0_), channel_id=1, source_target_pairs={{0,1},{1,0},{2,3},{3,2},{4,5},{5,4},{6,7},{7,6},{8,9},{9,8},{10,11... | collective-permute-start | bytes 2801672 | tf_op jit(solution)/shard_map/ppermute | solution.py:748
  31.3 22.1 %collective-permute-start.10 = (bf16[192,1536]{1,0:T(8,128)(2,1)S(1)}, bf16[192,1536]{1,0:T(8,128)(2,1)}, u32[]{:S(2)}, u32[]{:S(2)}) collective-permute-start(bf16[192,1536]{1,0:T(8,128)(2,1)S(1)} %copy-done.32), channel_id=1, source_target_pairs={{0,2},{1,3},{2,0},{3,1},{4,6},{5,7},{6,4},{7,5},{8,10},{9,11},{10,... | collective-permute-start | bytes 1769480 | tf_op jit(solution)/shard_map/ppermute | solution.py:748
  32.9 33.2 %collective-permute-start.13 = (bf16[192,2304]{1,0:T(8,128)(2,1)}, bf16[192,2304]{1,0:T(8,128)(2,1)}, u32[]{:S(2)}, u32[]{:S(2)}) collective-permute-start(bf16[192,2304]{1,0:T(8,128)(2,1)} %constant_dynamic-update-slice_fusion.2.refs_5_.refs_9_.refs_13_), channel_id=1, source_target_pairs={{0,2},{1,3},{2,0},{3,1},{4,6},{5,7},{6,4},{7,5},{8,10},{9,11},{10,... | collective-permute-start | bytes 2654216 | tf_op jit(solution)/shard_map/ppermute | solution.py:748
  53.2 14.3 %collective-permute-start.9 = (bf16[192,1536]{1,0:T(8,128)(2,1)S(1)}, bf16[192,1536]{1,0:T(8,128)(2,1)S(1)}, u32[]{:S(2)}, u32[]{:S(2)}) collective-permute-start(bf16[192,1536]{1,0:T(8,128)(2,1)S(1)} %copy-done.32), channel_id=1, source_target_pairs={{0,1},{1,0},{2,3},{3,2},{4,5},{5,4},{6,7},{7,6},{8,9},{9,8},{10,11... | collective-permute-start | bytes 1769480 | tf_op jit(solution)/shard_map/ppermute | solution.py:748
  53.3 14.3 %collective-permute-start.11 = (bf16[192,1536]{1,0:T(8,128)(2,1)}, bf16[192,1536]{1,0:T(8,128)(2,1)}, u32[]{:S(2)}, u32[]{:S(2)}) collective-permute-start(bf16[192,1536]{1,0:T(8,128)(2,1)} %collective-permute-done.10.refs_2_), channel_id=1, source_target_pairs={{0,1},{1,0},{2,3},{3,2},{4,5},{5,4},{6,7},{7,6},{8,9},{9,8},{10,11... | collective-permute-start | bytes 1769480 | tf_op jit(solution)/shard_map/ppermute | solution.py:748
  61.0 11.7 %collective-permute-start.12 = (bf16[192,2304]{1,0:T(8,128)(2,1)}, bf16[192,2304]{1,0:T(8,128)(2,1)S(1)}, u32[]{:S(2)}, u32[]{:S(2)}) collective-permute-start(bf16[192,2304]{1,0:T(8,128)(2,1)} %constant_dynamic-update-slice_fusion.2.refs_5_.refs_9_.refs_13_), channel_id=1, source_target_pairs={{0,1},{1,0},{2,3},{3,2},{4,5},{5,4},{6,7},{7,6},{8,9},{9,8},{10,11... | collective-permute-start | bytes 2654216 | tf_op jit(solution)/shard_map/ppermute | solution.py:748
  66.1 20.3 %collective-permute-start.19 = (bf16[512,768]{1,0:T(8,128)(2,1)}, bf16[512,768]{1,0:T(8,128)(2,1)}, u32[]{:S(2)}, u32[]{:S(2)}) collective-permute-start(bf16[512,768]{1,0:T(8,128)(2,1)} %pad_maximum_fusion.2), channel_id=1, source_target_pairs={{0,2},{1,3},{2,0},{3,1},{4,6},{5,7},{6,4},{7,5},{8,10},{9,11},{10,... | collective-permute-start | bytes 2359304 | tf_op jit(solution)/shard_map/ppermute | solution.py:748
  106.7 9.2 %collective-permute-start.21 = (bf16[128,768]{1,0:T(8,128)(2,1)}, bf16[128,768]{1,0:T(8,128)(2,1)S(1)}, u32[]{:S(2)}, u32[]{:S(2)}) collective-permute-start(bf16[128,768]{1,0:T(8,128)(2,1)} %get-tuple-element.151), channel_id=1, source_target_pairs={{0,1},{1,0},{2,3},{3,2},{4,5},{5,4},{6,7},{7,6},{8,9},{9,8},{10,11... | collective-permute-start | bytes 589832 | tf_op jit(solution)/shard_map/ppermute | solution.py:748
  108.6 9.8 %collective-permute-start.23 = (bf16[128,768]{1,0:T(8,128)(2,1)}, bf16[128,768]{1,0:T(8,128)(2,1)S(1)}, u32[]{:S(2)}, u32[]{:S(2)}) collective-permute-start(bf16[128,768]{1,0:T(8,128)(2,1)} %get-tuple-element.153), channel_id=1, source_target_pairs={{0,3},{1,2},{2,1},{3,0},{4,7},{5,6},{6,5},{7,4},{8,11},{9,10},{10,... | collective-permute-start | bytes 589832 | tf_op jit(solution)/shard_map/ppermute | solution.py:748
  110.5 19.5 %collective-permute-start.27 = (bf16[384,768]{1,0:T(8,128)(2,1)}, bf16[384,768]{1,0:T(8,128)(2,1)}, u32[]{:S(2)}, u32[]{:S(2)}) collective-permute-start(bf16[384,768]{1,0:T(8,128)(2,1)} %slice.242), channel_id=1, source_target_pairs={{0,4},{4,0},{8,12},{12,8},{16,20},{20,16},{24,28},{28,24},{1,5},{5... | collective-permute-start | bytes 1769480 | tf_op jit(solution)/shard_map/ppermute | solution.py:748
  114.4 16.8 %collective-permute-start.26 = (bf16[192,1536]{1,0:T(8,128)(2,1)}, bf16[192,1536]{1,0:T(8,128)(2,1)}, u32[]{:S(2)}, u32[]{:S(2)}) collective-permute-start(bf16[192,1536]{1,0:T(8,128)(2,1)} %pad_maximum_fusion.3), channel_id=1, source_target_pairs={{0,2},{1,3},{2,0},{3,1},{4,6},{5,7},{6,4},{7,5},{8,10},{9,11},{10,... | collective-permute-start | bytes 1769480 | tf_op jit(solution)/shard_map/ppermute | solution.py:748
  140.4 24.3 %collective-permute-start.24 = (bf16[2,128,768]{2,1,0:T(8,128)(2,1)}, bf16[2,128,768]{2,1,0:T(8,128)(2,1)S(1)}, u32[]{:S(2)}, u32[]{:S(2)}) collective-permute-start(bf16[2,128,768]{2,1,0:T(8,128)(2,1)} %get-tuple-element.155), channel_id=1, source_target_pairs={{0,1},{1,0},{2,3},{3,2},{4,5},{5,4},{6,7},{7,6},{8,9},{9,8},{10,11... | collective-permute-start | bytes 1179656 | tf_op jit(solution)/shard_map/ppermute | solution.py:748
  142.0 16.9 %collective-permute-start.31 = (bf16[192,768]{1,0:T(8,128)(2,1)S(1)}, bf16[192,768]{1,0:T(8,128)(2,1)}, u32[]{:S(2)}, u32[]{:S(2)}) collective-permute-start(bf16[192,768]{1,0:T(8,128)(2,1)S(1)} %get-tuple-element.236), channel_id=1, source_target_pairs={{0,8},{4,12},{8,0},{12,4},{16,24},{20,28},{24,16},{28,20},{1,9},{5... | collective-permute-start | bytes 884744 | tf_op jit(solution)/shard_map/ppermute | solution.py:748
  143.5 17.1 %collective-permute-start.30 = (bf16[96,3072]{1,0:T(8,128)(2,1)S(1)}, bf16[96,3072]{1,0:T(8,128)(2,1)S(1)}, u32[]{:S(2)}, u32[]{:S(2)}) collective-permute-start(bf16[96,3072]{1,0:T(8,128)(2,1)S(1)} %slice.317), channel_id=1, source_target_pairs={{0,4},{4,0},{8,12},{12,8},{16,20},{20,16},{24,28},{28,24},{1,5},{5... | collective-permute-start | bytes 1769480 | tf_op jit(solution)/shard_map/ppermute | solution.py:748
  148.1 35.4 %collective-permute-start.33 = (bf16[192,3840]{1,0:T(8,128)(2,1)}, bf16[192,3840]{1,0:T(8,128)(2,1)}, u32[]{:S(2)}, u32[]{:S(2)}) collective-permute-start(bf16[192,3840]{1,0:T(8,128)(2,1)} %add_convert_fusion), channel_id=1, source_target_pairs={{0,2},{1,3},{2,0},{3,1},{4,6},{5,7},{6,4},{7,5},{8,10},{9,11},{10,... | collective-permute-start | bytes 4423688 | tf_op jit(solution)/shard_map/ppermute | solution.py:748
  161.5 40.4 %collective-permute-start.35 = (bf16[48,3072]{1,0:T(8,128)(2,1)}, bf16[48,3072]{1,0:T(8,128)(2,1)}, u32[]{:S(2)}, u32[]{:S(2)}) collective-permute-start(bf16[48,3072]{1,0:T(8,128)(2,1)} %get-tuple-element.234), channel_id=1, source_target_pairs={{0,8},{4,12},{8,0},{12,4},{16,24},{20,28},{24,16},{28,20},{1,9},{5... | collective-permute-start | bytes 884744 | tf_op jit(solution)/shard_map/ppermute | solution.py:748
  163.3 35.4 %collective-permute-start.36 = (bf16[96,768]{1,0:T(8,128)(2,1)}, bf16[96,768]{1,0:T(8,128)(2,1)}, u32[]{:S(2)}, u32[]{:S(2)}) collective-permute-start(bf16[96,768]{1,0:T(8,128)(2,1)} %add_convert_fusion.25), channel_id=1, source_target_pairs={{0,16},{4,20},{8,24},{12,28},{16,0},{20,4},{24,8},{28,12},{1,17},{... | collective-permute-start | bytes 442376 | tf_op jit(solution)/shard_map/ppermute | solution.py:748
  165.5 31.4 %collective-permute-start.29 = (bf16[128,768]{1,0:T(8,128)(2,1)}, bf16[128,768]{1,0:T(8,128)(2,1)}, u32[]{:S(2)}, u32[]{:S(2)}) collective-permute-start(bf16[128,768]{1,0:T(8,128)(2,1)} %fusion.7), channel_id=1, source_target_pairs={{0,2},{1,3},{2,0},{3,1},{4,6},{5,7},{6,4},{7,5},{8,10},{9,11},{10,... | collective-permute-start | bytes 589832 | tf_op jit(solution)/shard_map/ppermute | solution.py:748
  174.0 19.7 %collective-permute-start.32 = (bf16[384,2304]{1,0:T(8,128)(2,1)}, bf16[384,2304]{1,0:T(8,128)(2,1)}, u32[]{:S(2)}, u32[]{:S(2)}) collective-permute-start(bf16[384,2304]{1,0:T(8,128)(2,1)} %get-tuple-element.184), channel_id=1, source_target_pairs={{0,1},{1,0},{2,3},{3,2},{4,5},{5,4},{6,7},{7,6},{8,9},{9,8},{10,11... | collective-permute-start | bytes 5308424 | tf_op jit(solution)/shard_map/ppermute | solution.py:748
  187.0 17.6 %collective-permute-start.39 = (bf16[96,3840]{1,0:T(8,128)(2,1)}, bf16[96,3840]{1,0:T(8,128)(2,1)}, u32[]{:S(2)}, u32[]{:S(2)}) collective-permute-start(bf16[96,3840]{1,0:T(8,128)(2,1)} %get-tuple-element.230), channel_id=1, source_target_pairs={{0,4},{4,0},{8,12},{12,8},{16,20},{20,16},{24,28},{28,24},{1,5},{5... | collective-permute-start | bytes 2211848 | tf_op jit(solution)/shard_map/ppermute | solution.py:748
  195.2 20.8 %collective-permute-start.34 = (bf16[192,2304]{1,0:T(8,128)(2,1)S(1)}, bf16[192,2304]{1,0:T(8,128)(2,1)S(1)}, u32[]{:S(2)}, u32[]{:S(2)}) collective-permute-start(bf16[192,2304]{1,0:T(8,128)(2,1)S(1)} %add_convert_fusion.1), channel_id=1, source_target_pairs={{0,2},{1,3},{2,0},{3,1},{4,6},{5,7},{6,4},{7,5},{8,10},{9,11},{10,... | collective-permute-start | bytes 2654216 | tf_op jit(solution)/shard_map/ppermute | solution.py:748
  199.7 12.5 %collective-permute-start.38 = (bf16[96,768]{1,0:T(8,128)(2,1)S(1)}, bf16[96,768]{1,0:T(8,128)(2,1)S(1)}, u32[]{:S(2)}, u32[]{:S(2)}) collective-permute-start(bf16[96,768]{1,0:T(8,128)(2,1)S(1)} %add_convert_fusion.23), channel_id=1, source_target_pairs={{0,16},{4,20},{8,24},{12,28},{16,0},{20,4},{24,8},{28,12},{1,17},{... | collective-permute-start | bytes 442376 | tf_op jit(solution)/shard_map/ppermute | solution.py:748
  202.8 11.5 %collective-permute-start.37 = (bf16[24,3072]{1,0:T(8,128)(2,1)S(1)}, bf16[24,3072]{1,0:T(8,128)(2,1)S(1)}, u32[]{:S(2)}, u32[]{:S(2)}) collective-permute-start(bf16[24,3072]{1,0:T(8,128)(2,1)S(1)} %add_convert_fusion.21), channel_id=1, source_target_pairs={{0,16},{4,20},{8,24},{12,28},{16,0},{20,4},{24,8},{28,12},{1,17},{... | collective-permute-start | bytes 442376 | tf_op jit(solution)/shard_map/ppermute | solution.py:748
  205.9 20.7 %collective-permute-start.41 = (bf16[48,3840]{1,0:T(8,128)(2,1)S(1)}, bf16[48,3840]{1,0:T(8,128)(2,1)S(1)}, u32[]{:S(2)}, u32[]{:S(2)}) collective-permute-start(bf16[48,3840]{1,0:T(8,128)(2,1)S(1)} %get-tuple-element.246), channel_id=1, source_target_pairs={{0,8},{4,12},{8,0},{12,4},{16,24},{20,28},{24,16},{28,20},{1,9},{5... | collective-permute-start | bytes 1105928 | tf_op jit(solution)/shard_map/ppermute | solution.py:748
  212.3 22.4 %collective-permute-start.44 = (bf16[192,768]{1,0:T(8,128)(2,1)S(1)}, bf16[192,768]{1,0:T(8,128)(2,1)S(1)}, u32[]{:S(2)}, u32[]{:S(2)}) collective-permute-start(bf16[192,768]{1,0:T(8,128)(2,1)S(1)} %pad_maximum_fusion.10), channel_id=1, source_target_pairs={{0,8},{4,12},{8,0},{12,4},{16,24},{20,28},{24,16},{28,20},{1,9},{5... | collective-permute-start | bytes 884744 | tf_op jit(solution)/shard_map/ppermute | solution.py:748
  215.3 20.4 %collective-permute-start.43 = (bf16[24,3072]{1,0:T(8,128)(2,1)S(1)}, bf16[24,3072]{1,0:T(8,128)(2,1)S(1)}, u32[]{:S(2)}, u32[]{:S(2)}) collective-permute-start(bf16[24,3072]{1,0:T(8,128)(2,1)S(1)} %add_convert_fusion.20), channel_id=1, source_target_pairs={{0,16},{4,20},{8,24},{12,28},{16,0},{20,4},{24,8},{28,12},{1,17},{... | collective-permute-start | bytes 442376 | tf_op jit(solution)/shard_map/ppermute | solution.py:748
  217.6 13.2 %collective-permute-start.45 = (bf16[96,2304]{1,0:T(8,128)(2,1)S(1)}, bf16[96,2304]{1,0:T(8,128)(2,1)S(1)}, u32[]{:S(2)}, u32[]{:S(2)}) collective-permute-start(bf16[96,2304]{1,0:T(8,128)(2,1)S(1)} %get-tuple-element.232), channel_id=1, source_target_pairs={{0,4},{4,0},{8,12},{12,8},{16,20},{20,16},{24,28},{28,24},{1,5},{5... | collective-permute-start | bytes 1327112 | tf_op jit(solution)/shard_map/ppermute | solution.py:748
  218.3 29.3 %collective-permute-start.40 = (bf16[512,768]{1,0:T(8,128)(2,1)S(1)}, bf16[512,768]{1,0:T(8,128)(2,1)S(1)}, u32[]{:S(2)}, u32[]{:S(2)}) collective-permute-start(bf16[512,768]{1,0:T(8,128)(2,1)S(1)} %slice.280), channel_id=1, source_target_pairs={{0,4},{4,0},{8,12},{12,8},{16,20},{20,16},{24,28},{28,24},{1,5},{5... | collective-permute-start | bytes 2359304 | tf_op jit(solution)/shard_map/ppermute | solution.py:748
  226.7 9.2 %collective-permute-start.42 = (bf16[24,3840]{1,0:T(8,128)(2,1)S(1)}, bf16[24,3840]{1,0:T(8,128)(2,1)S(1)}, u32[]{:S(2)}, u32[]{:S(2)}) collective-permute-start(bf16[24,3840]{1,0:T(8,128)(2,1)S(1)} %add_convert_fusion.18), channel_id=1, source_target_pairs={{0,16},{4,20},{8,24},{12,28},{16,0},{20,4},{24,8},{28,12},{1,17},{... | collective-permute-start | bytes 552968 | tf_op jit(solution)/shard_map/ppermute | solution.py:748
  230.9 18.6 %collective-permute-start.49 = (bf16[48,2304]{1,0:T(8,128)(2,1)S(1)}, bf16[48,2304]{1,0:T(8,128)(2,1)S(1)}, u32[]{:S(2)}, u32[]{:S(2)}) collective-permute-start(bf16[48,2304]{1,0:T(8,128)(2,1)S(1)} %get-tuple-element.256), channel_id=1, source_target_pairs={{0,8},{4,12},{8,0},{12,4},{16,24},{20,28},{24,16},{28,20},{1,9},{5... | collective-permute-start | bytes 663560 | tf_op jit(solution)/shard_map/ppermute | solution.py:748
  234.8 42.6 %collective-permute-start.53 = (bf16[384,768]{1,0:T(8,128)(2,1)S(1)}, bf16[384,768]{1,0:T(8,128)(2,1)S(1)}, u32[]{:S(2)}, u32[]{:S(2)}) collective-permute-start(bf16[384,768]{1,0:T(8,128)(2,1)S(1)} %pad_maximum_fusion.4), channel_id=1, source_target_pairs={{0,4},{4,0},{8,12},{12,8},{16,20},{20,16},{24,28},{28,24},{1,5},{5... | collective-permute-start | bytes 1769480 | tf_op jit(solution)/shard_map/ppermute | solution.py:748
  235.8 15.3 %collective-permute-start.48 = (bf16[48,3072]{1,0:T(8,128)(2,1)S(1)}, bf16[48,3072]{1,0:T(8,128)(2,1)S(1)}, u32[]{:S(2)}, u32[]{:S(2)}) collective-permute-start(bf16[48,3072]{1,0:T(8,128)(2,1)S(1)} %pad_maximum_fusion.11), channel_id=1, source_target_pairs={{0,8},{4,12},{8,0},{12,4},{16,24},{20,28},{24,16},{28,20},{1,9},{5... | collective-permute-start | bytes 884744 | tf_op jit(solution)/shard_map/ppermute | solution.py:748
  236.0 16.0 %collective-permute-start.47 = (bf16[24,3840]{1,0:T(8,128)(2,1)S(1)}, bf16[24,3840]{1,0:T(8,128)(2,1)S(1)}, u32[]{:S(2)}, u32[]{:S(2)}) collective-permute-start(bf16[24,3840]{1,0:T(8,128)(2,1)S(1)} %add_convert_fusion.17), channel_id=1, source_target_pairs={{0,16},{4,20},{8,24},{12,28},{16,0},{20,4},{24,8},{28,12},{1,17},{... | collective-permute-start | bytes 552968 | tf_op jit(solution)/shard_map/ppermute | solution.py:748
  247.9 14.7 %collective-permute-start.46 = (bf16[256,768]{1,0:T(8,128)(2,1)S(1)}, bf16[256,768]{1,0:T(8,128)(2,1)S(1)}, u32[]{:S(2)}, u32[]{:S(2)}) collective-permute-start(bf16[256,768]{1,0:T(8,128)(2,1)S(1)} %slice.329), channel_id=1, source_target_pairs={{0,8},{4,12},{8,0},{12,4},{16,24},{20,28},{24,16},{28,20},{1,9},{5... | collective-permute-start | bytes 1179656 | tf_op jit(solution)/shard_map/ppermute | solution.py:748
  249.5 13.2 %collective-permute-start.51 = (bf16[24,2304]{1,0:T(8,128)(2,1)S(1)}, bf16[24,2304]{1,0:T(8,128)(2,1)S(1)}, u32[]{:S(2)}, u32[]{:S(2)}) collective-permute-start(bf16[24,2304]{1,0:T(8,128)(2,1)S(1)} %add_convert_fusion.28), channel_id=1, source_target_pairs={{0,16},{4,20},{8,24},{12,28},{16,0},{20,4},{24,8},{28,12},{1,17},{... | collective-permute-start | bytes 331784 | tf_op jit(solution)/shard_map/ppermute | solution.py:748
  251.3 27.7 %collective-permute-start.56 = (bf16[96,3072]{1,0:T(8,128)(2,1)S(1)}, bf16[96,3072]{1,0:T(8,128)(2,1)S(1)}, u32[]{:S(2)}, u32[]{:S(2)}) collective-permute-start(bf16[96,3072]{1,0:T(8,128)(2,1)S(1)} %pad_maximum_fusion.5.own_ref), channel_id=1, source_target_pairs={{0,4},{4,0},{8,12},{12,8},{16,20},{20,16},{24,28},{28,24},{1,5},{5... | collective-permute-start | bytes 1769480 | tf_op jit(solution)/shard_map/ppermute | solution.py:748
  252.0 21.9 %collective-permute-start.54 = (bf16[48,3840]{1,0:T(8,128)(2,1)S(1)}, bf16[48,3840]{1,0:T(8,128)(2,1)S(1)}, u32[]{:S(2)}, u32[]{:S(2)}) collective-permute-start(bf16[48,3840]{1,0:T(8,128)(2,1)S(1)} %pad_maximum_fusion.9), channel_id=1, source_target_pairs={{0,8},{4,12},{8,0},{12,4},{16,24},{20,28},{24,16},{28,20},{1,9},{5... | collective-permute-start | bytes 1105928 | tf_op jit(solution)/shard_map/ppermute | solution.py:748
  262.7 10.4 %collective-permute-start.50 = (bf16[128,768]{1,0:T(8,128)(2,1)S(1)}, bf16[128,768]{1,0:T(8,128)(2,1)S(1)}, u32[]{:S(2)}, u32[]{:S(2)}) collective-permute-start(bf16[128,768]{1,0:T(8,128)(2,1)S(1)} %slice.333), channel_id=1, source_target_pairs={{0,16},{4,20},{8,24},{12,28},{16,0},{20,4},{24,8},{28,12},{1,17},{... | collective-permute-start | bytes 589832 | tf_op jit(solution)/shard_map/ppermute | solution.py:748
  262.8 15.4 %collective-permute-start.52 = (bf16[24,2304]{1,0:T(8,128)(2,1)S(1)}, bf16[24,2304]{1,0:T(8,128)(2,1)S(1)}, u32[]{:S(2)}, u32[]{:S(2)}) collective-permute-start(bf16[24,2304]{1,0:T(8,128)(2,1)S(1)} %add_convert_fusion.26), channel_id=1, source_target_pairs={{0,16},{4,20},{8,24},{12,28},{16,0},{20,4},{24,8},{28,12},{1,17},{... | collective-permute-start | bytes 331784 | tf_op jit(solution)/shard_map/ppermute | solution.py:748
  275.2 15.4 %collective-permute-start.58 = (bf16[96,3840]{1,0:T(8,128)(2,1)}, bf16[96,3840]{1,0:T(8,128)(2,1)S(1)}, u32[]{:S(2)}, u32[]{:S(2)}) collective-permute-start(bf16[96,3840]{1,0:T(8,128)(2,1)} %pad_maximum_fusion.1), channel_id=1, source_target_pairs={{0,4},{4,0},{8,12},{12,8},{16,20},{20,16},{24,28},{28,24},{1,5},{5... | collective-permute-start | bytes 2211848 | tf_op jit(solution)/shard_map/ppermute | solution.py:748
  279.0 9.8 %collective-permute-start.55 = (bf16[48,2304]{1,0:T(8,128)(2,1)}, bf16[48,2304]{1,0:T(8,128)(2,1)}, u32[]{:S(2)}, u32[]{:S(2)}) collective-permute-start(bf16[48,2304]{1,0:T(8,128)(2,1)} %pad_maximum_fusion.12), channel_id=1, source_target_pairs={{0,8},{4,12},{8,0},{12,4},{16,24},{20,28},{24,16},{28,20},{1,9},{5... | collective-permute-start | bytes 663560 | tf_op jit(solution)/shard_map/ppermute | solution.py:748
  (60 other events, 328.5 us)
